TPU v7x, 32 devices: a whole 2x2x4 slice. The times are simulated.
32 devices in a mesh: wide: 8 (over y, x, core), narrow: 4 (over z).
Axes of the slice: x: 2, y: 2, z: 4, core: 2. Of those that a mesh axis runs over, the one named last changes fastest.
Arguments:
- tokens: bfloat16 [4096, 1024], P(('wide', 'narrow')), may hold values from -6 to 6
- log_decay: float32 [8, 4096], P(None, 'wide'), as said below
- lengths: int32 [1], replicated, may hold values from 1024 to 4096, as said below
- pad_counts: int32 [1], replicated, may hold values from 0 to 255
- w_query: bfloat16 [1024, 1024], replicated, may hold values from -0.1875 to 0.1875
- w_key: bfloat16 [1024, 1024], replicated, may hold values from -0.1875 to 0.1875
- w_value: bfloat16 [1024, 1024], replicated, may hold values from -0.1875 to 0.1875
- w_gate: bfloat16 [1024, 1024], replicated, may hold values from -0.1875 to 0.1875
- w_out: bfloat16 [1024, 1024], replicated, may hold values from -0.375 to 0.375
- w_first: bfloat16 [1024, 2816], P(None, 'narrow'), may hold values from -0.1875 to 0.1875
- w_second: bfloat16 [1024, 2816], P(None, 'narrow'), may hold values from -0.1875 to 0.1875
- w_third: bfloat16 [2816, 1024], P('narrow'), may hold values from -0.109375 to 0.109375
- cotangent: bfloat16 [4096, 1024], P(('wide', 'narrow')), may hold values from -6 to 6
Outputs:
- output: bfloat16 [4096, 1024], P(('wide', 'narrow'))
- grad_tokens: float32 [4096, 1024], P(('wide', 'narrow'))
- grad_w_query: float32 [1024, 1024], replicated
- grad_w_key: float32 [1024, 1024], replicated
- grad_w_value: float32 [1024, 1024], replicated
- grad_w_gate: float32 [1024, 1024], replicated
- grad_w_out: float32 [1024, 1024], replicated
- grad_w_first: float32 [1024, 2816], P(None, 'narrow')
- grad_w_second: float32 [1024, 2816], P(None, 'narrow')
- grad_w_third: float32 [2816, 1024], P('narrow')
Inputs may be any that keep to these rules, and one draw needn't show every extreme that they name: `lengths`: multiples of 256 that sum to 4096; the longest is exactly 4096. `log_decay`: strictly negative.
All inputs are finite; a program needn't handle non-finite values.
Results may differ from a plain program's by a relative error of at most 0.017.
Values may be sent and summed in bfloat16 or wider, within the bound.
No kernel may reach another device: no remote copies, remote signals or barrier semaphores. Data moves between devices by JAX's collectives and lax.ppermute only.
A program may use at most 192 MiB of HBM per device.

v0:
```python
import jax
import jax.numpy as jnp
from jax import lax
from jax.sharding import PartitionSpec as P

BLOCK = 256
LONGEST = 8192


epsilon = 1e-06
precise = lax.Precision.HIGHEST


def from_behind(block, axis, distance):
    devices = range(lax.axis_size(axis))
    route = [(i - distance, i) for i in devices if i - distance in devices]
    return lax.ppermute(block, axis, route)


def rms_norm(values):
    return values * lax.rsqrt(jnp.mean(values * values, axis=-1, keepdims=True) + epsilon)


def rms_back(values, gradient):
    inverse_rms = lax.rsqrt(jnp.mean(values * values, axis=-1, keepdims=True) + epsilon)
    normed = values * inverse_rms
    return inverse_rms * (gradient - normed * jnp.mean(gradient * normed, axis=-1, keepdims=True))


def silu_slope(values):
    squashed = jax.nn.sigmoid(values)
    return squashed * (1.0 + values * (1.0 - squashed))


def token_layout(lengths, pad_counts, anchor, total_rows):
    ends = jnp.cumsum(lengths, dtype=jnp.int32)
    starts = ends - lengths
    position = anchor + jnp.arange(total_rows, dtype=jnp.int32)
    inside = (position[:, None] >= starts[None, :]) & (position[:, None] < ends[None, :])
    limit = jnp.sum(jnp.where(inside, (ends - pad_counts)[None, :], 0), axis=1, dtype=jnp.int32)
    live = (position < limit).astype(jnp.float32)
    opening = jnp.any(position[:, None] == starts[None, :], axis=1).astype(jnp.float32)
    return (live, opening)


def project(left_hand, right_hand):
    return jnp.dot(left_hand, right_hand, preferred_element_type=jnp.float32)


def weight_grad(left_hand, right_hand):
    return jnp.einsum("tc,td->cd", left_hand, right_hand, preferred_element_type=jnp.float32)


def transposed(left_hand, right_hand):
    return jnp.einsum("td,cd->tc", left_hand, right_hand, preferred_element_type=jnp.float32)


def to_blocks(values, head_count, block_len):
    row_count, model_width = values.shape
    shaped = values.reshape(
        row_count // block_len, block_len, head_count, model_width // head_count
    )
    return shaped.transpose(0, 2, 1, 3)


def from_blocks(values):
    block_count, head_count, block_len, head_size = values.shape
    return values.transpose(0, 2, 1, 3).reshape(block_count * block_len, head_count * head_size)


def body(
    tokens,
    log_decay,
    lengths,
    pad_counts,
    w_query,
    w_key,
    w_value,
    w_gate,
    w_out,
    w_first,
    w_second,
    w_third,
    cotangent,
):
    head_count = log_decay.shape[0]
    local_rows = log_decay.shape[1]
    share_rows = tokens.shape[0]
    block_len = BLOCK
    block_count = local_rows // block_len
    own_start = lax.axis_index("narrow") * share_rows
    live, opening = token_layout(
        lengths, pad_counts, lax.axis_index("wide") * local_rows, local_rows
    )
    keep_block = 1.0 - opening.reshape(block_count, block_len)[:, 0]
    whole_rows = lax.all_gather(tokens, "narrow", axis=0, tiled=True)
    normed_one = rms_norm(whole_rows.astype(jnp.float32)).astype(jnp.bfloat16)
    query_lin = project(normed_one, w_query)
    key_lin = project(normed_one, w_key)
    value_lin = project(normed_one, w_value)
    gate_act = jax.nn.sigmoid(project(normed_one, w_gate))
    query_blk = to_blocks(jax.nn.silu(query_lin).astype(jnp.bfloat16), head_count, block_len)
    key_blk = to_blocks(
        (jax.nn.silu(key_lin) * live[:, None]).astype(jnp.bfloat16), head_count, block_len
    )
    value_blk = to_blocks(value_lin.astype(jnp.bfloat16), head_count, block_len)
    cumulative = jnp.cumsum(
        log_decay.reshape(head_count, block_count, block_len), axis=2
    ).transpose(1, 0, 2)
    positions = jnp.arange(block_len, dtype=jnp.int32)
    causal = positions[:, None] >= positions[None, :]
    spread = cumulative[:, :, :, None] - cumulative[:, :, None, :]
    weights = jnp.where(causal, jnp.exp(jnp.where(causal, spread, 0.0)), 0.0)
    rise = jnp.exp(cumulative)
    tail = jnp.exp(cumulative[:, :, -1:] - cumulative)
    block_decay = jnp.exp(cumulative[:, :, -1]) * keep_block[:, None]
    query_float = query_blk.astype(jnp.float32)
    key_tail = key_blk.astype(jnp.float32) * tail[..., None]
    value_float = value_blk.astype(jnp.float32)
    contrib = jnp.einsum("bhsd,bhse->bhde", key_tail, value_float, precision=precise)

    def run_states(carry, inputs):
        decay_now, contrib_now = inputs
        return (decay_now[:, None, None] * carry + contrib_now, carry)

    zero_state = jnp.zeros(contrib.shape[1:], jnp.float32)
    local_final, local_enter = lax.scan(run_states, zero_state, (block_decay, contrib))
    factor_all = jnp.prod(block_decay, axis=0)
    ones_row = jnp.ones((1, head_count), jnp.float32)
    prefix = jnp.cumprod(jnp.concatenate([ones_row, block_decay[:-1]], axis=0), axis=0)
    after_factor = jnp.flip(
        jnp.cumprod(jnp.flip(jnp.concatenate([block_decay[1:], ones_row], axis=0), 0), axis=0), 0
    )
    hop_count = min(lax.axis_size("wide") - 1, LONGEST // local_rows + 1)

    def relay_step(step_index, incoming):
        return from_behind(factor_all[:, None, None] * incoming + local_final, "wide", 1)

    incoming = lax.fori_loop(0, hop_count, relay_step, zero_state)
    entering = local_enter + prefix[:, :, None, None] * incoming[None]
    kept_enter = entering * keep_block[:, None, None, None]
    raw_scores = jnp.einsum(
        "bhtd,bhsd->bhts", query_blk, key_blk, preferred_element_type=jnp.float32
    )
    scores = (raw_scores * weights).astype(jnp.bfloat16)
    intra = jnp.einsum("bhts,bhsd->bhtd", scores, value_blk, preferred_element_type=jnp.float32)
    query_rise = query_float * rise[..., None]
    inter = jnp.einsum("bhtd,bhde->bhte", query_rise, kept_enter, precision=precise)
    attended = from_blocks(intra + inter)
    attn_normed = rms_norm(attended)
    gated = (attn_normed * gate_act).astype(jnp.bfloat16)
    gated_own = lax.dynamic_slice_in_dim(gated, own_start, share_rows, 0)
    hidden_state = tokens.astype(jnp.float32) + project(gated_own, w_out)
    normed_two = rms_norm(hidden_state).astype(jnp.bfloat16)
    gathered_two = lax.all_gather(normed_two, "narrow", axis=0, tiled=True)
    first_lin = project(gathered_two, w_first)
    second_lin = project(gathered_two, w_second)
    product = (first_lin * second_lin).astype(jnp.bfloat16)
    ffn_own = lax.psum_scatter(
        project(product, w_third).astype(jnp.bfloat16), "narrow", scatter_dimension=0, tiled=True
    ).astype(jnp.float32)
    output = (hidden_state + ffn_own).astype(jnp.bfloat16)
    grad_whole = lax.all_gather(cotangent, "narrow", axis=0, tiled=True)
    grad_w_third = weight_grad(product, grad_whole)
    grad_product = transposed(grad_whole, w_third)
    grad_first = (grad_product * second_lin).astype(jnp.bfloat16)
    grad_second = (grad_product * first_lin).astype(jnp.bfloat16)
    grad_w_first = weight_grad(gathered_two, grad_first)
    grad_w_second = weight_grad(gathered_two, grad_second)
    grad_normed_two = lax.psum_scatter(
        transposed(grad_first, w_first) + transposed(grad_second, w_second),
        "narrow",
        scatter_dimension=0,
        tiled=True,
    )
    grad_hidden = cotangent.astype(jnp.float32) + rms_back(hidden_state, grad_normed_two)
    grad_hidden_low = grad_hidden.astype(jnp.bfloat16)
    grad_hidden_whole = lax.all_gather(grad_hidden_low, "narrow", axis=0, tiled=True)
    grad_gated = transposed(grad_hidden_whole, w_out)
    grad_gate_lin = (grad_gated * attn_normed * gate_act * (1.0 - gate_act)).astype(jnp.bfloat16)
    grad_attended = rms_back(attended, grad_gated * gate_act).astype(jnp.bfloat16)
    grad_blk = to_blocks(grad_attended, head_count, block_len)
    grad_float = grad_blk.astype(jnp.float32)
    grad_value = jnp.einsum("bhts,bhtd->bhsd", scores, grad_blk, preferred_element_type=jnp.float32)
    grad_raw = (
        jnp.einsum("bhtd,bhsd->bhts", grad_blk, value_blk, preferred_element_type=jnp.float32)
        * weights
    ).astype(jnp.bfloat16)
    grad_query = jnp.einsum(
        "bhts,bhsd->bhtd", grad_raw, key_blk, preferred_element_type=jnp.float32
    )
    grad_key = jnp.einsum(
        "bhts,bhtd->bhsd", grad_raw, query_blk, preferred_element_type=jnp.float32
    )
    grad_query = grad_query + rise[..., None] * jnp.einsum(
        "bhte,bhde->bhtd", grad_float, kept_enter, precision=precise
    )
    enter_direct = keep_block[:, None, None, None] * jnp.einsum(
        "bhtd,bhte->bhde", query_rise, grad_float, precision=precise
    )

    def back_states(carry, inputs):
        decay_now, direct_now = inputs
        return (direct_now + decay_now[:, None, None] * carry, carry)

    local_first, local_after = lax.scan(
        back_states, zero_state, (block_decay, enter_direct), reverse=True
    )
    hop_count = min(lax.axis_size("wide") - 1, LONGEST // local_rows + 1)

    def relay_back(step_index, arriving):
        return from_behind(
            (factor_all[:, None, None] * arriving + local_first).astype(jnp.bfloat16), "wide", -1
        ).astype(jnp.float32)

    arriving = lax.fori_loop(0, hop_count, relay_back, zero_state)
    grad_contrib = local_after + after_factor[:, :, None, None] * arriving[None]
    grad_key = grad_key + tail[..., None] * jnp.einsum(
        "bhse,bhde->bhsd", value_float, grad_contrib, precision=precise
    )
    grad_value = grad_value + jnp.einsum(
        "bhsd,bhde->bhse", key_tail, grad_contrib, precision=precise
    )
    grad_query_lin = (from_blocks(grad_query) * silu_slope(query_lin)).astype(jnp.bfloat16)
    grad_key_lin = (from_blocks(grad_key) * live[:, None] * silu_slope(key_lin)).astype(
        jnp.bfloat16
    )
    grad_value_lin = from_blocks(grad_value).astype(jnp.bfloat16)
    grad_normed_one = (
        transposed(grad_query_lin, w_query)
        + transposed(grad_key_lin, w_key)
        + transposed(grad_value_lin, w_value)
        + transposed(grad_gate_lin, w_gate)
    )
    grad_own = lax.dynamic_slice_in_dim(grad_normed_one, own_start, share_rows, 0)
    grad_tokens = grad_hidden + rms_back(tokens.astype(jnp.float32), grad_own)
    summed = (
        lax.psum(weight_grad(normed_one, grad_query_lin).astype(jnp.bfloat16), "wide").astype(
            jnp.float32
        ),
        lax.psum(weight_grad(normed_one, grad_key_lin).astype(jnp.bfloat16), "wide").astype(
            jnp.float32
        ),
        lax.psum(weight_grad(normed_one, grad_value_lin).astype(jnp.bfloat16), "wide").astype(
            jnp.float32
        ),
        lax.psum(weight_grad(normed_one, grad_gate_lin).astype(jnp.bfloat16), "wide").astype(
            jnp.float32
        ),
        lax.psum(weight_grad(gated, grad_hidden_whole).astype(jnp.bfloat16), "wide").astype(
            jnp.float32
        ),
        lax.psum(grad_w_first.astype(jnp.bfloat16), "wide").astype(jnp.float32),
        lax.psum(grad_w_second.astype(jnp.bfloat16), "wide").astype(jnp.float32),
        lax.psum(grad_w_third.astype(jnp.bfloat16), "wide").astype(jnp.float32),
    )
    mixer_total = summed[:5]
    glu_total = summed[5:]
    return (
        output,
        grad_tokens,
        mixer_total[0],
        mixer_total[1],
        mixer_total[2],
        mixer_total[3],
        mixer_total[4],
        glu_total[0],
        glu_total[1],
        glu_total[2],
    )


def solution(mesh):
    in_specs = (
        P(("wide", "narrow"), None),
        P(None, "wide"),
        P(),
        P(),
        P(),
        P(),
        P(),
        P(),
        P(),
        P(None, "narrow"),
        P(None, "narrow"),
        P("narrow", None),
        P(("wide", "narrow"), None),
    )
    out_specs = (
        P(("wide", "narrow"), None),
        P(("wide", "narrow"), None),
        P(),
        P(),
        P(),
        P(),
        P(),
        P(None, "narrow"),
        P(None, "narrow"),
        P("narrow", None),
    )
    return jax.shard_map(body, mesh=mesh, in_specs=in_specs, out_specs=out_specs, check_vma=False)
```

profile of v0, /device:TPU:0, one launch (start us, length us, event | category | flops | bytes accessed | tf_op | source)
XLA Modules:
  0.0 669.9 jit_solution(619893740103989016)
XLA Ops:
  12.5 27.8 %all-gather.5.cloned.1.call-done = bf16[512,1024]{1,0:T(8,128)(2,1)} async-done(((bf16[128,1024]{1,0:T(8,128)(2,1)}), bf16[512,1024]{1,0:T(8,128)(2,1)}) %all-gather.5.cloned.1.call-update) | async-done | bytes 1048592 | tf_op jit(solution)/shard_map/all_gather | solution.py:96
  41.8 3.2 fusion.96
  48.4 2.4 copy.127
  50.8 3.2 fusion.94
  59.9 3.5 fusion.12
  64.6 4.0 while.52
  68.6 2.4 copy.107
  71.0 3.1 multiply_convert_fusion.1
  76.3 73.8 %while.51 = (s32[]{:T(128)}, f32[8,128,128]{2,1,0:T(8,128)S(1)}, f32[8]{0:T(128)S(1)}, f32[8,128,128]{2,1,0:T(8,128)S(1)}, s32[]{:T(128)}) while((s32[]{:T(128)}, f32[8,128,128]{2,1,0:T(8,128)S(1)}, f32[8]{0:T(128)S(1)}, f32[8,128,128]{2,1,0:T(8,128)S(1)}, s32[]{:T(128)}) %tuple.105), condition=%wide.region_8.9_spmd, body=%wide.region_7.8_spmd.sunk | while | flops 262146 | bytes 3670149 | solution.py:139
  81.2 8.8 %collective-permute-start = (f32[8,128,128]{2,1,0:T(8,128)}, f32[8,128,128]{2,1,0:T(8,128)S(1)}, u32[]{:S(2)}, u32[]{:S(2)}) collective-permute-start(f32[8,128,128]{2,1,0:T(8,128)} %multiply_add_fusion.6), channel_id=1, source_target_pairs={{0,4},{4,8},{8,12},{12,16},{16,20},{20,24},{24,28},{1,5},{5,9},{9,... | collective-permute-start | bytes 1572872 | tf_op jit(solution)/shard_map/while/body/eval_jaxpr/ppermute | solution.py:17
  92.6 9.0 %collective-permute-start = (f32[8,128,128]{2,1,0:T(8,128)}, f32[8,128,128]{2,1,0:T(8,128)S(1)}, u32[]{:S(2)}, u32[]{:S(2)}) collective-permute-start(f32[8,128,128]{2,1,0:T(8,128)} %multiply_add_fusion.6), channel_id=1, source_target_pairs={{0,4},{4,8},{8,12},{12,16},{16,20},{20,24},{24,28},{1,5},{5,9},{9,... | collective-permute-start | bytes 1572872 | tf_op jit(solution)/shard_map/while/body/eval_jaxpr/ppermute | solution.py:17
  104.2 9.0 %collective-permute-start = (f32[8,128,128]{2,1,0:T(8,128)}, f32[8,128,128]{2,1,0:T(8,128)S(1)}, u32[]{:S(2)}, u32[]{:S(2)}) collective-permute-start(f32[8,128,128]{2,1,0:T(8,128)} %multiply_add_fusion.6), channel_id=1, source_target_pairs={{0,4},{4,8},{8,12},{12,16},{16,20},{20,24},{24,28},{1,5},{5,9},{9,... | collective-permute-start | bytes 1572872 | tf_op jit(solution)/shard_map/while/body/eval_jaxpr/ppermute | solution.py:17
  115.8 9.0 %collective-permute-start = (f32[8,128,128]{2,1,0:T(8,128)}, f32[8,128,128]{2,1,0:T(8,128)S(1)}, u32[]{:S(2)}, u32[]{:S(2)}) collective-permute-start(f32[8,128,128]{2,1,0:T(8,128)} %multiply_add_fusion.6), channel_id=1, source_target_pairs={{0,4},{4,8},{8,12},{12,16},{16,20},{20,24},{24,28},{1,5},{5,9},{9,... | collective-permute-start | bytes 1572872 | tf_op jit(solution)/shard_map/while/body/eval_jaxpr/ppermute | solution.py:17
  127.4 9.0 %collective-permute-start = (f32[8,128,128]{2,1,0:T(8,128)}, f32[8,128,128]{2,1,0:T(8,128)S(1)}, u32[]{:S(2)}, u32[]{:S(2)}) collective-permute-start(f32[8,128,128]{2,1,0:T(8,128)} %multiply_add_fusion.6), channel_id=1, source_target_pairs={{0,4},{4,8},{8,12},{12,16},{16,20},{20,24},{24,28},{1,5},{5,9},{9,... | collective-permute-start | bytes 1572872 | tf_op jit(solution)/shard_map/while/body/eval_jaxpr/ppermute | solution.py:17
  139.0 9.0 %collective-permute-start = (f32[8,128,128]{2,1,0:T(8,128)}, f32[8,128,128]{2,1,0:T(8,128)S(1)}, u32[]{:S(2)}, u32[]{:S(2)}) collective-permute-start(f32[8,128,128]{2,1,0:T(8,128)} %multiply_add_fusion.6), channel_id=1, source_target_pairs={{0,4},{4,8},{8,12},{12,16},{16,20},{20,24},{24,28},{1,5},{5,9},{9,... | collective-permute-start | bytes 1572872 | tf_op jit(solution)/shard_map/while/body/eval_jaxpr/ppermute | solution.py:17
  150.2 6.0 multiply_reduce_fusion.1
  156.2 2.9 copy.119
  159.2 5.0 multiply_convert_fusion.4
  166.9 40.0 %all-gather.7.cloned.1.call-done = bf16[512,1024]{1,0:T(8,128)(2,1)} async-done(((bf16[128,1024]{1,0:T(8,128)(2,1)}), bf16[512,1024]{1,0:T(8,128)(2,1)}) %all-gather.7.cloned.1.call-update) | async-done | bytes 1048592 | tf_op jit(solution)/shard_map/all_gather | solution.py:155
  206.9 3.9 fusion.100
  212.8 23.0 %all-gather.9.cloned.1.call-done = bf16[512,1024]{1,0:T(8,128)(2,1)} async-done(((bf16[128,1024]{1,0:T(8,128)(2,1)}), bf16[512,1024]{1,0:T(8,128)(2,1)}) %all-gather.9.cloned.1.call-update) | async-done | bytes 1048592 | tf_op jit(solution)/shard_map/all_gather | solution.py:163
  235.8 4.5 multiply_convert_fusion.7
  244.7 43.1 %reduce-scatter.5.cloned.1.call-done = f32[128,1024]{1,0:T(8,128)} async-done(((f32[512,1024]{1,0:T(8,128)}), f32[128,1024]{1,0:T(8,128)}) %reduce-scatter.5.cloned.1.call-update) | async-done | bytes 524304 | tf_op jit(solution)/shard_map/reduce_scatter | solution.py:170
  292.5 3.6 convolution_convert_fusion.8
  296.3 3.7 convolution_convert_fusion.6
  304.1 14.3 %all-gather.11.cloned.1.call-done = bf16[512,1024]{1,0:T(8,128)(2,1)} async-done(((bf16[128,1024]{1,0:T(8,128)(2,1)}), bf16[512,1024]{1,0:T(8,128)(2,1)}) %all-gather.11.cloned.1.call-update) | async-done | bytes 1048592 | tf_op jit(solution)/shard_map/all_gather | solution.py:178
  318.4 6.1 multiply_reduce_fusion
  335.5 4.0 while.53
  339.6 67.9 %while.54 = (s32[]{:T(128)}, f32[8,128,128]{2,1,0:T(8,128)}, f32[8]{0:T(128)S(1)}, f32[8,128,128]{2,1,0:T(8,128)S(1)}, s32[]{:T(128)}, /*index=5*/s32[]{:T(128)}) while((s32[]{:T(128)}, f32[8,128,128]{2,1,0:T(8,128)}, f32[8]{0:T(128)S(1)}, f32[8,128,128]{2,1,0:T(8,128)S(1)}, s32[]{:T(128)}, /*index=5*/s32[]{:T(128)}) %tuple.129), condition=%wide.region_20.21_spmd.clone, body=%wide.region_19.20_spmd.clone.sunk | while | flops 655363 | bytes 3145879 | solution.py:216
  348.0 5.6 collective-permute-done.1
  357.7 6.6 collective-permute-done.1
  368.3 6.6 collective-permute-done.1
  378.9 6.6 collective-permute-done.1
  389.5 6.6 collective-permute-done.1
  400.0 6.6 collective-permute-done.1
  407.5 4.1 fusion.11
  422.5 2.6 convolution_convert_fusion
  425.1 2.7 convolution_convert_fusion.4
  428.7 2.7 convolution_convert_fusion.3
  431.4 2.7 convolution_convert_fusion.2
  434.1 2.7 convolution_convert_fusion.1
  437.9 2.9 fusion.106
  449.7 193.0 %all-reduce.4.cloned.1.call-done = (bf16[1024,1024]{1,0:T(8,128)(2,1)}, bf16[1024,1024]{1,0:T(8,128)(2,1)}, bf16[1024,1024]{1,0:T(8,128)(2,1)}, bf16[1024,1024]{...) async-done(((bf16[1024,1024]{1,0:T(8,128)(2,1)}, ...) | async-done | bytes 14811152 | tf_op jit(solution)/shard_map/psum | solution.py:238
  642.7 4.2 convert_element_type.176
  646.9 2.5 convert_element_type.178
  649.4 2.5 convert_element_type.180
  651.8 2.5 convert_element_type.182
  654.3 2.5 convert_element_type.184
  (317 shorter events, 130.9 us)
Async XLA Ops:
  7.2 152.0 %copy-start = (bf16[1024,1024]{1,0:T(8,128)(2,1)S(1)}, bf16[1024,1024]{1,0:T(8,128)(2,1)}, u32[]{:S(2)}) copy-start(bf16[1024,1024]{1,0:T(8,128)(2,1)} %param.28) | copy-start | bytes 6291460
  7.2 33.1 %all-gather.5.cloned.1.call-start = ((), (), s32[]{:S(2)}) async-start(), calls=%async_computation.2 | async-start | bytes 1310720 | tf_op jit(solution)/shard_map/all_gather | solution.py:96
  7.9 198.9 %all-gather.7.cloned.1.call-start = ((), (), s32[]{:S(2)}) async-start(), calls=%async_computation.3 | async-start | bytes 1310720 | tf_op jit(solution)/shard_map/all_gather | solution.py:155
  10.1 35.0 %copy-start.59 = (f32[8,2,2]{0,1,2:T(2,128)}, f32[8,2,2]{0,1,2:T(2,128)S(1)}, u32[]{:S(2)}) copy-start(f32[8,2,2]{0,1,2:T(2,128)S(1)} %copy.112) | copy-start | bytes 388
  11.5 138.7 %copy-start.70 = (f32[2]{0:T(128)}, f32[2]{0:T(128)S(1)}, u32[]{:S(2)}) copy-start(f32[2]{0:T(128)S(1)} %fusion.84) | copy-start | bytes 28
  11.6 59.4 %copy-start.57 = (f32[2,8,256]{2,1,0:T(8,128)}, f32[2,8,256]{2,1,0:T(8,128)S(1)}, u32[]{:S(2)}) copy-start(f32[2,8,256]{2,1,0:T(8,128)S(1)} %bitcast_bitcast_fusion.1) | copy-start | bytes 49156
  11.7 33.3 %copy-start.64 = (f32[2,8]{1,0:T(2,128)}, f32[2,8]{1,0:T(2,128)S(1)}, u32[]{:S(2)}) copy-start(f32[2,8]{1,0:T(2,128)S(1)} %slice_reduce_fusion) | copy-start | bytes 196
  12.4 137.8 %copy-start.65 = (f32[2,8]{1,0:T(2,128)}, f32[2,8]{1,0:T(2,128)S(1)}, u32[]{:S(2)}) copy-start(f32[2,8]{1,0:T(2,128)S(1)} %reduce_window.14) | copy-start | bytes 196
  12.4 41.6 %copy-start.62 = (f32[512]{0:T(512)}, f32[512]{0:T(512)S(1)}, u32[]{:S(2)}) copy-start(f32[512]{0:T(512)S(1)} %fusion.81) | copy-start | bytes 6148
  41.8 117.3 %copy-start.74 = (f32[512]{0:T(512)}, f32[512]{0:T(512)S(1)}, u32[]{:S(2)}) copy-start(f32[512]{0:T(512)S(1)} %add_rsqrt_fusion) | copy-start | bytes 6148
  58.8 4.6 copy-start.10
  68.6 5.5 copy-start.72
  77.2 3.0 collective-permute-start
  81.2 10.5 %collective-permute-start = (f32[8,128,128]{2,1,0:T(8,128)}, f32[8,128,128]{2,1,0:T(8,128)S(1)}, u32[]{:S(2)}, u32[]{:S(2)}) collective-permute-start(f32[8,128,128]{2,1,0:T(8,128)} %multiply_add_fusion.6), channel_id=1, source_target_pairs={{0,4},{4,8},{8,12},{12,16},{16,20},{20,24},{24,28},{1,5},{5,9},{9,... | collective-permute-start | bytes 1572872 | tf_op jit(solution)/shard_map/while/body/eval_jaxpr/ppermute | solution.py:17
  92.6 10.7 %collective-permute-start = (f32[8,128,128]{2,1,0:T(8,128)}, f32[8,128,128]{2,1,0:T(8,128)S(1)}, u32[]{:S(2)}, u32[]{:S(2)}) collective-permute-start(f32[8,128,128]{2,1,0:T(8,128)} %multiply_add_fusion.6), channel_id=1, source_target_pairs={{0,4},{4,8},{8,12},{12,16},{16,20},{20,24},{24,28},{1,5},{5,9},{9,... | collective-permute-start | bytes 1572872 | tf_op jit(solution)/shard_map/while/body/eval_jaxpr/ppermute | solution.py:17
  104.2 10.7 %collective-permute-start = (f32[8,128,128]{2,1,0:T(8,128)}, f32[8,128,128]{2,1,0:T(8,128)S(1)}, u32[]{:S(2)}, u32[]{:S(2)}) collective-permute-start(f32[8,128,128]{2,1,0:T(8,128)} %multiply_add_fusion.6), channel_id=1, source_target_pairs={{0,4},{4,8},{8,12},{12,16},{16,20},{20,24},{24,28},{1,5},{5,9},{9,... | collective-permute-start | bytes 1572872 | tf_op jit(solution)/shard_map/while/body/eval_jaxpr/ppermute | solution.py:17
  115.8 10.7 %collective-permute-start = (f32[8,128,128]{2,1,0:T(8,128)}, f32[8,128,128]{2,1,0:T(8,128)S(1)}, u32[]{:S(2)}, u32[]{:S(2)}) collective-permute-start(f32[8,128,128]{2,1,0:T(8,128)} %multiply_add_fusion.6), channel_id=1, source_target_pairs={{0,4},{4,8},{8,12},{12,16},{16,20},{20,24},{24,28},{1,5},{5,9},{9,... | collective-permute-start | bytes 1572872 | tf_op jit(solution)/shard_map/while/body/eval_jaxpr/ppermute | solution.py:17
  127.4 10.7 %collective-permute-start = (f32[8,128,128]{2,1,0:T(8,128)}, f32[8,128,128]{2,1,0:T(8,128)S(1)}, u32[]{:S(2)}, u32[]{:S(2)}) collective-permute-start(f32[8,128,128]{2,1,0:T(8,128)} %multiply_add_fusion.6), channel_id=1, source_target_pairs={{0,4},{4,8},{8,12},{12,16},{16,20},{20,24},{24,28},{1,5},{5,9},{9,... | collective-permute-start | bytes 1572872 | tf_op jit(solution)/shard_map/while/body/eval_jaxpr/ppermute | solution.py:17
  139.0 10.7 %collective-permute-start = (f32[8,128,128]{2,1,0:T(8,128)}, f32[8,128,128]{2,1,0:T(8,128)S(1)}, u32[]{:S(2)}, u32[]{:S(2)}) collective-permute-start(f32[8,128,128]{2,1,0:T(8,128)} %multiply_add_fusion.6), channel_id=1, source_target_pairs={{0,4},{4,8},{8,12},{12,16},{16,20},{20,24},{24,28},{1,5},{5,9},{9,... | collective-permute-start | bytes 1572872 | tf_op jit(solution)/shard_map/while/body/eval_jaxpr/ppermute | solution.py:17
  150.2 6.0 copy-start.55
  159.1 5.1 copy-start.60
  159.2 5.1 copy-start.16
  159.2 5.1 copy-start.25
  165.2 123.8 %copy-start.5 = (f32[128,1024]{1,0:T(8,128)}, f32[128,1024]{1,0:T(8,128)S(1)}, u32[]{:S(2)}) copy-start(f32[128,1024]{1,0:T(8,128)S(1)} %get-tuple-element.310) | copy-start | bytes 1572868
  165.2 123.8 %copy-start.68 = (f32[128]{0:T(128)}, f32[128]{0:T(128)S(1)}, u32[]{:S(2)}) copy-start(f32[128]{0:T(128)S(1)} %add_rsqrt_fusion.2) | copy-start | bytes 1540
  166.1 69.7 %all-gather.9.cloned.1.call-start = ((), (), s32[]{:S(2)}) async-start(), calls=%async_computation.5 | async-start | bytes 1310720 | tf_op jit(solution)/shard_map/all_gather | solution.py:163
  166.8 120.9 %reduce-scatter.5.cloned.1.call-start = ((), (), s32[]{:S(2)}) async-start(), calls=%async_computation.6 | async-start | bytes 2621440 | tf_op jit(solution)/shard_map/reduce_scatter | solution.py:170
  235.8 4.5 copy-start.83
  244.6 44.5 %copy-start.31 = (bf16[128,1024]{1,0:T(8,128)(2,1)S(1)}, bf16[128,1024]{1,0:T(8,128)(2,1)}, u32[]{:S(2)}) copy-start(bf16[128,1024]{1,0:T(8,128)(2,1)} %param.33) | copy-start | bytes 786436
  244.6 46.5 %copy-start.76 = (f32[1,8]{1,0:T(1,128)S(1)}, f32[1,8]{1,0:T(1,128)}, u32[]{:S(2)}) copy-start(f32[1,8]{1,0:T(1,128)} %get-tuple-element.303) | copy-start | bytes 100
  244.6 73.8 %all-gather.11.cloned.1.call-start = ((), (), s32[]{:S(2)}) async-start(), calls=%async_computation.7 | async-start | bytes 1310720 | tf_op jit(solution)/shard_map/all_gather | solution.py:178
  291.0 156.0 %reduce-scatter.3.cloned.1.call-start = ((), (), s32[]{:S(2)}) async-start(), calls=%async_computation.4 | async-start | bytes 1310720 | tf_op jit(solution)/shard_map/reduce_scatter | solution.py:159
  296.1 346.6 %all-reduce.4.cloned.1.call-start = ((), (), s32[]{:S(2)}) async-start(), calls=%async_computation.8 | async-start | bytes 29622272 | tf_op jit(solution)/shard_map/psum | solution.py:238
  302.0 16.4 %copy-start.61 = (f32[1,2,2,128]{3,1,2,0:T(2,128)S(1)}, f32[1,2,2,128]{3,1,2,0:T(2,128)}, u32[]{:S(2)}) copy-start(f32[1,2,2,128]{3,1,2,0:T(2,128)} %copy-done.60) | copy-start | bytes 6148
  318.4 6.1 copy-start.2
  325.3 5.0 copy-start.3
  339.6 67.9 %copy-start.67 = (f32[2,8]{1,0:T(2,128)S(1)}, f32[2,8]{1,0:T(2,128)}, u32[]{:S(2)}) copy-start(f32[2,8]{1,0:T(2,128)} %rev.8) | copy-start | bytes 196
  340.4 3.6 collective-permute-start.1
  346.7 6.9 %collective-permute-start.1 = (bf16[8,128,128]{2,1,0:T(8,128)(2,1)}, bf16[8,128,128]{2,1,0:T(8,128)(2,1)S(1)}, u32[]{:S(2)}, u32[]{:S(2)}) collective-permute-start(bf16[8,128,128]{2,1,0:T(8,128)(2,1)} %fusion.155), channel_id=1, source_target_pairs={{4,0},{8,4},{12,8},{16,12},{20,16},{24,20},{28,24},{5,1},{9,5},{13... | collective-permute-start | bytes 786440 | tf_op jit(solution)/shard_map/while/body/eval_jaxpr/ppermute | solution.py:17
  356.4 7.9 %collective-permute-start.1 = (bf16[8,128,128]{2,1,0:T(8,128)(2,1)}, bf16[8,128,128]{2,1,0:T(8,128)(2,1)S(1)}, u32[]{:S(2)}, u32[]{:S(2)}) collective-permute-start(bf16[8,128,128]{2,1,0:T(8,128)(2,1)} %fusion.155), channel_id=1, source_target_pairs={{4,0},{8,4},{12,8},{16,12},{20,16},{24,20},{28,24},{5,1},{9,5},{13... | collective-permute-start | bytes 786440 | tf_op jit(solution)/shard_map/while/body/eval_jaxpr/ppermute | solution.py:17
  367.0 7.9 %collective-permute-start.1 = (bf16[8,128,128]{2,1,0:T(8,128)(2,1)}, bf16[8,128,128]{2,1,0:T(8,128)(2,1)S(1)}, u32[]{:S(2)}, u32[]{:S(2)}) collective-permute-start(bf16[8,128,128]{2,1,0:T(8,128)(2,1)} %fusion.155), channel_id=1, source_target_pairs={{4,0},{8,4},{12,8},{16,12},{20,16},{24,20},{28,24},{5,1},{9,5},{13... | collective-permute-start | bytes 786440 | tf_op jit(solution)/shard_map/while/body/eval_jaxpr/ppermute | solution.py:17
  377.6 7.9 %collective-permute-start.1 = (bf16[8,128,128]{2,1,0:T(8,128)(2,1)}, bf16[8,128,128]{2,1,0:T(8,128)(2,1)S(1)}, u32[]{:S(2)}, u32[]{:S(2)}) collective-permute-start(bf16[8,128,128]{2,1,0:T(8,128)(2,1)} %fusion.155), channel_id=1, source_target_pairs={{4,0},{8,4},{12,8},{16,12},{20,16},{24,20},{28,24},{5,1},{9,5},{13... | collective-permute-start | bytes 786440 | tf_op jit(solution)/shard_map/while/body/eval_jaxpr/ppermute | solution.py:17
  388.2 7.9 %collective-permute-start.1 = (bf16[8,128,128]{2,1,0:T(8,128)(2,1)}, bf16[8,128,128]{2,1,0:T(8,128)(2,1)S(1)}, u32[]{:S(2)}, u32[]{:S(2)}) collective-permute-start(bf16[8,128,128]{2,1,0:T(8,128)(2,1)} %fusion.155), channel_id=1, source_target_pairs={{4,0},{8,4},{12,8},{16,12},{20,16},{24,20},{28,24},{5,1},{9,5},{13... | collective-permute-start | bytes 786440 | tf_op jit(solution)/shard_map/while/body/eval_jaxpr/ppermute | solution.py:17
  398.8 7.9 %collective-permute-start.1 = (bf16[8,128,128]{2,1,0:T(8,128)(2,1)}, bf16[8,128,128]{2,1,0:T(8,128)(2,1)S(1)}, u32[]{:S(2)}, u32[]{:S(2)}) collective-permute-start(bf16[8,128,128]{2,1,0:T(8,128)(2,1)} %fusion.155), channel_id=1, source_target_pairs={{4,0},{8,4},{12,8},{16,12},{20,16},{24,20},{28,24},{5,1},{9,5},{13... | collective-permute-start | bytes 786440 | tf_op jit(solution)/shard_map/while/body/eval_jaxpr/ppermute | solution.py:17
  407.5 4.1 copy-start.4
  407.5 4.1 copy-start.20
  413.2 18.2 %copy-start.51 = (bf16[2,256,8,128]{3,2,1,0:T(8,128)(2,1)}, bf16[2,256,8,128]{3,2,1,0:T(8,128)(2,1)S(1)}, u32[]{:S(2)}) copy-start(bf16[2,256,8,128]{3,2,1,0:T(8,128)(2,1)S(1)} %copy.126) | copy-start | bytes 3145732
  642.7 4.2 copy-start.35
  (61 other events, 128.8 us)
Sparse Core Ops, SparseCore 0:
  9.6 30.6 all-gather.4
  166.2 40.5 all-gather.6
  208.4 27.3 all-gather.8
  244.7 43.0 reduce-scatter.4
  291.1 27.1 all-gather.10
  320.5 26.6 reduce-scatter.2
  437.0 205.6 all-reduce.3
where the time goes:
time: 679 us; the launch traced here: 670 us
  waiting for transfers between devices  395 us (58%)
  matrix products  95.4 us (14%)
  other arithmetic  66.9 us (10%)
  starting transfers between devices  64.5 us (9%)
  local copies, waits for them, and re-layouts  30.2 us (4%)
  between operations  16.8 us (2%)
    psum x1, waiting for transfers between devices, body(): lax.psum(weight_grad(normed_one, grad_query_lin).astype(jnp.bfloat16), 'w...  193 us
    ppermute x14, starting transfers between devices, from_behind(): return lax.ppermute(block, axis, route)  64 us
    ppermute x14, waiting for transfers between devices, from_behind(): return lax.ppermute(block, axis, route)  52.8 us
    reduce_scatter x1, waiting for transfers between devices, body(): lax.psum_scatter(transposed(grad_first, w_first) + transposed(grad_second...  43.1 us
    all_gather x1, waiting for transfers between devices, body(): gathered_two = lax.all_gather(normed_two, 'narrow', axis=0, tiled=True)  40 us
    all_gather x1, waiting for transfers between devices, body(): whole_rows = lax.all_gather(tokens, 'narrow', axis=0, tiled=True)  27.8 us
    all_gather x1, waiting for transfers between devices, body(): grad_whole = lax.all_gather(cotangent, 'narrow', axis=0, tiled=True)  23 us
    dot_general x8, matrix products, project(): return jnp.dot(left_hand, right_hand, preferred_element_type=jnp.float32)  22.8 us
  transfers between devices with their start and end apart: 21, of which 20 were waited for; matrix products, arithmetic and copies ran while one was open for 14% of the time, Pallas kernels for 0%

commit v1 on v0

v1 whole, which is shorter than its diff:
```python
import functools

import jax
import jax.numpy as jnp
from jax import lax
from jax.experimental import pallas as pl
from jax.experimental.pallas import tpu as pltpu
from jax.sharding import PartitionSpec as P

BLOCK = 256
epsilon = 1e-06
bf16 = jnp.bfloat16
f32 = jnp.float32
SMEM = pl.BlockSpec(memory_space=pltpu.SMEM)
PARAMS = pltpu.CompilerParams(dimension_semantics=("arbitrary",), vmem_limit_bytes=56 << 20)


def mm(a, b):
    return lax.dot_general(a, b, (((1,), (0,)), ((), ())), preferred_element_type=f32)


def mt(a, b):
    return lax.dot_general(a, b, (((1,), (1,)), ((), ())), preferred_element_type=f32)


def tm(a, b):
    return lax.dot_general(a, b, (((0,), (0,)), ((), ())), preferred_element_type=f32)


def inv_rms(values):
    return lax.rsqrt(jnp.mean(values * values, axis=-1, keepdims=True) + epsilon)


def sigmoid(values):
    return 1.0 / (1.0 + jnp.exp(-values))


def slope(values):
    squashed = sigmoid(values)
    return squashed * (1.0 + values * (1.0 - squashed))


def rms_back(values, inverse, gradient):
    normed = values * inverse
    return inverse * (gradient - normed * jnp.mean(gradient * normed, axis=-1, keepdims=True))


def token_layout(lengths, pad_counts, anchor, total_rows):
    ends = jnp.cumsum(lengths, dtype=jnp.int32)
    starts = ends - lengths
    position = anchor + jnp.arange(total_rows, dtype=jnp.int32)
    inside = (position[:, None] >= starts[None, :]) & (position[:, None] < ends[None, :])
    limit = jnp.sum(jnp.where(inside, (ends - pad_counts)[None, :], 0), axis=1, dtype=jnp.int32)
    live = (position < limit).astype(f32)
    opening = jnp.any(position[:, None] == starts[None, :], axis=1).astype(f32)
    return (live, opening)


def whole(shape):
    zeros = (0,) * len(shape)
    return pl.BlockSpec(shape, lambda *_: zeros)


def rows(shape, index):
    rest = (0,) * (len(shape) - 1)
    return pl.BlockSpec(shape, lambda b: (index(b), *rest))


def decay_weights(g_col, g_row):
    size = g_col.shape[0]
    causal = lax.broadcasted_iota(jnp.int32, (size, size), 0) >= lax.broadcasted_iota(
        jnp.int32, (size, size), 1
    )
    return jnp.where(causal, jnp.exp(jnp.where(causal, g_col - g_row, 0.0)), 0.0)


def forward_kernel(hn, hd, decay, tok, wq, wk, wv, live, gcol, grow, tail,
                   n1, ql, kl, q, k, v, intra, contrib, final, state):
    b = pl.program_id(0)
    values = tok[...].astype(f32)
    normed = (values * inv_rms(values)).astype(bf16)
    n1[...] = normed
    q_lin = mm(normed, wq[...])
    k_lin = mm(normed, wk[...])
    ql[...] = q_lin
    kl[...] = k_lin
    q[...] = (q_lin * sigmoid(q_lin)).astype(bf16)
    k[...] = (k_lin * sigmoid(k_lin) * live[...]).astype(bf16)
    v[...] = mm(normed, wv[...]).astype(bf16)
    for h in range(hn):
        at = slice(h * hd, (h + 1) * hd)
        qh, kh, vh = q[:, at], k[:, at], v[:, at]
        weights = decay_weights(gcol[:, h : h + 1], grow[0, h : h + 1, :])
        scores = (mt(qh, kh) * weights).astype(bf16)
        intra[:, at] = mm(scores, vh)
        key_tail = (kh.astype(f32) * tail[:, h : h + 1]).astype(bf16)
        now = tm(key_tail, vh)
        contrib[0, h] = now
        before = jnp.where(b == 0, 0.0, state[h])
        state[h] = decay[b, h] * before + now
        final[h] = state[h].astype(bf16)


def attend_kernel(hn, hd, wide, decay, keep, coef, gathered, contrib, q, intra, rise,
                  att, kent, state):
    b = pl.program_id(0)
    for h in range(hn):
        @pl.when(b == 0)
        def _():
            total = coef[0, h] * gathered[0, h].astype(f32)
            for j in range(1, wide):
                total = total + coef[j, h] * gathered[j, h].astype(f32)
            state[h] = total
        at = slice(h * hd, (h + 1) * hd)
        entering = state[h]
        kept = (keep[b] * entering).astype(bf16)
        kent[0, h] = kept
        att[:, at] = (intra[:, at] + rise[:, h : h + 1] * mm(q[:, at], kept)).astype(bf16)
        state[h] = decay[b, h] * entering + contrib[0, h]


def join(parts):
    return jnp.concatenate([parts[i] for i in range(parts.shape[0])], axis=1)


def hidden_kernel(att, gate, tok, wo, hidden, n2):
    values = join(att).astype(f32)
    gated = (values * inv_rms(values) * gate[...]).astype(bf16)
    hid = tok[...].astype(f32) + mm(gated, wo[...])
    hidden[...] = hid
    n2[...] = (hid * inv_rms(hid)).astype(bf16)


def ffn_kernel(n2, cot, w1, w2, w3, product, gf, gs, gn2):
    normed = n2[...]
    first = mm(normed, w1[...])
    second = mm(normed, w2[...])
    product[...] = (first * second).astype(bf16)
    grad = mt(cot[...], w3[...])
    gf[...] = (grad * second).astype(bf16)
    gs[...] = (grad * first).astype(bf16)
    gn2[...] = (mt(gf[...], w1[...]) + mt(gs[...], w2[...])).astype(bf16)


def residual_kernel(parts, gn2, hidden, cot, wo, att, gate, grad_hidden, packed, ga, ggl):
    hid = hidden[...]
    gh = cot[...].astype(f32) + rms_back(hid, inv_rms(hid), gn2[...].astype(f32))
    grad_hidden[...] = gh
    low = gh.astype(bf16)
    width = low.shape[1]
    gg = mt(low, wo[...])
    values = join(att).astype(f32)
    inverse = inv_rms(values)
    act = gate[...]
    ggl[...] = (gg * (values * inverse) * act * (1.0 - act)).astype(bf16)
    back = rms_back(values, inverse, gg * act).astype(bf16)
    size = width // parts
    for i in range(parts):
        ga[i] = back[:, i * size : (i + 1) * size]
    packed[:, :width] = low
    high = inverse.astype(bf16)
    rest = inverse - high.astype(f32)
    middle = rest.astype(bf16)
    tailing = (rest - middle.astype(f32)).astype(bf16)
    lane = lax.broadcasted_iota(jnp.int32, (low.shape[0], 128), 1)
    spread = jnp.where(
        lane == 0, high.astype(f32), jnp.where(lane == 1, middle.astype(f32), tailing.astype(f32))
    )
    packed[:, width:] = spread.astype(bf16)


def query_kernel(hn, hd, blocks, decay, keep, ga, q, k, v, ql, kent, gcol, grow, rise,
                 dq, gk, gv, direct, first, state):
    i = pl.program_id(0)
    b = blocks - 1 - i
    for h in range(hn):
        at = slice(h * hd, (h + 1) * hd)
        g, qh, kh, vh = ga[:, at], q[:, at], k[:, at], v[:, at]
        weights = decay_weights(gcol[:, h : h + 1], grow[0, h : h + 1, :])
        scores = (mt(qh, kh) * weights).astype(bf16)
        raw = (mt(g, vh) * weights).astype(bf16)
        up = rise[:, h : h + 1]
        gq = mm(raw, kh) + up * mt(g, kent[0, h])
        dq[:, at] = (gq * slope(ql[:, at])).astype(bf16)
        gk[:, at] = tm(raw, qh)
        gv[:, at] = tm(scores, g)
        now = keep[b] * tm((qh.astype(f32) * up).astype(bf16), g)
        direct[0, h] = now
        after = jnp.where(i == 0, 0.0, state[h])
        state[h] = now + decay[b, h] * after
        first[h] = state[h].astype(bf16)


def spread(wide, own, source, keep, send, item):
    tall = source.shape[0] // wide
    for j in range(wide):
        at = pl.ds(pl.multiple_of((own ^ j) * tall, tall), tall)
        out = keep if j % 2 == 0 else send
        out[j // 2, item] = source[at, :].astype(bf16)


def key_kernel(hn, hd, wide, blocks, own, decay, coef, gathered, direct, n1, dq, k, v, kl, gk, gv,
               tail, live, wq, wk, wv, kept, sent, gn1, state, dk, dv, aq, ak, av):
    i = pl.program_id(0)
    b = blocks - 1 - i
    for h in range(hn):
        @pl.when(i == 0)
        def _():
            total = coef[0, h] * gathered[0, h].astype(f32)
            for j in range(1, wide):
                total = total + coef[j, h] * gathered[j, h].astype(f32)
            state[h] = total
        at = slice(h * hd, (h + 1) * hd)
        after = state[h]
        low = after.astype(bf16)
        down = tail[:, h : h + 1]
        grad_key = gk[:, at] + down * mt(v[:, at], low)
        dk[:, at] = (grad_key * live[...] * slope(kl[:, at])).astype(bf16)
        dv[:, at] = (gv[:, at] + down * mm(k[:, at], low)).astype(bf16)
        state[h] = direct[0, h] + decay[b, h] * after
    normed = n1[...]
    for item, (acc, part) in enumerate(((aq, dq), (ak, dk), (av, dv))):
        now = tm(normed, part[...])

        @pl.when(i == 0)
        def _():
            acc[...] = now

        @pl.when(i > 0)
        def _():
            acc[...] += now

        @pl.when(i == blocks - 1)
        def _():
            spread(wide, own[0], acc, kept, sent, item)

    gn1[...] = (mt(dq[...], wq[...]) + mt(dk[...], wk[...]) + mt(dv[...], wv[...])).astype(bf16)


def gate_kernel(wide, narrow, own, packed, att, n1, wg, wo, kept, sent, acc, acc_out):
    width = n1.shape[1]
    grads = packed[:, :width]
    extra = packed[:, width:].astype(f32)
    inverse = extra[:, 0:1] + extra[:, 1:2] + extra[:, 2:3]
    normed = n1[...]
    act = sigmoid(mm(normed, wg[...]))
    scaled = att[...].astype(f32) * inverse
    gated = (scaled * act).astype(bf16)
    gg = mt(grads, wo[...])
    ggl = (gg * scaled * act * (1.0 - act)).astype(bf16)
    acc[...] = tm(normed, ggl)
    spread(wide, own[0], acc, kept, sent, 0)
    acc_out[...] = tm(gated, grads)
    cols = gated.shape[1]
    short = cols // wide
    for j in range(wide):
        at = pl.ds(pl.multiple_of((own[0] ^ j) * short, short), short)
        out = kept if j % 2 == 0 else sent
        for i in range(narrow):
            out[j // 2, 1, i * short : (i + 1) * short, :] = acc_out[
                at, i * cols : (i + 1) * cols
            ].astype(bf16)


def ffn_grad_kernel(wide, own, n2, cot, product, gf, gs, kept, sent, acc):
    item = pl.program_id(0)
    for i, (left, right) in enumerate(((n2, gf), (n2, gs), (cot, product))):
        @pl.when(item == i)
        def _():
            acc[...] = tm(left[...], right[...])

    spread(wide, own[0], acc, kept, sent, 0)


def tokens_kernel(gn1, ggl, wg, tok, gh, out):
    grad = gn1[...].astype(f32) + mt(ggl[...], wg[...])
    values = tok[...].astype(f32)
    out[...] = gh[...] + rms_back(values, inv_rms(values), grad)


def exchange(values, bit):
    size = lax.axis_size("wide")
    return lax.ppermute(values, "wide", [(i, i ^ (1 << bit)) for i in range(size)])


def reduce_over_wide(kept, sent):
    bits = (lax.axis_size("wide") - 1).bit_length()
    total = kept + exchange(sent, 0)
    rest = total.shape[1:]
    half = rest[-2] // 2

    def run(part, order):
        part = part.reshape((2,) * (bits - 1) + part.shape[1:])
        left = list(range(bits - 1, 0, -1))
        for bit in order:
            axis = left.index(bit)
            mine = lax.index_in_dim(part, 0, axis, keepdims=False)
            part = mine + exchange(lax.index_in_dim(part, 1, axis, keepdims=False), bit)
            left.remove(bit)
        return part

    up = list(range(1, bits))
    return (run(total[..., :half, :], up), run(total[..., half:, :], up[::-1]))


def gather_over_wide(lower, upper):
    bits = (lax.axis_size("wide") - 1).bit_length()

    def run(part, order):
        full = part[None]
        for bit in order:
            full = jnp.concatenate([full, exchange(full, bit)], axis=0)
        return full

    up = list(range(1, bits))
    low, high = run(lower, up[::-1]), run(upper, up)
    return (low, high, exchange(low, 0), exchange(high, 0))


def reversed_bits(value, count):
    out = 0
    for i in range(count):
        out = out | (((value >> i) & 1) << (count - 1 - i))
    return out


def slot_specs(wide, shape):
    bits = (wide - 1).bit_length() - 1
    zeros = (0,) * len(shape)
    last = wide // 2 - 1

    def spec(other, flip):
        def index(c, s, own):
            at = reversed_bits(s, bits) if flip else s
            stay = reversed_bits(last, bits) if not other else 0
            return (jnp.where(c == other, at, stay), *zeros)

        return pl.BlockSpec((1, *shape), index)

    return [spec(0, True), spec(0, False), spec(1, True), spec(1, False)]


def place(low, high, c, write):
    @pl.when(c == 0)
    def _():
        write(low[0], high[0])

    @pl.when(c == 1)
    def _():
        write(low[1], high[1])


def widen_square_kernel(count, narrow, own, low, high, low_other, high_other, *outs):
    def write(source_low, source_high):
        half = source_low.shape[-2]
        cols = source_low.shape[-1]
        for item in range(count):
            for n in range(narrow):
                at = slice(n * cols, (n + 1) * cols)
                outs[item][:half, at] = source_low[0, n, item].astype(f32)
                outs[item][half:, at] = source_high[0, n, item].astype(f32)

    place((low, low_other), (high, high_other), pl.program_id(0), write)


def widen_gate_kernel(narrow, own, low, high, low_other, high_other, gate, out):
    def write(source_low, source_high):
        half = source_low.shape[-2]
        cols = source_low.shape[-1]
        short = 2 * half // narrow
        for n in range(narrow):
            at = slice(n * cols, (n + 1) * cols)
            gate[:half, at] = source_low[0, n, 0].astype(f32)
            gate[half:, at] = source_high[0, n, 0].astype(f32)
            for i in range(narrow):
                source = source_low if i * short < half else source_high
                start = i * short % half
                out[n, :, i * cols : (i + 1) * cols] = source[
                    0, n, 1, start : start + short, :
                ].astype(f32)

    place((low, low_other), (high, high_other), pl.program_id(0), write)


def widen_ffn_kernel(own, low, high, low_other, high_other, *outs):
    def write(source_low, source_high):
        half = source_low.shape[-2]
        for item in range(3):
            outs[item][:half] = source_low[0, item].astype(f32)
            outs[item][half:] = source_high[0, item].astype(f32)

    place((low, low_other), (high, high_other), pl.program_id(0), write)


def ones_like_product(factors, own, first):
    count = factors.shape[0]
    j = jnp.arange(count)[:, None]
    i = jnp.arange(count)[None, :]
    if first:
        between = (i > j) & (i < own)
        wanted = j[:, 0] < own
    else:
        between = (i < j) & (i > own)
        wanted = j[:, 0] > own
    terms = jnp.where(between[:, :, None], factors[None], 1.0)
    return jnp.where(wanted[:, None], jnp.prod(terms, axis=1), 0.0)


def body(tokens, log_decay, lengths, pad_counts, w_query, w_key, w_value, w_gate, w_out,
         w_first, w_second, w_third, cotangent):
    wide, narrow = lax.axis_size("wide"), lax.axis_size("narrow")
    own_wide, own_narrow = lax.axis_index("wide"), lax.axis_index("narrow")
    heads, local = log_decay.shape
    share, width = tokens.shape
    hn, cols, hd = heads // narrow, width // narrow, width // heads
    blocks = local // BLOCK
    sds = jax.ShapeDtypeStruct

    tok = lax.all_gather(tokens, "narrow", axis=0, tiled=True)
    cot = lax.all_gather(cotangent, "narrow", axis=0, tiled=True)

    live, opening = token_layout(lengths, pad_counts, own_wide * local, local)
    live = live[:, None]
    keep = 1.0 - opening.reshape(blocks, BLOCK)[:, 0]
    own_decay = lax.dynamic_slice_in_dim(log_decay, own_narrow * hn, hn, 0)
    summed = jnp.cumsum(own_decay.reshape(hn, blocks, BLOCK), axis=2)
    last = summed[:, :, -1:]
    grow = summed.transpose(1, 0, 2)
    gcol = summed.reshape(hn, local).T
    rise = jnp.exp(summed).reshape(hn, local).T
    tail = jnp.exp(last - summed).reshape(hn, local).T
    decay = (jnp.exp(last[:, :, 0]) * keep[None]).T
    factors = lax.all_gather(jnp.prod(decay, axis=0), "wide", axis=0)
    coef_in = ones_like_product(factors, own_wide, True)
    coef_out = ones_like_product(factors, own_wide, False)

    def own_cols(weight):
        return lax.dynamic_slice_in_dim(weight, own_narrow * cols, cols, 1)

    wq, wk, wv, wg = (own_cols(w) for w in (w_query, w_key, w_value, w_gate))
    wo = lax.dynamic_slice_in_dim(w_out, own_narrow * cols, cols, 0)
    own_tok = tokens.astype(f32)
    own_n1 = (own_tok * inv_rms(own_tok)).astype(bf16)
    gate = jax.nn.sigmoid(jnp.dot(own_n1, w_gate, preferred_element_type=f32))

    up = lambda b: b
    down = lambda b: blocks - 1 - b

    def blk(w, index, size=BLOCK):
        return rows((size, w), index)

    def states(index):
        return rows((1, hn, hd, hd), index)

    state_spec = whole((hn, hd, hd))
    state_scratch = pltpu.VMEM((hn, hd, hd), f32)
    n1, ql, kl, q, k, v, intra, contrib, final = pl.pallas_call(
        functools.partial(forward_kernel, hn, hd),
        grid=(blocks,),
        in_specs=[SMEM, blk(width, up), *[whole((width, cols))] * 3, blk(1, up), blk(hn, up),
                  rows((1, hn, BLOCK), up), blk(hn, up)],
        out_specs=[blk(width, up), *[blk(cols, up)] * 6, states(up), state_spec],
        out_shape=[sds((local, width), bf16), *[sds((local, cols), f32)] * 2,
                   *[sds((local, cols), bf16)] * 3, sds((local, cols), f32),
                   sds((blocks, hn, hd, hd), f32), sds((hn, hd, hd), bf16)],
        scratch_shapes=[state_scratch],
        compiler_params=PARAMS,
        name="mixer_forward",
    )(decay, tok, wq, wk, wv, live, gcol, grow, tail)

    gathered = lax.all_gather(final, "wide", axis=0)
    att, kent = pl.pallas_call(
        functools.partial(attend_kernel, hn, hd, wide),
        grid=(blocks,),
        in_specs=[SMEM, SMEM, SMEM, whole((wide, hn, hd, hd)), states(up), blk(cols, up),
                  blk(cols, up), blk(hn, up)],
        out_specs=[blk(cols, up), states(up)],
        out_shape=[sds((local, cols), bf16), sds((blocks, hn, hd, hd), bf16)],
        scratch_shapes=[state_scratch],
        compiler_params=PARAMS,
        name="mixer_attend",
    )(decay, keep, coef_in, gathered, contrib, q, intra, rise)

    att_own = lax.all_to_all(att.reshape(narrow, share, cols), "narrow", 0, 0)
    hidden, n2 = pl.pallas_call(
        hidden_kernel,
        out_shape=[sds((share, width), f32), sds((share, width), bf16)],
        compiler_params=pltpu.CompilerParams(vmem_limit_bytes=56 << 20),
        name="mixer_out",
    )(att_own, gate, tokens, w_out)

    n2_all = lax.all_gather(n2, "narrow", axis=0, tiled=True)
    ff = w_first.shape[1]
    product, gf, gs, gn2_part = pl.pallas_call(
        ffn_kernel,
        grid=(blocks,),
        in_specs=[blk(width, up), blk(width, up), whole((width, ff)), whole((width, ff)),
                  whole((ff, width))],
        out_specs=[blk(ff, up)] * 3 + [blk(width, up)],
        out_shape=[sds((local, ff), bf16)] * 3 + [sds((local, width), bf16)],
        compiler_params=PARAMS,
        name="ffn",
    )(n2_all, cot, w_first, w_second, w_third)
    gn2 = lax.psum_scatter(gn2_part, "narrow", scatter_dimension=0, tiled=True)
    ffn_part = jnp.dot(product, w_third, preferred_element_type=f32).astype(bf16)
    ffn_own = lax.psum_scatter(ffn_part, "narrow", scatter_dimension=0, tiled=True)
    output = (hidden + ffn_own.astype(f32)).astype(bf16)
    tall = width // wide
    own_ref = own_wide.astype(jnp.int32)[None]
    kept, sent = pl.pallas_call(
        functools.partial(ffn_grad_kernel, wide),
        grid=(3,),
        in_specs=[SMEM, *[whole((local, width))] * 2, *[whole((local, ff))] * 3],
        out_specs=[pl.BlockSpec((wide // 2, 1, tall, ff), lambda i: (0, i, 0, 0))] * 2,
        out_shape=[sds((wide // 2, 3, tall, ff), bf16)] * 2,
        scratch_shapes=[pltpu.VMEM((width, ff), f32)],
        compiler_params=PARAMS,
        name="ffn_grads",
    )(own_ref, n2_all, cot, product, gf, gs)
    ff_pieces = gather_over_wide(*reduce_over_wide(kept, sent))
    widened = pltpu.CompilerParams(dimension_semantics=("arbitrary", "arbitrary"))

    def out_row(c, s, own):
        return own[0] ^ (2 * s + c)

    grad_first, grad_second, third_turned = pl.pallas_call(
        widen_ffn_kernel,
        grid_spec=pltpu.PrefetchScalarGridSpec(
            num_scalar_prefetch=1,
            grid=(2, wide // 2),
            in_specs=slot_specs(wide, (3, tall // 2, ff)),
            out_specs=[pl.BlockSpec((tall, ff), lambda c, s, own: (out_row(c, s, own), 0))] * 3,
        ),
        out_shape=[sds((width, ff), f32)] * 3,
        compiler_params=widened,
        name="widen_ffn",
    )(own_ref, *ff_pieces)
    grad_third = third_turned.T

    grad_hidden, packed, ga, ggl = pl.pallas_call(
        functools.partial(residual_kernel, narrow),
        out_shape=[sds((share, width), f32), sds((share, width + 128), bf16),
                   sds((narrow, share, cols), bf16), sds((share, width), bf16)],
        compiler_params=pltpu.CompilerParams(vmem_limit_bytes=56 << 20),
        name="residual_back",
    )(gn2, hidden, cotangent, w_out, att_own, gate)
    ga_cols = lax.all_to_all(ga, "narrow", 0, 0).reshape(local, cols)
    packed_all = lax.all_gather(packed, "narrow", axis=0, tiled=True)

    dq, gk, gv, direct, first = pl.pallas_call(
        functools.partial(query_kernel, hn, hd, blocks),
        grid=(blocks,),
        in_specs=[SMEM, SMEM, *[blk(cols, down)] * 5, states(down), blk(hn, down),
                  rows((1, hn, BLOCK), down), blk(hn, down)],
        out_specs=[*[blk(cols, down)] * 3, states(down), state_spec],
        out_shape=[sds((local, cols), bf16), *[sds((local, cols), f32)] * 2,
                   sds((blocks, hn, hd, hd), f32), sds((hn, hd, hd), bf16)],
        scratch_shapes=[state_scratch],
        compiler_params=PARAMS,
        name="mixer_query_back",
    )(decay, keep, ga_cols, q, k, v, ql, kent, gcol, grow, rise)

    arrived = lax.all_gather(first, "wide", axis=0)
    pair = (wide // 2, 3, tall, cols)
    kept, sent, gn1_part = pl.pallas_call(
        functools.partial(key_kernel, hn, hd, wide, blocks),
        grid=(blocks,),
        in_specs=[SMEM, SMEM, SMEM, whole((wide, hn, hd, hd)), states(down), blk(width, down),
                  *[blk(cols, down)] * 6, blk(hn, down), blk(1, down),
                  *[whole((width, cols))] * 3],
        out_specs=[*[whole(pair)] * 2, blk(width, down)],
        out_shape=[*[sds(pair, bf16)] * 2, sds((local, width), bf16)],
        scratch_shapes=[state_scratch, *[pltpu.VMEM((BLOCK, cols), bf16)] * 2,
                        *[pltpu.VMEM((width, cols), f32)] * 3],
        compiler_params=PARAMS,
        name="mixer_key_back",
    )(own_ref, decay, coef_out, arrived, direct, n1, dq, k, v, kl, gk, gv, tail, live, wq, wk, wv)

    def collect(kept, sent):
        lower, upper = reduce_over_wide(kept, sent)
        both = lax.all_gather(jnp.stack([lower, upper]), "narrow", axis=0)
        return gather_over_wide(both[:, 0], both[:, 1])

    square_pieces = collect(kept, sent)
    pair = (wide // 2, 2, tall, cols)
    kept, sent = pl.pallas_call(
        functools.partial(gate_kernel, wide, narrow),
        in_specs=[SMEM, *[pl.BlockSpec(memory_space=pltpu.VMEM)] * 5],
        out_shape=[sds(pair, bf16)] * 2,
        scratch_shapes=[pltpu.VMEM((width, cols), f32), pltpu.VMEM((cols, width), f32)],
        compiler_params=pltpu.CompilerParams(vmem_limit_bytes=56 << 20),
        name="gate_back",
    )(own_ref, packed_all, att, n1, wg, wo)
    gate_pieces = collect(kept, sent)

    gn1 = lax.psum_scatter(gn1_part, "narrow", scatter_dimension=0, tiled=True)
    grad_tokens = pl.pallas_call(
        tokens_kernel,
        out_shape=sds((share, width), f32),
        compiler_params=pltpu.CompilerParams(vmem_limit_bytes=56 << 20),
        name="tokens_back",
    )(gn1, ggl, w_gate, tokens, grad_hidden)

    grad_query, grad_key, grad_value = pl.pallas_call(
        functools.partial(widen_square_kernel, 3, narrow),
        grid_spec=pltpu.PrefetchScalarGridSpec(
            num_scalar_prefetch=1,
            grid=(2, wide // 2),
            in_specs=slot_specs(wide, (narrow, 3, tall // 2, cols)),
            out_specs=[pl.BlockSpec((tall, width), lambda c, s, own: (out_row(c, s, own), 0))] * 3,
        ),
        out_shape=[sds((width, width), f32)] * 3,
        compiler_params=widened,
        name="widen_square",
    )(own_ref, *square_pieces)
    short = cols // wide
    grad_gate, grad_out = pl.pallas_call(
        functools.partial(widen_gate_kernel, narrow),
        grid_spec=pltpu.PrefetchScalarGridSpec(
            num_scalar_prefetch=1,
            grid=(2, wide // 2),
            in_specs=slot_specs(wide, (narrow, 2, tall // 2, cols)),
            out_specs=[
                pl.BlockSpec((tall, width), lambda c, s, own: (out_row(c, s, own), 0)),
                pl.BlockSpec((narrow, short, width), lambda c, s, own: (0, out_row(c, s, own), 0)),
            ],
        ),
        out_shape=[sds((width, width), f32), sds((narrow, cols, width), f32)],
        compiler_params=widened,
        name="widen_gate",
    )(own_ref, *gate_pieces)
    mixer = (grad_query, grad_key, grad_value, grad_gate, grad_out.reshape(width, width))
    return (output, grad_tokens, *mixer, grad_first, grad_second, grad_third)


def solution(mesh):
    both = P(("wide", "narrow"), None)
    in_specs = (both, P(None, "wide"), P(), P(), P(), P(), P(), P(), P(),
                P(None, "narrow"), P(None, "narrow"), P("narrow", None), both)
    out_specs = (both, both, P(), P(), P(), P(), P(),
                 P(None, "narrow"), P(None, "narrow"), P("narrow", None))
    return jax.shard_map(body, mesh=mesh, in_specs=in_specs, out_specs=out_specs, check_vma=False)
```

time: 679 us -> 398 us (0.59); the launches traced: 670 us -> 396 us
  waiting for transfers between devices: 395 us -> 134 us
  matrix products: 95.4 us -> 3.3 us
  Pallas kernels: 0 us -> 78.5 us
  blocking collectives: 0 us -> 71.1 us
  other arithmetic: 66.9 us -> 19.7 us
  starting transfers between devices: 64.5 us -> 36.1 us
    psum x1 -> x0, waiting for transfers between devices: 193 us -> none  [body(): lax.psum(weight_grad(normed_one, grad_query_lin).astype(jnp.bfloat16), 'w...]
    dot_general x36 -> x2, matrix products: 95.4 us -> 3.3 us  [the longest x1 1.95 us: body(): jnp.dot(product, w_third, preferred_element_type=f32).astype(bf16)]
    all_gather x4, waiting for transfers between devices: 105 us -> 26.1 us  [the longest x1 23.8 us: body(): n2_all = lax.all_gather(n2, 'narrow', axis=0, tiled=True)]
    pallas_call x0 -> x13, Pallas kernels: none -> 78.5 us  [the longest x1 9.54 us: body(): pl.pallas_call(functools.partial(widen_square_kernel, 3, narrow), grid_sp...]
    all_gather x0 -> x4, blocking collectives: none -> 55.6 us  [the longest x2 32.9 us: collect(): both = lax.all_gather(jnp.stack([lower, upper]), 'narrow', axis=0)]
    convert_element_type x27 -> x2, other arithmetic: 42.4 us -> 2.64 us  [the longest x1 1.87 us: body(): output = (hidden + ffn_own.astype(f32)).astype(bf16)]
    ppermute x14 -> x33, starting transfers between devices: 64 us -> 28.1 us  [exchange(): lax.ppermute(values, 'wide', [(i, i ^ 1 << bit) for i in range(size)])]
    reduce_scatter x2 -> x3, waiting for transfers between devices: 43.1 us -> 16.3 us  [the longest x1 16.3 us: body(): gn2 = lax.psum_scatter(gn2_part, 'narrow', scatter_dimension=0, tiled=True)]
  transfers between devices with their start and end apart: 21 -> 42, of which waited for: 20 -> 19; matrix products, arithmetic and copies ran while one was open for 14% -> 14% of each run, Pallas kernels for 0% -> 16%
where the time goes in v1:
time: 398 us; the launch traced here: 396 us
  waiting for transfers between devices  134 us (34%)
  Pallas kernels  78.5 us (20%)
  blocking collectives  71.1 us (18%)
  local copies, waits for them, and re-layouts  36.7 us (9%)
  starting transfers between devices  36.1 us (9%)
  other arithmetic  19.7 us (5%)
  between operations  16.7 us (4%)
    ppermute x33, waiting for transfers between devices, exchange(): lax.ppermute(values, 'wide', [(i, i ^ 1 << bit) for i in range(size)])  75.9 us
    all_gather x2, blocking collectives, collect(): both = lax.all_gather(jnp.stack([lower, upper]), 'narrow', axis=0)  32.9 us
    ppermute x33, starting transfers between devices, exchange(): lax.ppermute(values, 'wide', [(i, i ^ 1 << bit) for i in range(size)])  28.1 us
    all_gather x1, waiting for transfers between devices, body(): n2_all = lax.all_gather(n2, 'narrow', axis=0, tiled=True)  23.8 us
    unnamed x63, local copies, waits for them, and re-layouts  17.6 us
    reduce_scatter x1, waiting for transfers between devices, body(): gn2 = lax.psum_scatter(gn2_part, 'narrow', scatter_dimension=0, tiled=True)  16.3 us
    unnamed x1, blocking collectives  15.5 us
    all_gather x1, blocking collectives, body(): gathered = lax.all_gather(final, 'wide', axis=0)  11.8 us
  transfers between devices with their start and end apart: 42, of which 19 were waited for; matrix products, arithmetic and copies ran while one was open for 14% of the time, Pallas kernels for 16%

profile of v1, /device:TPU:0, one launch (start us, length us, event | category | flops | bytes accessed | tf_op | source)
XLA Modules:
  0.0 395.9 jit_solution(7822748950653353560)
XLA Ops:
  14.4 15.5 %all-reduce = f32[16]{0:T(128)S(1)} all-reduce(f32[16]{0:T(128)S(1)} %dynamic-update-slice), channel_id=2, replica_groups=mesh['wide'=8,'narrow'=4] {'wide'}, use_global_device_ids=true, to_apply=%add | all-reduce | flops 16 | bytes 128
  35.1 2.3 constant_dynamic-slice_fusion.2
  38.1 2.3 all-gather.10.cloned.1.call-done.tok
  40.3 5.5 %mixer_forward.1 = (bf16[512,1024]{1,0:T(8,128)(2,1)}, f32[512,256]{1,0:T(8,128)}, f32[512,256]{1,0:T(8,128)}, bf16[512,256]{1,0:T(8,128)(2,1)}, bf16[512,256]{1...) custom-call(f32[2,2]{1,0:T(2,128)} %get-tuple-element.161.decay, ...), custom_call_target="tpu_custom_call" | custom-call | tf_op jit(solution)/shard_map/mixer_forward/pallas_call | solution.py:457
  45.8 11.8 %all-gather.1 = bf16[16,128,128]{2,1,0:T(8,128)(2,1)} all-gather(bf16[2,128,128]{2,1,0:T(8,128)(2,1)} %get-tuple-element.51), channel_id=3, replica_groups=mesh['wide'=8,'narrow'=4] {'wide'}, dimensions={0}, use_global_device_ids=true | all-gather | bytes 589824 | tf_op jit(solution)/shard_map/all_gather | solution.py:471
  57.7 2.9 mixer_attend.1
  60.5 3.4 all-to-all-start
  65.4 9.7 %all-to-all-done.att = bf16[4,128,256]{2,1,0:T(8,128)(2,1)S(1)} async-done(((bf16[4,128,256]{2,1,0:T(8,128)(2,1)}), bf16[4,128,256]{2,1,0:T(8,128)(2,1)S(1)}, u32[]{:S(2)}, u32[]{:S(2)}) %all-to-all-start) | async-done | bytes 262176 | tf_op jit(solution)/shard_map/all_to_all | solution.py:484
  75.8 3.3 mixer_out.1
  82.3 23.8 %all-gather.12.cloned.1.call-done.n2 = bf16[512,1024]{1,0:T(8,128)(2,1)} async-done(((bf16[128,1024]{1,0:T(8,128)(2,1)}), bf16[512,1024]{1,0:T(8,128)(2,1)}) %all-gather.12.cloned.1.call-update) | async-done | bytes 1048592 | tf_op jit(solution)/shard_map/all_gather | solution.py:492
  106.1 9.4 %ffn.1 = (bf16[512,704]{1,0:T(8,128)(2,1)}, bf16[512,704]{1,0:T(8,128)(2,1)}, bf16[512,704]{1,0:T(8,128)(2,1)}, bf16[512,1024]{1,0:T(8,128)(2,1)}) custom-call(bf16[512,1024]{1,0:T(8,128)(2,1)} %all-gather.12.cloned.1.call-done.n2, bf16[512,1024]{1,0:T(8,128)(2,1)} %all-gather.14.cloned.1.call-done.cot, bf16[1024,704]{1,0:T(8,128)(2,1)} %copy.134.w1, ...), custom_call_target="tpu_custom_call" | custom-call | tf_op jit(solution)/shard_map/ffn/pallas_call | solution.py:494
  115.8 7.2 %ffn_grads.1 = (bf16[4,3,128,704]{3,2,1,0:T(8,128)(2,1)}, bf16[4,3,128,704]{3,2,1,0:T(8,128)(2,1)}) custom-call(s32[1]{0:T(128)} %bitcast.15.own, bf16[512,1024]{1,0:T(8,128)(2,1)} %all-gather.12.cloned.1.call-done.n2, bf16[512,1024]{1,0:T(8,128)(2,1)} %all-gather.14.cloned.1.call-done.cot, bf16[512,704]{1,0:T(8,128)(2,1)} %get-tuple-element.58.product, ...), custom_call_target="tpu_custom_call" | custom-call | tf_op jit(solution)/shard_map/ffn_grads/pallas_call | solution.py:510
  122.9 3.0 copy.145
  126.0 16.3 %reduce-scatter.6.cloned.1.call-done.gn2 = bf16[128,1024]{1,0:T(8,128)(2,1)} async-done(((bf16[512,1024]{1,0:T(8,128)(2,1)}), bf16[128,1024]{1,0:T(8,128)(2,1)}) %reduce-scatter.6.cloned.1.call-update) | async-done | bytes 262160 | tf_op jit(solution)/shard_map/reduce_scatter | solution.py:504
  142.4 3.9 residual_back.1
  146.3 4.2 %copy.146 = bf16[4,3,128,704]{3,2,1,0:T(8,128)(2,1)} copy(bf16[4,3,128,704]{2,3,1,0:T(8,128)(2,1)} %collective-permute-done.22) | data formatting | bytes 4325376 | tf_op jit(solution)/shard_map/ppermute | solution.py:283
  150.5 3.2 add.123
  156.2 1.9 constant_dynamic-slice_fusion.1.wg
  158.7 4.1 %all-to-all-start.1 = ((bf16[4,128,256]{2,1,0:T(8,128)(2,1)}), bf16[4,128,256]{2,1,0:T(8,128)(2,1)}, u32[]{:S(2)}, u32[]{:S(2)}) async-start(bf16[4,128,256]{2,1,0:T(8,128)(2,1)} %get-tuple-element.60), calls=%async_computation.3 | async-start | bytes 524288 | tf_op jit(solution)/shard_map/all_to_all | solution.py:547
  165.2 4.4 %collective-permute-done.23 = bf16[2,3,64,704]{3,2,1,0:T(8,128)(2,1)} collective-permute-done((bf16[2,3,64,704]{3,2,1,0:T(8,128)(2,1)}, bf16[2,3,64,704]{3,2,1,0:T(8,128)(2,1)}, u32[]{:S(2)}, u32[]{:S(2)}) %collective-permute-start.23) | collective-permute-done | bytes 540704 | tf_op jit(solution)/shard_map/ppermute | solution.py:283
  173.1 2.0 convolution_convert_fusion
  175.1 4.3 %all-to-all-done.1 = bf16[4,128,256]{2,1,0:T(8,128)(2,1)} async-done(((bf16[4,128,256]{2,1,0:T(8,128)(2,1)}), bf16[4,128,256]{2,1,0:T(8,128)(2,1)}, u32[]{:S(2)}, u32[]{:S(2)}) %all-to-all-start.1) | async-done | bytes 262176 | tf_op jit(solution)/shard_map/all_to_all | solution.py:547
  179.4 3.9 mixer_query_back.1
  183.3 10.8 %all-gather.2 = bf16[16,128,128]{2,1,0:T(8,128)(2,1)} all-gather(bf16[2,128,128]{2,1,0:T(8,128)(2,1)} %get-tuple-element.65), channel_id=4, replica_groups=mesh['wide'=8,'narrow'=4] {'wide'}, dimensions={0}, use_global_device_ids=true | all-gather | bytes 589824 | tf_op jit(solution)/shard_map/all_gather | solution.py:563
  194.1 9.2 %mixer_key_back.1 = (bf16[4,3,128,256]{3,2,1,0:T(8,128)(2,1)}, bf16[4,3,128,256]{3,2,1,0:T(8,128)(2,1)}, bf16[512,1024]{1,0:T(8,128)(2,1)}) custom-call(s32[1]{0:T(128)} %bitcast.15.own, f32[2,2]{1,0:T(2,128)} %get-tuple-element.161.decay, f32[8,2]{1,0:T(8,128)} %broadcast_select_fusion.coef, bf16[8,2,128,128]{3,2,1,0:T(8,128)(2,1)} %bitcast.157, ...), custom_call_target="tpu_custom_call" | custom-call | tf_op jit(solution)/shard_map/mixer_key_back/pallas_call | solution.py:565
  207.8 5.1 %collective-permute-done.25 = bf16[1,3,64,704]{3,2,1,0:T(8,128)(2,1)S(1)} collective-permute-done((bf16[1,3,64,704]{3,2,1,0:T(8,128)(2,1)S(1)}, bf16[1,3,64,704]{3,2,1,0:T(8,128)(2,1)S(1)}, u32[]{:S(2)}, u32[]{:S(2)}) %collective-permute-start.25) | collective-permute-done | bytes 270368 | tf_op jit(solution)/shard_map/ppermute | solution.py:283
  217.9 3.7 collective-permute-done.3
  222.2 12.1 %collective-permute-done.1 = bf16[2,3,64,256]{3,2,1,0:T(8,128)(2,1)S(1)} collective-permute-done((bf16[2,3,64,256]{3,2,1,0:T(8,128)(2,1)S(1)}, bf16[2,3,64,256]{3,2,1,0:T(8,128)(2,1)S(1)}, u32[]{:S(2)}, u32[]{:S(2)}) %collective-permute-start.1) | collective-permute-done | bytes 196640 | tf_op jit(solution)/shard_map/ppermute | solution.py:283
  235.6 3.4 collective-permute-done.2
  239.1 16.9 %all-gather.3 = bf16[8,3,64,256]{3,2,1,0:T(8,128)(2,1)S(1)} all-gather(bf16[2,3,64,256]{3,2,1,0:T(8,128)(2,1)S(1)} %pad_maximum_fusion.12), channel_id=5, replica_groups=mesh['wide'=8,'narrow'=4] {'narrow'}, dimensions={0}, use_global_device_ids=true | all-gather | bytes 983040 | tf_op jit(solution)/shard_map/all_gather | solution.py:581
  257.2 1.9 constant_dynamic-slice_fusion.wo
  260.1 4.4 %gate_back.1 = (bf16[4,2,128,256]{3,2,1,0:T(8,128)(2,1)}, bf16[4,2,128,256]{3,2,1,0:T(8,128)(2,1)}) custom-call(s32[1]{0:T(128)} %bitcast.15.own, bf16[512,1152]{1,0:T(8,128)(2,1)} %all-gather.16.cloned.1.call-done.packed, bf16[512,256]{1,0:T(8,128)(2,1)} %get-tuple-element.55.att, bf16[512,1024]{1,0:T(8,128)(2,1)} %get-tuple-element.67.n1, ...), custom_call_target="tpu_custom_call" | custom-call | tf_op jit(solution)/shard_map/gate_back/pallas_call | solution.py:586
  270.8 20.0 %collective-permute-done.14 = bf16[2,2,64,256]{3,2,1,0:T(8,128)(2,1)S(1)} collective-permute-done((bf16[2,2,64,256]{3,2,1,0:T(8,128)(2,1)S(1)}, bf16[2,2,64,256]{3,2,1,0:T(8,128)(2,1)S(1)}, u32[]{:S(2)}, u32[]{:S(2)}) %collective-permute-start.14) | collective-permute-done | bytes 131104 | tf_op jit(solution)/shard_map/ppermute | solution.py:283
  291.8 3.9 collective-permute-done.12
  296.8 3.2 collective-permute-done.15
  301.0 3.2 collective-permute-done.13
  304.3 16.0 %all-gather.4 = bf16[8,2,64,256]{3,2,1,0:T(8,128)(2,1)S(1)} all-gather(bf16[2,2,64,256]{3,2,1,0:T(8,128)(2,1)S(1)} %pad_maximum_fusion.13), channel_id=6, replica_groups=mesh['wide'=8,'narrow'=4] {'narrow'}, dimensions={0}, use_global_device_ids=true | all-gather | bytes 655360 | tf_op jit(solution)/shard_map/all_gather | solution.py:581
  323.7 4.1 %collective-permute-done.16 = bf16[1,4,2,64,256]{4,3,2,1,0:T(8,128)(2,1)S(1)} collective-permute-done((bf16[1,4,2,64,256]{4,3,2,1,0:T(8,128)(2,1)S(1)}, bf16[1,4,2,64,256]{4,3,2,1,0:T(8,128)(2,1)S(1)}, u32[]{:S(2)}, u32[]{:S(2)}) %collective-permute-start.16) | collective-permute-done | bytes 262176 | tf_op jit(solution)/shard_map/ppermute | solution.py:283
  331.3 5.1 %collective-permute-done.30 = bf16[2,3,64,704]{3,2,1,0:T(8,128)(2,1)S(1)} collective-permute-done((bf16[2,3,64,704]{3,2,1,0:T(8,128)(2,1)S(1)}, bf16[2,3,64,704]{3,2,1,0:T(8,128)(2,1)S(1)}, u32[]{:S(2)}, u32[]{:S(2)}) %collective-permute-start.30) | collective-permute-done | bytes 540704 | tf_op jit(solution)/shard_map/ppermute | solution.py:283
  337.5 4.8 %collective-permute-done.17 = bf16[2,4,2,64,256]{4,3,2,1,0:T(8,128)(2,1)S(1)} collective-permute-done((bf16[2,4,2,64,256]{4,3,2,1,0:T(8,128)(2,1)S(1)}, bf16[2,4,2,64,256]{4,3,2,1,0:T(8,128)(2,1)S(1)}, u32[]{:S(2)}, u32[]{:S(2)}) %collective-permute-start.17) | collective-permute-done | bytes 524320 | tf_op jit(solution)/shard_map/ppermute | solution.py:283
  343.5 1.9 collective-permute-done.19
  349.9 3.7 tokens_back.1
  353.5 8.0 %widen_ffn.1 = (f32[1024,704]{1,0:T(8,128)}, f32[1024,704]{1,0:T(8,128)}, f32[1024,704]{1,0:T(8,128)}) custom-call(s32[1]{0:T(128)} %bitcast.15.own, bf16[4,3,64,704]{3,2,1,0:T(8,128)(2,1)} %copy-done.4, bf16[4,3,64,704]{3,2,1,0:T(8,128)(2,1)} %pad_maximum_fusion.3.high, bf16[4,3,64,704]{3,2,1,0:T(8,128)(2,1)} %copy-done.20, ...), custom_call_target="tpu_custom_call" | custom-call | tf_op jit(solution)/shard_map/widen_ffn/pallas_call | solution.py:526
  361.5 3.4 copy.149
  365.0 3.4 copy.150
  368.4 3.4 copy.151
  371.9 9.5 %widen_square.1 = (f32[1024,1024]{1,0:T(8,128)}, f32[1024,1024]{1,0:T(8,128)}, f32[1024,1024]{1,0:T(8,128)}) custom-call(s32[1]{0:T(128)} %bitcast.15.own, bf16[4,4,3,64,256]{4,3,2,1,0:T(8,128)(2,1)} %copy-done.2, bf16[4,4,3,64,256]{4,3,2,1,0:T(8,128)(2,1)} %copy-done.3, bf16[4,4,3,64,256]{4,3,2,1,0:T(8,128)(2,1)} %collective-permute-done.9.low_other, ...), custom_call_target="tpu_custom_call" | custom-call | tf_op jit(solution)/shard_map/widen_square/pallas_call | solution.py:604
  381.4 7.7 %widen_gate.1 = (f32[1024,1024]{1,0:T(8,128)}, f32[4,256,1024]{2,1,0:T(8,128)}) custom-call(s32[1]{0:T(128)} %bitcast.15.own, bf16[4,4,2,64,256]{4,3,2,1,0:T(8,128)(2,1)} %pad_maximum_fusion.4.low, bf16[4,4,2,64,256]{4,3,2,1,0:T(8,128)(2,1)} %pad_maximum_fusion.5.high, bf16[4,4,2,64,256]{4,3,2,1,0:T(8,128)(2,1)} %collective-permute-done.20.low_other, ...), custom_call_target="tpu_custom_call" | custom-call | tf_op jit(solution)/shard_map/widen_gate/pallas_call | solution.py:617
  (206 shorter events, 62.2 us)
Async XLA Ops:
  7.2 27.0 %copy-start = (bf16[1024,1024]{1,0:T(8,128)(2,1)S(1)}, bf16[1024,1024]{1,0:T(8,128)(2,1)}, u32[]{:S(2)}) copy-start(bf16[1024,1024]{1,0:T(8,128)(2,1)} %param.17) | copy-start | bytes 6291460
  7.2 27.8 %copy-start.6 = (bf16[128,1024]{1,0:T(8,128)(2,1)S(1)}, bf16[128,1024]{1,0:T(8,128)(2,1)}, u32[]{:S(2)}) copy-start(bf16[128,1024]{1,0:T(8,128)(2,1)} %tok.3) | copy-start | bytes 786436
  7.2 33.1 %all-gather.10.cloned.1.call-start = ((), (), s32[]{:S(2)}) async-start(), calls=%async_computation.5 | async-start | bytes 1310720 | tf_op jit(solution)/shard_map/all_gather | solution.py:419
  7.9 74.3 %all-gather.14.cloned.1.call-start = ((), (), s32[]{:S(2)}) async-start(), calls=%async_computation.7 | async-start | bytes 1310720 | tf_op jit(solution)/shard_map/all_gather | solution.py:420
  8.8 28.5 %copy-start.26 = (f32[2]{0:T(128)}, f32[2]{0:T(128)S(1)}, u32[]{:S(2)}) copy-start(f32[2]{0:T(128)S(1)} %fusion.30.keep) | copy-start | bytes 28
  45.8 18.2 %copy-start.7 = (bf16[1024,1024]{1,0:T(8,128)(2,1)S(1)}, bf16[1024,1024]{1,0:T(8,128)(2,1)}, u32[]{:S(2)}) copy-start(bf16[1024,1024]{1,0:T(8,128)(2,1)} %wg.1) | copy-start | bytes 6291460
  60.5 14.5 %all-to-all-start = ((bf16[4,128,256]{2,1,0:T(8,128)(2,1)}), bf16[4,128,256]{2,1,0:T(8,128)(2,1)S(1)}, u32[]{:S(2)}, u32[]{:S(2)}) async-start(bf16[4,128,256]{2,1,0:T(8,128)(2,1)} %bitcast.164), calls=%async_computation | async-start | bytes 524288 | tf_op jit(solution)/shard_map/all_to_all | solution.py:484
  63.9 42.1 %all-gather.12.cloned.1.call-start = ((), (), s32[]{:S(2)}) async-start(), calls=%async_computation.6 | async-start | bytes 1310720 | tf_op jit(solution)/shard_map/all_gather | solution.py:492
  79.1 63.3 %reduce-scatter.6.cloned.1.call-start = ((), (), s32[]{:S(2)}) async-start(), calls=%async_computation.9 | async-start | bytes 1310720 | tf_op jit(solution)/shard_map/reduce_scatter | solution.py:504
  115.5 144.6 %all-gather.16.cloned.1.call-start = ((), (), s32[]{:S(2)}) async-start(), calls=%async_computation.11 | async-start | bytes 1474560 | tf_op jit(solution)/shard_map/all_gather | solution.py:548
  126.0 20.4 %collective-permute-start.22 = (bf16[4,3,128,704]{2,3,1,0:T(8,128)(2,1)S(1)}, bf16[4,3,128,704]{2,3,1,0:T(8,128)(2,1)}, u32[]{:S(2)}, u32[]{:S(2)}) collective-permute-start(bf16[4,3,128,704]{2,3,1,0:T(8,128)(2,1)S(1)} %copy.145), channel_id=1, source_target_pairs={{0,4},{4,0},{8,12},{12,8},{16,20},{20,16},{24,28},{28,24},{1,5},{5... | collective-permute-start | bytes 6488072 | tf_op jit(solution)/shard_map/ppermute | solution.py:283
  154.7 14.9 %collective-permute-start.23 = (bf16[2,3,64,704]{3,2,1,0:T(8,128)(2,1)}, bf16[2,3,64,704]{3,2,1,0:T(8,128)(2,1)}, u32[]{:S(2)}, u32[]{:S(2)}) collective-permute-start(bf16[2,3,64,704]{3,2,1,0:T(8,128)(2,1)} %slice_bitcast_fusion), channel_id=1, source_target_pairs={{0,8},{4,12},{8,0},{12,4},{16,24},{20,28},{24,16},{28,20},{1,9},{5... | collective-permute-start | bytes 1622024 | tf_op jit(solution)/shard_map/ppermute | solution.py:283
  158.7 20.7 %all-to-all-start.1 = ((bf16[4,128,256]{2,1,0:T(8,128)(2,1)}), bf16[4,128,256]{2,1,0:T(8,128)(2,1)}, u32[]{:S(2)}, u32[]{:S(2)}) async-start(bf16[4,128,256]{2,1,0:T(8,128)(2,1)} %get-tuple-element.60), calls=%async_computation.3 | async-start | bytes 524288 | tf_op jit(solution)/shard_map/all_to_all | solution.py:547
  162.8 185.2 %reduce-scatter.4.cloned.1.call-start = ((), (), s32[]{:S(2)}) async-start(), calls=%async_computation.8 | async-start | bytes 1310720 | tf_op jit(solution)/shard_map/reduce_scatter | solution.py:506
  163.7 41.7 %collective-permute-start.27 = (bf16[2,3,64,704]{3,2,1,0:T(8,128)(2,1)}, bf16[2,3,64,704]{3,2,1,0:T(8,128)(2,1)}, u32[]{:S(2)}, u32[]{:S(2)}) collective-permute-start(bf16[2,3,64,704]{3,2,1,0:T(8,128)(2,1)} %slice.190), channel_id=1, source_target_pairs={{0,16},{4,20},{8,24},{12,28},{16,0},{20,4},{24,8},{28,12},{1,17},{... | collective-permute-start | bytes 1622024 | tf_op jit(solution)/shard_map/ppermute | solution.py:283
  171.5 32.2 %collective-permute-start.24 = (bf16[3,64,704]{2,1,0:T(8,128)(2,1)S(1)}, bf16[3,64,704]{2,1,0:T(8,128)(2,1)S(1)}, u32[]{:S(2)}, u32[]{:S(2)}) collective-permute-start(bf16[3,64,704]{2,1,0:T(8,128)(2,1)S(1)} %slice_bitcast_fusion.6), channel_id=1, source_target_pairs={{0,16},{4,20},{8,24},{12,28},{16,0},{20,4},{24,8},{28,12},{1,17},{... | collective-permute-start | bytes 811016 | tf_op jit(solution)/shard_map/ppermute | solution.py:283
  175.0 174.8 %reduce-scatter.8.cloned.1.call-start = ((), (), s32[]{:S(2)}) async-start(), calls=%async_computation.10 | async-start | bytes 1310720 | tf_op jit(solution)/shard_map/reduce_scatter | solution.py:596
  203.3 12.1 %collective-permute-start = (bf16[4,3,128,256]{3,2,1,0:T(8,128)(2,1)}, bf16[4,3,128,256]{3,2,1,0:T(8,128)(2,1)S(1)}, u32[]{:S(2)}, u32[]{:S(2)}) collective-permute-start(bf16[4,3,128,256]{3,2,1,0:T(8,128)(2,1)} %get-tuple-element.76), channel_id=1, source_target_pairs={{0,4},{4,0},{8,12},{12,8},{16,20},{20,16},{24,28},{28,24},{1,5},{5... | collective-permute-start | bytes 2359304 | tf_op jit(solution)/shard_map/ppermute | solution.py:283
  203.8 9.1 %collective-permute-start.25 = (bf16[1,3,64,704]{3,2,1,0:T(8,128)(2,1)S(1)}, bf16[1,3,64,704]{3,2,1,0:T(8,128)(2,1)S(1)}, u32[]{:S(2)}, u32[]{:S(2)}) collective-permute-start(bf16[1,3,64,704]{3,2,1,0:T(8,128)(2,1)S(1)} %fusion.9), channel_id=1, source_target_pairs={{0,16},{4,20},{8,24},{12,28},{16,0},{20,4},{24,8},{28,12},{1,17},{... | collective-permute-start | bytes 811016 | tf_op jit(solution)/shard_map/ppermute | solution.py:283
  207.4 57.1 %collective-permute-start.28 = (bf16[3,64,704]{2,1,0:T(8,128)(2,1)}, bf16[3,64,704]{2,1,0:T(8,128)(2,1)S(1)}, u32[]{:S(2)}, u32[]{:S(2)}) collective-permute-start(bf16[3,64,704]{2,1,0:T(8,128)(2,1)} %slice_bitcast_fusion.4), channel_id=1, source_target_pairs={{0,8},{4,12},{8,0},{12,4},{16,24},{20,28},{24,16},{28,20},{1,9},{5... | collective-permute-start | bytes 811016 | tf_op jit(solution)/shard_map/ppermute | solution.py:283
  213.9 51.8 %collective-permute-start.26 = (bf16[2,3,64,704]{3,2,1,0:T(8,128)(2,1)}, bf16[2,3,64,704]{3,2,1,0:T(8,128)(2,1)}, u32[]{:S(2)}, u32[]{:S(2)}) collective-permute-start(bf16[2,3,64,704]{3,2,1,0:T(8,128)(2,1)} %pad_maximum_fusion.8), channel_id=1, source_target_pairs={{0,8},{4,12},{8,0},{12,4},{16,24},{20,28},{24,16},{28,20},{1,9},{5... | collective-permute-start | bytes 1622024 | tf_op jit(solution)/shard_map/ppermute | solution.py:283
  215.7 5.9 %collective-permute-start.3 = (bf16[2,3,64,256]{3,2,1,0:T(8,128)(2,1)S(1)}, bf16[2,3,64,256]{3,2,1,0:T(8,128)(2,1)S(1)}, u32[]{:S(2)}, u32[]{:S(2)}) collective-permute-start(bf16[2,3,64,256]{3,2,1,0:T(8,128)(2,1)S(1)} %slice.168), channel_id=1, source_target_pairs={{0,16},{4,20},{8,24},{12,28},{16,0},{20,4},{24,8},{28,12},{1,17},{... | collective-permute-start | bytes 589832 | tf_op jit(solution)/shard_map/ppermute | solution.py:283
  216.3 18.0 %collective-permute-start.1 = (bf16[2,3,64,256]{3,2,1,0:T(8,128)(2,1)S(1)}, bf16[2,3,64,256]{3,2,1,0:T(8,128)(2,1)S(1)}, u32[]{:S(2)}, u32[]{:S(2)}) collective-permute-start(bf16[2,3,64,256]{3,2,1,0:T(8,128)(2,1)S(1)} %slice_bitcast_fusion.10), channel_id=1, source_target_pairs={{0,8},{4,12},{8,0},{12,4},{16,24},{20,28},{24,16},{28,20},{1,9},{5... | collective-permute-start | bytes 589832 | tf_op jit(solution)/shard_map/ppermute | solution.py:283
  221.6 13.9 %collective-permute-start.4 = (bf16[3,64,256]{2,1,0:T(8,128)(2,1)S(1)}, bf16[3,64,256]{2,1,0:T(8,128)(2,1)S(1)}, u32[]{:S(2)}, u32[]{:S(2)}) collective-permute-start(bf16[3,64,256]{2,1,0:T(8,128)(2,1)S(1)} %slice_bitcast_fusion.14), channel_id=1, source_target_pairs={{0,8},{4,12},{8,0},{12,4},{16,24},{20,28},{24,16},{28,20},{1,9},{5... | collective-permute-start | bytes 294920 | tf_op jit(solution)/shard_map/ppermute | solution.py:283
  234.3 4.7 %collective-permute-start.2 = (bf16[3,64,256]{2,1,0:T(8,128)(2,1)S(1)}, bf16[3,64,256]{2,1,0:T(8,128)(2,1)S(1)}, u32[]{:S(2)}, u32[]{:S(2)}) collective-permute-start(bf16[3,64,256]{2,1,0:T(8,128)(2,1)S(1)} %slice_bitcast_fusion.16), channel_id=1, source_target_pairs={{0,16},{4,20},{8,24},{12,28},{16,0},{20,4},{24,8},{28,12},{1,17},{... | collective-permute-start | bytes 294920 | tf_op jit(solution)/shard_map/ppermute | solution.py:283
  256.0 11.1 %collective-permute-start.5 = (bf16[1,4,3,64,256]{4,3,2,1,0:T(8,128)(2,1)S(1)}, bf16[1,4,3,64,256]{4,3,2,1,0:T(8,128)(2,1)S(1)}, u32[]{:S(2)}, u32[]{:S(2)}) collective-permute-start(bf16[1,4,3,64,256]{4,3,2,1,0:T(8,128)(2,1)S(1)} %get-tuple-element.155), channel_id=1, source_target_pairs={{0,16},{4,20},{8,24},{12,28},{16,0},{20,4},{24,8},{28,12},{1,17},{... | collective-permute-start | bytes 1179656 | tf_op jit(solution)/shard_map/ppermute | solution.py:283
  259.1 9.2 %collective-permute-start.7 = (bf16[1,4,3,64,256]{4,3,2,1,0:T(8,128)(2,1)S(1)}, bf16[1,4,3,64,256]{4,3,2,1,0:T(8,128)(2,1)S(1)}, u32[]{:S(2)}, u32[]{:S(2)}) collective-permute-start(bf16[1,4,3,64,256]{4,3,2,1,0:T(8,128)(2,1)S(1)} %get-tuple-element.154), channel_id=1, source_target_pairs={{0,8},{4,12},{8,0},{12,4},{16,24},{20,28},{24,16},{28,20},{1,9},{5... | collective-permute-start | bytes 1179656 | tf_op jit(solution)/shard_map/ppermute | solution.py:283
  264.5 5.0 %collective-permute-start.11 = (bf16[4,2,128,256]{3,2,1,0:T(8,128)(2,1)}, bf16[4,2,128,256]{3,2,1,0:T(8,128)(2,1)S(1)}, u32[]{:S(2)}, u32[]{:S(2)}) collective-permute-start(bf16[4,2,128,256]{3,2,1,0:T(8,128)(2,1)} %get-tuple-element.82), channel_id=1, source_target_pairs={{0,4},{4,0},{8,12},{12,8},{16,20},{20,16},{24,28},{28,24},{1,5},{5... | collective-permute-start | bytes 1572872 | tf_op jit(solution)/shard_map/ppermute | solution.py:283
  264.5 56.9 %collective-permute-start.29 = (bf16[1,3,64,704]{3,2,1,0:T(8,128)(2,1)S(1)}, bf16[1,3,64,704]{3,2,1,0:T(8,128)(2,1)S(1)}, u32[]{:S(2)}, u32[]{:S(2)}) collective-permute-start(bf16[1,3,64,704]{3,2,1,0:T(8,128)(2,1)S(1)} %fusion.7), channel_id=1, source_target_pairs={{0,8},{4,12},{8,0},{12,4},{16,24},{20,28},{24,16},{28,20},{1,9},{5... | collective-permute-start | bytes 811016 | tf_op jit(solution)/shard_map/ppermute | solution.py:283
  266.9 79.6 %collective-permute-start.31 = (bf16[4,3,64,704]{3,2,1,0:T(8,128)(2,1)S(1)}, bf16[4,3,64,704]{3,2,1,0:T(8,128)(2,1)S(1)}, u32[]{:S(2)}, u32[]{:S(2)}) collective-permute-start(bf16[4,3,64,704]{3,2,1,0:T(8,128)(2,1)S(1)} %pad_maximum_fusion.2.low), channel_id=1, source_target_pairs={{0,4},{4,0},{8,12},{12,8},{16,20},{20,16},{24,28},{28,24},{1,5},{5... | collective-permute-start | bytes 3244040 | tf_op jit(solution)/shard_map/ppermute | solution.py:283
  267.2 55.3 %collective-permute-start.6 = (bf16[2,4,3,64,256]{4,3,2,1,0:T(8,128)(2,1)S(1)}, bf16[2,4,3,64,256]{4,3,2,1,0:T(8,128)(2,1)S(1)}, u32[]{:S(2)}, u32[]{:S(2)}) collective-permute-start(bf16[2,4,3,64,256]{4,3,2,1,0:T(8,128)(2,1)S(1)} %pad_maximum_fusion.6), channel_id=1, source_target_pairs={{0,8},{4,12},{8,0},{12,4},{16,24},{20,28},{24,16},{28,20},{1,9},{5... | collective-permute-start | bytes 2359304 | tf_op jit(solution)/shard_map/ppermute | solution.py:283
  268.4 61.6 %collective-permute-start.8 = (bf16[2,4,3,64,256]{4,3,2,1,0:T(8,128)(2,1)S(1)}, bf16[2,4,3,64,256]{4,3,2,1,0:T(8,128)(2,1)S(1)}, u32[]{:S(2)}, u32[]{:S(2)}) collective-permute-start(bf16[2,4,3,64,256]{4,3,2,1,0:T(8,128)(2,1)S(1)} %pad_maximum_fusion.7), channel_id=1, source_target_pairs={{0,16},{4,20},{8,24},{12,28},{16,0},{20,4},{24,8},{28,12},{1,17},{... | collective-permute-start | bytes 2359304 | tf_op jit(solution)/shard_map/ppermute | solution.py:283
  269.7 21.0 %collective-permute-start.14 = (bf16[2,2,64,256]{3,2,1,0:T(8,128)(2,1)S(1)}, bf16[2,2,64,256]{3,2,1,0:T(8,128)(2,1)S(1)}, u32[]{:S(2)}, u32[]{:S(2)}) collective-permute-start(bf16[2,2,64,256]{3,2,1,0:T(8,128)(2,1)S(1)} %slice.179), channel_id=1, source_target_pairs={{0,16},{4,20},{8,24},{12,28},{16,0},{20,4},{24,8},{28,12},{1,17},{... | collective-permute-start | bytes 393224 | tf_op jit(solution)/shard_map/ppermute | solution.py:283
  290.7 5.0 %collective-permute-start.12 = (bf16[2,2,64,256]{3,2,1,0:T(8,128)(2,1)S(1)}, bf16[2,2,64,256]{3,2,1,0:T(8,128)(2,1)S(1)}, u32[]{:S(2)}, u32[]{:S(2)}) collective-permute-start(bf16[2,2,64,256]{3,2,1,0:T(8,128)(2,1)S(1)} %slice_bitcast_fusion.12), channel_id=1, source_target_pairs={{0,8},{4,12},{8,0},{12,4},{16,24},{20,28},{24,16},{28,20},{1,9},{5... | collective-permute-start | bytes 393224 | tf_op jit(solution)/shard_map/ppermute | solution.py:283
  295.7 4.3 %collective-permute-start.15 = (bf16[2,64,256]{2,1,0:T(8,128)(2,1)S(1)}, bf16[2,64,256]{2,1,0:T(8,128)(2,1)S(1)}, u32[]{:S(2)}, u32[]{:S(2)}) collective-permute-start(bf16[2,64,256]{2,1,0:T(8,128)(2,1)S(1)} %slice_bitcast_fusion.18), channel_id=1, source_target_pairs={{0,8},{4,12},{8,0},{12,4},{16,24},{20,28},{24,16},{28,20},{1,9},{5... | collective-permute-start | bytes 196616 | tf_op jit(solution)/shard_map/ppermute | solution.py:283
  300.0 4.3 %collective-permute-start.13 = (bf16[2,64,256]{2,1,0:T(8,128)(2,1)S(1)}, bf16[2,64,256]{2,1,0:T(8,128)(2,1)S(1)}, u32[]{:S(2)}, u32[]{:S(2)}) collective-permute-start(bf16[2,64,256]{2,1,0:T(8,128)(2,1)S(1)} %slice_bitcast_fusion.20), channel_id=1, source_target_pairs={{0,16},{4,20},{8,24},{12,28},{16,0},{20,4},{24,8},{28,12},{1,17},{... | collective-permute-start | bytes 196616 | tf_op jit(solution)/shard_map/ppermute | solution.py:283
  304.2 19.3 %copy-start.16 = (bf16[1,4,3,64,256]{4,3,2,1,0:T(8,128)(2,1)S(1)}, bf16[1,4,3,64,256]{4,3,2,1,0:T(8,128)(2,1)}, u32[]{:S(2)}) copy-start(bf16[1,4,3,64,256]{4,3,2,1,0:T(8,128)(2,1)} %copy-done.15) | copy-start | bytes 1179652
  320.3 7.5 %collective-permute-start.16 = (bf16[1,4,2,64,256]{4,3,2,1,0:T(8,128)(2,1)S(1)}, bf16[1,4,2,64,256]{4,3,2,1,0:T(8,128)(2,1)S(1)}, u32[]{:S(2)}, u32[]{:S(2)}) collective-permute-start(bf16[1,4,2,64,256]{4,3,2,1,0:T(8,128)(2,1)S(1)} %get-tuple-element.157), channel_id=1, source_target_pairs={{0,16},{4,20},{8,24},{12,28},{16,0},{20,4},{24,8},{28,12},{1,17},{... | collective-permute-start | bytes 786440 | tf_op jit(solution)/shard_map/ppermute | solution.py:283
  321.5 14.9 %collective-permute-start.30 = (bf16[2,3,64,704]{3,2,1,0:T(8,128)(2,1)S(1)}, bf16[2,3,64,704]{3,2,1,0:T(8,128)(2,1)S(1)}, u32[]{:S(2)}, u32[]{:S(2)}) collective-permute-start(bf16[2,3,64,704]{3,2,1,0:T(8,128)(2,1)S(1)} %pad_maximum_fusion.9), channel_id=1, source_target_pairs={{0,16},{4,20},{8,24},{12,28},{16,0},{20,4},{24,8},{28,12},{1,17},{... | collective-permute-start | bytes 1622024 | tf_op jit(solution)/shard_map/ppermute | solution.py:283
  322.6 6.4 %collective-permute-start.18 = (bf16[1,4,2,64,256]{4,3,2,1,0:T(8,128)(2,1)S(1)}, bf16[1,4,2,64,256]{4,3,2,1,0:T(8,128)(2,1)S(1)}, u32[]{:S(2)}, u32[]{:S(2)}) collective-permute-start(bf16[1,4,2,64,256]{4,3,2,1,0:T(8,128)(2,1)S(1)} %get-tuple-element.156), channel_id=1, source_target_pairs={{0,8},{4,12},{8,0},{12,4},{16,24},{20,28},{24,16},{28,20},{1,9},{5... | collective-permute-start | bytes 786440 | tf_op jit(solution)/shard_map/ppermute | solution.py:283
  327.8 44.0 %collective-permute-start.9 = (bf16[4,4,3,64,256]{4,3,2,1,0:T(8,128)(2,1)S(1)}, bf16[4,4,3,64,256]{4,3,2,1,0:T(8,128)(2,1)}, u32[]{:S(2)}, u32[]{:S(2)}) collective-permute-start(bf16[4,4,3,64,256]{4,3,2,1,0:T(8,128)(2,1)S(1)} %pad_maximum_fusion.low), channel_id=1, source_target_pairs={{0,4},{4,0},{8,12},{12,8},{16,20},{20,16},{24,28},{28,24},{1,5},{5... | collective-permute-start | bytes 4718600 | tf_op jit(solution)/shard_map/ppermute | solution.py:283
  328.9 13.4 %collective-permute-start.17 = (bf16[2,4,2,64,256]{4,3,2,1,0:T(8,128)(2,1)S(1)}, bf16[2,4,2,64,256]{4,3,2,1,0:T(8,128)(2,1)S(1)}, u32[]{:S(2)}, u32[]{:S(2)}) collective-permute-start(bf16[2,4,2,64,256]{4,3,2,1,0:T(8,128)(2,1)S(1)} %pad_maximum_fusion.10), channel_id=1, source_target_pairs={{0,8},{4,12},{8,0},{12,4},{16,24},{20,28},{24,16},{28,20},{1,9},{5... | collective-permute-start | bytes 1572872 | tf_op jit(solution)/shard_map/ppermute | solution.py:283
  330.0 15.4 %collective-permute-start.19 = (bf16[2,4,2,64,256]{4,3,2,1,0:T(8,128)(2,1)S(1)}, bf16[2,4,2,64,256]{4,3,2,1,0:T(8,128)(2,1)S(1)}, u32[]{:S(2)}, u32[]{:S(2)}) collective-permute-start(bf16[2,4,2,64,256]{4,3,2,1,0:T(8,128)(2,1)S(1)} %pad_maximum_fusion.11), channel_id=1, source_target_pairs={{0,16},{4,20},{8,24},{12,28},{16,0},{20,4},{24,8},{28,12},{1,17},{... | collective-permute-start | bytes 1572872 | tf_op jit(solution)/shard_map/ppermute | solution.py:283
  336.4 35.5 %collective-permute-start.10 = (bf16[4,4,3,64,256]{4,3,2,1,0:T(8,128)(2,1)S(1)}, bf16[4,4,3,64,256]{4,3,2,1,0:T(8,128)(2,1)}, u32[]{:S(2)}, u32[]{:S(2)}) collective-permute-start(bf16[4,4,3,64,256]{4,3,2,1,0:T(8,128)(2,1)S(1)} %pad_maximum_fusion.1.high), channel_id=1, source_target_pairs={{0,4},{4,0},{8,12},{12,8},{16,20},{20,16},{24,28},{28,24},{1,5},{5... | collective-permute-start | bytes 4718600 | tf_op jit(solution)/shard_map/ppermute | solution.py:283
  342.3 11.2 %collective-permute-start.32 = (bf16[4,3,64,704]{3,2,1,0:T(8,128)(2,1)}, bf16[4,3,64,704]{3,2,1,0:T(8,128)(2,1)}, u32[]{:S(2)}, u32[]{:S(2)}) collective-permute-start(bf16[4,3,64,704]{3,2,1,0:T(8,128)(2,1)} %pad_maximum_fusion.3.high), channel_id=1, source_target_pairs={{0,4},{4,0},{8,12},{12,8},{16,20},{20,16},{24,28},{28,24},{1,5},{5... | collective-permute-start | bytes 3244040 | tf_op jit(solution)/shard_map/ppermute | solution.py:283
  345.4 36.0 %collective-permute-start.20 = (bf16[4,4,2,64,256]{4,3,2,1,0:T(8,128)(2,1)}, bf16[4,4,2,64,256]{4,3,2,1,0:T(8,128)(2,1)}, u32[]{:S(2)}, u32[]{:S(2)}) collective-permute-start(bf16[4,4,2,64,256]{4,3,2,1,0:T(8,128)(2,1)} %pad_maximum_fusion.4.low), channel_id=1, source_target_pairs={{0,4},{4,0},{8,12},{12,8},{16,20},{20,16},{24,28},{28,24},{1,5},{5... | collective-permute-start | bytes 3145736 | tf_op jit(solution)/shard_map/ppermute | solution.py:283
  347.5 33.9 %collective-permute-start.21 = (bf16[4,4,2,64,256]{4,3,2,1,0:T(8,128)(2,1)}, bf16[4,4,2,64,256]{4,3,2,1,0:T(8,128)(2,1)}, u32[]{:S(2)}, u32[]{:S(2)}) collective-permute-start(bf16[4,4,2,64,256]{4,3,2,1,0:T(8,128)(2,1)} %pad_maximum_fusion.5.high), channel_id=1, source_target_pairs={{0,4},{4,0},{8,12},{12,8},{16,20},{20,16},{24,28},{28,24},{1,5},{5... | collective-permute-start | bytes 3145736 | tf_op jit(solution)/shard_map/ppermute | solution.py:283
  371.9 17.2 %copy-start.1 = (bf16[1024,1024]{1,0:T(8,128)(2,1)S(1)}, bf16[1024,1024]{1,0:T(8,128)(2,1)}, u32[]{:S(2)}) copy-start(bf16[1024,1024]{1,0:T(8,128)(2,1)} %param.17) | copy-start | bytes 6291460
  (21 other events, 124.4 us)
Sparse Core Ops, SparseCore 0:
  9.6 30.7 all-gather.9
  41.9 29.4 all-gather.13
  79.2 26.8 all-gather.11
  115.7 26.6 reduce-scatter.5
  146.5 34.6 all-gather.15
  183.9 26.1 reduce-scatter.3
  259.2 26.8 reduce-scatter.7

commit v2 on v0

v2 whole, which is shorter than its diff:
```python
import functools

import jax
import jax.numpy as jnp
from jax import lax
from jax.experimental import pallas as pl
from jax.experimental.pallas import tpu as pltpu
from jax.sharding import PartitionSpec as P

BLOCK = 256
epsilon = 1e-06
bf16 = jnp.bfloat16
f32 = jnp.float32
SMEM = pl.BlockSpec(memory_space=pltpu.SMEM)
ANY = pl.BlockSpec(memory_space=pl.ANY)
PARAMS = pltpu.CompilerParams(dimension_semantics=("arbitrary",), vmem_limit_bytes=56 << 20)
sds = jax.ShapeDtypeStruct


def mm(a, b):
    return lax.dot_general(a, b, (((1,), (0,)), ((), ())), preferred_element_type=f32)


def mt(a, b):
    return lax.dot_general(a, b, (((1,), (1,)), ((), ())), preferred_element_type=f32)


def tm(a, b):
    return lax.dot_general(a, b, (((0,), (0,)), ((), ())), preferred_element_type=f32)


def inv_rms(values):
    return lax.rsqrt(jnp.mean(values * values, axis=-1, keepdims=True) + epsilon)


def sigmoid(values):
    return 1.0 / (1.0 + jnp.exp(-values))


def slope(values):
    squashed = sigmoid(values)
    return squashed * (1.0 + values * (1.0 - squashed))


def rms_back(values, inverse, gradient):
    normed = values * inverse
    return inverse * (gradient - normed * jnp.mean(gradient * normed, axis=-1, keepdims=True))


def whole(shape):
    zeros = (0,) * len(shape)
    return pl.BlockSpec(shape, lambda *_: zeros)


def rows(shape, index):
    rest = (0,) * (len(shape) - 1)
    return pl.BlockSpec(shape, lambda b, *_: (index(b), *rest))


def causal_of(size, flip):
    return (lax.broadcasted_iota(jnp.int32, (size, size), 0) ^ flip) >= (
        lax.broadcasted_iota(jnp.int32, (size, size), 1) ^ flip
    )


def decay_weights(causal, g_col, g_row):
    return jnp.where(causal, jnp.exp(jnp.where(causal, g_col - g_row, 0.0)), 0.0)


def flip_of(own, share):
    return share * (own[1] & (BLOCK // share - 1))


def forward_kernel(hn, hd, share, own, tok_a, tok_b, wq, wk, wv, wg, live, gcol, grow, tail, *refs):
    n1, tok, ql, kl, q, k, v, act, intra, contrib = refs[-10:]
    i = pl.program_id(0)

    @pl.when(i == 0)
    def _():
        for part, source in enumerate((tok_a, tok_b)):
            at = slice(part * share, (part + 1) * share)
            tok[at, :] = source[...]
            values = source[...].astype(f32)
            n1[at, :] = (values * inv_rms(values)).astype(bf16)

    normed = n1[...]
    q_lin = mm(normed, wq[...])
    k_lin = mm(normed, wk[...])

    @pl.when(i == own[1])
    def _():
        ql[...] = q_lin
        kl[...] = k_lin

    q[...] = (q_lin * sigmoid(q_lin)).astype(bf16)
    k[...] = (k_lin * sigmoid(k_lin) * live[...]).astype(bf16)
    v[...] = mm(normed, wv[...]).astype(bf16)
    act[...] = sigmoid(mm(normed, wg[...]))
    causal = causal_of(BLOCK, flip_of(own, share))
    for h in range(hn):
        at = slice(h * hd, (h + 1) * hd)
        qh, kh, vh = q[:, at], k[:, at], v[:, at]
        weights = decay_weights(causal, gcol[0, :, h : h + 1], grow[0, h : h + 1, :])
        scores = (mt(qh, kh) * weights).astype(bf16)
        intra[:, at] = mm(scores, vh)
        key_tail = (kh.astype(f32) * tail[0, :, h : h + 1]).astype(bf16)
        contrib[0, h] = tm(key_tail, vh)


def out_kernel(heads, hn, hd, share, own, keep, enter, other, *refs):
    narrow = heads // hn
    states = refs[:narrow]
    contrib, q, intra, act, tok, rise, wo, att, inverse, hidden, n2, kent = refs[narrow:]
    b = pl.program_id(0)
    for h in range(heads):
        at = slice(h * hd, (h + 1) * hd)
        part = own[1] ^ (h // hn)
        base = states[0][h % hn].astype(f32)
        for j in range(1, narrow):
            base = jnp.where(part == j, states[j][h % hn].astype(f32), base)
        entering = enter[b, h] * base + other[b, h] * contrib[1 - b, h]
        kept = (keep[b] * entering).astype(bf16)

        @pl.when(part == 0)
        def _():
            kent[0, h % hn] = kept

        att[:, at] = (intra[:, at] + rise[h // hn, :, h % hn : h % hn + 1] * mm(q[:, at], kept)).astype(bf16)
    values = att[...].astype(f32)
    scale = inv_rms(values)
    inverse[...] = scale
    gated = (values * scale * act[...]).astype(bf16)
    hid = tok[...].astype(f32) + mm(gated, wo[...])

    @pl.when(b == 0)
    def _():
        hidden[...] = hid[:share]

    n2[...] = (hid * inv_rms(hid)).astype(bf16)


def ffn_kernel(share, n2, cot, w1, w2, w3, product, gf, gs, *pieces):
    b = pl.program_id(0)
    normed = n2[...]
    first = mt(normed, w1[...])
    second = mt(normed, w2[...])
    product[...] = (first * second).astype(bf16)
    grad = mt(cot[...], w3[...])
    gf[...] = (grad * second).astype(bf16)
    gs[...] = (grad * first).astype(bf16)
    back = (mm(gf[...], w1[...]) + mm(gs[...], w2[...])).astype(bf16)
    per = BLOCK // share
    for i, piece in enumerate(pieces):
        @pl.when(b == i // per)
        def _():
            piece[...] = back[(i % per) * share : (i % per + 1) * share]


def reversed_bits(value, count):
    out = 0
    for i in range(count):
        out = out | (((value >> i) & 1) << (count - 1 - i))
    return out


def position(offset, parity, wide):
    bits = (wide - 1).bit_length() - 1
    high = offset >> 1
    return jnp.where(parity == 0, reversed_bits(high, bits), high)


def scatter(wide, own, kept, sent, item, piece_of):
    for t in range(wide):
        offset = own[0] ^ t
        parity = own[0] & 1

        @pl.when(offset & 1 == 0)
        def _():
            kept[position(offset, parity, wide), item] = piece_of(t).astype(bf16)

        @pl.when(offset & 1 == 1)
        def _():
            sent[position(offset, 1 - parity, wide), item] = piece_of(t).astype(bf16)


def ffn_cut(wide, ff, width):
    across = min(wide, width // 128)
    return ff // (wide // across), width // across, across


def ffn_grad_kernel(wide, share, own, n2, cot, product, gf, gs, w3, kept, sent, *refs):
    pieces, acc = refs[:-1], refs[-1]
    item = pl.program_id(0)
    for i, (left, right) in enumerate(((gf, n2), (gs, n2), (product, cot))):
        @pl.when(item == i)
        def _():
            acc[...] = tm(left[...], right[...])

    tall, cols, across = ffn_cut(wide, *acc.shape)

    def piece_of(t):
        row, col = t // across * tall, t % across * cols
        return acc[row : row + tall, col : col + cols]

    scatter(wide, own, kept, sent, 0, piece_of)

    @pl.when(item == 2)
    def _():
        for i, piece in enumerate(pieces):
            piece[...] = mm(product[i * share : (i + 1) * share, :], w3[...]).astype(bf16)


def residual_kernel(narrow, own, *refs):
    parts = refs[:narrow]
    hidden, cot, wo, att, inverse, act, grad_hidden, low_out, ggl = refs[narrow : narrow + 9]
    ga = refs[narrow + 9 :]
    gn2 = parts[0][...].astype(f32)
    for part in parts[1:]:
        gn2 = gn2 + part[...].astype(f32)
    hid = hidden[...]
    gh = cot[...].astype(f32) + rms_back(hid, inv_rms(hid), gn2)
    grad_hidden[...] = gh
    low = gh.astype(bf16)
    low_out[...] = low
    gg = mt(low, wo[...])
    values = att[...].astype(f32)
    gate = act[...]
    ggl[...] = (gg * (values * inverse[...]) * gate * (1.0 - gate)).astype(bf16)
    back = rms_back(values, inverse[...], gg * gate).astype(bf16)
    size = back.shape[1] // narrow
    for i in range(narrow):
        for k in range(narrow):
            @pl.when(own[1] ^ i == k)
            def _():
                ga[k][...] = back[:, i * size : (i + 1) * size]


def query_kernel(hn, hd, share, own, keep, ahead, *refs):
    per = BLOCK // share
    ga = refs[: -14]
    q, k, v, ql, kent, gcol, grow, rise, dq, gk, gv, direct, first, grad = refs[-14:]
    b = pl.program_id(0)
    for i, piece in enumerate(ga):
        @pl.when(b == i // per)
        def _():
            grad[(i % per) * share : (i % per + 1) * share, :] = piece[...]

    causal = causal_of(BLOCK, flip_of(own, share))
    for h in range(hn):
        at = slice(h * hd, (h + 1) * hd)
        g, qh, kh, vh = grad[:, at], q[:, at], k[:, at], v[:, at]
        weights = decay_weights(causal, gcol[:, h : h + 1], grow[0, h : h + 1, :])
        scores = (mt(qh, kh) * weights).astype(bf16)
        raw = (mt(g, vh) * weights).astype(bf16)
        up = rise[:, h : h + 1]
        gq = mm(raw, kh) + up * mt(g, kent[0, h])
        dq[:, at] = (gq * slope(ql[:, at])).astype(bf16)
        gk[:, at] = tm(raw, qh)
        gv[:, at] = tm(scores, g)
        now = keep[b] * tm((qh.astype(f32) * up).astype(bf16), g)
        direct[0, h] = now

        @pl.when(b == 0)
        def _():
            first[h] = ahead[b, h] * now

        @pl.when(b > 0)
        def _():
            first[h] += ahead[b, h] * now


def key_kernel(hn, hd, wide, share, own, leave, other, arrived, direct, n1, dq, k, v, kl, gk, gv,
               tail, live, wq, wk, wv, kept, sent, *refs):
    pieces = refs[:-5]
    dk, dv, aq, ak, av = refs[-5:]
    per = BLOCK // share
    b = pl.program_id(0)
    last = pl.num_programs(0) - 1
    for h in range(hn):
        at = slice(h * hd, (h + 1) * hd)
        low = (leave[b, h] * arrived[h] + other[b, h] * direct[1 - b, h]).astype(bf16)
        down = tail[:, h : h + 1]
        grad_key = gk[:, at] + down * mt(v[:, at], low)
        dk[:, at] = (grad_key * live[...] * slope(kl[:, at])).astype(bf16)
        dv[:, at] = (gv[:, at] + down * mm(k[:, at], low)).astype(bf16)
    normed = n1[...]
    tall = normed.shape[1] // wide
    for item, (acc, part) in enumerate(((aq, dq), (ak, dk), (av, dv))):
        now = tm(normed, part[...])

        @pl.when(b == 0)
        def _():
            acc[...] = now

        @pl.when(b > 0)
        def _():
            acc[...] += now

        @pl.when(b == last)
        def _():
            scatter(wide, own, kept, sent, item, lambda t: acc[t * tall : (t + 1) * tall, :])

    back = (mt(dq[...], wq[...]) + mt(dk[...], wk[...]) + mt(dv[...], wv[...])).astype(bf16)
    for i, piece in enumerate(pieces):
        @pl.when(b == i // per)
        def _():
            piece[...] = back[(i % per) * share : (i % per + 1) * share]


def gate_kernel(wide, narrow, share, own, *refs):
    lows = refs[:narrow]
    att, inverse, act, n1, wo, kept, sent, grads, acc, acc_out = refs[narrow:]
    for i, piece in enumerate(lows):
        grads[i * share : (i + 1) * share, :] = piece[...]
    gate = act[...]
    scaled = att[...].astype(f32) * inverse[...]
    gated = (scaled * gate).astype(bf16)
    gg = mt(grads[...], wo[...])
    ggl = (gg * scaled * gate * (1.0 - gate)).astype(bf16)
    acc[...] = tm(n1[...], ggl)
    tall = acc.shape[0] // wide
    scatter(wide, own, kept, sent, 0, lambda t: acc[t * tall : (t + 1) * tall, :])
    acc_out[...] = tm(gated, grads[...])
    cols = gated.shape[1]
    short = cols // wide

    def piece_of(t):
        mine = acc_out[t * short : (t + 1) * short, :]
        return jnp.concatenate([mine[:, i * cols : (i + 1) * cols] for i in range(narrow)], axis=0)

    scatter(wide, own, kept, sent, 1, piece_of)


def tokens_kernel(narrow, *refs):
    parts = refs[:narrow]
    ggl, wg, tok, gh, out = refs[narrow:]
    grad = mt(ggl[...], wg[...])
    for part in parts:
        grad = grad + part[...].astype(f32)
    values = tok[...].astype(f32)
    out[...] = gh[...] + rms_back(values, inv_rms(values), grad)


def output_kernel(narrow, *refs):
    hidden, out = refs[narrow:]
    total = hidden[...]
    for part in refs[:narrow]:
        total = total + part[...].astype(f32)
    out[...] = total.astype(bf16)


def swap_narrow(values, k):
    size = lax.axis_size("narrow")
    return lax.ppermute(values, "narrow", [(i, i ^ k) for i in range(size)])


def gather_narrow(values):
    return [values] + [swap_narrow(values, k) for k in range(1, lax.axis_size("narrow"))]


def trade_narrow(pieces):
    return [pieces[0]] + [swap_narrow(pieces[k], k) for k in range(1, len(pieces))]


def swap_core(values):
    size = lax.axis_size("wide")
    return lax.ppermute(values, "wide", [(i, i ^ 1) for i in range(size)])


def swap_step(values, step):
    size = lax.axis_size("wide")
    bits = (size - 1).bit_length()
    flip = lambda i: i ^ (1 << (1 + step if i % 2 == 0 else bits - 1 - step))
    return lax.ppermute(values, "wide", [(i, flip(i)) for i in range(size)])


def reduce_wide(kept, sent):
    got = swap_core(sent)
    steps = (lax.axis_size("wide") - 1).bit_length() - 1
    low, high = kept, got
    for step in range(steps):
        half = low.shape[0] // 2
        away = low[half:] + high[half:]
        low, high = low[:half] + high[:half], swap_step(away, step)
    return (low + high)[0]


def gather_wide(piece):
    steps = (lax.axis_size("wide") - 1).bit_length() - 1
    full = [piece]
    for step in reversed(range(steps)):
        full = full + [swap_step(part, step) for part in full]
    return full, [swap_core(part) for part in full]


def target(own, place, other, wide):
    bits = (wide - 1).bit_length() - 1
    parity = (own[0] & 1) ^ other
    high = jnp.where(parity == 0, reversed_bits(place, bits), place)
    return own[0] ^ other ^ (2 * high)


def widen_square_kernel(count, narrow, places, own, *refs):
    pieces, outs = refs[:places], refs[-count:]
    for j, piece in enumerate(pieces):
        @pl.when(pl.program_id(0) == j)
        def _():
            cols = piece.shape[-1]
            for item in range(count):
                for n in range(narrow):
                    outs[item][:, n * cols : (n + 1) * cols] = piece[own[1] ^ n, item].astype(f32)


def widen_gate_kernel(narrow, places, own, *refs):
    pieces, (gate, out) = refs[:places], refs[-2:]
    for j, piece in enumerate(pieces):
        @pl.when(pl.program_id(0) == j)
        def _():
            cols = piece.shape[-1]
            short = piece.shape[-2] // narrow
            for n in range(narrow):
                gate[:, n * cols : (n + 1) * cols] = piece[own[1] ^ n, 0].astype(f32)
                for i in range(narrow):
                    out[n, :, i * cols : (i + 1) * cols] = piece[
                        own[1] ^ n, 1, i * short : (i + 1) * short, :
                    ].astype(f32)


def widen_ffn_kernel(places, own, *refs):
    pieces, outs = refs[:places], refs[-3:]
    for j, piece in enumerate(pieces):
        @pl.when(pl.program_id(0) == j)
        def _():
            for item in range(3):
                outs[item][...] = piece[item].astype(f32)


def widen(kernel, own, halves, blocks, shapes, name):
    outs = []
    for other, pieces in enumerate(halves):
        places = len(pieces)

        def spec(shape, index):
            return pl.BlockSpec(shape, lambda i, own: index(target(own, i, other, 2 * places)))

        outs = pl.pallas_call(
            functools.partial(kernel, places),
            grid_spec=pltpu.PrefetchScalarGridSpec(
                num_scalar_prefetch=1,
                grid=(places,),
                in_specs=[whole(p.shape) for p in pieces] + [ANY] * len(outs),
                out_specs=[spec(*block) for block in blocks],
            ),
            out_shape=[sds(shape, f32) for shape in shapes],
            input_output_aliases={1 + places + i: i for i in range(len(outs))},
            compiler_params=PARAMS,
            name=f"{name}_{other}",
        )(own, *pieces, *outs)
    return outs


def xor_order(values, own, axis):
    count = values.shape[axis]
    for bit in range((count - 1).bit_length()):
        step = 1 << bit
        shape = values.shape
        split = values.reshape(shape[:axis] + (count // (2 * step), 2, step) + shape[axis + 1 :])
        flipped = jnp.flip(split, axis + 1)
        values = jnp.where((own >> bit) & 1 == 1, flipped, split).reshape(shape)
    return values


def gather_factors(values):
    size, own = lax.axis_size("wide"), lax.axis_index("wide")
    full = values[None]
    for bit in range((size - 1).bit_length()):
        got = lax.ppermute(full, "wide", [(i, i ^ (1 << bit)) for i in range(size)])
        full = jnp.concatenate([full, got], axis=0)
    return xor_order(full, own, 0)


def between(factors, own, before):
    count = factors.shape[0]
    j = jnp.arange(count)[:, None]
    i = jnp.arange(count)[None, :]
    if before:
        inner, wanted = (i > j) & (i < own), j[:, 0] < own
    else:
        inner, wanted = (i < j) & (i > own), j[:, 0] > own
    terms = jnp.where(inner[:, :, None], factors[None], 1.0)
    return jnp.where(wanted[:, None], jnp.prod(terms, axis=1), 0.0)


def pass_states(message, coef):
    gathered = lax.all_gather(message, "wide", axis=0)
    return jnp.sum(coef[:, :, None, None] * gathered.astype(f32), axis=0)


def body(tokens, log_decay, lengths, pad_counts, w_query, w_key, w_value, w_gate, w_out,
         w_first, w_second, w_third, cotangent):
    wide, narrow = lax.axis_size("wide"), lax.axis_size("narrow")
    own_wide, own_narrow = lax.axis_index("wide"), lax.axis_index("narrow")
    heads, local = log_decay.shape
    share, width = tokens.shape
    hn, cols, hd = heads // narrow, width // narrow, width // heads
    blocks, per = local // BLOCK, BLOCK // share
    own = jnp.stack([own_wide, own_narrow]).astype(jnp.int32)

    tok = gather_narrow(tokens)
    cot = gather_narrow(cotangent)
    cot_all = jnp.concatenate(cot, axis=0)

    ends = jnp.cumsum(lengths, dtype=jnp.int32)
    starts = ends - lengths
    place = jnp.arange(local, dtype=jnp.int32)
    spot = own_wide * local + ((place // share) ^ own_narrow) * share + place % share
    inside = (spot[:, None] >= starts[None, :]) & (spot[:, None] < ends[None, :])
    limit = jnp.sum(jnp.where(inside, (ends - pad_counts)[None, :], 0), axis=1, dtype=jnp.int32)
    live = (spot < limit).astype(f32)[:, None]
    first_spot = own_wide * local + BLOCK * jnp.arange(blocks, dtype=jnp.int32)
    keep_seq = 1.0 - jnp.any(first_spot[:, None] == starts[None, :], axis=1).astype(f32)
    summed = jnp.cumsum(log_decay.reshape(heads, blocks, BLOCK), axis=2)
    last = summed[:, :, -1]
    decay = (jnp.exp(last) * keep_seq[None]).T
    factors = gather_factors(jnp.prod(decay, axis=0))
    factors = lax.dynamic_slice_in_dim(factors, own_narrow * hn, hn, 1)
    coef_in, coef_out = between(factors, own_wide, True), between(factors, own_wide, False)

    def slots(first, second):
        return jnp.where(own_narrow // per == 0, jnp.stack([first, second]), jnp.stack([second, first]))

    def own_heads(values):
        return lax.dynamic_slice_in_dim(values, own_narrow * hn, hn, 1)

    one, zero = jnp.ones_like(decay[0]), jnp.zeros_like(decay[0])
    keep = slots(keep_seq[0], keep_seq[1])
    ends_in = slots(decay[1], one)
    enter, enter_other = slots(one, decay[0]), slots(zero, one)
    ahead, leave_other = own_heads(slots(one, decay[0])), own_heads(slots(one, zero))
    leave = own_heads(ends_in)
    g = xor_order(summed.reshape(heads, narrow, share), own_narrow, 1).reshape(heads, local)
    last_of = jnp.where(own_narrow // per == 0, last, last[:, ::-1])

    def columns(values):
        return values.reshape(narrow, hn, local).transpose(0, 2, 1)

    gcol, rise = columns(g), columns(jnp.exp(g))
    tail = columns(jnp.exp(jnp.repeat(last_of, BLOCK, axis=1) - g))
    grow = g.reshape(narrow, hn, blocks, BLOCK).transpose(2, 0, 1, 3).reshape(blocks * narrow, hn, BLOCK)

    shapes = [sds((local, width), bf16), sds((local, width), bf16), *[sds((local, cols), f32)] * 2,
              *[sds((local, width), bf16)] * 3, *[sds((local, width), f32)] * 2,
              sds((blocks, heads, hd, hd), f32)]
    made = []
    for s in range(blocks):
        weight = pl.BlockSpec((width, cols), lambda i, own: (0, i))
        column = pl.BlockSpec((1, BLOCK, hn), lambda i, own, s=s: (i, s, 0))
        full = pl.BlockSpec((BLOCK, width), lambda i, own, s=s: (s, 0))
        mine = pl.BlockSpec((BLOCK, cols), lambda i, own, s=s: (s, 0))
        part = pl.BlockSpec((BLOCK, cols), lambda i, own, s=s: (s, i))
        made = pl.pallas_call(
            functools.partial(forward_kernel, hn, hd, share),
            grid_spec=pltpu.PrefetchScalarGridSpec(
                num_scalar_prefetch=1,
                grid=(narrow,),
                in_specs=[*[whole((share, width))] * 2, *[weight] * 4,
                          pl.BlockSpec((BLOCK, 1), lambda i, own, s=s: (s, 0)), column,
                          pl.BlockSpec((1, hn, BLOCK), lambda i, own, s=s: (s * narrow + i, 0, 0)),
                          column, *[ANY] * len(made)],
                out_specs=[full, full, mine, mine, *[part] * 5,
                           pl.BlockSpec((1, hn, hd, hd), lambda i, own, s=s: (s, i, 0, 0))],
            ),
            out_shape=shapes,
            input_output_aliases={11 + i: i for i in range(len(made))},
            compiler_params=PARAMS,
            name=f"mixer_forward_{s}",
        )(own, tok[per * s], tok[per * s + 1], w_query, w_key, w_value, w_gate, live, gcol, grow, tail, *made)
    n1, tok_all, ql, kl, q, k, v, act, intra, contrib = made

    message = own_heads(contrib)
    message = jnp.sum(own_heads(ends_in)[:, :, None, None] * message, axis=0).astype(bf16)
    states = gather_narrow(pass_states(message, coef_in).astype(bf16))

    up = lambda b: b
    all_blk, part_blk = rows((BLOCK, width), up), rows((BLOCK, cols), up)
    own_blk = pl.BlockSpec((BLOCK, cols), lambda b, own: (b, own[1]))
    own_kent = rows((1, hn, hd, hd), up)
    att, inverse, hidden, n2, kent = pl.pallas_call(
        functools.partial(out_kernel, heads, hn, hd, share),
        grid_spec=pltpu.PrefetchScalarGridSpec(
            num_scalar_prefetch=1,
            grid=(blocks,),
            in_specs=[SMEM, SMEM, SMEM, *[whole((hn, hd, hd))] * narrow, whole((blocks, heads, hd, hd)),
                      *[all_blk] * 4, pl.BlockSpec((narrow, BLOCK, hn), lambda b, own: (0, b, 0)),
                      whole((width, width))],
            out_specs=[all_blk, rows((BLOCK, 1), up), whole((share, width)), all_blk, own_kent],
        ),
        out_shape=[sds((local, width), bf16), sds((local, 1), f32), sds((share, width), f32),
                   sds((local, width), bf16), sds((blocks, hn, hd, hd), bf16)],
        compiler_params=PARAMS,
        name="mixer_out",
    )(own, keep, enter, enter_other, *states, contrib, q, intra, act, tok_all, rise, w_out)

    ff = w_first.shape[1]
    first_t, second_t = w_first.T, w_second.T
    ff_blk = rows((BLOCK, ff), up)
    piece_spec, piece_shape = whole((share, width)), sds((share, width), bf16)
    product, gf, gs, *gn2 = pl.pallas_call(
        functools.partial(ffn_kernel, share),
        grid=(blocks,),
        in_specs=[all_blk, all_blk, *[whole((ff, width))] * 3],
        out_specs=[*[ff_blk] * 3, *[piece_spec] * narrow],
        out_shape=[*[sds((local, ff), bf16)] * 3, *[piece_shape] * narrow],
        compiler_params=PARAMS,
        name="ffn",
    )(n2, cot_all, first_t, second_t, w_third)
    gn2 = trade_narrow(gn2)

    tall, across = ffn_cut(wide, ff, width)[:2]
    slot = (wide // 2, 3, tall, across)
    slot_spec = pl.BlockSpec((wide // 2, 1, tall, across), lambda i, own: (0, i, 0, 0))
    kept, sent, *ffn_part = pl.pallas_call(
        functools.partial(ffn_grad_kernel, wide, share),
        grid_spec=pltpu.PrefetchScalarGridSpec(
            num_scalar_prefetch=1,
            grid=(3,),
            in_specs=[*[whole((local, width))] * 2, *[whole((local, ff))] * 3, whole((ff, width))],
            out_specs=[slot_spec, slot_spec, *[piece_spec] * narrow],
            scratch_shapes=[pltpu.VMEM((ff, width), f32)],
        ),
        out_shape=[sds(slot, bf16), sds(slot, bf16), *[piece_shape] * narrow],
        compiler_params=PARAMS,
        name="ffn_grads",
    )(own, n2, cot_all, product, gf, gs, w_third)
    ff_halves = gather_wide(reduce_wide(kept, sent))
    ffn_part = trade_narrow(ffn_part)
    output = pl.pallas_call(
        functools.partial(output_kernel, narrow),
        out_shape=sds((share, width), bf16),
        compiler_params=pltpu.CompilerParams(vmem_limit_bytes=56 << 20),
        name="output",
    )(*ffn_part, hidden)

    def single(shape, index=None):
        where = index or (lambda own: (0,) * len(shape))
        return pl.BlockSpec(shape, lambda b, own: where(own))

    row_spec = single((share, width))
    grad_hidden, low, ggl, *ga = pl.pallas_call(
        functools.partial(residual_kernel, narrow),
        grid_spec=pltpu.PrefetchScalarGridSpec(
            num_scalar_prefetch=1,
            grid=(1,),
            in_specs=[*[row_spec] * (narrow + 2), single((width, width)), row_spec, single((share, 1)), row_spec],
            out_specs=[row_spec] * 3 + [single((share, cols))] * narrow,
        ),
        out_shape=[sds((share, width), f32), sds((share, width), bf16), sds((share, width), bf16),
                   *[sds((share, cols), bf16)] * narrow],
        compiler_params=PARAMS,
        name="residual_back",
    )(own, *gn2, hidden, cotangent, w_out, att, inverse, act)
    ga = trade_narrow(ga)
    lows = gather_narrow(low)

    own_col = pl.BlockSpec((None, BLOCK, hn), lambda b, own: (own[1], b, 0))
    own_row = pl.BlockSpec((1, hn, BLOCK), lambda b, own: (b * narrow + own[1], 0, 0))
    dq, gk, gv, direct, message = pl.pallas_call(
        functools.partial(query_kernel, hn, hd, share),
        grid_spec=pltpu.PrefetchScalarGridSpec(
            num_scalar_prefetch=1,
            grid=(blocks,),
            in_specs=[SMEM, SMEM, *[whole((share, cols))] * narrow, *[own_blk] * 3, part_blk, own_kent,
                      own_col, own_row, own_col],
            out_specs=[*[part_blk] * 3, own_kent, whole((hn, hd, hd))],
            scratch_shapes=[pltpu.VMEM((BLOCK, cols), bf16)],
        ),
        out_shape=[sds((local, cols), bf16), *[sds((local, cols), f32)] * 2,
                   sds((blocks, hn, hd, hd), f32), sds((hn, hd, hd), f32)],
        compiler_params=PARAMS,
        name="mixer_query_back",
    )(own, keep, ahead, *ga, q, k, v, ql, kent, gcol, grow, rise)

    arrived = pass_states(message.astype(bf16), coef_out)
    pair = (wide // 2, 3, width // wide, cols)
    own_weight = pl.BlockSpec((width, cols), lambda b, own: (0, own[1]))
    kept, sent, *gn1 = pl.pallas_call(
        functools.partial(key_kernel, hn, hd, wide, share),
        grid_spec=pltpu.PrefetchScalarGridSpec(
            num_scalar_prefetch=1,
            grid=(blocks,),
            in_specs=[SMEM, SMEM, whole((hn, hd, hd)), whole((blocks, hn, hd, hd)), all_blk, part_blk,
                      own_blk, own_blk, *[part_blk] * 3, own_col, rows((BLOCK, 1), up), *[own_weight] * 3],
            out_specs=[*[whole(pair)] * 2, *[piece_spec] * narrow],
            scratch_shapes=[*[pltpu.VMEM((BLOCK, cols), bf16)] * 2, *[pltpu.VMEM((width, cols), f32)] * 3],
        ),
        out_shape=[*[sds(pair, bf16)] * 2, *[piece_shape] * narrow],
        compiler_params=PARAMS,
        name="mixer_key_back",
    )(own, leave, leave_other, arrived, direct, n1, dq, k, v, kl, gk, gv, tail, live, w_query, w_key, w_value)

    def collect(kept, sent):
        return gather_wide(jnp.stack(gather_narrow(reduce_wide(kept, sent))))

    pair = (wide // 2, 2, width // wide, cols)
    own_cols = single((local, cols), lambda own: (0, own[1]))
    gate_kept, gate_sent = pl.pallas_call(
        functools.partial(gate_kernel, wide, narrow, share),
        grid_spec=pltpu.PrefetchScalarGridSpec(
            num_scalar_prefetch=1,
            grid=(1,),
            in_specs=[*[row_spec] * narrow, own_cols, single((local, 1)), own_cols, single((local, width)),
                      single((cols, width), lambda own: (own[1], 0))],
            out_specs=[single(pair)] * 2,
            scratch_shapes=[pltpu.VMEM((local, width), bf16), pltpu.VMEM((width, cols), f32),
                            pltpu.VMEM((cols, width), f32)],
        ),
        out_shape=[sds(pair, bf16)] * 2,
        compiler_params=PARAMS,
        name="gate_back",
    )(own, *lows, att, inverse, act, n1, w_out)
    gate_halves = collect(gate_kept, gate_sent)
    square_halves = collect(kept, sent)

    gn1 = trade_narrow(gn1)
    grad_tokens = pl.pallas_call(
        functools.partial(tokens_kernel, narrow),
        out_shape=sds((share, width), f32),
        compiler_params=pltpu.CompilerParams(vmem_limit_bytes=56 << 20),
        name="tokens_back",
    )(*gn1, ggl, w_gate, tokens, grad_hidden)

    chunks = width // across
    grad_first, grad_second, grad_third = widen(
        widen_ffn_kernel, own, ff_halves, [((tall, across), lambda t: (t // chunks, t % chunks))] * 3,
        [(ff, width)] * 3, "widen_ffn",
    )
    square = ((width // wide, width), lambda t: (t, 0))
    grad_gate, grad_out = widen(
        functools.partial(widen_gate_kernel, narrow), own, gate_halves,
        [square, ((narrow, cols // wide, width), lambda t: (0, t, 0))],
        [(width, width), (narrow, cols, width)], "widen_gate",
    )
    mixer = widen(
        functools.partial(widen_square_kernel, 3, narrow), own, square_halves, [square] * 3,
        [(width, width)] * 3, "widen_square",
    )
    return (output, grad_tokens, *mixer, grad_gate, grad_out.reshape(width, width),
            grad_first.T, grad_second.T, grad_third)


def solution(mesh):
    both = P(("wide", "narrow"), None)
    in_specs = (both, P(None, "wide"), P(), P(), P(), P(), P(), P(), P(),
                P(None, "narrow"), P(None, "narrow"), P("narrow", None), both)
    out_specs = (both, both, P(), P(), P(), P(), P(),
                 P(None, "narrow"), P(None, "narrow"), P("narrow", None))
    return jax.shard_map(body, mesh=mesh, in_specs=in_specs, out_specs=out_specs, check_vma=False)
```

time: 679 us -> 362 us (0.53); the launches traced: 670 us -> 360 us
  waiting for transfers between devices: 395 us -> 117 us
  Pallas kernels: 0 us -> 114 us
  matrix products: 95.4 us -> 0 us
  other arithmetic: 66.9 us -> 11 us
  blocking collectives: 0 us -> 20.1 us
  starting transfers between devices: 64.5 us -> 80.2 us
  local copies, waits for them, and re-layouts: 30.2 us -> 15.3 us
  between operations: 16.8 us -> 2.68 us
    psum x1 -> x0, waiting for transfers between devices: 193 us -> none  [body(): lax.psum(weight_grad(normed_one, grad_query_lin).astype(jnp.bfloat16), 'w...]
    pallas_call x0 -> x17, Pallas kernels: none -> 114 us  [the longest x6 30 us: widen(): pl.pallas_call(functools.partial(kernel, places), grid_spec=pltpu.Prefetc...]
    all_gather x4 -> x0, waiting for transfers between devices: 105 us -> none  [the longest x1 40 us: body(): gathered_two = lax.all_gather(normed_two, 'narrow', axis=0, tiled=True)]
    dot_general x36 -> x0, matrix products: 95.4 us -> none  [the longest x8 22.8 us: project(): return jnp.dot(left_hand, right_hand, preferred_element_type=jnp.float32)]
    ppermute x14 -> x63, waiting for transfers between devices: 52.8 us -> 117 us  [the longest x30 71.9 us: swap_narrow(): return lax.ppermute(values, 'narrow', [(i, i ^ k) for i in range(size)])]
    reduce_scatter x2 -> x0, waiting for transfers between devices: 43.1 us -> none  [the longest x1 43.1 us: body(): lax.psum_scatter(transposed(grad_first, w_first) + transposed(grad_second...]
    convert_element_type x27 -> x2, other arithmetic: 42.4 us -> 1.74 us  [the longest x1 0.92 us: body(): arrived = pass_states(message.astype(bf16), coef_out)]
    all_gather x0 -> x2, blocking collectives: none -> 20.1 us  [pass_states(): gathered = lax.all_gather(message, 'wide', axis=0)]
  transfers between devices with their start and end apart: 21 -> 63, of which waited for: 20 -> 24; matrix products, arithmetic and copies ran while one was open for 14% -> 6% of each run, Pallas kernels for 0% -> 22%
where the time goes in v2:
time: 362 us; the launch traced here: 360 us
  waiting for transfers between devices  117 us (32%)
  Pallas kernels  114 us (31%)
  starting transfers between devices  80.2 us (22%)
  blocking collectives  20.1 us (6%)
  local copies, waits for them, and re-layouts  15.3 us (4%)
  other arithmetic  11 us (3%)
    ppermute x30, waiting for transfers between devices, swap_narrow(): return lax.ppermute(values, 'narrow', [(i, i ^ k) for i in range(size)])  71.9 us
    ppermute x30, starting transfers between devices, swap_narrow(): return lax.ppermute(values, 'narrow', [(i, i ^ k) for i in range(size)])  49.9 us
    ppermute x15, waiting for transfers between devices, swap_step(): return lax.ppermute(values, 'wide', [(i, flip(i)) for i in range(size)])  40.4 us
    pallas_call x6, Pallas kernels, widen(): pl.pallas_call(functools.partial(kernel, places), grid_spec=pltpu.Prefetc...  30 us
    pallas_call x2, Pallas kernels, body(): pl.pallas_call(functools.partial(forward_kernel, hn, hd, share), grid_spe...  20.5 us
    all_gather x2, blocking collectives, pass_states(): gathered = lax.all_gather(message, 'wide', axis=0)  20.1 us
    ppermute x15, starting transfers between devices, swap_step(): return lax.ppermute(values, 'wide', [(i, flip(i)) for i in range(size)])  17.4 us
    pallas_call x1, Pallas kernels, body(): pl.pallas_call(functools.partial(key_kernel, hn, hd, wide, share), grid_s...  10.4 us
  transfers between devices with their start and end apart: 63, of which 24 were waited for; matrix products, arithmetic and copies ran while one was open for 6% of the time, Pallas kernels for 22%

profile of v2, /device:TPU:0, one launch (start us, length us, event | category | flops | bytes accessed | tf_op | source)
XLA Modules:
  0.0 360.2 jit_solution(18202888957554067608)
XLA Ops:
  0.7 4.1 %collective-permute-start.3 = (bf16[128,1024]{1,0:T(8,128)(2,1)}, bf16[128,1024]{1,0:T(8,128)(2,1)S(1)}, u32[]{:S(2)}, u32[]{:S(2)}) collective-permute-start(bf16[128,1024]{1,0:T(8,128)(2,1)} %refs_6_.3), channel_id=1, source_target_pairs={{0,2},{1,3},{2,0},{3,1},{4,6},{5,7},{6,4},{7,5},{8,10},{9,11},{10,... | collective-permute-start | bytes 786440 | tf_op jit(solution)/shard_map/ppermute | solution.py:354
  32.5 10.2 %mixer_forward_0.1 = (bf16[512,1024]{1,0:T(8,128)(2,1)}, bf16[512,1024]{1,0:T(8,128)(2,1)}, f32[512,256]{1,0:T(8,128)}, f32[512,256]{1,0:T(8,128)}, bf16[512,102...) custom-call(s32[2]{0:T(128)} %pad_add_fusion.own, ...), custom_call_target="tpu_custom_call" | custom-call | tf_op jit(solution)/shard_map/mixer_forward_0/pallas_call | solution.py:561
  43.5 10.3 %mixer_forward_1.1 = (bf16[512,1024]{1,0:T(8,128)(2,1)}, bf16[512,1024]{1,0:T(8,128)(2,1)}, f32[512,256]{1,0:T(8,128)}, f32[512,256]{1,0:T(8,128)}, bf16[512,102...) custom-call(s32[2]{0:T(128)} %pad_add_fusion.own, ...), custom_call_target="tpu_custom_call", output_to_operand_aliasing={{0}: (11, {}), {1}: (12, {}), {2}: (13, {}), {3}: (14, {}),... | custom-call | tf_op jit(solution)/shard_map/mixer_forward_1/pallas_call | solution.py:561
  54.9 10.0 %all-gather = bf16[16,128,128]{2,1,0:T(8,128)(2,1)S(1)} all-gather(bf16[2,128,128]{2,1,0:T(8,128)(2,1)S(1)} %multiply_reduce_fusion), channel_id=2, replica_groups=mesh['wide'=8,'narrow'=4] {'wide'}, dimensions={0}, use_global_device_ids=true | all-gather | bytes 589824 | tf_op jit(solution)/shard_map/all_gather | solution.py:495
  66.3 2.4 collective-permute-start.7
  69.7 4.3 %collective-permute-done.7.refs_2_ = bf16[2,128,128]{2,1,0:T(8,128)(2,1)S(1)} collective-permute-done((bf16[2,128,128]{2,1,0:T(8,128)(2,1)S(1)}, bf16[2,128,128]{2,1,0:T(8,128)(2,1)S(1)}, u32[]{:S(2)}, u32[]{:S(2)}) %collective-permute-start.7) | collective-permute-done | bytes 65568 | tf_op jit(solution)/shard_map/ppermute | solution.py:354
  75.3 9.6 %mixer_out.1 = (bf16[512,1024]{1,0:T(8,128)(2,1)}, f32[512,1]{1,0:T(8,128)}, f32[128,1024]{1,0:T(8,128)}, bf16[512,1024]{1,0:T(8,128)(2,1)}, bf16[2,2,128,128]{3,2,1,0:T(8,128)(2,1)}) custom-call(s32[2]{0:T(128)} %pad_add_fusion.own, f32[2]{0:T(128)} %broadcast_select_fusion.6.keep, f32[2,8]{1,0:T(2,128)} %select_select_fusion.enter, ...), custom_call_target="tpu_custom_call" | custom-call | tf_op jit(solution)/shard_map/mixer_out/pallas_call | solution.py:588
  85.0 10.1 %ffn.1 = (bf16[512,704]{1,0:T(8,128)(2,1)}, bf16[512,704]{1,0:T(8,128)(2,1)}, bf16[512,704]{1,0:T(8,128)(2,1)}, bf16[128,1024]{1,0:T(8,128)(2,1)}, bf16[128,1024...) custom-call(bf16[512,1024]{1,0:T(8,128)(2,1)} %get-tuple-element.99.n2, ...), custom_call_target="tpu_custom_call" | custom-call | tf_op jit(solution)/shard_map/ffn/pallas_call | solution.py:608
  95.1 10.3 %ffn_grads.1 = (bf16[4,3,704,128]{3,2,1,0:T(8,128)(2,1)}, bf16[4,3,704,128]{3,2,1,0:T(8,128)(2,1)}, bf16[128,1024]{1,0:T(8,128)(2,1)}, bf16[128,1024]{1,0:T(8,12...) custom-call(s32[2]{0:T(128)} %pad_add_fusion.own, bf16[512,1024]{1,0:T(8,128)(2,1)} %get-tuple-element.99.n2, ...), custom_call_target="tpu_custom_call" | custom-call | tf_op jit(solution)/shard_map/ffn_grads/pallas_call | solution.py:622
  111.3 7.9 %collective-permute-done.15.refs_1_ = bf16[128,1024]{1,0:T(8,128)(2,1)S(1)} collective-permute-done((bf16[128,1024]{1,0:T(8,128)(2,1)S(1)}, bf16[128,1024]{1,0:T(8,128)(2,1)S(1)}, u32[]{:S(2)}, u32[]{:S(2)}) %collective-permute-start.15) | collective-permute-done | bytes 262176 | tf_op jit(solution)/shard_map/ppermute | solution.py:354
  119.2 9.0 %collective-permute-done.16.refs_2_ = bf16[128,1024]{1,0:T(8,128)(2,1)S(1)} collective-permute-done((bf16[128,1024]{1,0:T(8,128)(2,1)S(1)}, bf16[128,1024]{1,0:T(8,128)(2,1)S(1)}, u32[]{:S(2)}, u32[]{:S(2)}) %collective-permute-start.16) | collective-permute-done | bytes 262176 | tf_op jit(solution)/shard_map/ppermute | solution.py:354
  129.1 5.4 %residual_back.1 = (f32[128,1024]{1,0:T(8,128)}, bf16[128,1024]{1,0:T(8,128)(2,1)}, bf16[128,1024]{1,0:T(8,128)(2,1)}, bf16[128,256]{1,0:T(8,128)(2,1)}, bf16[12...) custom-call(s32[2]{0:T(128)} %pad_add_fusion.own, ...), custom_call_target="tpu_custom_call" | custom-call | tf_op jit(solution)/shard_map/residual_back/pallas_call | solution.py:649
  134.5 5.3 %collective-permute-start.18 = (bf16[128,256]{1,0:T(8,128)(2,1)}, bf16[128,256]{1,0:T(8,128)(2,1)S(1)}, u32[]{:S(2)}, u32[]{:S(2)}) collective-permute-start(bf16[128,256]{1,0:T(8,128)(2,1)} %get-tuple-element.115), channel_id=1, source_target_pairs={{0,1},{1,0},{2,3},{3,2},{4,5},{5,4},{6,7},{7,6},{8,9},{9,8},{10,11... | collective-permute-start | bytes 196616 | tf_op jit(solution)/shard_map/ppermute | solution.py:354
  145.2 2.6 collective-permute-done.19.refs_2_
  150.3 5.4 %mixer_query_back.1 = (bf16[512,256]{1,0:T(8,128)(2,1)}, f32[512,256]{1,0:T(8,128)}, f32[512,256]{1,0:T(8,128)}, f32[2,2,128,128]{3,2,1,0:T(8,128)}, f32[2,128,128]{2,1,0:T(8,128)}) custom-call(s32[2]{0:T(128)} %pad_add_fusion.own, f32[2]{0:T(128)} %broadcast_select_fusion.6.keep, f32[2,2]{1,0:T(2,128)} %constant_dynamic-slice_fusion.ahead, ...), custom_call_target="tpu_custom_call" | custom-call | tf_op jit(solution)/shard_map/mixer_query_back/pallas_call | solution.py:667
  156.7 10.1 %all-gather.1 = bf16[16,128,128]{2,1,0:T(8,128)(2,1)S(1)} all-gather(bf16[2,128,128]{2,1,0:T(8,128)(2,1)S(1)} %convert_element_type.48), channel_id=3, replica_groups=mesh['wide'=8,'narrow'=4] {'wide'}, dimensions={0}, use_global_device_ids=true | all-gather | bytes 589824 | tf_op jit(solution)/shard_map/all_gather | solution.py:495
  167.5 10.4 %mixer_key_back.1 = (bf16[4,3,128,256]{3,2,1,0:T(8,128)(2,1)}, bf16[4,3,128,256]{3,2,1,0:T(8,128)(2,1)}, bf16[128,1024]{1,0:T(8,128)(2,1)}, bf16[128,1024]{1,0:T...) custom-call(s32[2]{0:T(128)} %pad_add_fusion.own, f32[2,2]{1,0:T(2,128)} %copy-done.43, ...), custom_call_target="tpu_custom_call" | custom-call | tf_op jit(solution)/shard_map/mixer_key_back/pallas_call | solution.py:686
  179.9 5.9 %gate_back.1 = (bf16[4,2,128,256]{3,2,1,0:T(8,128)(2,1)}, bf16[4,2,128,256]{3,2,1,0:T(8,128)(2,1)}) custom-call(s32[2]{0:T(128)} %pad_add_fusion.own, bf16[128,1024]{1,0:T(8,128)(2,1)} %get-tuple-element.143.refs_0_, bf16[128,1024]{1,0:T(8,128)(2,1)} %copy-done.31, bf16[128,1024]{1,0:T(8,128)(2,1)} %copy-done.32, bf16[128,1024]{1,0:T(8,128)(2,1)} %copy-done.33, ...), custom_call_target="tpu_custom_call" | custom-call | tf_op jit(solution)/shard_map/gate_back/pallas_call | solution.py:706
  192.1 3.3 collective-permute-done.41
  196.1 2.4 collective-permute-start.13
  198.5 3.3 collective-permute-done.42
  203.9 3.6 %collective-permute-done.12.refs_1_ = bf16[128,1024]{1,0:T(8,128)(2,1)S(1)} collective-permute-done((bf16[128,1024]{1,0:T(8,128)(2,1)S(1)}, bf16[128,1024]{1,0:T(8,128)(2,1)S(1)}, u32[]{:S(2)}, u32[]{:S(2)}) %collective-permute-start.12) | collective-permute-done | bytes 262176 | tf_op jit(solution)/shard_map/ppermute | solution.py:354
  207.6 2.6 collective-permute-start.43
  210.3 8.7 %collective-permute-done.13.refs_2_ = bf16[128,1024]{1,0:T(8,128)(2,1)S(1)} collective-permute-done((bf16[128,1024]{1,0:T(8,128)(2,1)S(1)}, bf16[128,1024]{1,0:T(8,128)(2,1)S(1)}, u32[]{:S(2)}, u32[]{:S(2)}) %collective-permute-start.13) | collective-permute-done | bytes 262176 | tf_op jit(solution)/shard_map/ppermute | solution.py:354
  220.5 2.2 collective-permute-start.14
  222.6 3.3 collective-permute-done.44
  226.0 2.4 collective-permute-start.22
  228.5 2.3 collective-permute-start.47
  232.2 2.3 collective-permute-done.21.refs_1_
  236.3 15.9 %collective-permute-done.22.refs_2_ = bf16[128,1024]{1,0:T(8,128)(2,1)S(1)} collective-permute-done((bf16[128,1024]{1,0:T(8,128)(2,1)S(1)}, bf16[128,1024]{1,0:T(8,128)(2,1)S(1)}, u32[]{:S(2)}, u32[]{:S(2)}) %collective-permute-start.22) | collective-permute-done | bytes 262176 | tf_op jit(solution)/shard_map/ppermute | solution.py:354
  252.2 2.6 collective-permute-start.27
  256.0 4.5 %collective-permute-done.28 = bf16[3,128,256]{2,1,0:T(8,128)(2,1)S(1)} collective-permute-done((bf16[3,128,256]{2,1,0:T(8,128)(2,1)S(1)}, bf16[3,128,256]{2,1,0:T(8,128)(2,1)S(1)}, u32[]{:S(2)}, u32[]{:S(2)}) %collective-permute-start.28) | collective-permute-done | bytes 196640 | tf_op jit(solution)/shard_map/ppermute | solution.py:354
  263.1 8.1 %collective-permute-done.23.refs_3_ = bf16[128,1024]{1,0:T(8,128)(2,1)S(1)} collective-permute-done((bf16[128,1024]{1,0:T(8,128)(2,1)S(1)}, bf16[128,1024]{1,0:T(8,128)(2,1)S(1)}, u32[]{:S(2)}, u32[]{:S(2)}) %collective-permute-start.23) | collective-permute-done | bytes 262176 | tf_op jit(solution)/shard_map/ppermute | solution.py:354
  276.6 11.0 %collective-permute-done.51.refs_3_ = bf16[4,2,128,256]{3,2,1,0:T(8,128)(2,1)S(1)} collective-permute-done((bf16[4,2,128,256]{3,2,1,0:T(8,128)(2,1)S(1)}, bf16[4,2,128,256]{3,2,1,0:T(8,128)(2,1)S(1)}, u32[]{:S(2)}, u32[]{:S(2)}) %collective-permute-start.51) | collective-permute-done | bytes 524320 | tf_op jit(solution)/shard_map/ppermute | solution.py:374
  287.6 3.0 collective-permute-done.31.refs_1_
  290.6 2.4 collective-permute-start.35
  293.1 8.1 %collective-permute-done.33.refs_2_ = bf16[4,3,128,256]{3,2,1,0:T(8,128)(2,1)S(1)} collective-permute-done((bf16[4,3,128,256]{3,2,1,0:T(8,128)(2,1)S(1)}, bf16[4,3,128,256]{3,2,1,0:T(8,128)(2,1)S(1)}, u32[]{:S(2)}, u32[]{:S(2)}) %collective-permute-start.33) | collective-permute-done | bytes 786464 | tf_op jit(solution)/shard_map/ppermute | solution.py:374
  305.2 4.5 %collective-permute-done.35.refs_3_ = bf16[4,3,128,256]{3,2,1,0:T(8,128)(2,1)S(1)} collective-permute-done((bf16[4,3,128,256]{3,2,1,0:T(8,128)(2,1)S(1)}, bf16[4,3,128,256]{3,2,1,0:T(8,128)(2,1)S(1)}, u32[]{:S(2)}, u32[]{:S(2)}) %collective-permute-start.35) | collective-permute-done | bytes 786464 | tf_op jit(solution)/shard_map/ppermute | solution.py:374
  312.2 3.4 collective-permute-done.59.refs_2_
  317.5 3.9 %collective-permute-done.61.refs_3_ = bf16[3,704,128]{2,1,0:T(8,128)(2,1)} collective-permute-done((bf16[3,704,128]{2,1,0:T(8,128)(2,1)S(1)}, bf16[3,704,128]{2,1,0:T(8,128)(2,1)}, u32[]{:S(2)}, u32[]{:S(2)}) %collective-permute-start.61) | collective-permute-done | bytes 540704 | tf_op jit(solution)/shard_map/ppermute | solution.py:374
  323.0 2.2 output.1
  325.2 4.0 %tokens_back.1 = f32[128,1024]{1,0:T(8,128)} custom-call(bf16[128,1024]{1,0:T(8,128)(2,1)} %get-tuple-element.129.refs_0_, bf16[128,1024]{1,0:T(8,128)(2,1)} %copy-done.28, bf16[128,1024]{1,0:T(8,128)(2,1)} %copy-done.29, bf16[128,1024]{1,0:T(8,128)(2,1)} %copy-done.30, bf16[128,1024]{1,0:T(8,128)(2,1)} %get-tuple-element.133.refs_4_, ...), custom_call_target="tpu_custom_call" | custom-call | tf_op jit(solution)/shard_map/tokens_back/pallas_call | solution.py:725
  329.3 4.7 %widen_gate_0.1 = (f32[1024,1024]{1,0:T(8,128)}, f32[4,256,1024]{2,1,0:T(8,128)}) custom-call(s32[2]{0:T(128)} %pad_add_fusion.own, bf16[4,2,128,256]{3,2,1,0:T(8,128)(2,1)} %copy-done.4, bf16[4,2,128,256]{3,2,1,0:T(8,128)(2,1)} %copy-done.15, bf16[4,2,128,256]{3,2,1,0:T(8,128)(2,1)} %copy-done.16, bf16[4,2,128,256]{3,2,1,0:T(8,128)(2,1)} %copy-done.17), custom_call_target="tpu_custom_call" | custom-call | tf_op jit(solution)/shard_map/widen_gate_0/pallas_call | solution.py:446
  333.9 4.7 %widen_gate_1.1 = (f32[1024,1024]{1,0:T(8,128)}, f32[4,256,1024]{2,1,0:T(8,128)}) custom-call(s32[2]{0:T(128)} %pad_add_fusion.own, bf16[4,2,128,256]{3,2,1,0:T(8,128)(2,1)} %copy-done.18, bf16[4,2,128,256]{3,2,1,0:T(8,128)(2,1)} %copy-done.19, bf16[4,2,128,256]{3,2,1,0:T(8,128)(2,1)} %copy-done.20, ...), custom_call_target="tpu_custom_call", output_to_operand_aliasing={{0}: (5, {}), {1}: (6, {})} | custom-call | tf_op jit(solution)/shard_map/widen_gate_1/pallas_call | solution.py:446
  338.6 5.6 %widen_square_0.1 = (f32[1024,1024]{1,0:T(8,128)}, f32[1024,1024]{1,0:T(8,128)}, f32[1024,1024]{1,0:T(8,128)}) custom-call(s32[2]{0:T(128)} %pad_add_fusion.own, bf16[4,3,128,256]{3,2,1,0:T(8,128)(2,1)} %copy-done.1, bf16[4,3,128,256]{3,2,1,0:T(8,128)(2,1)} %copy-done.11, bf16[4,3,128,256]{3,2,1,0:T(8,128)(2,1)} %copy-done.12, ...), custom_call_target="tpu_custom_call" | custom-call | tf_op jit(solution)/shard_map/widen_square_0/pallas_call | solution.py:446
  345.1 5.6 %widen_square_1.1 = (f32[1024,1024]{1,0:T(8,128)}, f32[1024,1024]{1,0:T(8,128)}, f32[1024,1024]{1,0:T(8,128)}) custom-call(s32[2]{0:T(128)} %pad_add_fusion.own, bf16[4,3,128,256]{3,2,1,0:T(8,128)(2,1)} %copy-done.6, bf16[4,3,128,256]{3,2,1,0:T(8,128)(2,1)} %copy-done.7, ...), custom_call_target="tpu_custom_call", output_to_operand_aliasing={{0}: (5, {}), {1}: (6, {}), {2}: (7, {})} | custom-call | tf_op jit(solution)/shard_map/widen_square_1/pallas_call | solution.py:446
  350.6 4.8 %widen_ffn_0.1 = (f32[704,1024]{1,0:T(8,128)}, f32[704,1024]{1,0:T(8,128)}, f32[704,1024]{1,0:T(8,128)}) custom-call(s32[2]{0:T(128)} %pad_add_fusion.own, bf16[3,704,128]{2,1,0:T(8,128)(2,1)} %copy-done.3, bf16[3,704,128]{2,1,0:T(8,128)(2,1)} %copy-done.14, bf16[3,704,128]{2,1,0:T(8,128)(2,1)} %collective-permute-done.59.refs_2_, ...), custom_call_target="tpu_custom_call" | custom-call | tf_op jit(solution)/shard_map/widen_ffn_0/pallas_call | solution.py:446
  355.4 4.8 %widen_ffn_1.1 = (f32[704,1024]{1,0:T(8,128)}, f32[704,1024]{1,0:T(8,128)}, f32[704,1024]{1,0:T(8,128)}) custom-call(s32[2]{0:T(128)} %pad_add_fusion.own, bf16[3,704,128]{2,1,0:T(8,128)(2,1)} %collective-permute-done.56.refs_0_, bf16[3,704,128]{2,1,0:T(8,128)(2,1)} %collective-permute-done.58.refs_1_, ...), custom_call_target="tpu_custom_call", output_to_operand_aliasing={{0}: (5, {}), {1}: (6, {}), {2}: (7, {})} | custom-call | tf_op jit(solution)/shard_map/widen_ffn_1/pallas_call | solution.py:446
  (284 shorter events, 84.2 us)
Async XLA Ops:
  0.7 42.0 %collective-permute-start.3 = (bf16[128,1024]{1,0:T(8,128)(2,1)}, bf16[128,1024]{1,0:T(8,128)(2,1)S(1)}, u32[]{:S(2)}, u32[]{:S(2)}) collective-permute-start(bf16[128,1024]{1,0:T(8,128)(2,1)} %refs_6_.3), channel_id=1, source_target_pairs={{0,2},{1,3},{2,0},{3,1},{4,6},{5,7},{6,4},{7,5},{8,10},{9,11},{10,... | collective-permute-start | bytes 786440 | tf_op jit(solution)/shard_map/ppermute | solution.py:354
  4.8 37.9 %collective-permute-start.4 = (bf16[128,1024]{1,0:T(8,128)(2,1)}, bf16[128,1024]{1,0:T(8,128)(2,1)S(1)}, u32[]{:S(2)}, u32[]{:S(2)}) collective-permute-start(bf16[128,1024]{1,0:T(8,128)(2,1)} %refs_6_.3), channel_id=1, source_target_pairs={{0,3},{1,2},{2,1},{3,0},{4,7},{5,6},{6,5},{7,4},{8,11},{9,10},{10,... | collective-permute-start | bytes 786440 | tf_op jit(solution)/shard_map/ppermute | solution.py:354
  6.2 25.4 %collective-permute-start.5 = (bf16[128,1024]{1,0:T(8,128)(2,1)}, bf16[128,1024]{1,0:T(8,128)(2,1)S(1)}, u32[]{:S(2)}, u32[]{:S(2)}) collective-permute-start(bf16[128,1024]{1,0:T(8,128)(2,1)} %refs_6_.3), channel_id=1, source_target_pairs={{0,1},{1,0},{2,3},{3,2},{4,5},{5,4},{6,7},{7,6},{8,9},{9,8},{10,11... | collective-permute-start | bytes 786440 | tf_op jit(solution)/shard_map/ppermute | solution.py:354
  8.8 13.2 %collective-permute-start = (f32[1,8]{1,0:T(1,128)S(1)}, f32[1,8]{1,0:T(1,128)S(1)}, u32[]{:S(2)}, u32[]{:S(2)}) collective-permute-start(f32[1,8]{1,0:T(1,128)S(1)} %bitcast.85), channel_id=1, source_target_pairs={{0,4},{4,0},{8,12},{12,8},{16,20},{20,16},{24,28},{28,24},{1,5},{5... | collective-permute-start | bytes 104 | tf_op jit(solution)/shard_map/ppermute | solution.py:477
  8.8 59.8 %collective-permute-start.9 = (bf16[128,1024]{1,0:T(8,128)(2,1)}, bf16[128,1024]{1,0:T(8,128)(2,1)S(1)}, u32[]{:S(2)}, u32[]{:S(2)}) collective-permute-start(bf16[128,1024]{1,0:T(8,128)(2,1)} %refs_5_.2), channel_id=1, source_target_pairs={{0,1},{1,0},{2,3},{3,2},{4,5},{5,4},{6,7},{7,6},{8,9},{9,8},{10,11... | collective-permute-start | bytes 786440 | tf_op jit(solution)/shard_map/ppermute | solution.py:354
  29.4 40.2 %collective-permute-start.10 = (bf16[128,1024]{1,0:T(8,128)(2,1)S(1)}, bf16[128,1024]{1,0:T(8,128)(2,1)S(1)}, u32[]{:S(2)}, u32[]{:S(2)}) collective-permute-start(bf16[128,1024]{1,0:T(8,128)(2,1)S(1)} %copy-done.5), channel_id=1, source_target_pairs={{0,2},{1,3},{2,0},{3,1},{4,6},{5,7},{6,4},{7,5},{8,10},{9,11},{10,... | collective-permute-start | bytes 786440 | tf_op jit(solution)/shard_map/ppermute | solution.py:354
  31.5 38.1 %collective-permute-start.11 = (bf16[128,1024]{1,0:T(8,128)(2,1)S(1)}, bf16[128,1024]{1,0:T(8,128)(2,1)S(1)}, u32[]{:S(2)}, u32[]{:S(2)}) collective-permute-start(bf16[128,1024]{1,0:T(8,128)(2,1)S(1)} %copy-done.5), channel_id=1, source_target_pairs={{0,3},{1,2},{2,1},{3,0},{4,7},{5,6},{6,5},{7,4},{8,11},{9,10},{10,... | collective-permute-start | bytes 786440 | tf_op jit(solution)/shard_map/ppermute | solution.py:354
  105.4 85.7 %collective-permute-start.53 = (bf16[4,3,704,128]{3,2,1,0:T(8,128)(2,1)}, bf16[4,3,704,128]{3,2,1,0:T(8,128)(2,1)S(1)}, u32[]{:S(2)}, u32[]{:S(2)}) collective-permute-start(bf16[4,3,704,128]{3,2,1,0:T(8,128)(2,1)} %get-tuple-element.151), channel_id=1, source_target_pairs={{0,4},{4,0},{8,12},{12,8},{16,20},{20,16},{24,28},{28,24},{1,5},{5... | collective-permute-start | bytes 6488072 | tf_op jit(solution)/shard_map/ppermute | solution.py:367
  105.5 13.7 %collective-permute-start.15 = (bf16[128,1024]{1,0:T(8,128)(2,1)S(1)}, bf16[128,1024]{1,0:T(8,128)(2,1)S(1)}, u32[]{:S(2)}, u32[]{:S(2)}) collective-permute-start(bf16[128,1024]{1,0:T(8,128)(2,1)S(1)} %copy-done.56), channel_id=1, source_target_pairs={{0,1},{1,0},{2,3},{3,2},{4,5},{5,4},{6,7},{7,6},{8,9},{9,8},{10,11... | collective-permute-start | bytes 786440 | tf_op jit(solution)/shard_map/ppermute | solution.py:354
  106.9 21.4 %collective-permute-start.16 = (bf16[128,1024]{1,0:T(8,128)(2,1)S(1)}, bf16[128,1024]{1,0:T(8,128)(2,1)S(1)}, u32[]{:S(2)}, u32[]{:S(2)}) collective-permute-start(bf16[128,1024]{1,0:T(8,128)(2,1)S(1)} %copy-done.55), channel_id=1, source_target_pairs={{0,2},{1,3},{2,0},{3,1},{4,6},{5,7},{6,4},{7,5},{8,10},{9,11},{10,... | collective-permute-start | bytes 786440 | tf_op jit(solution)/shard_map/ppermute | solution.py:354
  108.4 19.8 %collective-permute-start.17 = (bf16[128,1024]{1,0:T(8,128)(2,1)S(1)}, bf16[128,1024]{1,0:T(8,128)(2,1)S(1)}, u32[]{:S(2)}, u32[]{:S(2)}) collective-permute-start(bf16[128,1024]{1,0:T(8,128)(2,1)S(1)} %copy-done.54), channel_id=1, source_target_pairs={{0,3},{1,2},{2,1},{3,0},{4,7},{5,6},{6,5},{7,4},{8,11},{9,10},{10,... | collective-permute-start | bytes 786440 | tf_op jit(solution)/shard_map/ppermute | solution.py:354
  142.3 36.0 %collective-permute-start.37 = (bf16[128,1024]{1,0:T(8,128)(2,1)}, bf16[128,1024]{1,0:T(8,128)(2,1)S(1)}, u32[]{:S(2)}, u32[]{:S(2)}) collective-permute-start(bf16[128,1024]{1,0:T(8,128)(2,1)} %get-tuple-element.143.refs_0_), channel_id=1, source_target_pairs={{0,1},{1,0},{2,3},{3,2},{4,5},{5,4},{6,7},{7,6},{8,9},{9,8},{10,11... | collective-permute-start | bytes 786440 | tf_op jit(solution)/shard_map/ppermute | solution.py:354
  143.4 35.0 %collective-permute-start.38 = (bf16[128,1024]{1,0:T(8,128)(2,1)}, bf16[128,1024]{1,0:T(8,128)(2,1)S(1)}, u32[]{:S(2)}, u32[]{:S(2)}) collective-permute-start(bf16[128,1024]{1,0:T(8,128)(2,1)} %get-tuple-element.143.refs_0_), channel_id=1, source_target_pairs={{0,2},{1,3},{2,0},{3,1},{4,6},{5,7},{6,4},{7,5},{8,10},{9,11},{10,... | collective-permute-start | bytes 786440 | tf_op jit(solution)/shard_map/ppermute | solution.py:354
  147.8 30.5 %collective-permute-start.39 = (bf16[128,1024]{1,0:T(8,128)(2,1)}, bf16[128,1024]{1,0:T(8,128)(2,1)S(1)}, u32[]{:S(2)}, u32[]{:S(2)}) collective-permute-start(bf16[128,1024]{1,0:T(8,128)(2,1)} %get-tuple-element.143.refs_0_), channel_id=1, source_target_pairs={{0,3},{1,2},{2,1},{3,0},{4,7},{5,6},{6,5},{7,4},{8,11},{9,10},{10,... | collective-permute-start | bytes 786440 | tf_op jit(solution)/shard_map/ppermute | solution.py:354
  177.9 11.6 %collective-permute-start.24 = (bf16[4,3,128,256]{3,2,1,0:T(8,128)(2,1)}, bf16[4,3,128,256]{3,2,1,0:T(8,128)(2,1)S(1)}, u32[]{:S(2)}, u32[]{:S(2)}) collective-permute-start(bf16[4,3,128,256]{3,2,1,0:T(8,128)(2,1)} %get-tuple-element.136), channel_id=1, source_target_pairs={{0,4},{4,0},{8,12},{12,8},{16,20},{20,16},{24,28},{28,24},{1,5},{5... | collective-permute-start | bytes 2359304 | tf_op jit(solution)/shard_map/ppermute | solution.py:367
  189.6 18.0 %collective-permute-start.25 = (bf16[2,3,128,256]{3,2,1,0:T(8,128)(2,1)S(1)}, bf16[2,3,128,256]{3,2,1,0:T(8,128)(2,1)S(1)}, u32[]{:S(2)}, u32[]{:S(2)}) collective-permute-start(bf16[2,3,128,256]{3,2,1,0:T(8,128)(2,1)S(1)} %get-tuple-element.163), channel_id=1, source_target_pairs={{0,8},{4,20},{8,0},{12,28},{16,24},{20,4},{24,16},{28,12},{1,9},{5... | collective-permute-start | bytes 1179656 | tf_op jit(solution)/shard_map/ppermute | solution.py:374
  191.5 60.7 %collective-permute-start.54 = (bf16[2,3,704,128]{3,2,1,0:T(8,128)(2,1)S(1)}, bf16[2,3,704,128]{3,2,1,0:T(8,128)(2,1)S(1)}, u32[]{:S(2)}, u32[]{:S(2)}) collective-permute-start(bf16[2,3,704,128]{3,2,1,0:T(8,128)(2,1)S(1)} %get-tuple-element.161), channel_id=1, source_target_pairs={{0,8},{4,20},{8,0},{12,28},{16,24},{20,4},{24,16},{28,12},{1,9},{5... | collective-permute-start | bytes 3244040 | tf_op jit(solution)/shard_map/ppermute | solution.py:374
  196.0 11.5 %collective-permute-start.12 = (bf16[128,1024]{1,0:T(8,128)(2,1)S(1)}, bf16[128,1024]{1,0:T(8,128)(2,1)S(1)}, u32[]{:S(2)}, u32[]{:S(2)}) collective-permute-start(bf16[128,1024]{1,0:T(8,128)(2,1)S(1)} %copy-done.50), channel_id=1, source_target_pairs={{0,1},{1,0},{2,3},{3,2},{4,5},{5,4},{6,7},{7,6},{8,9},{9,8},{10,11... | collective-permute-start | bytes 786440 | tf_op jit(solution)/shard_map/ppermute | solution.py:354
  196.1 22.8 %collective-permute-start.13 = (bf16[128,1024]{1,0:T(8,128)(2,1)S(1)}, bf16[128,1024]{1,0:T(8,128)(2,1)S(1)}, u32[]{:S(2)}, u32[]{:S(2)}) collective-permute-start(bf16[128,1024]{1,0:T(8,128)(2,1)S(1)} %copy-done.49), channel_id=1, source_target_pairs={{0,2},{1,3},{2,0},{3,1},{4,6},{5,7},{6,4},{7,5},{8,10},{9,11},{10,... | collective-permute-start | bytes 786440 | tf_op jit(solution)/shard_map/ppermute | solution.py:354
  201.8 18.6 %collective-permute-start.45 = (bf16[2,128,256]{2,1,0:T(8,128)(2,1)S(1)}, bf16[2,128,256]{2,1,0:T(8,128)(2,1)S(1)}, u32[]{:S(2)}, u32[]{:S(2)}) collective-permute-start(bf16[2,128,256]{2,1,0:T(8,128)(2,1)S(1)} %bitcast.64), channel_id=1, source_target_pairs={{0,3},{1,2},{2,1},{3,0},{4,7},{5,6},{6,5},{7,4},{8,11},{9,10},{10,... | collective-permute-start | bytes 393224 | tf_op jit(solution)/shard_map/ppermute | solution.py:354
  207.5 18.4 %collective-permute-start.44 = (bf16[2,128,256]{2,1,0:T(8,128)(2,1)S(1)}, bf16[2,128,256]{2,1,0:T(8,128)(2,1)S(1)}, u32[]{:S(2)}, u32[]{:S(2)}) collective-permute-start(bf16[2,128,256]{2,1,0:T(8,128)(2,1)S(1)} %bitcast.65), channel_id=1, source_target_pairs={{0,2},{1,3},{2,0},{3,1},{4,6},{5,7},{6,4},{7,5},{8,10},{9,11},{10,... | collective-permute-start | bytes 393224 | tf_op jit(solution)/shard_map/ppermute | solution.py:354
  207.6 18.3 %collective-permute-start.43 = (bf16[2,128,256]{2,1,0:T(8,128)(2,1)S(1)}, bf16[2,128,256]{2,1,0:T(8,128)(2,1)S(1)}, u32[]{:S(2)}, u32[]{:S(2)}) collective-permute-start(bf16[2,128,256]{2,1,0:T(8,128)(2,1)S(1)} %bitcast.66), channel_id=1, source_target_pairs={{0,1},{1,0},{2,3},{3,2},{4,5},{5,4},{6,7},{7,6},{8,9},{9,8},{10,11... | collective-permute-start | bytes 393224 | tf_op jit(solution)/shard_map/ppermute | solution.py:354
  219.0 9.5 %collective-permute-start.26 = (bf16[1,3,128,256]{3,2,1,0:T(8,128)(2,1)S(1)}, bf16[1,3,128,256]{3,2,1,0:T(8,128)(2,1)S(1)}, u32[]{:S(2)}, u32[]{:S(2)}) collective-permute-start(bf16[1,3,128,256]{3,2,1,0:T(8,128)(2,1)S(1)} %slice_add_fusion.8), channel_id=1, source_target_pairs={{0,16},{4,12},{8,24},{12,4},{16,0},{20,28},{24,8},{28,20},{1,17},{... | collective-permute-start | bytes 589832 | tf_op jit(solution)/shard_map/ppermute | solution.py:374
  220.5 11.2 %collective-permute-start.14 = (bf16[128,1024]{1,0:T(8,128)(2,1)S(1)}, bf16[128,1024]{1,0:T(8,128)(2,1)}, u32[]{:S(2)}, u32[]{:S(2)}) collective-permute-start(bf16[128,1024]{1,0:T(8,128)(2,1)S(1)} %copy-done.48), channel_id=1, source_target_pairs={{0,3},{1,2},{2,1},{3,0},{4,7},{5,6},{6,5},{7,4},{8,11},{9,10},{10,... | collective-permute-start | bytes 786440 | tf_op jit(solution)/shard_map/ppermute | solution.py:354
  226.0 26.2 %collective-permute-start.22 = (bf16[128,1024]{1,0:T(8,128)(2,1)S(1)}, bf16[128,1024]{1,0:T(8,128)(2,1)S(1)}, u32[]{:S(2)}, u32[]{:S(2)}) collective-permute-start(bf16[128,1024]{1,0:T(8,128)(2,1)S(1)} %copy-done.52), channel_id=1, source_target_pairs={{0,2},{1,3},{2,0},{3,1},{4,6},{5,7},{6,4},{7,5},{8,10},{9,11},{10,... | collective-permute-start | bytes 786440 | tf_op jit(solution)/shard_map/ppermute | solution.py:354
  228.5 32.1 %collective-permute-start.47 = (bf16[4,2,128,256]{3,2,1,0:T(8,128)(2,1)S(1)}, bf16[4,2,128,256]{3,2,1,0:T(8,128)(2,1)S(1)}, u32[]{:S(2)}, u32[]{:S(2)}) collective-permute-start(bf16[4,2,128,256]{3,2,1,0:T(8,128)(2,1)S(1)} %pad_maximum_fusion.1.refs_0_), channel_id=1, source_target_pairs={{0,16},{4,12},{8,24},{12,4},{16,0},{20,28},{24,8},{28,20},{1,17},{... | collective-permute-start | bytes 1572872 | tf_op jit(solution)/shard_map/ppermute | solution.py:374
  231.6 41.1 %collective-permute-start.49 = (bf16[4,2,128,256]{3,2,1,0:T(8,128)(2,1)S(1)}, bf16[4,2,128,256]{3,2,1,0:T(8,128)(2,1)S(1)}, u32[]{:S(2)}, u32[]{:S(2)}) collective-permute-start(bf16[4,2,128,256]{3,2,1,0:T(8,128)(2,1)S(1)} %pad_maximum_fusion.1.refs_0_), channel_id=1, source_target_pairs={{0,8},{4,20},{8,0},{12,28},{16,24},{20,4},{24,16},{28,12},{1,9},{5... | collective-permute-start | bytes 1572872 | tf_op jit(solution)/shard_map/ppermute | solution.py:374
  234.4 20.5 %collective-permute-start.29 = (bf16[3,128,256]{2,1,0:T(8,128)(2,1)S(1)}, bf16[3,128,256]{2,1,0:T(8,128)(2,1)S(1)}, u32[]{:S(2)}, u32[]{:S(2)}) collective-permute-start(bf16[3,128,256]{2,1,0:T(8,128)(2,1)S(1)} %bitcast.61), channel_id=1, source_target_pairs={{0,3},{1,2},{2,1},{3,0},{4,7},{5,6},{6,5},{7,4},{8,11},{9,10},{10,... | collective-permute-start | bytes 589832 | tf_op jit(solution)/shard_map/ppermute | solution.py:354
  254.9 19.5 %collective-permute-start.55 = (bf16[1,3,704,128]{3,2,1,0:T(8,128)(2,1)S(1)}, bf16[1,3,704,128]{3,2,1,0:T(8,128)(2,1)S(1)}, u32[]{:S(2)}, u32[]{:S(2)}) collective-permute-start(bf16[1,3,704,128]{3,2,1,0:T(8,128)(2,1)S(1)} %slice_add_fusion.2), channel_id=1, source_target_pairs={{0,16},{4,12},{8,24},{12,4},{16,0},{20,28},{24,8},{28,20},{1,17},{... | collective-permute-start | bytes 1622024 | tf_op jit(solution)/shard_map/ppermute | solution.py:374
  260.5 12.2 %collective-permute-start.46 = (bf16[4,2,128,256]{3,2,1,0:T(8,128)(2,1)S(1)}, bf16[4,2,128,256]{3,2,1,0:T(8,128)(2,1)S(1)}, u32[]{:S(2)}, u32[]{:S(2)}) collective-permute-start(bf16[4,2,128,256]{3,2,1,0:T(8,128)(2,1)S(1)} %pad_maximum_fusion.1.refs_0_), channel_id=1, source_target_pairs={{0,4},{4,0},{8,12},{12,8},{16,20},{20,16},{24,28},{28,24},{1,5},{5... | collective-permute-start | bytes 1572872 | tf_op jit(solution)/shard_map/ppermute | solution.py:367
  260.5 13.1 %collective-permute-start.48 = (bf16[4,2,128,256]{3,2,1,0:T(8,128)(2,1)S(1)}, bf16[4,2,128,256]{3,2,1,0:T(8,128)(2,1)S(1)}, u32[]{:S(2)}, u32[]{:S(2)}) collective-permute-start(bf16[4,2,128,256]{3,2,1,0:T(8,128)(2,1)S(1)} %collective-permute-done.47.refs_1_), channel_id=1, source_target_pairs={{0,4},{4,0},{8,12},{12,8},{16,20},{20,16},{24,28},{28,24},{1,5},{5... | collective-permute-start | bytes 1572872 | tf_op jit(solution)/shard_map/ppermute | solution.py:367
  261.0 10.2 %collective-permute-start.23 = (bf16[128,1024]{1,0:T(8,128)(2,1)S(1)}, bf16[128,1024]{1,0:T(8,128)(2,1)S(1)}, u32[]{:S(2)}, u32[]{:S(2)}) collective-permute-start(bf16[128,1024]{1,0:T(8,128)(2,1)S(1)} %copy-done.51), channel_id=1, source_target_pairs={{0,3},{1,2},{2,1},{3,0},{4,7},{5,6},{6,5},{7,4},{8,11},{9,10},{10,... | collective-permute-start | bytes 786440 | tf_op jit(solution)/shard_map/ppermute | solution.py:354
  271.2 19.4 %collective-permute-start.31 = (bf16[4,3,128,256]{3,2,1,0:T(8,128)(2,1)S(1)}, bf16[4,3,128,256]{3,2,1,0:T(8,128)(2,1)S(1)}, u32[]{:S(2)}, u32[]{:S(2)}) collective-permute-start(bf16[4,3,128,256]{3,2,1,0:T(8,128)(2,1)S(1)} %pad_maximum_fusion.refs_0_), channel_id=1, source_target_pairs={{0,16},{4,12},{8,24},{12,4},{16,0},{20,28},{24,8},{28,20},{1,17},{... | collective-permute-start | bytes 2359304 | tf_op jit(solution)/shard_map/ppermute | solution.py:374
  272.8 14.9 %collective-permute-start.51 = (bf16[4,2,128,256]{3,2,1,0:T(8,128)(2,1)S(1)}, bf16[4,2,128,256]{3,2,1,0:T(8,128)(2,1)S(1)}, u32[]{:S(2)}, u32[]{:S(2)}) collective-permute-start(bf16[4,2,128,256]{3,2,1,0:T(8,128)(2,1)S(1)} %collective-permute-done.47.refs_1_), channel_id=1, source_target_pairs={{0,8},{4,20},{8,0},{12,28},{16,24},{20,4},{24,16},{28,12},{1,9},{5... | collective-permute-start | bytes 1572872 | tf_op jit(solution)/shard_map/ppermute | solution.py:374
  273.6 19.5 %collective-permute-start.30 = (bf16[4,3,128,256]{3,2,1,0:T(8,128)(2,1)S(1)}, bf16[4,3,128,256]{3,2,1,0:T(8,128)(2,1)S(1)}, u32[]{:S(2)}, u32[]{:S(2)}) collective-permute-start(bf16[4,3,128,256]{3,2,1,0:T(8,128)(2,1)S(1)} %pad_maximum_fusion.refs_0_), channel_id=1, source_target_pairs={{0,4},{4,0},{8,12},{12,8},{16,20},{20,16},{24,28},{28,24},{1,5},{5... | collective-permute-start | bytes 2359304 | tf_op jit(solution)/shard_map/ppermute | solution.py:367
  274.4 26.9 %collective-permute-start.33 = (bf16[4,3,128,256]{3,2,1,0:T(8,128)(2,1)S(1)}, bf16[4,3,128,256]{3,2,1,0:T(8,128)(2,1)S(1)}, u32[]{:S(2)}, u32[]{:S(2)}) collective-permute-start(bf16[4,3,128,256]{3,2,1,0:T(8,128)(2,1)S(1)} %pad_maximum_fusion.refs_0_), channel_id=1, source_target_pairs={{0,8},{4,20},{8,0},{12,28},{16,24},{20,4},{24,16},{28,12},{1,9},{5... | collective-permute-start | bytes 2359304 | tf_op jit(solution)/shard_map/ppermute | solution.py:374
  275.8 28.8 %collective-permute-start.57 = (bf16[3,704,128]{2,1,0:T(8,128)(2,1)S(1)}, bf16[3,704,128]{2,1,0:T(8,128)(2,1)S(1)}, u32[]{:S(2)}, u32[]{:S(2)}) collective-permute-start(bf16[3,704,128]{2,1,0:T(8,128)(2,1)S(1)} %fusion.3.refs_0_), channel_id=1, source_target_pairs={{0,16},{4,12},{8,24},{12,4},{16,0},{20,28},{24,8},{28,20},{1,17},{... | collective-permute-start | bytes 1622024 | tf_op jit(solution)/shard_map/ppermute | solution.py:374
  287.6 15.6 %collective-permute-start.52 = (bf16[4,2,128,256]{3,2,1,0:T(8,128)(2,1)S(1)}, bf16[4,2,128,256]{3,2,1,0:T(8,128)(2,1)S(1)}, u32[]{:S(2)}, u32[]{:S(2)}) collective-permute-start(bf16[4,2,128,256]{3,2,1,0:T(8,128)(2,1)S(1)} %collective-permute-done.51.refs_3_), channel_id=1, source_target_pairs={{0,4},{4,0},{8,12},{12,8},{16,20},{20,16},{24,28},{28,24},{1,5},{5... | collective-permute-start | bytes 1572872 | tf_op jit(solution)/shard_map/ppermute | solution.py:367
  290.6 19.1 %collective-permute-start.35 = (bf16[4,3,128,256]{3,2,1,0:T(8,128)(2,1)S(1)}, bf16[4,3,128,256]{3,2,1,0:T(8,128)(2,1)S(1)}, u32[]{:S(2)}, u32[]{:S(2)}) collective-permute-start(bf16[4,3,128,256]{3,2,1,0:T(8,128)(2,1)S(1)} %collective-permute-done.31.refs_1_), channel_id=1, source_target_pairs={{0,8},{4,20},{8,0},{12,28},{16,24},{20,4},{24,16},{28,12},{1,9},{5... | collective-permute-start | bytes 2359304 | tf_op jit(solution)/shard_map/ppermute | solution.py:374
  293.1 18.7 %collective-permute-start.32 = (bf16[4,3,128,256]{3,2,1,0:T(8,128)(2,1)S(1)}, bf16[4,3,128,256]{3,2,1,0:T(8,128)(2,1)S(1)}, u32[]{:S(2)}, u32[]{:S(2)}) collective-permute-start(bf16[4,3,128,256]{3,2,1,0:T(8,128)(2,1)S(1)} %collective-permute-done.31.refs_1_), channel_id=1, source_target_pairs={{0,4},{4,0},{8,12},{12,8},{16,20},{20,16},{24,28},{28,24},{1,5},{5... | collective-permute-start | bytes 2359304 | tf_op jit(solution)/shard_map/ppermute | solution.py:367
  301.3 10.5 %collective-permute-start.34 = (bf16[4,3,128,256]{3,2,1,0:T(8,128)(2,1)S(1)}, bf16[4,3,128,256]{3,2,1,0:T(8,128)(2,1)S(1)}, u32[]{:S(2)}, u32[]{:S(2)}) collective-permute-start(bf16[4,3,128,256]{3,2,1,0:T(8,128)(2,1)S(1)} %collective-permute-done.33.refs_2_), channel_id=1, source_target_pairs={{0,4},{4,0},{8,12},{12,8},{16,20},{20,16},{24,28},{28,24},{1,5},{5... | collective-permute-start | bytes 2359304 | tf_op jit(solution)/shard_map/ppermute | solution.py:367
  303.2 12.4 %collective-permute-start.59 = (bf16[3,704,128]{2,1,0:T(8,128)(2,1)S(1)}, bf16[3,704,128]{2,1,0:T(8,128)(2,1)}, u32[]{:S(2)}, u32[]{:S(2)}) collective-permute-start(bf16[3,704,128]{2,1,0:T(8,128)(2,1)S(1)} %fusion.3.refs_0_), channel_id=1, source_target_pairs={{0,8},{4,20},{8,0},{12,28},{16,24},{20,4},{24,16},{28,12},{1,9},{5... | collective-permute-start | bytes 1622024 | tf_op jit(solution)/shard_map/ppermute | solution.py:374
  304.6 16.8 %collective-permute-start.61 = (bf16[3,704,128]{2,1,0:T(8,128)(2,1)S(1)}, bf16[3,704,128]{2,1,0:T(8,128)(2,1)}, u32[]{:S(2)}, u32[]{:S(2)}) collective-permute-start(bf16[3,704,128]{2,1,0:T(8,128)(2,1)S(1)} %collective-permute-done.57.refs_1_), channel_id=1, source_target_pairs={{0,8},{4,20},{8,0},{12,28},{16,24},{20,4},{24,16},{28,12},{1,9},{5... | collective-permute-start | bytes 1622024 | tf_op jit(solution)/shard_map/ppermute | solution.py:374
  309.7 34.5 %collective-permute-start.36 = (bf16[4,3,128,256]{3,2,1,0:T(8,128)(2,1)S(1)}, bf16[4,3,128,256]{3,2,1,0:T(8,128)(2,1)S(1)}, u32[]{:S(2)}, u32[]{:S(2)}) collective-permute-start(bf16[4,3,128,256]{3,2,1,0:T(8,128)(2,1)S(1)} %collective-permute-done.35.refs_3_), channel_id=1, source_target_pairs={{0,4},{4,0},{8,12},{12,8},{16,20},{20,16},{24,28},{28,24},{1,5},{5... | collective-permute-start | bytes 2359304 | tf_op jit(solution)/shard_map/ppermute | solution.py:367
  311.7 43.7 %collective-permute-start.56 = (bf16[3,704,128]{2,1,0:T(8,128)(2,1)S(1)}, bf16[3,704,128]{2,1,0:T(8,128)(2,1)}, u32[]{:S(2)}, u32[]{:S(2)}) collective-permute-start(bf16[3,704,128]{2,1,0:T(8,128)(2,1)S(1)} %fusion.3.refs_0_), channel_id=1, source_target_pairs={{0,4},{4,0},{8,12},{12,8},{16,20},{20,16},{24,28},{28,24},{1,5},{5... | collective-permute-start | bytes 1622024 | tf_op jit(solution)/shard_map/ppermute | solution.py:367
  311.8 43.6 %collective-permute-start.58 = (bf16[3,704,128]{2,1,0:T(8,128)(2,1)S(1)}, bf16[3,704,128]{2,1,0:T(8,128)(2,1)}, u32[]{:S(2)}, u32[]{:S(2)}) collective-permute-start(bf16[3,704,128]{2,1,0:T(8,128)(2,1)S(1)} %collective-permute-done.57.refs_1_), channel_id=1, source_target_pairs={{0,4},{4,0},{8,12},{12,8},{16,20},{20,16},{24,28},{28,24},{1,5},{5... | collective-permute-start | bytes 1622024 | tf_op jit(solution)/shard_map/ppermute | solution.py:367
  315.6 39.8 %collective-permute-start.60 = (bf16[3,704,128]{2,1,0:T(8,128)(2,1)}, bf16[3,704,128]{2,1,0:T(8,128)(2,1)}, u32[]{:S(2)}, u32[]{:S(2)}) collective-permute-start(bf16[3,704,128]{2,1,0:T(8,128)(2,1)} %collective-permute-done.59.refs_2_), channel_id=1, source_target_pairs={{0,4},{4,0},{8,12},{12,8},{16,20},{20,16},{24,28},{28,24},{1,5},{5... | collective-permute-start | bytes 1622024 | tf_op jit(solution)/shard_map/ppermute | solution.py:367
  321.4 34.0 %collective-permute-start.62 = (bf16[3,704,128]{2,1,0:T(8,128)(2,1)}, bf16[3,704,128]{2,1,0:T(8,128)(2,1)}, u32[]{:S(2)}, u32[]{:S(2)}) collective-permute-start(bf16[3,704,128]{2,1,0:T(8,128)(2,1)} %collective-permute-done.61.refs_3_), channel_id=1, source_target_pairs={{0,4},{4,0},{8,12},{12,8},{16,20},{20,16},{24,28},{28,24},{1,5},{5... | collective-permute-start | bytes 1622024 | tf_op jit(solution)/shard_map/ppermute | solution.py:367
  (72 other events, 1146.1 us)

commit v3 on v2

--- a/solution.py
+++ b/solution.py
@@ -15,6 +15,10 @@
 ANY = pl.BlockSpec(memory_space=pl.ANY)
 PARAMS = pltpu.CompilerParams(dimension_semantics=("arbitrary",), vmem_limit_bytes=56 << 20)
 sds = jax.ShapeDtypeStruct
+
+
+def cost(micros):
+    return pl.CostEstimate(flops=0, transcendentals=0, bytes_accessed=int(micros * 3.2e6))
 
 
 def mm(a, b):
@@ -110,7 +114,7 @@
 def out_kernel(heads, hn, hd, share, own, keep, enter, other, *refs):
     narrow = heads // hn
     states = refs[:narrow]
-    contrib, q, intra, act, tok, rise, wo, att, inverse, hidden, n2, kent = refs[narrow:]
+    contrib, q, intra, act, tok, rise, wo, att, inverse, gated, hidden, n2, kent = refs[narrow:]
     b = pl.program_id(0)
     for h in range(heads):
         at = slice(h * hd, (h + 1) * hd)
@@ -129,8 +133,8 @@
     values = att[...].astype(f32)
     scale = inv_rms(values)
     inverse[...] = scale
-    gated = (values * scale * act[...]).astype(bf16)
-    hid = tok[...].astype(f32) + mm(gated, wo[...])
+    gated[...] = (values * scale * act[...]).astype(bf16)
+    hid = tok[...].astype(f32) + mm(gated[...], wo[...])
 
     @pl.when(b == 0)
     def _():
@@ -212,8 +216,8 @@
 
 def residual_kernel(narrow, own, *refs):
     parts = refs[:narrow]
-    hidden, cot, wo, att, inverse, act, grad_hidden, low_out, ggl = refs[narrow : narrow + 9]
-    ga = refs[narrow + 9 :]
+    hidden, cot, wo, att, inverse, act, grad_hidden, ggl = refs[narrow : narrow + 8]
+    trios = refs[narrow + 8 :]
     gn2 = parts[0][...].astype(f32)
     for part in parts[1:]:
         gn2 = gn2 + part[...].astype(f32)
@@ -221,7 +225,6 @@
     gh = cot[...].astype(f32) + rms_back(hid, inv_rms(hid), gn2)
     grad_hidden[...] = gh
     low = gh.astype(bf16)
-    low_out[...] = low
     gg = mt(low, wo[...])
     values = att[...].astype(f32)
     gate = act[...]
@@ -232,7 +235,10 @@
         for k in range(narrow):
             @pl.when(own[1] ^ i == k)
             def _():
-                ga[k][...] = back[:, i * size : (i + 1) * size]
+                at = slice(i * size, (i + 1) * size)
+                trios[k][:, :size] = back[:, at]
+                trios[k][:, size : 2 * size] = ggl[:, at]
+                trios[k][:, 2 * size :] = low[:, at]
 
 
 def query_kernel(hn, hd, share, own, keep, ahead, *refs):
@@ -243,7 +249,7 @@
     for i, piece in enumerate(ga):
         @pl.when(b == i // per)
         def _():
-            grad[(i % per) * share : (i % per + 1) * share, :] = piece[...]
+            grad[(i % per) * share : (i % per + 1) * share, :] = piece[:, : grad.shape[1]]
 
     causal = causal_of(BLOCK, flip_of(own, share))
     for h in range(hn):
@@ -270,7 +276,7 @@
 
 
 def key_kernel(hn, hd, wide, share, own, leave, other, arrived, direct, n1, dq, k, v, kl, gk, gv,
-               tail, live, wq, wk, wv, kept, sent, *refs):
+               tail, live, _kept, _sent, kept, sent, *refs):
     pieces = refs[:-5]
     dk, dv, aq, ak, av = refs[-5:]
     per = BLOCK // share
@@ -300,43 +306,45 @@
         def _():
             scatter(wide, own, kept, sent, item, lambda t: acc[t * tall : (t + 1) * tall, :])
 
-    back = (mt(dq[...], wq[...]) + mt(dk[...], wk[...]) + mt(dv[...], wv[...])).astype(bf16)
+    cols = dq.shape[1]
     for i, piece in enumerate(pieces):
         @pl.when(b == i // per)
         def _():
-            piece[...] = back[(i % per) * share : (i % per + 1) * share]
-
-
-def gate_kernel(wide, narrow, share, own, *refs):
-    lows = refs[:narrow]
-    att, inverse, act, n1, wo, kept, sent, grads, acc, acc_out = refs[narrow:]
-    for i, piece in enumerate(lows):
-        grads[i * share : (i + 1) * share, :] = piece[...]
-    gate = act[...]
-    scaled = att[...].astype(f32) * inverse[...]
-    gated = (scaled * gate).astype(bf16)
-    gg = mt(grads[...], wo[...])
-    ggl = (gg * scaled * gate * (1.0 - gate)).astype(bf16)
-    acc[...] = tm(n1[...], ggl)
+            for item, part in enumerate((dq, dk, dv)):
+                piece[:, item * cols : (item + 1) * cols] = part[(i % per) * share : (i % per + 1) * share, :]
+
+
+def gate_kernel(wide, share, own, *refs):
+    trios = refs[:-6]
+    n1, gated, kept, sent, grads, acc = refs[-6:]
+    item = pl.program_id(0)
+    cols = acc.shape[1]
     tall = acc.shape[0] // wide
+    for step, left in enumerate((n1, gated)):
+        @pl.when(item == step)
+        def _():
+            at = slice((step + 1) * cols, (step + 2) * cols)
+            for i, piece in enumerate(trios):
+                grads[i * share : (i + 1) * share, :] = piece[:, at]
+            acc[...] = tm(left[...], grads[...])
+
     scatter(wide, own, kept, sent, 0, lambda t: acc[t * tall : (t + 1) * tall, :])
-    acc_out[...] = tm(gated, grads[...])
-    cols = gated.shape[1]
-    short = cols // wide
-
-    def piece_of(t):
-        mine = acc_out[t * short : (t + 1) * short, :]
-        return jnp.concatenate([mine[:, i * cols : (i + 1) * cols] for i in range(narrow)], axis=0)
-
-    scatter(wide, own, kept, sent, 1, piece_of)
-
-
-def tokens_kernel(narrow, *refs):
+
+
+def tokens_kernel(narrow, own, *refs):
     parts = refs[:narrow]
-    ggl, wg, tok, gh, out = refs[narrow:]
+    ggl, wq, wk, wv, wg, tok, gh, out, *grads = refs[narrow:]
+    cols = parts[0].shape[1] // 3
+    for i in range(narrow):
+        for k in range(narrow):
+            @pl.when(own[1] ^ i == k)
+            def _():
+                for item, full in enumerate(grads):
+                    full[:, i * cols : (i + 1) * cols] = parts[k][:, item * cols : (item + 1) * cols]
+
     grad = mt(ggl[...], wg[...])
-    for part in parts:
-        grad = grad + part[...].astype(f32)
+    for full, weight in zip(grads, (wq, wk, wv)):
+        grad = grad + mt(full[...], weight[...])
     values = tok[...].astype(f32)
     out[...] = gh[...] + rms_back(values, inv_rms(values), grad)
 
@@ -374,23 +382,21 @@
     return lax.ppermute(values, "wide", [(i, flip(i)) for i in range(size)])
 
 
-def reduce_wide(kept, sent):
-    got = swap_core(sent)
-    steps = (lax.axis_size("wide") - 1).bit_length() - 1
-    low, high = kept, got
-    for step in range(steps):
-        half = low.shape[0] // 2
-        away = low[half:] + high[half:]
-        low, high = low[:half] + high[:half], swap_step(away, step)
-    return (low + high)[0]
-
-
-def gather_wide(piece):
-    steps = (lax.axis_size("wide") - 1).bit_length() - 1
-    full = [piece]
-    for step in reversed(range(steps)):
-        full = full + [swap_step(part, step) for part in full]
-    return full, [swap_core(part) for part in full]
+def fence(*values):
+    return lax.optimization_barrier(values)
+
+
+def halved(low, high):
+    half = low.shape[0] // 2
+    return low[:half] + high[:half], low[half:] + high[half:]
+
+
+def swap_all(parts, step):
+    return [swap_step(part, step) for part in parts]
+
+
+def swap_cores(parts):
+    return [swap_core(part) for part in parts]
 
 
 def target(own, place, other, wide):
@@ -411,21 +417,6 @@
                     outs[item][:, n * cols : (n + 1) * cols] = piece[own[1] ^ n, item].astype(f32)
 
 
-def widen_gate_kernel(narrow, places, own, *refs):
-    pieces, (gate, out) = refs[:places], refs[-2:]
-    for j, piece in enumerate(pieces):
-        @pl.when(pl.program_id(0) == j)
-        def _():
-            cols = piece.shape[-1]
-            short = piece.shape[-2] // narrow
-            for n in range(narrow):
-                gate[:, n * cols : (n + 1) * cols] = piece[own[1] ^ n, 0].astype(f32)
-                for i in range(narrow):
-                    out[n, :, i * cols : (i + 1) * cols] = piece[
-                        own[1] ^ n, 1, i * short : (i + 1) * short, :
-                    ].astype(f32)
-
-
 def widen_ffn_kernel(places, own, *refs):
     pieces, outs = refs[:places], refs[-3:]
     for j, piece in enumerate(pieces):
@@ -435,28 +426,23 @@
                 outs[item][...] = piece[item].astype(f32)
 
 
-def widen(kernel, own, halves, blocks, shapes, name):
-    outs = []
-    for other, pieces in enumerate(halves):
-        places = len(pieces)
-
-        def spec(shape, index):
-            return pl.BlockSpec(shape, lambda i, own: index(target(own, i, other, 2 * places)))
-
-        outs = pl.pallas_call(
-            functools.partial(kernel, places),
-            grid_spec=pltpu.PrefetchScalarGridSpec(
-                num_scalar_prefetch=1,
-                grid=(places,),
-                in_specs=[whole(p.shape) for p in pieces] + [ANY] * len(outs),
-                out_specs=[spec(*block) for block in blocks],
-            ),
-            out_shape=[sds(shape, f32) for shape in shapes],
-            input_output_aliases={1 + places + i: i for i in range(len(outs))},
-            compiler_params=PARAMS,
-            name=f"{name}_{other}",
-        )(own, *pieces, *outs)
-    return outs
+def widen(kernel, own, other, pieces, block, cut, shape, outs, count, name):
+    places = len(pieces)
+    spec = pl.BlockSpec(block, lambda i, own: cut(target(own, i, other, 2 * places)))
+    return pl.pallas_call(
+        functools.partial(kernel, places),
+        grid_spec=pltpu.PrefetchScalarGridSpec(
+            num_scalar_prefetch=1,
+            grid=(places,),
+            in_specs=[whole(p.shape) for p in pieces] + [ANY] * len(outs),
+            out_specs=[spec] * count,
+        ),
+        out_shape=[sds(shape, f32)] * count,
+        input_output_aliases={1 + places + i: i for i in range(len(outs))},
+        compiler_params=PARAMS,
+        cost_estimate=cost(4),
+        name=f"{name}_{other}",
+    )(own, *pieces, *outs)
 
 
 def xor_order(values, own, axis):
@@ -507,8 +493,6 @@
     own = jnp.stack([own_wide, own_narrow]).astype(jnp.int32)
 
     tok = gather_narrow(tokens)
-    cot = gather_narrow(cotangent)
-    cot_all = jnp.concatenate(cot, axis=0)
 
     ends = jnp.cumsum(lengths, dtype=jnp.int32)
     starts = ends - lengths
@@ -522,9 +506,6 @@
     summed = jnp.cumsum(log_decay.reshape(heads, blocks, BLOCK), axis=2)
     last = summed[:, :, -1]
     decay = (jnp.exp(last) * keep_seq[None]).T
-    factors = gather_factors(jnp.prod(decay, axis=0))
-    factors = lax.dynamic_slice_in_dim(factors, own_narrow * hn, hn, 1)
-    coef_in, coef_out = between(factors, own_wide, True), between(factors, own_wide, False)
 
     def slots(first, second):
         return jnp.where(own_narrow // per == 0, jnp.stack([first, second]), jnp.stack([second, first]))
@@ -553,6 +534,9 @@
               sds((blocks, heads, hd, hd), f32)]
     made = []
     for s in range(blocks):
+        if s == 1:
+            made, later, cotangent_now, product_now = fence(made, tok[per:], cotangent, jnp.prod(decay, axis=0))
+            tok = tok[:per] + list(later)
         weight = pl.BlockSpec((width, cols), lambda i, own: (0, i))
         column = pl.BlockSpec((1, BLOCK, hn), lambda i, own, s=s: (i, s, 0))
         full = pl.BlockSpec((BLOCK, width), lambda i, own, s=s: (s, 0))
@@ -573,19 +557,26 @@
             out_shape=shapes,
             input_output_aliases={11 + i: i for i in range(len(made))},
             compiler_params=PARAMS,
+            cost_estimate=cost(10),
             name=f"mixer_forward_{s}",
         )(own, tok[per * s], tok[per * s + 1], w_query, w_key, w_value, w_gate, live, gcol, grow, tail, *made)
     n1, tok_all, ql, kl, q, k, v, act, intra, contrib = made
 
+    cot = gather_narrow(cotangent_now)
+    factors = gather_factors(product_now)
+    factors = lax.dynamic_slice_in_dim(factors, own_narrow * hn, hn, 1)
+    coef_in, coef_out = between(factors, own_wide, True), between(factors, own_wide, False)
     message = own_heads(contrib)
     message = jnp.sum(own_heads(ends_in)[:, :, None, None] * message, axis=0).astype(bf16)
-    states = gather_narrow(pass_states(message, coef_in).astype(bf16))
+    entering, cot = fence(pass_states(message, coef_in).astype(bf16), cot)
+    cot_all = jnp.concatenate(cot, axis=0)
+    states = gather_narrow(entering)
 
     up = lambda b: b
     all_blk, part_blk = rows((BLOCK, width), up), rows((BLOCK, cols), up)
     own_blk = pl.BlockSpec((BLOCK, cols), lambda b, own: (b, own[1]))
     own_kent = rows((1, hn, hd, hd), up)
-    att, inverse, hidden, n2, kent = pl.pallas_call(
+    att, inverse, gated, hidden, n2, kent = pl.pallas_call(
         functools.partial(out_kernel, heads, hn, hd, share),
         grid_spec=pltpu.PrefetchScalarGridSpec(
             num_scalar_prefetch=1,
@@ -593,11 +584,12 @@
             in_specs=[SMEM, SMEM, SMEM, *[whole((hn, hd, hd))] * narrow, whole((blocks, heads, hd, hd)),
                       *[all_blk] * 4, pl.BlockSpec((narrow, BLOCK, hn), lambda b, own: (0, b, 0)),
                       whole((width, width))],
-            out_specs=[all_blk, rows((BLOCK, 1), up), whole((share, width)), all_blk, own_kent],
+            out_specs=[all_blk, rows((BLOCK, 1), up), all_blk, whole((share, width)), all_blk, own_kent],
         ),
-        out_shape=[sds((local, width), bf16), sds((local, 1), f32), sds((share, width), f32),
+        out_shape=[sds((local, width), bf16), sds((local, 1), f32), sds((local, width), bf16), sds((share, width), f32),
                    sds((local, width), bf16), sds((blocks, hn, hd, hd), bf16)],
         compiler_params=PARAMS,
+        cost_estimate=cost(9.5),
         name="mixer_out",
     )(own, keep, enter, enter_other, *states, contrib, q, intra, act, tok_all, rise, w_out)
 
@@ -612,10 +604,12 @@
         out_specs=[*[ff_blk] * 3, *[piece_spec] * narrow],
         out_shape=[*[sds((local, ff), bf16)] * 3, *[piece_shape] * narrow],
         compiler_params=PARAMS,
+        cost_estimate=cost(10),
         name="ffn",
     )(n2, cot_all, first_t, second_t, w_third)
+
     gn2 = trade_narrow(gn2)
-
+    product_now, _ = fence(product, gn2[1])
     tall, across = ffn_cut(wide, ff, width)[:2]
     slot = (wide // 2, 3, tall, across)
     slot_spec = pl.BlockSpec((wide // 2, 1, tall, across), lambda i, own: (0, i, 0, 0))
@@ -630,37 +624,35 @@
         ),
         out_shape=[sds(slot, bf16), sds(slot, bf16), *[piece_shape] * narrow],
         compiler_params=PARAMS,
+        cost_estimate=cost(10),
         name="ffn_grads",
-    )(own, n2, cot_all, product, gf, gs, w_third)
-    ff_halves = gather_wide(reduce_wide(kept, sent))
-    ffn_part = trade_narrow(ffn_part)
-    output = pl.pallas_call(
-        functools.partial(output_kernel, narrow),
-        out_shape=sds((share, width), bf16),
-        compiler_params=pltpu.CompilerParams(vmem_limit_bytes=56 << 20),
-        name="output",
-    )(*ffn_part, hidden)
+    )(own, n2, cot_all, product_now, gf, gs, w_third)
+    gn2, kept, sent = fence(gn2, kept, sent)
+    steps = (wide - 1).bit_length() - 1
 
     def single(shape, index=None):
         where = index or (lambda own: (0,) * len(shape))
         return pl.BlockSpec(shape, lambda b, own: where(own))
 
     row_spec = single((share, width))
-    grad_hidden, low, ggl, *ga = pl.pallas_call(
+    grad_hidden, ggl, *trios = pl.pallas_call(
         functools.partial(residual_kernel, narrow),
         grid_spec=pltpu.PrefetchScalarGridSpec(
             num_scalar_prefetch=1,
             grid=(1,),
             in_specs=[*[row_spec] * (narrow + 2), single((width, width)), row_spec, single((share, 1)), row_spec],
-            out_specs=[row_spec] * 3 + [single((share, cols))] * narrow,
+            out_specs=[row_spec] * 2 + [single((share, 3 * cols))] * narrow,
         ),
-        out_shape=[sds((share, width), f32), sds((share, width), bf16), sds((share, width), bf16),
-                   *[sds((share, cols), bf16)] * narrow],
+        out_shape=[sds((share, width), f32), sds((share, width), bf16),
+                   *[sds((share, 3 * cols), bf16)] * narrow],
         compiler_params=PARAMS,
+        cost_estimate=cost(5),
         name="residual_back",
     )(own, *gn2, hidden, cotangent, w_out, att, inverse, act)
-    ga = trade_narrow(ga)
-    lows = gather_narrow(low)
+    trios, kept, sent = fence(trios, kept, sent)
+    trios, kept, got = fence(trade_narrow(trios), kept, swap_core(sent))
+    low, away = halved(kept, got)
+    got = swap_step(away, 0)
 
     own_col = pl.BlockSpec((None, BLOCK, hn), lambda b, own: (own[1], b, 0))
     own_row = pl.BlockSpec((1, hn, BLOCK), lambda b, own: (b * narrow + own[1], 0, 0))
@@ -669,7 +661,7 @@
         grid_spec=pltpu.PrefetchScalarGridSpec(
             num_scalar_prefetch=1,
             grid=(blocks,),
-            in_specs=[SMEM, SMEM, *[whole((share, cols))] * narrow, *[own_blk] * 3, part_blk, own_kent,
+            in_specs=[SMEM, SMEM, *[whole((share, 3 * cols))] * narrow, *[own_blk] * 3, part_blk, own_kent,
                       own_col, own_row, own_col],
             out_specs=[*[part_blk] * 3, own_kent, whole((hn, hd, hd))],
             scratch_shapes=[pltpu.VMEM((BLOCK, cols), bf16)],
@@ -677,75 +669,127 @@
         out_shape=[sds((local, cols), bf16), *[sds((local, cols), f32)] * 2,
                    sds((blocks, hn, hd, hd), f32), sds((hn, hd, hd), f32)],
         compiler_params=PARAMS,
+        cost_estimate=cost(5.4),
         name="mixer_query_back",
-    )(own, keep, ahead, *ga, q, k, v, ql, kent, gcol, grow, rise)
-
-    arrived = pass_states(message.astype(bf16), coef_out)
-    pair = (wide // 2, 3, width // wide, cols)
-    own_weight = pl.BlockSpec((width, cols), lambda b, own: (0, own[1]))
-    kept, sent, *gn1 = pl.pallas_call(
+    )(own, keep, ahead, *trios, q, k, v, ql, kent, gcol, grow, rise)
+
+    arrived, low, got = fence(pass_states(message.astype(bf16), coef_out), low, got)
+    low_ff, away_ff = halved(low, got)
+
+    five = (wide // 2, 5, width // wide, cols)
+    one = pl.BlockSpec((wide // 2, 1, width // wide, cols), lambda i, own: (0, 3 + i, 0, 0))
+    kept, sent = pl.pallas_call(
+        functools.partial(gate_kernel, wide, share),
+        grid_spec=pltpu.PrefetchScalarGridSpec(
+            num_scalar_prefetch=1,
+            grid=(2,),
+            in_specs=[*[single((share, 3 * cols))] * narrow, *[single((local, width))] * 2],
+            out_specs=[one] * 2,
+            scratch_shapes=[pltpu.VMEM((local, cols), bf16), pltpu.VMEM((width, cols), f32)],
+        ),
+        out_shape=[sds(five, bf16)] * 2,
+        compiler_params=PARAMS,
+        cost_estimate=cost(5),
+        name="gate_back",
+    )(own, *trios, n1, gated)
+    three = whole((wide // 2, 3, width // wide, cols))
+    trio_spec, trio_shape = whole((share, 3 * cols)), sds((share, 3 * cols), bf16)
+    kept, sent, *dqkv = pl.pallas_call(
         functools.partial(key_kernel, hn, hd, wide, share),
         grid_spec=pltpu.PrefetchScalarGridSpec(
             num_scalar_prefetch=1,
             grid=(blocks,),
             in_specs=[SMEM, SMEM, whole((hn, hd, hd)), whole((blocks, hn, hd, hd)), all_blk, part_blk,
-                      own_blk, own_blk, *[part_blk] * 3, own_col, rows((BLOCK, 1), up), *[own_weight] * 3],
-            out_specs=[*[whole(pair)] * 2, *[piece_spec] * narrow],
+                      own_blk, own_blk, *[part_blk] * 3, own_col, rows((BLOCK, 1), up), ANY, ANY],
+            out_specs=[three, three, *[trio_spec] * narrow],
             scratch_shapes=[*[pltpu.VMEM((BLOCK, cols), bf16)] * 2, *[pltpu.VMEM((width, cols), f32)] * 3],
         ),
-        out_shape=[*[sds(pair, bf16)] * 2, *[piece_shape] * narrow],
+        out_shape=[*[sds(five, bf16)] * 2, *[trio_shape] * narrow],
+        input_output_aliases={14: 0, 15: 1},
         compiler_params=PARAMS,
+        cost_estimate=cost(9),
         name="mixer_key_back",
-    )(own, leave, leave_other, arrived, direct, n1, dq, k, v, kl, gk, gv, tail, live, w_query, w_key, w_value)
-
-    def collect(kept, sent):
-        return gather_wide(jnp.stack(gather_narrow(reduce_wide(kept, sent))))
-
-    pair = (wide // 2, 2, width // wide, cols)
-    own_cols = single((local, cols), lambda own: (0, own[1]))
-    gate_kept, gate_sent = pl.pallas_call(
-        functools.partial(gate_kernel, wide, narrow, share),
+    )(own, leave, leave_other, arrived, direct, n1, dq, k, v, kl, gk, gv, tail, live, kept, sent)
+
+    low, away = halved(kept, swap_core(sent))
+    low, away, dqkv, away_ff = fence(low, away, dqkv, away_ff)
+    low, high, dqkv, high_ff = fence(low, swap_step(away, 0), trade_narrow(dqkv), swap_step(away_ff, 1))
+    for step in range(1, steps):
+        low, away = halved(low, high)
+        high = swap_step(away, step)
+    for step in range(2, steps):
+        low_ff, away_ff = halved(low_ff, high_ff)
+        high_ff = swap_step(away_ff, step)
+    piece = (low + high)[0]
+    ff_piece = [(low_ff + high_ff)[0]]
+
+    for step in reversed(range(1, steps)):
+        ff_piece = ff_piece + swap_all(ff_piece, step)
+    gate_piece, piece, ff_piece = fence(jnp.stack(gather_narrow(piece[3:])), piece[:3], ff_piece)
+    chunks = width // across
+    ffn_form = (tall, across), lambda t: (t // chunks, t % chunks), (ff, width)
+    square_form = (width // wide, width), lambda t: (t, 0), (width, width)
+    gate_kernels = functools.partial(widen_square_kernel, 2, narrow)
+    square_kernels = functools.partial(widen_square_kernel, 3, narrow)
+
+    zs = gather_narrow(piece)
+    ff_piece = ff_piece + swap_all(ff_piece, 0)
+    gate_piece = [gate_piece]
+    for step in reversed(range(1, steps)):
+        gate_piece = gate_piece + swap_all(gate_piece, step)
+    half = len(gate_piece) // 2
+    gate_more = swap_all(gate_piece, 0)
+    dqkv, _ = fence(dqkv, zs[1])
+    grad_tokens = pl.pallas_call(
+        functools.partial(tokens_kernel, narrow),
         grid_spec=pltpu.PrefetchScalarGridSpec(
             num_scalar_prefetch=1,
             grid=(1,),
-            in_specs=[*[row_spec] * narrow, own_cols, single((local, 1)), own_cols, single((local, width)),
-                      single((cols, width), lambda own: (own[1], 0))],
-            out_specs=[single(pair)] * 2,
-            scratch_shapes=[pltpu.VMEM((local, width), bf16), pltpu.VMEM((width, cols), f32),
-                            pltpu.VMEM((cols, width), f32)],
+            in_specs=[*[single((share, 3 * cols))] * narrow, row_spec, *[single((width, width))] * 4,
+                      row_spec, row_spec],
+            out_specs=row_spec,
+            scratch_shapes=[pltpu.VMEM((share, width), bf16)] * 3,
         ),
-        out_shape=[sds(pair, bf16)] * 2,
+        out_shape=sds((share, width), f32),
         compiler_params=PARAMS,
-        name="gate_back",
-    )(own, *lows, att, inverse, act, n1, w_out)
-    gate_halves = collect(gate_kept, gate_sent)
-    square_halves = collect(kept, sent)
-
-    gn1 = trade_narrow(gn1)
-    grad_tokens = pl.pallas_call(
-        functools.partial(tokens_kernel, narrow),
-        out_shape=sds((share, width), f32),
+        cost_estimate=cost(8),
+        name="tokens_back",
+    )(own, *dqkv, ggl, w_query, w_key, w_value, w_gate, tokens, grad_hidden)
+    square_piece, gate_piece, ff_piece, ffn_part, grad_tokens = fence(
+        jnp.stack(zs), gate_piece + gate_more, ff_piece, ffn_part, grad_tokens
+    )
+
+    square_piece = [square_piece]
+    for step in reversed(range(1, steps)):
+        square_piece = square_piece + swap_all(square_piece, step)
+    square_more = swap_all(square_piece[:half], 0)
+    ffn_out = widen(widen_ffn_kernel, own, 0, ff_piece, *ffn_form, [], 3, "widen_ffn")
+    gate_out = widen(gate_kernels, own, 0, gate_piece, *square_form, [], 2, "widen_gate")
+    square_piece, square_more, ffn_out, gate_out, gate_other, ff_other, ffn_part = fence(
+        square_piece, square_more, ffn_out, gate_out, swap_cores(gate_piece), swap_cores(ff_piece), ffn_part
+    )
+
+    ffn_part = trade_narrow(ffn_part)
+    square_last = swap_all(square_piece[half:], 0)
+    ffn_out = widen(widen_ffn_kernel, own, 1, ff_other, *ffn_form, ffn_out, 3, "widen_ffn")
+    gate_out = widen(gate_kernels, own, 1, gate_other, *square_form, gate_out, 2, "widen_gate")
+    square_piece, ffn_out, gate_out, ffn_part = fence(
+        square_piece + square_more + square_last, ffn_out, gate_out, ffn_part
+    )
+
+    output = pl.pallas_call(
+        functools.partial(output_kernel, narrow),
+        out_shape=sds((share, width), bf16),
         compiler_params=pltpu.CompilerParams(vmem_limit_bytes=56 << 20),
-        name="tokens_back",
-    )(*gn1, ggl, w_gate, tokens, grad_hidden)
-
-    chunks = width // across
-    grad_first, grad_second, grad_third = widen(
-        widen_ffn_kernel, own, ff_halves, [((tall, across), lambda t: (t // chunks, t % chunks))] * 3,
-        [(ff, width)] * 3, "widen_ffn",
-    )
-    square = ((width // wide, width), lambda t: (t, 0))
-    grad_gate, grad_out = widen(
-        functools.partial(widen_gate_kernel, narrow), own, gate_halves,
-        [square, ((narrow, cols // wide, width), lambda t: (0, t, 0))],
-        [(width, width), (narrow, cols, width)], "widen_gate",
-    )
-    mixer = widen(
-        functools.partial(widen_square_kernel, 3, narrow), own, square_halves, [square] * 3,
-        [(width, width)] * 3, "widen_square",
-    )
-    return (output, grad_tokens, *mixer, grad_gate, grad_out.reshape(width, width),
-            grad_first.T, grad_second.T, grad_third)
+        cost_estimate=cost(2),
+        name="output",
+    )(*ffn_part, hidden)
+    mixer = widen(square_kernels, own, 0, square_piece, *square_form, [], 3, "widen_square")
+    square_other = swap_cores(square_piece)
+    mixer = widen(square_kernels, own, 1, square_other, *square_form, mixer, 3, "widen_square")
+    grad_first, grad_second, grad_third = ffn_out
+    grad_gate, grad_out = gate_out
+    return (output, grad_tokens, *mixer, grad_gate, grad_out, grad_first.T, grad_second.T, grad_third)
 
 
 def solution(mesh):

time: 362 us -> 319 us (0.88)
  waiting for transfers between devices: 117 us -> 89.2 us
  starting transfers between devices: 80.2 us -> 64.4 us
    ppermute x15 -> x13, waiting for transfers between devices: 40.4 us -> 20.4 us  [swap_step(): return lax.ppermute(values, 'wide', [(i, flip(i)) for i in range(size)])]
    ppermute x30 -> x27, waiting for transfers between devices: 71.9 us -> 64 us  [swap_narrow(): return lax.ppermute(values, 'narrow', [(i, i ^ k) for i in range(size)])]
    ppermute x30 -> x27, starting transfers between devices: 49.9 us -> 43.3 us  [swap_narrow(): return lax.ppermute(values, 'narrow', [(i, i ^ k) for i in range(size)])]
    ppermute x15 -> x14, starting transfers between devices: 9.68 us -> 4.78 us  [swap_core(): return lax.ppermute(values, 'wide', [(i, i ^ 1) for i in range(size)])]
    ppermute x15 -> x13, starting transfers between devices: 17.4 us -> 12.8 us  [swap_step(): return lax.ppermute(values, 'wide', [(i, flip(i)) for i in range(size)])]
    pallas_call x2, Pallas kernels: 9.83 us -> 13.6 us  [the longest x1 8.86 us: body(): pl.pallas_call(functools.partial(tokens_kernel, narrow), grid_spec=pltpu....]
  transfers between devices with their start and end apart: 63 -> 57, of which waited for: 24 -> 20; matrix products, arithmetic and copies ran while one was open for 6% -> 6% of each run, Pallas kernels for 22% -> 24%
where the time goes in v3:
time: 319 us; the launch traced here: 316 us
  Pallas kernels  116 us (36%)
  waiting for transfers between devices  89.2 us (28%)
  starting transfers between devices  64.4 us (20%)
  blocking collectives  19.8 us (6%)
  local copies, waits for them, and re-layouts  13.2 us (4%)
  other arithmetic  10.6 us (3%)
    ppermute x27, waiting for transfers between devices, swap_narrow(): return lax.ppermute(values, 'narrow', [(i, i ^ k) for i in range(size)])  64 us
    ppermute x27, starting transfers between devices, swap_narrow(): return lax.ppermute(values, 'narrow', [(i, i ^ k) for i in range(size)])  43.3 us
    pallas_call x6, Pallas kernels, widen(): pl.pallas_call(functools.partial(kernel, places), grid_spec=pltpu.Prefetc...  30 us
    pallas_call x2, Pallas kernels, body(): pl.pallas_call(functools.partial(forward_kernel, hn, hd, share), grid_spe...  20.7 us
    ppermute x13, waiting for transfers between devices, swap_step(): return lax.ppermute(values, 'wide', [(i, flip(i)) for i in range(size)])  20.4 us
    all_gather x2, blocking collectives, pass_states(): gathered = lax.all_gather(message, 'wide', axis=0)  19.8 us
    ppermute x13, starting transfers between devices, swap_step(): return lax.ppermute(values, 'wide', [(i, flip(i)) for i in range(size)])  12.8 us
    pallas_call x1, Pallas kernels, body(): pl.pallas_call(functools.partial(ffn_grad_kernel, wide, share), grid_spec...  10.2 us
  transfers between devices with their start and end apart: 57, of which 20 were waited for; matrix products, arithmetic and copies ran while one was open for 6% of the time, Pallas kernels for 24%

profile of v3, /device:TPU:0, one launch (start us, length us, event | category | flops | bytes accessed | tf_op | source)
XLA Modules:
  0.0 315.9 jit_solution(11241783878727588698)
XLA Ops:
  0.7 4.1 %collective-permute-start.1 = (bf16[128,1024]{1,0:T(8,128)(2,1)}, bf16[128,1024]{1,0:T(8,128)(2,1)S(1)}, u32[]{:S(2)}, u32[]{:S(2)}) collective-permute-start(bf16[128,1024]{1,0:T(8,128)(2,1)} %refs_9_.1), channel_id=1, source_target_pairs={{0,2},{1,3},{2,0},{3,1},{4,6},{5,7},{6,4},{7,5},{8,10},{9,11},{10,... | collective-permute-start | bytes 786440 | tf_op jit(solution)/shard_map/ppermute | solution.py:362
  13.9 1.9 broadcast_select_fusion.2.keep
  21.8 10.4 %mixer_forward_0.1 = (bf16[512,1024]{1,0:T(8,128)(2,1)}, bf16[512,1024]{1,0:T(8,128)(2,1)}, f32[512,256]{1,0:T(8,128)}, f32[512,256]{1,0:T(8,128)}, bf16[512,102...) custom-call(s32[2]{0:T(128)} %pad_add_fusion.own, ...), custom_call_target="tpu_custom_call" | custom-call | bytes 32000000 | tf_op jit(solution)/shard_map/mixer_forward_0/pallas_call | solution.py:545
  32.2 3.9 %collective-permute-start.8 = (bf16[128,1024]{1,0:T(8,128)(2,1)S(1)}, bf16[128,1024]{1,0:T(8,128)(2,1)S(1)}, u32[]{:S(2)}, u32[]{:S(2)}) collective-permute-start(bf16[128,1024]{1,0:T(8,128)(2,1)S(1)} %copy-done.6), channel_id=1, source_target_pairs={{0,3},{1,2},{2,1},{3,0},{4,7},{5,6},{6,5},{7,4},{8,11},{9,10},{10,... | collective-permute-start | bytes 786440 | tf_op jit(solution)/shard_map/ppermute | solution.py:362
  36.7 10.4 %mixer_forward_1.1 = (bf16[512,1024]{1,0:T(8,128)(2,1)}, bf16[512,1024]{1,0:T(8,128)(2,1)}, f32[512,256]{1,0:T(8,128)}, f32[512,256]{1,0:T(8,128)}, bf16[512,102...) custom-call(s32[2]{0:T(128)} %pad_add_fusion.own, ...), custom_call_target="tpu_custom_call", output_to_operand_aliasing={{0}: (11, {}), {1}: (12, {}), {2}: (13, {}), {3}: (14, {}),... | custom-call | bytes 32000000 | tf_op jit(solution)/shard_map/mixer_forward_1/pallas_call | solution.py:545
  50.8 1.7 collective-permute-start.5
  52.5 10.0 %all-gather = bf16[16,128,128]{2,1,0:T(8,128)(2,1)S(1)} all-gather(bf16[2,128,128]{2,1,0:T(8,128)(2,1)S(1)} %multiply_reduce_fusion), channel_id=2, replica_groups=mesh['wide'=8,'narrow'=4] {'wide'}, dimensions={0}, use_global_device_ids=true | all-gather | bytes 589824 | tf_op jit(solution)/shard_map/all_gather | solution.py:481
  63.2 3.7 %collective-permute-start.11 = (bf16[2,128,128]{2,1,0:T(8,128)(2,1)S(1)}, bf16[2,128,128]{2,1,0:T(8,128)(2,1)S(1)}, u32[]{:S(2)}, u32[]{:S(2)}) collective-permute-start(bf16[2,128,128]{2,1,0:T(8,128)(2,1)S(1)} %fusion.1.refs_0_), channel_id=1, source_target_pairs={{0,3},{1,2},{2,1},{3,0},{4,7},{5,6},{6,5},{7,4},{8,11},{9,10},{10,... | collective-permute-start | bytes 196616 | tf_op jit(solution)/shard_map/ppermute | solution.py:362
  67.7 2.3 collective-permute-done.11.refs_3_
  70.1 2.5 collective-permute-done.10.refs_2_
  73.2 9.8 %mixer_out.1 = (bf16[512,1024]{1,0:T(8,128)(2,1)}, f32[512,1]{1,0:T(8,128)}, bf16[512,1024]{1,0:T(8,128)(2,1)}, f32[128,1024]{1,0:T(8,128)}, bf16[512,1024]{1,0:...) custom-call(s32[2]{0:T(128)} %pad_add_fusion.own, f32[2]{0:T(128)} %broadcast_select_fusion.2.keep, ...), custom_call_target="tpu_custom_call" | custom-call | bytes 30400000 | tf_op jit(solution)/shard_map/mixer_out/pallas_call | solution.py:579
  83.0 10.1 %ffn.1 = (bf16[512,704]{1,0:T(8,128)(2,1)}, bf16[512,704]{1,0:T(8,128)(2,1)}, bf16[512,704]{1,0:T(8,128)(2,1)}, bf16[128,1024]{1,0:T(8,128)(2,1)}, bf16[128,1024...) custom-call(bf16[512,1024]{1,0:T(8,128)(2,1)} %get-tuple-element.224.n2, ...), custom_call_target="tpu_custom_call" | custom-call | bytes 32000000 | tf_op jit(solution)/shard_map/ffn/pallas_call | solution.py:600
  97.6 8.1 %collective-permute-done.12.refs_1_ = bf16[128,1024]{1,0:T(8,128)(2,1)S(1)} collective-permute-done((bf16[128,1024]{1,0:T(8,128)(2,1)}, bf16[128,1024]{1,0:T(8,128)(2,1)S(1)}, u32[]{:S(2)}, u32[]{:S(2)}) %collective-permute-start.12) | collective-permute-done | bytes 262176 | tf_op jit(solution)/shard_map/ppermute | solution.py:362
  105.7 10.2 %ffn_grads.1 = (bf16[4,3,704,128]{3,2,1,0:T(8,128)(2,1)}, bf16[4,3,704,128]{3,2,1,0:T(8,128)(2,1)}, bf16[128,1024]{1,0:T(8,128)(2,1)}, bf16[128,1024]{1,0:T(8,12...) custom-call(s32[2]{0:T(128)} %pad_add_fusion.own, bf16[512,1024]{1,0:T(8,128)(2,1)} %get-tuple-element.224.n2, ...), custom_call_target="tpu_custom_call" | custom-call | bytes 32000000 | tf_op jit(solution)/shard_map/ffn_grads/pallas_call | solution.py:616
  117.0 6.2 %residual_back.1 = (f32[128,1024]{1,0:T(8,128)}, bf16[128,1024]{1,0:T(8,128)(2,1)}, bf16[128,768]{1,0:T(8,128)(2,1)}, bf16[128,768]{1,0:T(8,128)(2,1)}, bf16[128...) custom-call(s32[2]{0:T(128)} %pad_add_fusion.own, bf16[128,1024]{1,0:T(8,128)(2,1)} %get-tuple-element.239.refs_0_, ...), custom_call_target="tpu_custom_call" | custom-call | bytes 16000000 | tf_op jit(solution)/shard_map/residual_back/pallas_call | solution.py:638
  123.3 4.5 %collective-permute-start.15 = (bf16[128,768]{1,0:T(8,128)(2,1)}, bf16[128,768]{1,0:T(8,128)(2,1)S(1)}, u32[]{:S(2)}, u32[]{:S(2)}) collective-permute-start(bf16[128,768]{1,0:T(8,128)(2,1)} %get-tuple-element.253), channel_id=1, source_target_pairs={{0,1},{1,0},{2,3},{3,2},{4,5},{5,4},{6,7},{7,6},{8,9},{9,8},{10,11... | collective-permute-start | bytes 589832 | tf_op jit(solution)/shard_map/ppermute | solution.py:362
  128.1 2.1 collective-permute-start.17
  130.2 6.6 %collective-permute-done.15.refs_1_ = bf16[128,768]{1,0:T(8,128)(2,1)S(1)} collective-permute-done((bf16[128,768]{1,0:T(8,128)(2,1)}, bf16[128,768]{1,0:T(8,128)(2,1)S(1)}, u32[]{:S(2)}, u32[]{:S(2)}) %collective-permute-start.15) | collective-permute-done | bytes 196640 | tf_op jit(solution)/shard_map/ppermute | solution.py:362
  136.8 8.3 %collective-permute-done.16.refs_2_ = bf16[128,768]{1,0:T(8,128)(2,1)S(1)} collective-permute-done((bf16[128,768]{1,0:T(8,128)(2,1)}, bf16[128,768]{1,0:T(8,128)(2,1)S(1)}, u32[]{:S(2)}, u32[]{:S(2)}) %collective-permute-start.16) | collective-permute-done | bytes 196640 | tf_op jit(solution)/shard_map/ppermute | solution.py:362
  147.8 5.6 %mixer_query_back.1 = (bf16[512,256]{1,0:T(8,128)(2,1)}, f32[512,256]{1,0:T(8,128)}, f32[512,256]{1,0:T(8,128)}, f32[2,2,128,128]{3,2,1,0:T(8,128)}, f32[2,128,128]{2,1,0:T(8,128)}) custom-call(s32[2]{0:T(128)} %pad_add_fusion.own, f32[2]{0:T(128)} %broadcast_select_fusion.2.keep, f32[2,2]{1,0:T(2,128)} %constant_dynamic-slice_fusion.ahead, ...), custom_call_target="tpu_custom_call" | custom-call | bytes 17280000 | tf_op jit(solution)/shard_map/mixer_query_back/pallas_call | solution.py:659
  154.3 4.8 %gate_back.1 = (bf16[4,5,128,256]{3,2,1,0:T(8,128)(2,1)}, bf16[4,5,128,256]{3,2,1,0:T(8,128)(2,1)}) custom-call(s32[2]{0:T(128)} %pad_add_fusion.own, bf16[128,768]{1,0:T(8,128)(2,1)} %get-tuple-element.258.refs_0_, bf16[128,768]{1,0:T(8,128)(2,1)} %copy-done.11, bf16[128,768]{1,0:T(8,128)(2,1)} %copy-done.12, bf16[128,768]{1,0:T(8,128)(2,1)} %copy-done.13, ...), custom_call_target="tpu_custom_call" | custom-call | bytes 16000000 | tf_op jit(solution)/shard_map/gate_back/pallas_call | solution.py:681
  159.1 9.8 %all-gather.1 = bf16[16,128,128]{2,1,0:T(8,128)(2,1)S(1)} all-gather(bf16[2,128,128]{2,1,0:T(8,128)(2,1)S(1)} %convert_element_type.48), channel_id=3, replica_groups=mesh['wide'=8,'narrow'=4] {'wide'}, dimensions={0}, use_global_device_ids=true | all-gather | bytes 589824 | tf_op jit(solution)/shard_map/all_gather | solution.py:481
  169.7 7.6 %mixer_key_back.1 = (bf16[4,5,128,256]{3,2,1,0:T(8,128)(2,1)}, bf16[4,5,128,256]{3,2,1,0:T(8,128)(2,1)}, bf16[128,768]{1,0:T(8,128)(2,1)}, bf16[128,768]{1,0:T(8...) custom-call(s32[2]{0:T(128)} %pad_add_fusion.own, ...), custom_call_target="tpu_custom_call", output_to_operand_aliasing={{0}: (14, {}), {1}: (15, {})} | custom-call | bytes 28800000 | tf_op jit(solution)/shard_map/mixer_key_back/pallas_call | solution.py:697
  177.8 2.8 collective-permute-done.20
  182.9 3.9 %collective-permute-start.22 = (bf16[128,768]{1,0:T(8,128)(2,1)S(1)}, bf16[128,768]{1,0:T(8,128)(2,1)S(1)}, u32[]{:S(2)}, u32[]{:S(2)}) collective-permute-start(bf16[128,768]{1,0:T(8,128)(2,1)S(1)} %copy-done.54), channel_id=1, source_target_pairs={{0,1},{1,0},{2,3},{3,2},{4,5},{5,4},{6,7},{7,6},{8,9},{9,8},{10,11... | collective-permute-start | bytes 589832 | tf_op jit(solution)/shard_map/ppermute | solution.py:362
  187.1 2.1 collective-permute-start.24
  189.2 5.5 %collective-permute-done.22.refs_1_ = bf16[128,768]{1,0:T(8,128)(2,1)S(1)} collective-permute-done((bf16[128,768]{1,0:T(8,128)(2,1)S(1)}, bf16[128,768]{1,0:T(8,128)(2,1)S(1)}, u32[]{:S(2)}, u32[]{:S(2)}) %collective-permute-start.22) | collective-permute-done | bytes 196640 | tf_op jit(solution)/shard_map/ppermute | solution.py:362
  194.7 9.2 %collective-permute-done.23.refs_2_ = bf16[128,768]{1,0:T(8,128)(2,1)S(1)} collective-permute-done((bf16[128,768]{1,0:T(8,128)(2,1)S(1)}, bf16[128,768]{1,0:T(8,128)(2,1)S(1)}, u32[]{:S(2)}, u32[]{:S(2)}) %collective-permute-start.23) | collective-permute-done | bytes 196640 | tf_op jit(solution)/shard_map/ppermute | solution.py:362
  206.2 4.9 %collective-permute-done.26 = bf16[1,5,128,256]{3,2,1,0:T(8,128)(2,1)S(1)} collective-permute-done((bf16[1,5,128,256]{3,2,1,0:T(8,128)(2,1)S(1)}, bf16[1,5,128,256]{3,2,1,0:T(8,128)(2,1)S(1)}, u32[]{:S(2)}, u32[]{:S(2)}) %collective-permute-start.26) | collective-permute-done | bytes 327712 | tf_op jit(solution)/shard_map/ppermute | solution.py:382
  211.2 1.8 collective-permute-start.29
  212.9 3.1 collective-permute-start.28
  216.1 3.4 %collective-permute-done.29 = bf16[2,128,256]{2,1,0:T(8,128)(2,1)S(1)} collective-permute-done((bf16[2,128,256]{2,1,0:T(8,128)(2,1)S(1)}, bf16[2,128,256]{2,1,0:T(8,128)(2,1)S(1)}, u32[]{:S(2)}, u32[]{:S(2)}) %collective-permute-start.29) | collective-permute-done | bytes 131104 | tf_op jit(solution)/shard_map/ppermute | solution.py:362
  219.5 5.3 %collective-permute-done.28 = bf16[2,128,256]{2,1,0:T(8,128)(2,1)S(1)} collective-permute-done((bf16[2,128,256]{2,1,0:T(8,128)(2,1)S(1)}, bf16[2,128,256]{2,1,0:T(8,128)(2,1)S(1)}, u32[]{:S(2)}, u32[]{:S(2)}) %collective-permute-start.28) | collective-permute-done | bytes 131104 | tf_op jit(solution)/shard_map/ppermute | solution.py:362
  228.8 5.1 %collective-permute-done.33 = bf16[3,128,256]{2,1,0:T(8,128)(2,1)S(1)} collective-permute-done((bf16[3,128,256]{2,1,0:T(8,128)(2,1)S(1)}, bf16[3,128,256]{2,1,0:T(8,128)(2,1)S(1)}, u32[]{:S(2)}, u32[]{:S(2)}) %collective-permute-start.33) | collective-permute-done | bytes 196640 | tf_op jit(solution)/shard_map/ppermute | solution.py:362
  235.4 4.3 %collective-permute-done.34.refs_1_ = bf16[4,2,128,256]{3,2,1,0:T(8,128)(2,1)S(1)} collective-permute-done((bf16[4,2,128,256]{3,2,1,0:T(8,128)(2,1)S(1)}, bf16[4,2,128,256]{3,2,1,0:T(8,128)(2,1)S(1)}, u32[]{:S(2)}, u32[]{:S(2)}) %collective-permute-start.34) | collective-permute-done | bytes 524320 | tf_op jit(solution)/shard_map/ppermute | solution.py:382
  239.8 8.9 %tokens_back.1 = f32[128,1024]{1,0:T(8,128)} custom-call(s32[2]{0:T(128)} %pad_add_fusion.own, bf16[128,768]{1,0:T(8,128)(2,1)} %get-tuple-element.309.refs_0_, bf16[128,768]{1,0:T(8,128)(2,1)} %copy-done.39, bf16[128,768]{1,0:T(8,128)(2,1)} %copy-done.40, bf16[128,768]{1,0:T(8,128)(2,1)} %copy-done.41, bf16[128,1024]{1,0:T(8,128)(2,1)} %get-tuple-element.313.refs_4_, ...), custom_call_target="tpu_custom_call" | custom-call | bytes 25600000 | tf_op jit(solution)/shard_map/tokens_back/pallas_call | solution.py:743
  248.9 5.0 %collective-permute-done.36.refs_3_ = bf16[4,2,128,256]{3,2,1,0:T(8,128)(2,1)S(1)} collective-permute-done((bf16[4,2,128,256]{3,2,1,0:T(8,128)(2,1)S(1)}, bf16[4,2,128,256]{3,2,1,0:T(8,128)(2,1)S(1)}, u32[]{:S(2)}, u32[]{:S(2)}) %collective-permute-start.36) | collective-permute-done | bytes 524320 | tf_op jit(solution)/shard_map/ppermute | solution.py:382
  260.8 4.7 %widen_gate_0.1 = (f32[1024,1024]{1,0:T(8,128)}, f32[1024,1024]{1,0:T(8,128)}) custom-call(s32[2]{0:T(128)} %pad_add_fusion.own, bf16[4,2,128,256]{3,2,1,0:T(8,128)(2,1)} %copy-done.5, bf16[4,2,128,256]{3,2,1,0:T(8,128)(2,1)} %copy-done.24, bf16[4,2,128,256]{3,2,1,0:T(8,128)(2,1)} %copy-done.25, bf16[4,2,128,256]{3,2,1,0:T(8,128)(2,1)} %copy-done.26), custom_call_target="tpu_custom_call" | custom-call | bytes 12800000 | tf_op jit(solution)/shard_map/widen_gate_0/pallas_call | solution.py:432
  265.4 4.8 %widen_ffn_0.1 = (f32[704,1024]{1,0:T(8,128)}, f32[704,1024]{1,0:T(8,128)}, f32[704,1024]{1,0:T(8,128)}) custom-call(s32[2]{0:T(128)} %pad_add_fusion.own, bf16[3,704,128]{2,1,0:T(8,128)(2,1)} %copy-done.4, bf16[3,704,128]{2,1,0:T(8,128)(2,1)} %copy-done.17, bf16[3,704,128]{2,1,0:T(8,128)(2,1)} %copy-done.18, bf16[3,704,128]{2,1,0:T(8,128)(2,1)} %copy-done.19), custom_call_target="tpu_custom_call" | custom-call | bytes 12800000 | tf_op jit(solution)/shard_map/widen_ffn_0/pallas_call | solution.py:432
  270.3 6.2 %collective-permute-done.40.refs_2_ = bf16[4,3,128,256]{3,2,1,0:T(8,128)(2,1)S(1)} collective-permute-done((bf16[4,3,128,256]{3,2,1,0:T(8,128)(2,1)S(1)}, bf16[4,3,128,256]{3,2,1,0:T(8,128)(2,1)S(1)}, u32[]{:S(2)}, u32[]{:S(2)}) %collective-permute-start.40) | collective-permute-done | bytes 786464 | tf_op jit(solution)/shard_map/ppermute | solution.py:382
  276.5 2.0 collective-permute-start.49
  278.5 2.7 collective-permute-start.51
  282.9 4.7 %widen_gate_1.1 = (f32[1024,1024]{1,0:T(8,128)}, f32[1024,1024]{1,0:T(8,128)}) custom-call(s32[2]{0:T(128)} %pad_add_fusion.own, bf16[4,2,128,256]{3,2,1,0:T(8,128)(2,1)} %collective-permute-done.41.refs_0_, bf16[4,2,128,256]{3,2,1,0:T(8,128)(2,1)} %collective-permute-done.42.refs_1_, ...), custom_call_target="tpu_custom_call", output_to_operand_aliasing={{0}: (5, {}), {1}: (6, {})} | custom-call | bytes 12800000 | tf_op jit(solution)/shard_map/widen_gate_1/pallas_call | solution.py:432
  287.6 4.8 %widen_ffn_1.1 = (f32[704,1024]{1,0:T(8,128)}, f32[704,1024]{1,0:T(8,128)}, f32[704,1024]{1,0:T(8,128)}) custom-call(s32[2]{0:T(128)} %pad_add_fusion.own, bf16[3,704,128]{2,1,0:T(8,128)(2,1)} %copy-done.20, bf16[3,704,128]{2,1,0:T(8,128)(2,1)} %copy-done.21, ...), custom_call_target="tpu_custom_call", output_to_operand_aliasing={{0}: (5, {}), {1}: (6, {}), {2}: (7, {})} | custom-call | bytes 12800000 | tf_op jit(solution)/shard_map/widen_ffn_1/pallas_call | solution.py:432
  292.3 7.4 %collective-permute-done.51.refs_2_ = bf16[128,1024]{1,0:T(8,128)(2,1)S(1)} collective-permute-done((bf16[128,1024]{1,0:T(8,128)(2,1)S(1)}, bf16[128,1024]{1,0:T(8,128)(2,1)S(1)}, u32[]{:S(2)}, u32[]{:S(2)}) %collective-permute-start.51) | collective-permute-done | bytes 262176 | tf_op jit(solution)/shard_map/ppermute | solution.py:362
  300.9 5.6 %widen_square_0.1 = (f32[1024,1024]{1,0:T(8,128)}, f32[1024,1024]{1,0:T(8,128)}, f32[1024,1024]{1,0:T(8,128)}) custom-call(s32[2]{0:T(128)} %pad_add_fusion.own, bf16[4,3,128,256]{3,2,1,0:T(8,128)(2,1)} %copy-done.2, bf16[4,3,128,256]{3,2,1,0:T(8,128)(2,1)} %copy-done.15, bf16[4,3,128,256]{3,2,1,0:T(8,128)(2,1)} %copy-done.14, ...), custom_call_target="tpu_custom_call" | custom-call | bytes 12800000 | tf_op jit(solution)/shard_map/widen_square_0/pallas_call | solution.py:432
  306.5 2.2 output.1
  310.4 5.6 %widen_square_1.1 = (f32[1024,1024]{1,0:T(8,128)}, f32[1024,1024]{1,0:T(8,128)}, f32[1024,1024]{1,0:T(8,128)}) custom-call(s32[2]{0:T(128)} %pad_add_fusion.own, bf16[4,3,128,256]{3,2,1,0:T(8,128)(2,1)} %copy-done.7, bf16[4,3,128,256]{3,2,1,0:T(8,128)(2,1)} %copy-done.8, ...), custom_call_target="tpu_custom_call", output_to_operand_aliasing={{0}: (5, {}), {1}: (6, {}), {2}: (7, {})} | custom-call | bytes 12800000 | tf_op jit(solution)/shard_map/widen_square_1/pallas_call | solution.py:432
  (267 shorter events, 52.9 us)
Async XLA Ops:
  0.7 31.4 %collective-permute-start.1 = (bf16[128,1024]{1,0:T(8,128)(2,1)}, bf16[128,1024]{1,0:T(8,128)(2,1)S(1)}, u32[]{:S(2)}, u32[]{:S(2)}) collective-permute-start(bf16[128,1024]{1,0:T(8,128)(2,1)} %refs_9_.1), channel_id=1, source_target_pairs={{0,2},{1,3},{2,0},{3,1},{4,6},{5,7},{6,4},{7,5},{8,10},{9,11},{10,... | collective-permute-start | bytes 786440 | tf_op jit(solution)/shard_map/ppermute | solution.py:362
  4.8 16.2 %collective-permute-start = (bf16[128,1024]{1,0:T(8,128)(2,1)}, bf16[128,1024]{1,0:T(8,128)(2,1)S(1)}, u32[]{:S(2)}, u32[]{:S(2)}) collective-permute-start(bf16[128,1024]{1,0:T(8,128)(2,1)} %refs_9_.1), channel_id=1, source_target_pairs={{0,1},{1,0},{2,3},{3,2},{4,5},{5,4},{6,7},{7,6},{8,9},{9,8},{10,11... | collective-permute-start | bytes 786440 | tf_op jit(solution)/shard_map/ppermute | solution.py:362
  6.4 25.8 %collective-permute-start.2 = (bf16[128,1024]{1,0:T(8,128)(2,1)}, bf16[128,1024]{1,0:T(8,128)(2,1)S(1)}, u32[]{:S(2)}, u32[]{:S(2)}) collective-permute-start(bf16[128,1024]{1,0:T(8,128)(2,1)} %refs_9_.1), channel_id=1, source_target_pairs={{0,3},{1,2},{2,1},{3,0},{4,7},{5,6},{6,5},{7,4},{8,11},{9,10},{10,... | collective-permute-start | bytes 786440 | tf_op jit(solution)/shard_map/ppermute | solution.py:362
  32.2 31.0 %collective-permute-start.8 = (bf16[128,1024]{1,0:T(8,128)(2,1)S(1)}, bf16[128,1024]{1,0:T(8,128)(2,1)S(1)}, u32[]{:S(2)}, u32[]{:S(2)}) collective-permute-start(bf16[128,1024]{1,0:T(8,128)(2,1)S(1)} %copy-done.6), channel_id=1, source_target_pairs={{0,3},{1,2},{2,1},{3,0},{4,7},{5,6},{6,5},{7,4},{8,11},{9,10},{10,... | collective-permute-start | bytes 786440 | tf_op jit(solution)/shard_map/ppermute | solution.py:362
  36.0 27.1 %collective-permute-start.7 = (bf16[128,1024]{1,0:T(8,128)(2,1)S(1)}, bf16[128,1024]{1,0:T(8,128)(2,1)S(1)}, u32[]{:S(2)}, u32[]{:S(2)}) collective-permute-start(bf16[128,1024]{1,0:T(8,128)(2,1)S(1)} %copy-done.6), channel_id=1, source_target_pairs={{0,2},{1,3},{2,0},{3,1},{4,6},{5,7},{6,4},{7,5},{8,10},{9,11},{10,... | collective-permute-start | bytes 786440 | tf_op jit(solution)/shard_map/ppermute | solution.py:362
  36.1 27.1 %collective-permute-start.6 = (bf16[128,1024]{1,0:T(8,128)(2,1)S(1)}, bf16[128,1024]{1,0:T(8,128)(2,1)S(1)}, u32[]{:S(2)}, u32[]{:S(2)}) collective-permute-start(bf16[128,1024]{1,0:T(8,128)(2,1)S(1)} %copy-done.6), channel_id=1, source_target_pairs={{0,1},{1,0},{2,3},{3,2},{4,5},{5,4},{6,7},{7,6},{8,9},{9,8},{10,11... | collective-permute-start | bytes 786440 | tf_op jit(solution)/shard_map/ppermute | solution.py:362
  36.7 10.4 %collective-permute-start.3 = (f32[1,8]{1,0:T(1,128)S(1)}, f32[1,8]{1,0:T(1,128)S(1)}, u32[]{:S(2)}, u32[]{:S(2)}) collective-permute-start(f32[1,8]{1,0:T(1,128)S(1)} %bitcast.81), channel_id=1, source_target_pairs={{0,4},{4,0},{8,12},{12,8},{16,20},{20,16},{24,28},{28,24},{1,5},{5... | collective-permute-start | bytes 104 | tf_op jit(solution)/shard_map/ppermute | solution.py:463
  50.8 11.7 %collective-permute-start.5 = (f32[4,8]{1,0:T(4,128)S(1)}, f32[4,8]{1,0:T(4,128)S(1)}, u32[]{:S(2)}, u32[]{:S(2)}) collective-permute-start(f32[4,8]{1,0:T(4,128)S(1)} %pad_maximum_fusion.3), channel_id=1, source_target_pairs={{0,16},{4,20},{8,24},{12,28},{16,0},{20,4},{24,8},{28,12},{1,17},{... | collective-permute-start | bytes 392 | tf_op jit(solution)/shard_map/ppermute | solution.py:463
  63.2 6.9 %collective-permute-start.11 = (bf16[2,128,128]{2,1,0:T(8,128)(2,1)S(1)}, bf16[2,128,128]{2,1,0:T(8,128)(2,1)S(1)}, u32[]{:S(2)}, u32[]{:S(2)}) collective-permute-start(bf16[2,128,128]{2,1,0:T(8,128)(2,1)S(1)} %fusion.1.refs_0_), channel_id=1, source_target_pairs={{0,3},{1,2},{2,1},{3,0},{4,7},{5,6},{6,5},{7,4},{8,11},{9,10},{10,... | collective-permute-start | bytes 196616 | tf_op jit(solution)/shard_map/ppermute | solution.py:362
  93.2 12.6 %collective-permute-start.12 = (bf16[128,1024]{1,0:T(8,128)(2,1)}, bf16[128,1024]{1,0:T(8,128)(2,1)S(1)}, u32[]{:S(2)}, u32[]{:S(2)}) collective-permute-start(bf16[128,1024]{1,0:T(8,128)(2,1)} %get-tuple-element.230), channel_id=1, source_target_pairs={{0,1},{1,0},{2,3},{3,2},{4,5},{5,4},{6,7},{7,6},{8,9},{9,8},{10,11... | collective-permute-start | bytes 786440 | tf_op jit(solution)/shard_map/ppermute | solution.py:362
  94.7 21.5 %collective-permute-start.13 = (bf16[128,1024]{1,0:T(8,128)(2,1)}, bf16[128,1024]{1,0:T(8,128)(2,1)S(1)}, u32[]{:S(2)}, u32[]{:S(2)}) collective-permute-start(bf16[128,1024]{1,0:T(8,128)(2,1)} %get-tuple-element.231), channel_id=1, source_target_pairs={{0,2},{1,3},{2,0},{3,1},{4,6},{5,7},{6,4},{7,5},{8,10},{9,11},{10,... | collective-permute-start | bytes 786440 | tf_op jit(solution)/shard_map/ppermute | solution.py:362
  96.2 20.0 %collective-permute-start.14 = (bf16[128,1024]{1,0:T(8,128)(2,1)}, bf16[128,1024]{1,0:T(8,128)(2,1)S(1)}, u32[]{:S(2)}, u32[]{:S(2)}) collective-permute-start(bf16[128,1024]{1,0:T(8,128)(2,1)} %get-tuple-element.232), channel_id=1, source_target_pairs={{0,3},{1,2},{2,1},{3,0},{4,7},{5,6},{6,5},{7,4},{8,11},{9,10},{10,... | collective-permute-start | bytes 786440 | tf_op jit(solution)/shard_map/ppermute | solution.py:362
  123.2 21.9 %collective-permute-start.18 = (bf16[4,3,704,128]{3,2,1,0:T(8,128)(2,1)S(1)}, bf16[4,3,704,128]{3,2,1,0:T(8,128)(2,1)S(1)}, u32[]{:S(2)}, u32[]{:S(2)}) collective-permute-start(bf16[4,3,704,128]{3,2,1,0:T(8,128)(2,1)S(1)} %copy-done.49), channel_id=1, source_target_pairs={{0,4},{4,0},{8,12},{12,8},{16,20},{20,16},{24,28},{28,24},{1,5},{5... | collective-permute-start | bytes 6488072 | tf_op jit(solution)/shard_map/ppermute | solution.py:375
  123.3 13.5 %collective-permute-start.15 = (bf16[128,768]{1,0:T(8,128)(2,1)}, bf16[128,768]{1,0:T(8,128)(2,1)S(1)}, u32[]{:S(2)}, u32[]{:S(2)}) collective-permute-start(bf16[128,768]{1,0:T(8,128)(2,1)} %get-tuple-element.253), channel_id=1, source_target_pairs={{0,1},{1,0},{2,3},{3,2},{4,5},{5,4},{6,7},{7,6},{8,9},{9,8},{10,11... | collective-permute-start | bytes 589832 | tf_op jit(solution)/shard_map/ppermute | solution.py:362
  127.8 17.4 %collective-permute-start.16 = (bf16[128,768]{1,0:T(8,128)(2,1)}, bf16[128,768]{1,0:T(8,128)(2,1)S(1)}, u32[]{:S(2)}, u32[]{:S(2)}) collective-permute-start(bf16[128,768]{1,0:T(8,128)(2,1)} %get-tuple-element.254), channel_id=1, source_target_pairs={{0,2},{1,3},{2,0},{3,1},{4,6},{5,7},{6,4},{7,5},{8,10},{9,11},{10,... | collective-permute-start | bytes 589832 | tf_op jit(solution)/shard_map/ppermute | solution.py:362
  128.1 17.1 %collective-permute-start.17 = (bf16[128,768]{1,0:T(8,128)(2,1)}, bf16[128,768]{1,0:T(8,128)(2,1)S(1)}, u32[]{:S(2)}, u32[]{:S(2)}) collective-permute-start(bf16[128,768]{1,0:T(8,128)(2,1)} %get-tuple-element.255), channel_id=1, source_target_pairs={{0,3},{1,2},{2,1},{3,0},{4,7},{5,6},{6,5},{7,4},{8,11},{9,10},{10,... | collective-permute-start | bytes 589832 | tf_op jit(solution)/shard_map/ppermute | solution.py:362
  145.9 23.9 %collective-permute-start.19 = (bf16[2,3,704,128]{3,2,1,0:T(8,128)(2,1)S(1)}, bf16[2,3,704,128]{3,2,1,0:T(8,128)(2,1)S(1)}, u32[]{:S(2)}, u32[]{:S(2)}) collective-permute-start(bf16[2,3,704,128]{3,2,1,0:T(8,128)(2,1)S(1)} %get-tuple-element.380), channel_id=1, source_target_pairs={{0,8},{4,20},{8,0},{12,28},{16,24},{20,4},{24,16},{28,12},{1,9},{5... | collective-permute-start | bytes 3244040 | tf_op jit(solution)/shard_map/ppermute | solution.py:382
  180.8 23.1 %collective-permute-start.21 = (bf16[2,5,128,256]{3,2,1,0:T(8,128)(2,1)S(1)}, bf16[2,5,128,256]{3,2,1,0:T(8,128)(2,1)S(1)}, u32[]{:S(2)}, u32[]{:S(2)}) collective-permute-start(bf16[2,5,128,256]{3,2,1,0:T(8,128)(2,1)S(1)} %get-tuple-element.288), channel_id=1, source_target_pairs={{0,8},{4,20},{8,0},{12,28},{16,24},{20,4},{24,16},{28,12},{1,9},{5... | collective-permute-start | bytes 1966088 | tf_op jit(solution)/shard_map/ppermute | solution.py:382
  181.4 22.5 %collective-permute-start.25 = (bf16[1,3,704,128]{3,2,1,0:T(8,128)(2,1)S(1)}, bf16[1,3,704,128]{3,2,1,0:T(8,128)(2,1)S(1)}, u32[]{:S(2)}, u32[]{:S(2)}) collective-permute-start(bf16[1,3,704,128]{3,2,1,0:T(8,128)(2,1)S(1)} %slice_add_fusion.4), channel_id=1, source_target_pairs={{0,16},{4,12},{8,24},{12,4},{16,0},{20,28},{24,8},{28,20},{1,17},{... | collective-permute-start | bytes 1622024 | tf_op jit(solution)/shard_map/ppermute | solution.py:382
  182.9 11.8 %collective-permute-start.22 = (bf16[128,768]{1,0:T(8,128)(2,1)S(1)}, bf16[128,768]{1,0:T(8,128)(2,1)S(1)}, u32[]{:S(2)}, u32[]{:S(2)}) collective-permute-start(bf16[128,768]{1,0:T(8,128)(2,1)S(1)} %copy-done.54), channel_id=1, source_target_pairs={{0,1},{1,0},{2,3},{3,2},{4,5},{5,4},{6,7},{7,6},{8,9},{9,8},{10,11... | collective-permute-start | bytes 589832 | tf_op jit(solution)/shard_map/ppermute | solution.py:362
  186.8 17.1 %collective-permute-start.23 = (bf16[128,768]{1,0:T(8,128)(2,1)S(1)}, bf16[128,768]{1,0:T(8,128)(2,1)S(1)}, u32[]{:S(2)}, u32[]{:S(2)}) collective-permute-start(bf16[128,768]{1,0:T(8,128)(2,1)S(1)} %copy-done.53), channel_id=1, source_target_pairs={{0,2},{1,3},{2,0},{3,1},{4,6},{5,7},{6,4},{7,5},{8,10},{9,11},{10,... | collective-permute-start | bytes 589832 | tf_op jit(solution)/shard_map/ppermute | solution.py:362
  187.1 16.8 %collective-permute-start.24 = (bf16[128,768]{1,0:T(8,128)(2,1)S(1)}, bf16[128,768]{1,0:T(8,128)(2,1)S(1)}, u32[]{:S(2)}, u32[]{:S(2)}) collective-permute-start(bf16[128,768]{1,0:T(8,128)(2,1)S(1)} %copy-done.52), channel_id=1, source_target_pairs={{0,3},{1,2},{2,1},{3,0},{4,7},{5,6},{6,5},{7,4},{8,11},{9,10},{10,... | collective-permute-start | bytes 589832 | tf_op jit(solution)/shard_map/ppermute | solution.py:362
  203.9 7.1 %collective-permute-start.26 = (bf16[1,5,128,256]{3,2,1,0:T(8,128)(2,1)S(1)}, bf16[1,5,128,256]{3,2,1,0:T(8,128)(2,1)S(1)}, u32[]{:S(2)}, u32[]{:S(2)}) collective-permute-start(bf16[1,5,128,256]{3,2,1,0:T(8,128)(2,1)S(1)} %slice_add_fusion.5), channel_id=1, source_target_pairs={{0,16},{4,12},{8,24},{12,4},{16,0},{20,28},{24,8},{28,20},{1,17},{... | collective-permute-start | bytes 983048 | tf_op jit(solution)/shard_map/ppermute | solution.py:382
  204.6 20.2 %collective-permute-start.30 = (bf16[3,704,128]{2,1,0:T(8,128)(2,1)S(1)}, bf16[3,704,128]{2,1,0:T(8,128)(2,1)S(1)}, u32[]{:S(2)}, u32[]{:S(2)}) collective-permute-start(bf16[3,704,128]{2,1,0:T(8,128)(2,1)S(1)} %add_bitcast_fusion.refs_0_), channel_id=1, source_target_pairs={{0,16},{4,12},{8,24},{12,4},{16,0},{20,28},{24,8},{28,20},{1,17},{... | collective-permute-start | bytes 1622024 | tf_op jit(solution)/shard_map/ppermute | solution.py:382
  211.2 8.3 %collective-permute-start.29 = (bf16[2,128,256]{2,1,0:T(8,128)(2,1)S(1)}, bf16[2,128,256]{2,1,0:T(8,128)(2,1)S(1)}, u32[]{:S(2)}, u32[]{:S(2)}) collective-permute-start(bf16[2,128,256]{2,1,0:T(8,128)(2,1)S(1)} %get-tuple-element.385), channel_id=1, source_target_pairs={{0,3},{1,2},{2,1},{3,0},{4,7},{5,6},{6,5},{7,4},{8,11},{9,10},{10,... | collective-permute-start | bytes 393224 | tf_op jit(solution)/shard_map/ppermute | solution.py:362
  212.9 11.8 %collective-permute-start.28 = (bf16[2,128,256]{2,1,0:T(8,128)(2,1)S(1)}, bf16[2,128,256]{2,1,0:T(8,128)(2,1)S(1)}, u32[]{:S(2)}, u32[]{:S(2)}) collective-permute-start(bf16[2,128,256]{2,1,0:T(8,128)(2,1)S(1)} %get-tuple-element.385), channel_id=1, source_target_pairs={{0,2},{1,3},{2,0},{3,1},{4,6},{5,7},{6,4},{7,5},{8,10},{9,11},{10,... | collective-permute-start | bytes 393224 | tf_op jit(solution)/shard_map/ppermute | solution.py:362
  216.1 8.7 %collective-permute-start.27 = (bf16[2,128,256]{2,1,0:T(8,128)(2,1)S(1)}, bf16[2,128,256]{2,1,0:T(8,128)(2,1)S(1)}, u32[]{:S(2)}, u32[]{:S(2)}) collective-permute-start(bf16[2,128,256]{2,1,0:T(8,128)(2,1)S(1)} %get-tuple-element.385), channel_id=1, source_target_pairs={{0,1},{1,0},{2,3},{3,2},{4,5},{5,4},{6,7},{7,6},{8,9},{9,8},{10,11... | collective-permute-start | bytes 393224 | tf_op jit(solution)/shard_map/ppermute | solution.py:362
  224.8 14.9 %collective-permute-start.34 = (bf16[4,2,128,256]{3,2,1,0:T(8,128)(2,1)S(1)}, bf16[4,2,128,256]{3,2,1,0:T(8,128)(2,1)S(1)}, u32[]{:S(2)}, u32[]{:S(2)}) collective-permute-start(bf16[4,2,128,256]{3,2,1,0:T(8,128)(2,1)S(1)} %pad_maximum_fusion.1.refs_0_), channel_id=1, source_target_pairs={{0,16},{4,12},{8,24},{12,4},{16,0},{20,28},{24,8},{28,20},{1,17},{... | collective-permute-start | bytes 1572872 | tf_op jit(solution)/shard_map/ppermute | solution.py:382
  225.0 8.9 %collective-permute-start.33 = (bf16[3,128,256]{2,1,0:T(8,128)(2,1)S(1)}, bf16[3,128,256]{2,1,0:T(8,128)(2,1)S(1)}, u32[]{:S(2)}, u32[]{:S(2)}) collective-permute-start(bf16[3,128,256]{2,1,0:T(8,128)(2,1)S(1)} %slice_bitcast_fusion), channel_id=1, source_target_pairs={{0,3},{1,2},{2,1},{3,0},{4,7},{5,6},{6,5},{7,4},{8,11},{9,10},{10,... | collective-permute-start | bytes 589832 | tf_op jit(solution)/shard_map/ppermute | solution.py:362
  226.7 22.1 %collective-permute-start.37 = (bf16[3,704,128]{2,1,0:T(8,128)(2,1)S(1)}, bf16[3,704,128]{2,1,0:T(8,128)(2,1)S(1)}, u32[]{:S(2)}, u32[]{:S(2)}) collective-permute-start(bf16[3,704,128]{2,1,0:T(8,128)(2,1)S(1)} %add_bitcast_fusion.refs_0_), channel_id=1, source_target_pairs={{0,8},{4,20},{8,0},{12,28},{16,24},{20,4},{24,16},{28,12},{1,9},{5... | collective-permute-start | bytes 1622024 | tf_op jit(solution)/shard_map/ppermute | solution.py:382
  228.2 20.6 %collective-permute-start.38 = (bf16[3,704,128]{2,1,0:T(8,128)(2,1)S(1)}, bf16[3,704,128]{2,1,0:T(8,128)(2,1)S(1)}, u32[]{:S(2)}, u32[]{:S(2)}) collective-permute-start(bf16[3,704,128]{2,1,0:T(8,128)(2,1)S(1)} %collective-permute-done.30.refs_1_), channel_id=1, source_target_pairs={{0,8},{4,20},{8,0},{12,28},{16,24},{20,4},{24,16},{28,12},{1,9},{5... | collective-permute-start | bytes 1622024 | tf_op jit(solution)/shard_map/ppermute | solution.py:382
  228.8 11.1 %collective-permute-start.31 = (bf16[3,128,256]{2,1,0:T(8,128)(2,1)S(1)}, bf16[3,128,256]{2,1,0:T(8,128)(2,1)S(1)}, u32[]{:S(2)}, u32[]{:S(2)}) collective-permute-start(bf16[3,128,256]{2,1,0:T(8,128)(2,1)S(1)} %slice_bitcast_fusion), channel_id=1, source_target_pairs={{0,1},{1,0},{2,3},{3,2},{4,5},{5,4},{6,7},{7,6},{8,9},{9,8},{10,11... | collective-permute-start | bytes 589832 | tf_op jit(solution)/shard_map/ppermute | solution.py:362
  233.9 14.9 %collective-permute-start.35 = (bf16[4,2,128,256]{3,2,1,0:T(8,128)(2,1)S(1)}, bf16[4,2,128,256]{3,2,1,0:T(8,128)(2,1)S(1)}, u32[]{:S(2)}, u32[]{:S(2)}) collective-permute-start(bf16[4,2,128,256]{3,2,1,0:T(8,128)(2,1)S(1)} %pad_maximum_fusion.1.refs_0_), channel_id=1, source_target_pairs={{0,8},{4,20},{8,0},{12,28},{16,24},{20,4},{24,16},{28,12},{1,9},{5... | collective-permute-start | bytes 1572872 | tf_op jit(solution)/shard_map/ppermute | solution.py:382
  239.7 14.1 %collective-permute-start.36 = (bf16[4,2,128,256]{3,2,1,0:T(8,128)(2,1)S(1)}, bf16[4,2,128,256]{3,2,1,0:T(8,128)(2,1)S(1)}, u32[]{:S(2)}, u32[]{:S(2)}) collective-permute-start(bf16[4,2,128,256]{3,2,1,0:T(8,128)(2,1)S(1)} %collective-permute-done.34.refs_1_), channel_id=1, source_target_pairs={{0,8},{4,20},{8,0},{12,28},{16,24},{20,4},{24,16},{28,12},{1,9},{5... | collective-permute-start | bytes 1572872 | tf_op jit(solution)/shard_map/ppermute | solution.py:382
  239.8 8.9 %collective-permute-start.32 = (bf16[3,128,256]{2,1,0:T(8,128)(2,1)S(1)}, bf16[3,128,256]{2,1,0:T(8,128)(2,1)S(1)}, u32[]{:S(2)}, u32[]{:S(2)}) collective-permute-start(bf16[3,128,256]{2,1,0:T(8,128)(2,1)S(1)} %slice_bitcast_fusion), channel_id=1, source_target_pairs={{0,2},{1,3},{2,0},{3,1},{4,6},{5,7},{6,4},{7,5},{8,10},{9,11},{10,... | collective-permute-start | bytes 589832 | tf_op jit(solution)/shard_map/ppermute | solution.py:362
  256.7 19.8 %collective-permute-start.40 = (bf16[4,3,128,256]{3,2,1,0:T(8,128)(2,1)S(1)}, bf16[4,3,128,256]{3,2,1,0:T(8,128)(2,1)S(1)}, u32[]{:S(2)}, u32[]{:S(2)}) collective-permute-start(bf16[4,3,128,256]{3,2,1,0:T(8,128)(2,1)S(1)} %pad_maximum_fusion.refs_0_), channel_id=1, source_target_pairs={{0,8},{4,20},{8,0},{12,28},{16,24},{20,4},{24,16},{28,12},{1,9},{5... | collective-permute-start | bytes 2359304 | tf_op jit(solution)/shard_map/ppermute | solution.py:382
  258.1 18.4 %collective-permute-start.39 = (bf16[4,3,128,256]{3,2,1,0:T(8,128)(2,1)S(1)}, bf16[4,3,128,256]{3,2,1,0:T(8,128)(2,1)S(1)}, u32[]{:S(2)}, u32[]{:S(2)}) collective-permute-start(bf16[4,3,128,256]{3,2,1,0:T(8,128)(2,1)S(1)} %pad_maximum_fusion.refs_0_), channel_id=1, source_target_pairs={{0,16},{4,12},{8,24},{12,4},{16,0},{20,28},{24,8},{28,20},{1,17},{... | collective-permute-start | bytes 2359304 | tf_op jit(solution)/shard_map/ppermute | solution.py:382
  258.9 11.3 %collective-permute-start.46 = (bf16[3,704,128]{2,1,0:T(8,128)(2,1)S(1)}, bf16[3,704,128]{2,1,0:T(8,128)(2,1)S(1)}, u32[]{:S(2)}, u32[]{:S(2)}) collective-permute-start(bf16[3,704,128]{2,1,0:T(8,128)(2,1)S(1)} %collective-permute-done.30.refs_1_), channel_id=1, source_target_pairs={{0,4},{4,0},{8,12},{12,8},{16,20},{20,16},{24,28},{28,24},{1,5},{5... | collective-permute-start | bytes 1622024 | tf_op jit(solution)/shard_map/ppermute | solution.py:375
  259.6 10.7 %collective-permute-start.47 = (bf16[3,704,128]{2,1,0:T(8,128)(2,1)S(1)}, bf16[3,704,128]{2,1,0:T(8,128)(2,1)S(1)}, u32[]{:S(2)}, u32[]{:S(2)}) collective-permute-start(bf16[3,704,128]{2,1,0:T(8,128)(2,1)S(1)} %collective-permute-done.37.refs_2_), channel_id=1, source_target_pairs={{0,4},{4,0},{8,12},{12,8},{16,20},{20,16},{24,28},{28,24},{1,5},{5... | collective-permute-start | bytes 1622024 | tf_op jit(solution)/shard_map/ppermute | solution.py:375
  260.4 9.9 %collective-permute-start.48 = (bf16[3,704,128]{2,1,0:T(8,128)(2,1)S(1)}, bf16[3,704,128]{2,1,0:T(8,128)(2,1)S(1)}, u32[]{:S(2)}, u32[]{:S(2)}) collective-permute-start(bf16[3,704,128]{2,1,0:T(8,128)(2,1)S(1)} %collective-permute-done.38.refs_3_), channel_id=1, source_target_pairs={{0,4},{4,0},{8,12},{12,8},{16,20},{20,16},{24,28},{28,24},{1,5},{5... | collective-permute-start | bytes 1622024 | tf_op jit(solution)/shard_map/ppermute | solution.py:375
  276.5 23.3 %collective-permute-start.49 = (bf16[4,3,128,256]{3,2,1,0:T(8,128)(2,1)S(1)}, bf16[4,3,128,256]{3,2,1,0:T(8,128)(2,1)S(1)}, u32[]{:S(2)}, u32[]{:S(2)}) collective-permute-start(bf16[4,3,128,256]{3,2,1,0:T(8,128)(2,1)S(1)} %collective-permute-done.39.refs_1_), channel_id=1, source_target_pairs={{0,8},{4,20},{8,0},{12,28},{16,24},{20,4},{24,16},{28,12},{1,9},{5... | collective-permute-start | bytes 2359304 | tf_op jit(solution)/shard_map/ppermute | solution.py:382
  278.5 13.9 %collective-permute-start.50 = (bf16[128,1024]{1,0:T(8,128)(2,1)}, bf16[128,1024]{1,0:T(8,128)(2,1)S(1)}, u32[]{:S(2)}, u32[]{:S(2)}) collective-permute-start(bf16[128,1024]{1,0:T(8,128)(2,1)} %get-tuple-element.355), channel_id=1, source_target_pairs={{0,1},{1,0},{2,3},{3,2},{4,5},{5,4},{6,7},{7,6},{8,9},{9,8},{10,11... | collective-permute-start | bytes 786440 | tf_op jit(solution)/shard_map/ppermute | solution.py:362
  278.5 21.3 %collective-permute-start.51 = (bf16[128,1024]{1,0:T(8,128)(2,1)S(1)}, bf16[128,1024]{1,0:T(8,128)(2,1)S(1)}, u32[]{:S(2)}, u32[]{:S(2)}) collective-permute-start(bf16[128,1024]{1,0:T(8,128)(2,1)S(1)} %copy-done.51), channel_id=1, source_target_pairs={{0,2},{1,3},{2,0},{3,1},{4,6},{5,7},{6,4},{7,5},{8,10},{9,11},{10,... | collective-permute-start | bytes 786440 | tf_op jit(solution)/shard_map/ppermute | solution.py:362
  281.2 18.6 %collective-permute-start.52 = (bf16[128,1024]{1,0:T(8,128)(2,1)S(1)}, bf16[128,1024]{1,0:T(8,128)(2,1)S(1)}, u32[]{:S(2)}, u32[]{:S(2)}) collective-permute-start(bf16[128,1024]{1,0:T(8,128)(2,1)S(1)} %copy-done.50), channel_id=1, source_target_pairs={{0,3},{1,2},{2,1},{3,0},{4,7},{5,6},{6,5},{7,4},{8,11},{9,10},{10,... | collective-permute-start | bytes 786440 | tf_op jit(solution)/shard_map/ppermute | solution.py:362
  299.8 8.9 %collective-permute-start.53 = (bf16[4,3,128,256]{3,2,1,0:T(8,128)(2,1)S(1)}, bf16[4,3,128,256]{3,2,1,0:T(8,128)(2,1)S(1)}, u32[]{:S(2)}, u32[]{:S(2)}) collective-permute-start(bf16[4,3,128,256]{3,2,1,0:T(8,128)(2,1)S(1)} %pad_maximum_fusion.refs_0_), channel_id=1, source_target_pairs={{0,4},{4,0},{8,12},{12,8},{16,20},{20,16},{24,28},{28,24},{1,5},{5... | collective-permute-start | bytes 2359304 | tf_op jit(solution)/shard_map/ppermute | solution.py:375
  299.9 8.8 %collective-permute-start.54 = (bf16[4,3,128,256]{3,2,1,0:T(8,128)(2,1)S(1)}, bf16[4,3,128,256]{3,2,1,0:T(8,128)(2,1)S(1)}, u32[]{:S(2)}, u32[]{:S(2)}) collective-permute-start(bf16[4,3,128,256]{3,2,1,0:T(8,128)(2,1)S(1)} %collective-permute-done.39.refs_1_), channel_id=1, source_target_pairs={{0,4},{4,0},{8,12},{12,8},{16,20},{20,16},{24,28},{28,24},{1,5},{5... | collective-permute-start | bytes 2359304 | tf_op jit(solution)/shard_map/ppermute | solution.py:375
  300.4 8.3 %collective-permute-start.55 = (bf16[4,3,128,256]{3,2,1,0:T(8,128)(2,1)S(1)}, bf16[4,3,128,256]{3,2,1,0:T(8,128)(2,1)S(1)}, u32[]{:S(2)}, u32[]{:S(2)}) collective-permute-start(bf16[4,3,128,256]{3,2,1,0:T(8,128)(2,1)S(1)} %collective-permute-done.40.refs_2_), channel_id=1, source_target_pairs={{0,4},{4,0},{8,12},{12,8},{16,20},{20,16},{24,28},{28,24},{1,5},{5... | collective-permute-start | bytes 2359304 | tf_op jit(solution)/shard_map/ppermute | solution.py:375
  300.5 8.3 %collective-permute-start.56 = (bf16[4,3,128,256]{3,2,1,0:T(8,128)(2,1)S(1)}, bf16[4,3,128,256]{3,2,1,0:T(8,128)(2,1)S(1)}, u32[]{:S(2)}, u32[]{:S(2)}) collective-permute-start(bf16[4,3,128,256]{3,2,1,0:T(8,128)(2,1)S(1)} %collective-permute-done.49.refs_3_), channel_id=1, source_target_pairs={{0,4},{4,0},{8,12},{12,8},{16,20},{20,16},{24,28},{28,24},{1,5},{5... | collective-permute-start | bytes 2359304 | tf_op jit(solution)/shard_map/ppermute | solution.py:375
  (64 other events, 724.5 us)

commit v4 on v3

--- a/solution.py
+++ b/solution.py
@@ -73,6 +73,68 @@
 
 def flip_of(own, share):
     return share * (own[1] & (BLOCK // share - 1))
+
+
+def exact(a, b, dims):
+    return lax.dot_general(a, b, (dims, ((), ())), precision=lax.Precision.HIGHEST, preferred_element_type=f32)
+
+
+KEEP, ENTER, ENDS, FIRST, SECOND = range(5)
+
+
+def layout_kernel(narrow, share, own, lengths, pads, log_decay, gcol, rise, tail, grow, live, coefs, total):
+    heads, local = log_decay.shape
+    hn = heads // narrow
+    per, blocks = BLOCK // share, local // BLOCK
+    base = own[0] * local
+    place = lax.broadcasted_iota(jnp.int32, (local, 1), 0)
+    spot = base + ((place // share) ^ own[1]) * share + place % share
+    alive = jnp.zeros((local, 1), f32)
+    keeps = [jnp.float32(1.0)] * blocks
+    end = jnp.int32(0)
+    for s in range(lengths.shape[0]):
+        start, end = end, end + lengths[s]
+        alive = jnp.where((spot >= start) & (spot < end - pads[s]), 1.0, alive)
+        keeps = [jnp.where(start == base + b * BLOCK, 0.0, keep) for b, keep in enumerate(keeps)]
+    live[...] = alive
+
+    size = (BLOCK, BLOCK)
+    upper = (lax.broadcasted_iota(jnp.int32, size, 0) <= lax.broadcasted_iota(jnp.int32, size, 1)).astype(f32)
+    eye = (lax.broadcasted_iota(jnp.int32, (heads, heads), 0)
+           == lax.broadcasted_iota(jnp.int32, (heads, heads), 1)).astype(f32)
+    turned = own[1] // per > 0
+    rows_of, ends_of, decay_of, keep_of = [], [], [], []
+    for b in range(blocks):
+        part = log_decay[:, b * BLOCK : (b + 1) * BLOCK]
+        g = exact(part, upper, ((1,), (0,)))
+        for bit in range((per - 1).bit_length()):
+            step = share << bit
+            flipped = [g[:, (i ^ 1) * step : ((i ^ 1) + 1) * step] for i in range(BLOCK // step)]
+            g = jnp.where((own[1] >> bit) & 1 == 1, jnp.concatenate(flipped, axis=1), g)
+        end_row = exact(jnp.ones_like(part), part, ((1,), (1,)))[0:1]
+        rows_of.append(g)
+        ends_of.append(end_row)
+        decay_of.append(jnp.exp(end_row) * keeps[b])
+        keep_of.append(jnp.full((1, heads), 1.0, f32) * keeps[b])
+    total[...] = decay_of[0] * decay_of[1]
+    one = jnp.ones((1, heads), f32)
+    kinds = (keep_of, (one, decay_of[0]), (decay_of[1], one), (one, 0.0 * one), (0.0 * one, one))
+    for s in range(blocks):
+        def mine(pair):
+            return jnp.where(turned, pair[1 - s], pair[s])
+
+        for kind, pair in enumerate(kinds):
+            coefs[kind, s : s + 1, :] = mine(pair)
+        g = mine(rows_of)
+        column = exact(g, eye, ((0,), (0,)))
+        up, down = jnp.exp(column), jnp.exp(mine(ends_of) - column)
+        at = slice(s * BLOCK, (s + 1) * BLOCK)
+        for n in range(narrow):
+            group = slice(n * hn, (n + 1) * hn)
+            gcol[n, at, :] = column[:, group]
+            rise[n, at, :] = up[:, group]
+            tail[n, at, :] = down[:, group]
+            grow[s * narrow + n] = g[group, :]
 
 
 def forward_kernel(hn, hd, share, own, tok_a, tok_b, wq, wk, wv, wg, live, gcol, grow, tail, *refs):
@@ -111,7 +173,7 @@
         contrib[0, h] = tm(key_tail, vh)
 
 
-def out_kernel(heads, hn, hd, share, own, keep, enter, other, *refs):
+def out_kernel(heads, hn, hd, share, own, coefs, *refs):
     narrow = heads // hn
     states = refs[:narrow]
     contrib, q, intra, act, tok, rise, wo, att, inverse, gated, hidden, n2, kent = refs[narrow:]
@@ -122,8 +184,8 @@
         base = states[0][h % hn].astype(f32)
         for j in range(1, narrow):
             base = jnp.where(part == j, states[j][h % hn].astype(f32), base)
-        entering = enter[b, h] * base + other[b, h] * contrib[1 - b, h]
-        kept = (keep[b] * entering).astype(bf16)
+        entering = coefs[ENTER, b, h] * base + coefs[SECOND, b, h] * contrib[1 - b, h]
+        kept = (coefs[KEEP, b, h] * entering).astype(bf16)
 
         @pl.when(part == 0)
         def _():
@@ -144,7 +206,6 @@
 
 
 def ffn_kernel(share, n2, cot, w1, w2, w3, product, gf, gs, *pieces):
-    b = pl.program_id(0)
     normed = n2[...]
     first = mt(normed, w1[...])
     second = mt(normed, w2[...])
@@ -153,11 +214,8 @@
     gf[...] = (grad * second).astype(bf16)
     gs[...] = (grad * first).astype(bf16)
     back = (mm(gf[...], w1[...]) + mm(gs[...], w2[...])).astype(bf16)
-    per = BLOCK // share
     for i, piece in enumerate(pieces):
-        @pl.when(b == i // per)
-        def _():
-            piece[...] = back[(i % per) * share : (i % per + 1) * share]
+        piece[...] = back[i * share : (i + 1) * share]
 
 
 def reversed_bits(value, count):
@@ -241,7 +299,7 @@
                 trios[k][:, 2 * size :] = low[:, at]
 
 
-def query_kernel(hn, hd, share, own, keep, ahead, *refs):
+def query_kernel(hn, hd, share, own, coefs, *refs):
     per = BLOCK // share
     ga = refs[: -14]
     q, k, v, ql, kent, gcol, grow, rise, dq, gk, gv, direct, first, grad = refs[-14:]
@@ -263,19 +321,20 @@
         dq[:, at] = (gq * slope(ql[:, at])).astype(bf16)
         gk[:, at] = tm(raw, qh)
         gv[:, at] = tm(scores, g)
-        now = keep[b] * tm((qh.astype(f32) * up).astype(bf16), g)
+        head = own[1] * hn + h
+        now = coefs[KEEP, b, head] * tm((qh.astype(f32) * up).astype(bf16), g)
         direct[0, h] = now
 
         @pl.when(b == 0)
         def _():
-            first[h] = ahead[b, h] * now
+            first[h] = coefs[ENTER, b, head] * now
 
         @pl.when(b > 0)
         def _():
-            first[h] += ahead[b, h] * now
-
-
-def key_kernel(hn, hd, wide, share, own, leave, other, arrived, direct, n1, dq, k, v, kl, gk, gv,
+            first[h] += coefs[ENTER, b, head] * now
+
+
+def key_kernel(hn, hd, wide, share, own, coefs, arrived, direct, n1, dq, k, v, kl, gk, gv,
                tail, live, _kept, _sent, kept, sent, *refs):
     pieces = refs[:-5]
     dk, dv, aq, ak, av = refs[-5:]
@@ -284,7 +343,8 @@
     last = pl.num_programs(0) - 1
     for h in range(hn):
         at = slice(h * hd, (h + 1) * hd)
-        low = (leave[b, h] * arrived[h] + other[b, h] * direct[1 - b, h]).astype(bf16)
+        head = own[1] * hn + h
+        low = (coefs[ENDS, b, head] * arrived[h] + coefs[FIRST, b, head] * direct[1 - b, h]).astype(bf16)
         down = tail[:, h : h + 1]
         grad_key = gk[:, at] + down * mt(v[:, at], low)
         dk[:, at] = (grad_key * live[...] * slope(kl[:, at])).astype(bf16)
@@ -426,9 +486,9 @@
                 outs[item][...] = piece[item].astype(f32)
 
 
-def widen(kernel, own, other, pieces, block, cut, shape, outs, count, name):
+def widen(kernel, own, other, first, total, pieces, block, cut, shape, outs, count, name):
     places = len(pieces)
-    spec = pl.BlockSpec(block, lambda i, own: cut(target(own, i, other, 2 * places)))
+    spec = pl.BlockSpec(block, lambda i, own: cut(target(own, first + i, other, 2 * total)))
     return pl.pallas_call(
         functools.partial(kernel, places),
         grid_spec=pltpu.PrefetchScalarGridSpec(
@@ -494,40 +554,18 @@
 
     tok = gather_narrow(tokens)
 
-    ends = jnp.cumsum(lengths, dtype=jnp.int32)
-    starts = ends - lengths
-    place = jnp.arange(local, dtype=jnp.int32)
-    spot = own_wide * local + ((place // share) ^ own_narrow) * share + place % share
-    inside = (spot[:, None] >= starts[None, :]) & (spot[:, None] < ends[None, :])
-    limit = jnp.sum(jnp.where(inside, (ends - pad_counts)[None, :], 0), axis=1, dtype=jnp.int32)
-    live = (spot < limit).astype(f32)[:, None]
-    first_spot = own_wide * local + BLOCK * jnp.arange(blocks, dtype=jnp.int32)
-    keep_seq = 1.0 - jnp.any(first_spot[:, None] == starts[None, :], axis=1).astype(f32)
-    summed = jnp.cumsum(log_decay.reshape(heads, blocks, BLOCK), axis=2)
-    last = summed[:, :, -1]
-    decay = (jnp.exp(last) * keep_seq[None]).T
-
-    def slots(first, second):
-        return jnp.where(own_narrow // per == 0, jnp.stack([first, second]), jnp.stack([second, first]))
+    columns = sds((narrow, local, hn), f32)
+    gcol, rise, tail, grow, live, coefs, total = pl.pallas_call(
+        functools.partial(layout_kernel, narrow, share),
+        in_specs=[SMEM, SMEM, SMEM, pl.BlockSpec(memory_space=pltpu.VMEM)],
+        out_shape=[columns, columns, columns, sds((blocks * narrow, hn, BLOCK), f32), sds((local, 1), f32),
+                   sds((5, blocks, heads), f32), sds((1, heads), f32)],
+        cost_estimate=cost(3),
+        name="layout",
+    )(own, lengths, pad_counts, log_decay)
 
     def own_heads(values):
         return lax.dynamic_slice_in_dim(values, own_narrow * hn, hn, 1)
-
-    one, zero = jnp.ones_like(decay[0]), jnp.zeros_like(decay[0])
-    keep = slots(keep_seq[0], keep_seq[1])
-    ends_in = slots(decay[1], one)
-    enter, enter_other = slots(one, decay[0]), slots(zero, one)
-    ahead, leave_other = own_heads(slots(one, decay[0])), own_heads(slots(one, zero))
-    leave = own_heads(ends_in)
-    g = xor_order(summed.reshape(heads, narrow, share), own_narrow, 1).reshape(heads, local)
-    last_of = jnp.where(own_narrow // per == 0, last, last[:, ::-1])
-
-    def columns(values):
-        return values.reshape(narrow, hn, local).transpose(0, 2, 1)
-
-    gcol, rise = columns(g), columns(jnp.exp(g))
-    tail = columns(jnp.exp(jnp.repeat(last_of, BLOCK, axis=1) - g))
-    grow = g.reshape(narrow, hn, blocks, BLOCK).transpose(2, 0, 1, 3).reshape(blocks * narrow, hn, BLOCK)
 
     shapes = [sds((local, width), bf16), sds((local, width), bf16), *[sds((local, cols), f32)] * 2,
               *[sds((local, width), bf16)] * 3, *[sds((local, width), f32)] * 2,
@@ -535,7 +573,7 @@
     made = []
     for s in range(blocks):
         if s == 1:
-            made, later, cotangent_now, product_now = fence(made, tok[per:], cotangent, jnp.prod(decay, axis=0))
+            made, later, cotangent_now, product_now = fence(made, tok[per:], cotangent, total)
             tok = tok[:per] + list(later)
         weight = pl.BlockSpec((width, cols), lambda i, own: (0, i))
         column = pl.BlockSpec((1, BLOCK, hn), lambda i, own, s=s: (i, s, 0))
@@ -563,11 +601,11 @@
     n1, tok_all, ql, kl, q, k, v, act, intra, contrib = made
 
     cot = gather_narrow(cotangent_now)
-    factors = gather_factors(product_now)
+    factors = gather_factors(product_now[0])
     factors = lax.dynamic_slice_in_dim(factors, own_narrow * hn, hn, 1)
     coef_in, coef_out = between(factors, own_wide, True), between(factors, own_wide, False)
     message = own_heads(contrib)
-    message = jnp.sum(own_heads(ends_in)[:, :, None, None] * message, axis=0).astype(bf16)
+    message = jnp.sum(own_heads(coefs[ENDS])[:, :, None, None] * message, axis=0).astype(bf16)
     entering, cot = fence(pass_states(message, coef_in).astype(bf16), cot)
     cot_all = jnp.concatenate(cot, axis=0)
     states = gather_narrow(entering)
@@ -581,7 +619,7 @@
         grid_spec=pltpu.PrefetchScalarGridSpec(
             num_scalar_prefetch=1,
             grid=(blocks,),
-            in_specs=[SMEM, SMEM, SMEM, *[whole((hn, hd, hd))] * narrow, whole((blocks, heads, hd, hd)),
+            in_specs=[SMEM, *[whole((hn, hd, hd))] * narrow, whole((blocks, heads, hd, hd)),
                       *[all_blk] * 4, pl.BlockSpec((narrow, BLOCK, hn), lambda b, own: (0, b, 0)),
                       whole((width, width))],
             out_specs=[all_blk, rows((BLOCK, 1), up), all_blk, whole((share, width)), all_blk, own_kent],
@@ -591,7 +629,7 @@
         compiler_params=PARAMS,
         cost_estimate=cost(9.5),
         name="mixer_out",
-    )(own, keep, enter, enter_other, *states, contrib, q, intra, act, tok_all, rise, w_out)
+    )(own, coefs, *states, contrib, q, intra, act, tok_all, rise, w_out)
 
     ff = w_first.shape[1]
     first_t, second_t = w_first.T, w_second.T
@@ -599,11 +637,8 @@
     piece_spec, piece_shape = whole((share, width)), sds((share, width), bf16)
     product, gf, gs, *gn2 = pl.pallas_call(
         functools.partial(ffn_kernel, share),
-        grid=(blocks,),
-        in_specs=[all_blk, all_blk, *[whole((ff, width))] * 3],
-        out_specs=[*[ff_blk] * 3, *[piece_spec] * narrow],
         out_shape=[*[sds((local, ff), bf16)] * 3, *[piece_shape] * narrow],
-        compiler_params=PARAMS,
+        compiler_params=pltpu.CompilerParams(vmem_limit_bytes=56 << 20),
         cost_estimate=cost(10),
         name="ffn",
     )(n2, cot_all, first_t, second_t, w_third)
@@ -650,7 +685,7 @@
         name="residual_back",
     )(own, *gn2, hidden, cotangent, w_out, att, inverse, act)
     trios, kept, sent = fence(trios, kept, sent)
-    trios, kept, got = fence(trade_narrow(trios), kept, swap_core(sent))
+    trios, kept, got, ffn_part = fence(trade_narrow(trios), kept, swap_core(sent), ffn_part)
     low, away = halved(kept, got)
     got = swap_step(away, 0)
 
@@ -661,7 +696,7 @@
         grid_spec=pltpu.PrefetchScalarGridSpec(
             num_scalar_prefetch=1,
             grid=(blocks,),
-            in_specs=[SMEM, SMEM, *[whole((share, 3 * cols))] * narrow, *[own_blk] * 3, part_blk, own_kent,
+            in_specs=[SMEM, *[whole((share, 3 * cols))] * narrow, *[own_blk] * 3, part_blk, own_kent,
                       own_col, own_row, own_col],
             out_specs=[*[part_blk] * 3, own_kent, whole((hn, hd, hd))],
             scratch_shapes=[pltpu.VMEM((BLOCK, cols), bf16)],
@@ -671,9 +706,10 @@
         compiler_params=PARAMS,
         cost_estimate=cost(5.4),
         name="mixer_query_back",
-    )(own, keep, ahead, *trios, q, k, v, ql, kent, gcol, grow, rise)
-
-    arrived, low, got = fence(pass_states(message.astype(bf16), coef_out), low, got)
+    )(own, coefs, *trios, q, k, v, ql, kent, gcol, grow, rise)
+
+    part_two = swap_narrow(ffn_part[2], 2)
+    arrived, low, got, part_two = fence(pass_states(message.astype(bf16), coef_out), low, got, part_two)
     low_ff, away_ff = halved(low, got)
 
     five = (wide // 2, 5, width // wide, cols)
@@ -699,17 +735,17 @@
         grid_spec=pltpu.PrefetchScalarGridSpec(
             num_scalar_prefetch=1,
             grid=(blocks,),
-            in_specs=[SMEM, SMEM, whole((hn, hd, hd)), whole((blocks, hn, hd, hd)), all_blk, part_blk,
+            in_specs=[SMEM, whole((hn, hd, hd)), whole((blocks, hn, hd, hd)), all_blk, part_blk,
                       own_blk, own_blk, *[part_blk] * 3, own_col, rows((BLOCK, 1), up), ANY, ANY],
             out_specs=[three, three, *[trio_spec] * narrow],
             scratch_shapes=[*[pltpu.VMEM((BLOCK, cols), bf16)] * 2, *[pltpu.VMEM((width, cols), f32)] * 3],
         ),
         out_shape=[*[sds(five, bf16)] * 2, *[trio_shape] * narrow],
-        input_output_aliases={14: 0, 15: 1},
+        input_output_aliases={13: 0, 14: 1},
         compiler_params=PARAMS,
         cost_estimate=cost(9),
         name="mixer_key_back",
-    )(own, leave, leave_other, arrived, direct, n1, dq, k, v, kl, gk, gv, tail, live, kept, sent)
+    )(own, coefs, arrived, direct, n1, dq, k, v, kl, gk, gv, tail, live, kept, sent)
 
     low, away = halved(kept, swap_core(sent))
     low, away, dqkv, away_ff = fence(low, away, dqkv, away_ff)
@@ -724,8 +760,12 @@
     ff_piece = [(low_ff + high_ff)[0]]
 
     for step in reversed(range(1, steps)):
+        ff_first = len(ff_piece)
         ff_piece = ff_piece + swap_all(ff_piece, step)
-    gate_piece, piece, ff_piece = fence(jnp.stack(gather_narrow(piece[3:])), piece[:3], ff_piece)
+    ff_more = swap_all(ff_piece[:ff_first], 0)
+    gate_piece, piece, ff_piece, ff_more = fence(
+        jnp.stack(gather_narrow(piece[3:])), piece[:3], ff_piece, ff_more
+    )
     chunks = width // across
     ffn_form = (tall, across), lambda t: (t // chunks, t % chunks), (ff, width)
     square_form = (width // wide, width), lambda t: (t, 0), (width, width)
@@ -733,7 +773,7 @@
     square_kernels = functools.partial(widen_square_kernel, 3, narrow)
 
     zs = gather_narrow(piece)
-    ff_piece = ff_piece + swap_all(ff_piece, 0)
+    ff_piece = ff_piece + ff_more + swap_all(ff_piece[ff_first:], 0)
     gate_piece = [gate_piece]
     for step in reversed(range(1, steps)):
         gate_piece = gate_piece + swap_all(gate_piece, step)
@@ -762,19 +802,23 @@
     square_piece = [square_piece]
     for step in reversed(range(1, steps)):
         square_piece = square_piece + swap_all(square_piece, step)
-    square_more = swap_all(square_piece[:half], 0)
-    ffn_out = widen(widen_ffn_kernel, own, 0, ff_piece, *ffn_form, [], 3, "widen_ffn")
-    gate_out = widen(gate_kernels, own, 0, gate_piece, *square_form, [], 2, "widen_gate")
-    square_piece, square_more, ffn_out, gate_out, gate_other, ff_other, ffn_part = fence(
-        square_piece, square_more, ffn_out, gate_out, swap_cores(gate_piece), swap_cores(ff_piece), ffn_part
+    square_piece = square_piece + swap_all(square_piece[:half], 0)
+    places = wide // 2
+    ffn_out = widen(widen_ffn_kernel, own, 0, 0, places, ff_piece, *ffn_form, [], 3, "widen_ffn")
+    gate_out = widen(gate_kernels, own, 0, 0, places, gate_piece, *square_form, [], 2, "widen_gate")
+    ff_other = swap_cores(ff_piece)
+    ffn_out = widen(widen_ffn_kernel, own, 1, 0, places, ff_other, *ffn_form, ffn_out, 3, "widen_ffn")
+    square_piece, ffn_out, gate_out, gate_other, ffn_part = fence(
+        square_piece, ffn_out, gate_out, swap_cores(gate_piece), ffn_part
     )
 
-    ffn_part = trade_narrow(ffn_part)
-    square_last = swap_all(square_piece[half:], 0)
-    ffn_out = widen(widen_ffn_kernel, own, 1, ff_other, *ffn_form, ffn_out, 3, "widen_ffn")
-    gate_out = widen(gate_kernels, own, 1, gate_other, *square_form, gate_out, 2, "widen_gate")
-    square_piece, ffn_out, gate_out, ffn_part = fence(
-        square_piece + square_more + square_last, ffn_out, gate_out, ffn_part
+    part_three, part_one = swap_narrow(ffn_part[3], 3), swap_narrow(ffn_part[1], 1)
+    square_last = swap_all(square_piece[half : places // 2], 0)
+    done = len(square_piece)
+    gate_out = widen(gate_kernels, own, 1, 0, places, gate_other, *square_form, gate_out, 2, "widen_gate")
+    mixer = widen(square_kernels, own, 0, 0, places, square_piece, *square_form, [], 3, "widen_square")
+    square_last, gate_out, mixer, square_piece, part_three, part_one = fence(
+        square_last, gate_out, mixer, square_piece, part_three, part_one
     )
 
     output = pl.pallas_call(
@@ -783,10 +827,10 @@
         compiler_params=pltpu.CompilerParams(vmem_limit_bytes=56 << 20),
         cost_estimate=cost(2),
         name="output",
-    )(*ffn_part, hidden)
-    mixer = widen(square_kernels, own, 0, square_piece, *square_form, [], 3, "widen_square")
-    square_other = swap_cores(square_piece)
-    mixer = widen(square_kernels, own, 1, square_other, *square_form, mixer, 3, "widen_square")
+    )(ffn_part[0], part_one, part_two, part_three, hidden)
+    mixer = widen(square_kernels, own, 0, done, places, square_last, *square_form, mixer, 3, "widen_last")
+    square_other = swap_cores(square_piece + square_last)
+    mixer = widen(square_kernels, own, 1, 0, places, square_other, *square_form, mixer, 3, "widen_square")
     grad_first, grad_second, grad_third = ffn_out
     grad_gate, grad_out = gate_out
     return (output, grad_tokens, *mixer, grad_gate, grad_out, grad_first.T, grad_second.T, grad_third)

time: 319 us -> 301 us (0.944)
  local copies, waits for them, and re-layouts: 13.2 us -> 5.59 us
  waiting for transfers between devices: 89.2 us -> 81.9 us
  other arithmetic: 10.6 us -> 4.56 us
  Pallas kernels: 116 us -> 122 us
    ppermute x27, waiting for transfers between devices: 64 us -> 54.1 us  [swap_narrow(): return lax.ppermute(values, 'narrow', [(i, i ^ k) for i in range(size)])]
    select_n x4 -> x0, other arithmetic: 3.82 us -> none  [slots(): jnp.where(own_narrow // per == 0, jnp.stack([first, second]), jnp.stack([...]
    pallas_call x1 -> x2, Pallas kernels: 10.1 us -> 13.3 us  [the longest x1 9.42 us: body(): pl.pallas_call(functools.partial(ffn_kernel, share), out_shape=[*[sds((lo...]
    pallas_call x6 -> x7, Pallas kernels: 30 us -> 32.5 us  [widen(): pl.pallas_call(functools.partial(kernel, places), grid_spec=pltpu.Prefetc...]
  transfers between devices with their start and end apart: 57 -> 57, of which waited for: 20 -> 18; matrix products, arithmetic and copies ran while one was open for 6% -> 2% of each run, Pallas kernels for 24% -> 28%
where the time goes in v4:
time: 301 us; the launch traced here: 300 us
  Pallas kernels  122 us (41%)
  waiting for transfers between devices  81.9 us (27%)
  starting transfers between devices  63.3 us (21%)
  blocking collectives  19.8 us (7%)
  local copies, waits for them, and re-layouts  5.59 us (2%)
  other arithmetic  4.56 us (2%)
    ppermute x27, waiting for transfers between devices, swap_narrow(): return lax.ppermute(values, 'narrow', [(i, i ^ k) for i in range(size)])  54.1 us
    ppermute x27, starting transfers between devices, swap_narrow(): return lax.ppermute(values, 'narrow', [(i, i ^ k) for i in range(size)])  45.2 us
    pallas_call x7, Pallas kernels, widen(): pl.pallas_call(functools.partial(kernel, places), grid_spec=pltpu.Prefetc...  32.5 us
    ppermute x13, waiting for transfers between devices, swap_step(): return lax.ppermute(values, 'wide', [(i, flip(i)) for i in range(size)])  22.2 us
    pallas_call x2, Pallas kernels, body(): pl.pallas_call(functools.partial(forward_kernel, hn, hd, share), grid_spe...  20.7 us
    all_gather x2, blocking collectives, pass_states(): gathered = lax.all_gather(message, 'wide', axis=0)  19.8 us
    ppermute x13, starting transfers between devices, swap_step(): return lax.ppermute(values, 'wide', [(i, flip(i)) for i in range(size)])  11.6 us
    pallas_call x1, Pallas kernels, body(): pl.pallas_call(functools.partial(ffn_grad_kernel, wide, share), grid_spec...  10.2 us
  transfers between devices with their start and end apart: 57, of which 18 were waited for; matrix products, arithmetic and copies ran while one was open for 2% of the time, Pallas kernels for 28%

profile of v4, /device:TPU:0, one launch (start us, length us, event | category | flops | bytes accessed | tf_op | source)
XLA Modules:
  0.0 299.7 jit_solution(17325999649428925008)
XLA Ops:
  0.6 4.1 %collective-permute-start.1 = (bf16[128,1024]{1,0:T(8,128)(2,1)}, bf16[128,1024]{1,0:T(8,128)(2,1)S(1)}, u32[]{:S(2)}, u32[]{:S(2)}) collective-permute-start(bf16[128,1024]{1,0:T(8,128)(2,1)} %refs_9_.1), channel_id=1, source_target_pairs={{0,2},{1,3},{2,0},{3,1},{4,6},{5,7},{6,4},{7,5},{8,10},{9,11},{10,... | collective-permute-start | bytes 786440 | tf_op jit(solution)/shard_map/ppermute | solution.py:422
  8.3 3.9 %layout.1 = (f32[4,512,2]{2,1,0:T(8,128)}, f32[4,512,2]{2,1,0:T(8,128)}, f32[4,512,2]{2,1,0:T(8,128)}, f32[8,2,256]{2,1,0:T(2,128)}, f32[512,1]{1,0:T(8,128)}, /*index=5*/f32[5,2,8]{2,1,0:T(2,128)}, f32[1,8]{1,0:T(1,128)}) custom-call(s32[2]{0:T(128)} %pad_add_fusion.own, s32[1]{0:T(128)S(6)} %copy.75.lengths, s32[1]{0:T(128)S(6)} %copy.76.pads, ...), custom_call_target="tpu_custom_call" | custom-call | bytes 9600000 | tf_op jit(solution)/shard_map/layout/pallas_call | solution.py:558
  12.9 4.5 %collective-permute-done.tok_b = bf16[128,1024]{1,0:T(8,128)(2,1)S(1)} collective-permute-done((bf16[128,1024]{1,0:T(8,128)(2,1)}, bf16[128,1024]{1,0:T(8,128)(2,1)S(1)}, u32[]{:S(2)}, u32[]{:S(2)}) %collective-permute-start) | collective-permute-done | bytes 262176 | tf_op jit(solution)/shard_map/ppermute | solution.py:422
  18.2 10.4 %mixer_forward_0.1 = (bf16[512,1024]{1,0:T(8,128)(2,1)}, bf16[512,1024]{1,0:T(8,128)(2,1)}, f32[512,256]{1,0:T(8,128)}, f32[512,256]{1,0:T(8,128)}, bf16[512,102...) custom-call(s32[2]{0:T(128)} %pad_add_fusion.own, ...), custom_call_target="tpu_custom_call" | custom-call | bytes 32000000 | tf_op jit(solution)/shard_map/mixer_forward_0/pallas_call | solution.py:583
  30.0 2.5 collective-permute-start.7
  33.1 10.4 %mixer_forward_1.1 = (bf16[512,1024]{1,0:T(8,128)(2,1)}, bf16[512,1024]{1,0:T(8,128)(2,1)}, f32[512,256]{1,0:T(8,128)}, f32[512,256]{1,0:T(8,128)}, bf16[512,102...) custom-call(s32[2]{0:T(128)} %pad_add_fusion.own, ...), custom_call_target="tpu_custom_call", output_to_operand_aliasing={{0}: (11, {}), {1}: (12, {}), {2}: (13, {}), {3}: (14, {}),... | custom-call | bytes 32000000 | tf_op jit(solution)/shard_map/mixer_forward_1/pallas_call | solution.py:583
  48.7 10.0 %all-gather = bf16[16,128,128]{2,1,0:T(8,128)(2,1)S(1)} all-gather(bf16[2,128,128]{2,1,0:T(8,128)(2,1)S(1)} %multiply_reduce_fusion), channel_id=2, replica_groups=mesh['wide'=8,'narrow'=4] {'wide'}, dimensions={0}, use_global_device_ids=true | all-gather | bytes 589824 | tf_op jit(solution)/shard_map/all_gather | solution.py:541
  64.0 2.4 collective-permute-done.11.refs_3_
  66.3 2.6 collective-permute-done.10.refs_2_
  69.6 9.8 %mixer_out.1 = (bf16[512,1024]{1,0:T(8,128)(2,1)}, f32[512,1]{1,0:T(8,128)}, bf16[512,1024]{1,0:T(8,128)(2,1)}, f32[128,1024]{1,0:T(8,128)}, bf16[512,1024]{1,0:...) custom-call(s32[2]{0:T(128)} %pad_add_fusion.own, f32[5,2,8]{2,1,0:T(2,128)} %get-tuple-element.202.coefs, ...), custom_call_target="tpu_custom_call" | custom-call | bytes 30400000 | tf_op jit(solution)/shard_map/mixer_out/pallas_call | solution.py:617
  79.4 9.4 %ffn.1 = (bf16[512,704]{1,0:T(8,128)(2,1)}, bf16[512,704]{1,0:T(8,128)(2,1)}, bf16[512,704]{1,0:T(8,128)(2,1)}, bf16[128,1024]{1,0:T(8,128)(2,1)}, bf16[128,1024...) custom-call(bf16[512,1024]{1,0:T(8,128)(2,1)} %get-tuple-element.239.n2, ...), custom_call_target="tpu_custom_call" | custom-call | bytes 32000000 | tf_op jit(solution)/shard_map/ffn/pallas_call | solution.py:638
  90.7 2.5 collective-permute-start.14
  93.2 8.3 %collective-permute-done.12.refs_1_ = bf16[128,1024]{1,0:T(8,128)(2,1)S(1)} collective-permute-done((bf16[128,1024]{1,0:T(8,128)(2,1)}, bf16[128,1024]{1,0:T(8,128)(2,1)S(1)}, u32[]{:S(2)}, u32[]{:S(2)}) %collective-permute-start.12) | collective-permute-done | bytes 262176 | tf_op jit(solution)/shard_map/ppermute | solution.py:422
  101.6 10.2 %ffn_grads.1 = (bf16[4,3,704,128]{3,2,1,0:T(8,128)(2,1)}, bf16[4,3,704,128]{3,2,1,0:T(8,128)(2,1)}, bf16[128,1024]{1,0:T(8,128)(2,1)}, bf16[128,1024]{1,0:T(8,12...) custom-call(s32[2]{0:T(128)} %pad_add_fusion.own, bf16[512,1024]{1,0:T(8,128)(2,1)} %get-tuple-element.239.n2, ...), custom_call_target="tpu_custom_call" | custom-call | bytes 32000000 | tf_op jit(solution)/shard_map/ffn_grads/pallas_call | solution.py:651
  112.6 6.3 %residual_back.1 = (f32[128,1024]{1,0:T(8,128)}, bf16[128,1024]{1,0:T(8,128)(2,1)}, bf16[128,768]{1,0:T(8,128)(2,1)}, bf16[128,768]{1,0:T(8,128)(2,1)}, bf16[128...) custom-call(s32[2]{0:T(128)} %pad_add_fusion.own, bf16[128,1024]{1,0:T(8,128)(2,1)} %get-tuple-element.254.refs_0_, ...), custom_call_target="tpu_custom_call" | custom-call | bytes 16000000 | tf_op jit(solution)/shard_map/residual_back/pallas_call | solution.py:673
  118.9 3.6 %collective-permute-start.15 = (bf16[128,768]{1,0:T(8,128)(2,1)}, bf16[128,768]{1,0:T(8,128)(2,1)S(1)}, u32[]{:S(2)}, u32[]{:S(2)}) collective-permute-start(bf16[128,768]{1,0:T(8,128)(2,1)} %get-tuple-element.268), channel_id=1, source_target_pairs={{0,1},{1,0},{2,3},{3,2},{4,5},{5,4},{6,7},{7,6},{8,9},{9,8},{10,11... | collective-permute-start | bytes 589832 | tf_op jit(solution)/shard_map/ppermute | solution.py:422
  122.5 2.4 collective-permute-start.17
  124.9 6.4 %collective-permute-done.15.refs_1_ = bf16[128,768]{1,0:T(8,128)(2,1)S(1)} collective-permute-done((bf16[128,768]{1,0:T(8,128)(2,1)}, bf16[128,768]{1,0:T(8,128)(2,1)S(1)}, u32[]{:S(2)}, u32[]{:S(2)}) %collective-permute-start.15) | collective-permute-done | bytes 196640 | tf_op jit(solution)/shard_map/ppermute | solution.py:422
  131.3 8.6 %collective-permute-done.16.refs_2_ = bf16[128,768]{1,0:T(8,128)(2,1)S(1)} collective-permute-done((bf16[128,768]{1,0:T(8,128)(2,1)}, bf16[128,768]{1,0:T(8,128)(2,1)S(1)}, u32[]{:S(2)}, u32[]{:S(2)}) %collective-permute-start.16) | collective-permute-done | bytes 196640 | tf_op jit(solution)/shard_map/ppermute | solution.py:422
  141.1 3.9 %collective-permute-start.20 = (bf16[128,1024]{1,0:T(8,128)(2,1)}, bf16[128,1024]{1,0:T(8,128)(2,1)S(1)}, u32[]{:S(2)}, u32[]{:S(2)}) collective-permute-start(bf16[128,1024]{1,0:T(8,128)(2,1)} %get-tuple-element.288), channel_id=1, source_target_pairs={{0,2},{1,3},{2,0},{3,1},{4,6},{5,7},{6,4},{7,5},{8,10},{9,11},{10,... | collective-permute-start | bytes 786440 | tf_op jit(solution)/shard_map/ppermute | solution.py:422
  145.1 5.6 %mixer_query_back.1 = (bf16[512,256]{1,0:T(8,128)(2,1)}, f32[512,256]{1,0:T(8,128)}, f32[512,256]{1,0:T(8,128)}, f32[2,2,128,128]{3,2,1,0:T(8,128)}, f32[2,128,128]{2,1,0:T(8,128)}) custom-call(s32[2]{0:T(128)} %pad_add_fusion.own, f32[5,2,8]{2,1,0:T(2,128)} %get-tuple-element.202.coefs, bf16[128,768]{1,0:T(8,128)(2,1)} %get-tuple-element.277.refs_0_, ...), custom_call_target="tpu_custom_call" | custom-call | bytes 17280000 | tf_op jit(solution)/shard_map/mixer_query_back/pallas_call | solution.py:694
  151.6 4.8 %gate_back.1 = (bf16[4,5,128,256]{3,2,1,0:T(8,128)(2,1)}, bf16[4,5,128,256]{3,2,1,0:T(8,128)(2,1)}) custom-call(s32[2]{0:T(128)} %pad_add_fusion.own, bf16[128,768]{1,0:T(8,128)(2,1)} %get-tuple-element.277.refs_0_, bf16[128,768]{1,0:T(8,128)(2,1)} %copy-done.12, bf16[128,768]{1,0:T(8,128)(2,1)} %copy-done.13, bf16[128,768]{1,0:T(8,128)(2,1)} %copy-done.14, ...), custom_call_target="tpu_custom_call" | custom-call | bytes 16000000 | tf_op jit(solution)/shard_map/gate_back/pallas_call | solution.py:717
  156.4 9.8 %all-gather.1 = bf16[16,128,128]{2,1,0:T(8,128)(2,1)S(1)} all-gather(bf16[2,128,128]{2,1,0:T(8,128)(2,1)S(1)} %convert_element_type.29), channel_id=3, replica_groups=mesh['wide'=8,'narrow'=4] {'wide'}, dimensions={0}, use_global_device_ids=true | all-gather | bytes 589824 | tf_op jit(solution)/shard_map/all_gather | solution.py:541
  167.0 7.6 %mixer_key_back.1 = (bf16[4,5,128,256]{3,2,1,0:T(8,128)(2,1)}, bf16[4,5,128,256]{3,2,1,0:T(8,128)(2,1)}, bf16[128,768]{1,0:T(8,128)(2,1)}, bf16[128,768]{1,0:T(8...) custom-call(s32[2]{0:T(128)} %pad_add_fusion.own, ...), custom_call_target="tpu_custom_call", output_to_operand_aliasing={{0}: (13, {}), {1}: (14, {})} | custom-call | bytes 28800000 | tf_op jit(solution)/shard_map/mixer_key_back/pallas_call | solution.py:733
  175.2 2.8 collective-permute-done.21
  180.2 2.9 collective-permute-start.24
  184.6 5.7 %collective-permute-done.23.refs_1_ = bf16[128,768]{1,0:T(8,128)(2,1)S(1)} collective-permute-done((bf16[128,768]{1,0:T(8,128)(2,1)S(1)}, bf16[128,768]{1,0:T(8,128)(2,1)S(1)}, u32[]{:S(2)}, u32[]{:S(2)}) %collective-permute-start.23) | collective-permute-done | bytes 196640 | tf_op jit(solution)/shard_map/ppermute | solution.py:422
  190.3 7.1 %collective-permute-done.24.refs_2_ = bf16[128,768]{1,0:T(8,128)(2,1)S(1)} collective-permute-done((bf16[128,768]{1,0:T(8,128)(2,1)S(1)}, bf16[128,768]{1,0:T(8,128)(2,1)S(1)}, u32[]{:S(2)}, u32[]{:S(2)}) %collective-permute-start.24) | collective-permute-done | bytes 196640 | tf_op jit(solution)/shard_map/ppermute | solution.py:422
  200.2 7.3 %collective-permute-done.27 = bf16[1,5,128,256]{3,2,1,0:T(8,128)(2,1)S(1)} collective-permute-done((bf16[1,5,128,256]{3,2,1,0:T(8,128)(2,1)S(1)}, bf16[1,5,128,256]{3,2,1,0:T(8,128)(2,1)S(1)}, u32[]{:S(2)}, u32[]{:S(2)}) %collective-permute-start.27) | collective-permute-done | bytes 327712 | tf_op jit(solution)/shard_map/ppermute | solution.py:442
  207.7 2.6 collective-permute-start.30
  210.2 3.1 %collective-permute-start.29 = (bf16[2,128,256]{2,1,0:T(8,128)(2,1)S(1)}, bf16[2,128,256]{2,1,0:T(8,128)(2,1)S(1)}, u32[]{:S(2)}, u32[]{:S(2)}) collective-permute-start(bf16[2,128,256]{2,1,0:T(8,128)(2,1)S(1)} %get-tuple-element.401), channel_id=1, source_target_pairs={{0,2},{1,3},{2,0},{3,1},{4,6},{5,7},{6,4},{7,5},{8,10},{9,11},{10,... | collective-permute-start | bytes 393224 | tf_op jit(solution)/shard_map/ppermute | solution.py:422
  213.4 2.3 collective-permute-done.30
  215.7 3.9 %collective-permute-done.29 = bf16[2,128,256]{2,1,0:T(8,128)(2,1)S(1)} collective-permute-done((bf16[2,128,256]{2,1,0:T(8,128)(2,1)S(1)}, bf16[2,128,256]{2,1,0:T(8,128)(2,1)S(1)}, u32[]{:S(2)}, u32[]{:S(2)}) %collective-permute-start.29) | collective-permute-done | bytes 131104 | tf_op jit(solution)/shard_map/ppermute | solution.py:422
  220.0 1.9 collective-permute-start.39
  222.5 12.1 %collective-permute-done.36.refs_1_ = bf16[4,2,128,256]{3,2,1,0:T(8,128)(2,1)S(1)} collective-permute-done((bf16[4,2,128,256]{3,2,1,0:T(8,128)(2,1)S(1)}, bf16[4,2,128,256]{3,2,1,0:T(8,128)(2,1)S(1)}, u32[]{:S(2)}, u32[]{:S(2)}) %collective-permute-start.36) | collective-permute-done | bytes 524320 | tf_op jit(solution)/shard_map/ppermute | solution.py:442
  234.8 2.8 collective-permute-start.35
  237.6 8.8 %tokens_back.1 = f32[128,1024]{1,0:T(8,128)} custom-call(s32[2]{0:T(128)} %pad_add_fusion.own, bf16[128,768]{1,0:T(8,128)(2,1)} %get-tuple-element.329.refs_0_, bf16[128,768]{1,0:T(8,128)(2,1)} %copy-done.41, bf16[128,768]{1,0:T(8,128)(2,1)} %copy-done.42, bf16[128,768]{1,0:T(8,128)(2,1)} %copy-done.43, bf16[128,1024]{1,0:T(8,128)(2,1)} %get-tuple-element.333.refs_4_, ...), custom_call_target="tpu_custom_call" | custom-call | bytes 25600000 | tf_op jit(solution)/shard_map/tokens_back/pallas_call | solution.py:783
  252.5 4.7 %widen_gate_0.1 = (f32[1024,1024]{1,0:T(8,128)}, f32[1024,1024]{1,0:T(8,128)}) custom-call(s32[2]{0:T(128)} %pad_add_fusion.own, bf16[4,2,128,256]{3,2,1,0:T(8,128)(2,1)} %copy-done.6, bf16[4,2,128,256]{3,2,1,0:T(8,128)(2,1)} %copy-done.25, bf16[4,2,128,256]{3,2,1,0:T(8,128)(2,1)} %copy-done.26, bf16[4,2,128,256]{3,2,1,0:T(8,128)(2,1)} %copy-done.27), custom_call_target="tpu_custom_call" | custom-call | bytes 12800000 | tf_op jit(solution)/shard_map/widen_gate_0/pallas_call | solution.py:492
  257.2 4.8 %widen_ffn_0.1 = (f32[704,1024]{1,0:T(8,128)}, f32[704,1024]{1,0:T(8,128)}, f32[704,1024]{1,0:T(8,128)}) custom-call(s32[2]{0:T(128)} %pad_add_fusion.own, bf16[3,704,128]{2,1,0:T(8,128)(2,1)} %copy-done.5, bf16[3,704,128]{2,1,0:T(8,128)(2,1)} %copy-done.19, bf16[3,704,128]{2,1,0:T(8,128)(2,1)} %copy-done.18, bf16[3,704,128]{2,1,0:T(8,128)(2,1)} %copy-done.20), custom_call_target="tpu_custom_call" | custom-call | bytes 12800000 | tf_op jit(solution)/shard_map/widen_ffn_0/pallas_call | solution.py:492
  262.0 4.9 %widen_ffn_1.1 = (f32[704,1024]{1,0:T(8,128)}, f32[704,1024]{1,0:T(8,128)}, f32[704,1024]{1,0:T(8,128)}) custom-call(s32[2]{0:T(128)} %pad_add_fusion.own, bf16[3,704,128]{2,1,0:T(8,128)(2,1)} %copy-done.21, bf16[3,704,128]{2,1,0:T(8,128)(2,1)} %copy-done.22, ...), custom_call_target="tpu_custom_call", output_to_operand_aliasing={{0}: (5, {}), {1}: (6, {}), {2}: (7, {})} | custom-call | bytes 12800000 | tf_op jit(solution)/shard_map/widen_ffn_1/pallas_call | solution.py:492
  267.0 2.7 collective-permute-done.41.refs_2_
  271.2 2.5 collective-permute-start.51
  274.4 4.8 %widen_square_0.1 = (f32[1024,1024]{1,0:T(8,128)}, f32[1024,1024]{1,0:T(8,128)}, f32[1024,1024]{1,0:T(8,128)}) custom-call(s32[2]{0:T(128)} %pad_add_fusion.own, bf16[4,3,128,256]{3,2,1,0:T(8,128)(2,1)} %copy-done.2, bf16[4,3,128,256]{3,2,1,0:T(8,128)(2,1)} %collective-permute-done.40.refs_1_, bf16[4,3,128,256]{3,2,1,0:T(8,128)(2,1)} %copy-done.15), custom_call_target="tpu_custom_call" | custom-call | bytes 12800000 | tf_op jit(solution)/shard_map/widen_square_0/pallas_call | solution.py:492
  279.2 4.8 %widen_gate_1.1 = (f32[1024,1024]{1,0:T(8,128)}, f32[1024,1024]{1,0:T(8,128)}) custom-call(s32[2]{0:T(128)} %pad_add_fusion.own, bf16[4,2,128,256]{3,2,1,0:T(8,128)(2,1)} %collective-permute-done.46.refs_0_, bf16[4,2,128,256]{3,2,1,0:T(8,128)(2,1)} %copy-done.28, bf16[4,2,128,256]{3,2,1,0:T(8,128)(2,1)} %copy-done.29, ...), custom_call_target="tpu_custom_call", output_to_operand_aliasing={{0}: (5, {}), {1}: (6, {})} | custom-call | bytes 12800000 | tf_op jit(solution)/shard_map/widen_gate_1/pallas_call | solution.py:492
  284.1 2.1 collective-permute-done.52.refs_1_
  287.3 3.0 widen_last_0.1
  290.2 2.2 output.1
  294.1 5.6 %widen_square_1.1 = (f32[1024,1024]{1,0:T(8,128)}, f32[1024,1024]{1,0:T(8,128)}, f32[1024,1024]{1,0:T(8,128)}) custom-call(s32[2]{0:T(128)} %pad_add_fusion.own, bf16[4,3,128,256]{3,2,1,0:T(8,128)(2,1)} %copy-done.8, bf16[4,3,128,256]{3,2,1,0:T(8,128)(2,1)} %copy-done.9, ...), custom_call_target="tpu_custom_call", output_to_operand_aliasing={{0}: (5, {}), {1}: (6, {}), {2}: (7, {})} | custom-call | bytes 12800000 | tf_op jit(solution)/shard_map/widen_square_1/pallas_call | solution.py:492
  (233 shorter events, 41.7 us)
Async XLA Ops:
  0.6 27.9 %collective-permute-start.1 = (bf16[128,1024]{1,0:T(8,128)(2,1)}, bf16[128,1024]{1,0:T(8,128)(2,1)S(1)}, u32[]{:S(2)}, u32[]{:S(2)}) collective-permute-start(bf16[128,1024]{1,0:T(8,128)(2,1)} %refs_9_.1), channel_id=1, source_target_pairs={{0,2},{1,3},{2,0},{3,1},{4,6},{5,7},{6,4},{7,5},{8,10},{9,11},{10,... | collective-permute-start | bytes 786440 | tf_op jit(solution)/shard_map/ppermute | solution.py:422
  4.8 12.7 %collective-permute-start = (bf16[128,1024]{1,0:T(8,128)(2,1)}, bf16[128,1024]{1,0:T(8,128)(2,1)S(1)}, u32[]{:S(2)}, u32[]{:S(2)}) collective-permute-start(bf16[128,1024]{1,0:T(8,128)(2,1)} %refs_9_.1), channel_id=1, source_target_pairs={{0,1},{1,0},{2,3},{3,2},{4,5},{5,4},{6,7},{7,6},{8,9},{9,8},{10,11... | collective-permute-start | bytes 786440 | tf_op jit(solution)/shard_map/ppermute | solution.py:422
  6.3 22.2 %collective-permute-start.2 = (bf16[128,1024]{1,0:T(8,128)(2,1)}, bf16[128,1024]{1,0:T(8,128)(2,1)S(1)}, u32[]{:S(2)}, u32[]{:S(2)}) collective-permute-start(bf16[128,1024]{1,0:T(8,128)(2,1)} %refs_9_.1), channel_id=1, source_target_pairs={{0,3},{1,2},{2,1},{3,0},{4,7},{5,6},{6,5},{7,4},{8,11},{9,10},{10,... | collective-permute-start | bytes 786440 | tf_op jit(solution)/shard_map/ppermute | solution.py:422
  28.6 30.8 %collective-permute-start.8 = (bf16[128,1024]{1,0:T(8,128)(2,1)S(1)}, bf16[128,1024]{1,0:T(8,128)(2,1)S(1)}, u32[]{:S(2)}, u32[]{:S(2)}) collective-permute-start(bf16[128,1024]{1,0:T(8,128)(2,1)S(1)} %copy-done.7), channel_id=1, source_target_pairs={{0,3},{1,2},{2,1},{3,0},{4,7},{5,6},{6,5},{7,4},{8,11},{9,10},{10,... | collective-permute-start | bytes 786440 | tf_op jit(solution)/shard_map/ppermute | solution.py:422
  30.0 29.4 %collective-permute-start.7 = (bf16[128,1024]{1,0:T(8,128)(2,1)S(1)}, bf16[128,1024]{1,0:T(8,128)(2,1)S(1)}, u32[]{:S(2)}, u32[]{:S(2)}) collective-permute-start(bf16[128,1024]{1,0:T(8,128)(2,1)S(1)} %copy-done.7), channel_id=1, source_target_pairs={{0,2},{1,3},{2,0},{3,1},{4,6},{5,7},{6,4},{7,5},{8,10},{9,11},{10,... | collective-permute-start | bytes 786440 | tf_op jit(solution)/shard_map/ppermute | solution.py:422
  32.5 26.9 %collective-permute-start.6 = (bf16[128,1024]{1,0:T(8,128)(2,1)S(1)}, bf16[128,1024]{1,0:T(8,128)(2,1)S(1)}, u32[]{:S(2)}, u32[]{:S(2)}) collective-permute-start(bf16[128,1024]{1,0:T(8,128)(2,1)S(1)} %copy-done.7), channel_id=1, source_target_pairs={{0,1},{1,0},{2,3},{3,2},{4,5},{5,4},{6,7},{7,6},{8,9},{9,8},{10,11... | collective-permute-start | bytes 786440 | tf_op jit(solution)/shard_map/ppermute | solution.py:422
  33.0 10.4 %collective-permute-start.3 = (f32[1,8]{1,0:T(1,128)S(1)}, f32[1,8]{1,0:T(1,128)S(1)}, u32[]{:S(2)}, u32[]{:S(2)}) collective-permute-start(f32[1,8]{1,0:T(1,128)S(1)} %copy-done.47), channel_id=1, source_target_pairs={{0,4},{4,0},{8,12},{12,8},{16,20},{20,16},{24,28},{28,24},{1,5},{5... | collective-permute-start | bytes 104 | tf_op jit(solution)/shard_map/ppermute | solution.py:523
  47.1 11.6 %collective-permute-start.5 = (f32[4,8]{1,0:T(4,128)S(1)}, f32[4,8]{1,0:T(4,128)S(1)}, u32[]{:S(2)}, u32[]{:S(2)}) collective-permute-start(f32[4,8]{1,0:T(4,128)S(1)} %pad_maximum_fusion.3), channel_id=1, source_target_pairs={{0,16},{4,20},{8,24},{12,28},{16,0},{20,4},{24,8},{28,12},{1,17},{... | collective-permute-start | bytes 392 | tf_op jit(solution)/shard_map/ppermute | solution.py:523
  59.4 6.9 %collective-permute-start.11 = (bf16[2,128,128]{2,1,0:T(8,128)(2,1)S(1)}, bf16[2,128,128]{2,1,0:T(8,128)(2,1)S(1)}, u32[]{:S(2)}, u32[]{:S(2)}) collective-permute-start(bf16[2,128,128]{2,1,0:T(8,128)(2,1)S(1)} %fusion.1.refs_0_), channel_id=1, source_target_pairs={{0,3},{1,2},{2,1},{3,0},{4,7},{5,6},{6,5},{7,4},{8,11},{9,10},{10,... | collective-permute-start | bytes 196616 | tf_op jit(solution)/shard_map/ppermute | solution.py:422
  60.8 8.2 %collective-permute-start.10 = (bf16[2,128,128]{2,1,0:T(8,128)(2,1)S(1)}, bf16[2,128,128]{2,1,0:T(8,128)(2,1)S(1)}, u32[]{:S(2)}, u32[]{:S(2)}) collective-permute-start(bf16[2,128,128]{2,1,0:T(8,128)(2,1)S(1)} %fusion.1.refs_0_), channel_id=1, source_target_pairs={{0,2},{1,3},{2,0},{3,1},{4,6},{5,7},{6,4},{7,5},{8,10},{9,11},{10,... | collective-permute-start | bytes 196616 | tf_op jit(solution)/shard_map/ppermute | solution.py:422
  62.4 6.5 %collective-permute-start.9 = (bf16[2,128,128]{2,1,0:T(8,128)(2,1)S(1)}, bf16[2,128,128]{2,1,0:T(8,128)(2,1)S(1)}, u32[]{:S(2)}, u32[]{:S(2)}) collective-permute-start(bf16[2,128,128]{2,1,0:T(8,128)(2,1)S(1)} %fusion.1.refs_0_), channel_id=1, source_target_pairs={{0,1},{1,0},{2,3},{3,2},{4,5},{5,4},{6,7},{7,6},{8,9},{9,8},{10,11... | collective-permute-start | bytes 196616 | tf_op jit(solution)/shard_map/ppermute | solution.py:422
  88.8 12.7 %collective-permute-start.12 = (bf16[128,1024]{1,0:T(8,128)(2,1)}, bf16[128,1024]{1,0:T(8,128)(2,1)S(1)}, u32[]{:S(2)}, u32[]{:S(2)}) collective-permute-start(bf16[128,1024]{1,0:T(8,128)(2,1)} %get-tuple-element.245), channel_id=1, source_target_pairs={{0,1},{1,0},{2,3},{3,2},{4,5},{5,4},{6,7},{7,6},{8,9},{9,8},{10,11... | collective-permute-start | bytes 786440 | tf_op jit(solution)/shard_map/ppermute | solution.py:422
  88.8 22.9 %collective-permute-start.13 = (bf16[128,1024]{1,0:T(8,128)(2,1)}, bf16[128,1024]{1,0:T(8,128)(2,1)S(1)}, u32[]{:S(2)}, u32[]{:S(2)}) collective-permute-start(bf16[128,1024]{1,0:T(8,128)(2,1)} %get-tuple-element.246), channel_id=1, source_target_pairs={{0,2},{1,3},{2,0},{3,1},{4,6},{5,7},{6,4},{7,5},{8,10},{9,11},{10,... | collective-permute-start | bytes 786440 | tf_op jit(solution)/shard_map/ppermute | solution.py:422
  90.7 21.1 %collective-permute-start.14 = (bf16[128,1024]{1,0:T(8,128)(2,1)}, bf16[128,1024]{1,0:T(8,128)(2,1)S(1)}, u32[]{:S(2)}, u32[]{:S(2)}) collective-permute-start(bf16[128,1024]{1,0:T(8,128)(2,1)} %get-tuple-element.247), channel_id=1, source_target_pairs={{0,3},{1,2},{2,1},{3,0},{4,7},{5,6},{6,5},{7,4},{8,11},{9,10},{10,... | collective-permute-start | bytes 786440 | tf_op jit(solution)/shard_map/ppermute | solution.py:422
  118.8 21.0 %collective-permute-start.18 = (bf16[4,3,704,128]{3,2,1,0:T(8,128)(2,1)S(1)}, bf16[4,3,704,128]{3,2,1,0:T(8,128)(2,1)S(1)}, u32[]{:S(2)}, u32[]{:S(2)}) collective-permute-start(bf16[4,3,704,128]{3,2,1,0:T(8,128)(2,1)S(1)} %copy-done.48), channel_id=1, source_target_pairs={{0,4},{4,0},{8,12},{12,8},{16,20},{20,16},{24,28},{28,24},{1,5},{5... | collective-permute-start | bytes 6488072 | tf_op jit(solution)/shard_map/ppermute | solution.py:435
  118.9 12.3 %collective-permute-start.15 = (bf16[128,768]{1,0:T(8,128)(2,1)}, bf16[128,768]{1,0:T(8,128)(2,1)S(1)}, u32[]{:S(2)}, u32[]{:S(2)}) collective-permute-start(bf16[128,768]{1,0:T(8,128)(2,1)} %get-tuple-element.268), channel_id=1, source_target_pairs={{0,1},{1,0},{2,3},{3,2},{4,5},{5,4},{6,7},{7,6},{8,9},{9,8},{10,11... | collective-permute-start | bytes 589832 | tf_op jit(solution)/shard_map/ppermute | solution.py:422
  122.5 17.4 %collective-permute-start.16 = (bf16[128,768]{1,0:T(8,128)(2,1)}, bf16[128,768]{1,0:T(8,128)(2,1)S(1)}, u32[]{:S(2)}, u32[]{:S(2)}) collective-permute-start(bf16[128,768]{1,0:T(8,128)(2,1)} %get-tuple-element.269), channel_id=1, source_target_pairs={{0,2},{1,3},{2,0},{3,1},{4,6},{5,7},{6,4},{7,5},{8,10},{9,11},{10,... | collective-permute-start | bytes 589832 | tf_op jit(solution)/shard_map/ppermute | solution.py:422
  122.5 17.3 %collective-permute-start.17 = (bf16[128,768]{1,0:T(8,128)(2,1)}, bf16[128,768]{1,0:T(8,128)(2,1)S(1)}, u32[]{:S(2)}, u32[]{:S(2)}) collective-permute-start(bf16[128,768]{1,0:T(8,128)(2,1)} %get-tuple-element.270), channel_id=1, source_target_pairs={{0,3},{1,2},{2,1},{3,0},{4,7},{5,6},{6,5},{7,4},{8,11},{9,10},{10,... | collective-permute-start | bytes 589832 | tf_op jit(solution)/shard_map/ppermute | solution.py:422
  140.6 26.5 %collective-permute-start.19 = (bf16[2,3,704,128]{3,2,1,0:T(8,128)(2,1)S(1)}, bf16[2,3,704,128]{3,2,1,0:T(8,128)(2,1)S(1)}, u32[]{:S(2)}, u32[]{:S(2)}) collective-permute-start(bf16[2,3,704,128]{3,2,1,0:T(8,128)(2,1)S(1)} %get-tuple-element.396), channel_id=1, source_target_pairs={{0,8},{4,20},{8,0},{12,28},{16,24},{20,4},{24,16},{28,12},{1,9},{5... | collective-permute-start | bytes 3244040 | tf_op jit(solution)/shard_map/ppermute | solution.py:442
  141.1 25.9 %collective-permute-start.20 = (bf16[128,1024]{1,0:T(8,128)(2,1)}, bf16[128,1024]{1,0:T(8,128)(2,1)S(1)}, u32[]{:S(2)}, u32[]{:S(2)}) collective-permute-start(bf16[128,1024]{1,0:T(8,128)(2,1)} %get-tuple-element.288), channel_id=1, source_target_pairs={{0,2},{1,3},{2,0},{3,1},{4,6},{5,7},{6,4},{7,5},{8,10},{9,11},{10,... | collective-permute-start | bytes 786440 | tf_op jit(solution)/shard_map/ppermute | solution.py:422
  178.1 19.3 %collective-permute-start.22 = (bf16[2,5,128,256]{3,2,1,0:T(8,128)(2,1)S(1)}, bf16[2,5,128,256]{3,2,1,0:T(8,128)(2,1)S(1)}, u32[]{:S(2)}, u32[]{:S(2)}) collective-permute-start(bf16[2,5,128,256]{3,2,1,0:T(8,128)(2,1)S(1)} %get-tuple-element.308), channel_id=1, source_target_pairs={{0,8},{4,20},{8,0},{12,28},{16,24},{20,4},{24,16},{28,12},{1,9},{5... | collective-permute-start | bytes 1966088 | tf_op jit(solution)/shard_map/ppermute | solution.py:442
  178.7 18.7 %collective-permute-start.26 = (bf16[1,3,704,128]{3,2,1,0:T(8,128)(2,1)S(1)}, bf16[1,3,704,128]{3,2,1,0:T(8,128)(2,1)S(1)}, u32[]{:S(2)}, u32[]{:S(2)}) collective-permute-start(bf16[1,3,704,128]{3,2,1,0:T(8,128)(2,1)S(1)} %slice_add_fusion.4), channel_id=1, source_target_pairs={{0,16},{4,12},{8,24},{12,4},{16,0},{20,28},{24,8},{28,20},{1,17},{... | collective-permute-start | bytes 1622024 | tf_op jit(solution)/shard_map/ppermute | solution.py:442
  180.2 10.1 %collective-permute-start.23 = (bf16[128,768]{1,0:T(8,128)(2,1)S(1)}, bf16[128,768]{1,0:T(8,128)(2,1)S(1)}, u32[]{:S(2)}, u32[]{:S(2)}) collective-permute-start(bf16[128,768]{1,0:T(8,128)(2,1)S(1)} %copy-done.53), channel_id=1, source_target_pairs={{0,1},{1,0},{2,3},{3,2},{4,5},{5,4},{6,7},{7,6},{8,9},{9,8},{10,11... | collective-permute-start | bytes 589832 | tf_op jit(solution)/shard_map/ppermute | solution.py:422
  180.2 17.2 %collective-permute-start.24 = (bf16[128,768]{1,0:T(8,128)(2,1)S(1)}, bf16[128,768]{1,0:T(8,128)(2,1)S(1)}, u32[]{:S(2)}, u32[]{:S(2)}) collective-permute-start(bf16[128,768]{1,0:T(8,128)(2,1)S(1)} %copy-done.52), channel_id=1, source_target_pairs={{0,2},{1,3},{2,0},{3,1},{4,6},{5,7},{6,4},{7,5},{8,10},{9,11},{10,... | collective-permute-start | bytes 589832 | tf_op jit(solution)/shard_map/ppermute | solution.py:422
  183.1 14.3 %collective-permute-start.25 = (bf16[128,768]{1,0:T(8,128)(2,1)S(1)}, bf16[128,768]{1,0:T(8,128)(2,1)S(1)}, u32[]{:S(2)}, u32[]{:S(2)}) collective-permute-start(bf16[128,768]{1,0:T(8,128)(2,1)S(1)} %copy-done.51), channel_id=1, source_target_pairs={{0,3},{1,2},{2,1},{3,0},{4,7},{5,6},{6,5},{7,4},{8,11},{9,10},{10,... | collective-permute-start | bytes 589832 | tf_op jit(solution)/shard_map/ppermute | solution.py:422
  197.4 10.1 %collective-permute-start.27 = (bf16[1,5,128,256]{3,2,1,0:T(8,128)(2,1)S(1)}, bf16[1,5,128,256]{3,2,1,0:T(8,128)(2,1)S(1)}, u32[]{:S(2)}, u32[]{:S(2)}) collective-permute-start(bf16[1,5,128,256]{3,2,1,0:T(8,128)(2,1)S(1)} %slice_add_fusion.5), channel_id=1, source_target_pairs={{0,16},{4,12},{8,24},{12,4},{16,0},{20,28},{24,8},{28,20},{1,17},{... | collective-permute-start | bytes 983048 | tf_op jit(solution)/shard_map/ppermute | solution.py:442
  198.1 21.6 %collective-permute-start.32 = (bf16[3,704,128]{2,1,0:T(8,128)(2,1)S(1)}, bf16[3,704,128]{2,1,0:T(8,128)(2,1)S(1)}, u32[]{:S(2)}, u32[]{:S(2)}) collective-permute-start(bf16[3,704,128]{2,1,0:T(8,128)(2,1)S(1)} %add_bitcast_fusion.refs_0_), channel_id=1, source_target_pairs={{0,8},{4,20},{8,0},{12,28},{16,24},{20,4},{24,16},{28,12},{1,9},{5... | collective-permute-start | bytes 1622024 | tf_op jit(solution)/shard_map/ppermute | solution.py:442
  199.7 20.0 %collective-permute-start.31 = (bf16[3,704,128]{2,1,0:T(8,128)(2,1)S(1)}, bf16[3,704,128]{2,1,0:T(8,128)(2,1)S(1)}, u32[]{:S(2)}, u32[]{:S(2)}) collective-permute-start(bf16[3,704,128]{2,1,0:T(8,128)(2,1)S(1)} %add_bitcast_fusion.refs_0_), channel_id=1, source_target_pairs={{0,16},{4,12},{8,24},{12,4},{16,0},{20,28},{24,8},{28,20},{1,17},{... | collective-permute-start | bytes 1622024 | tf_op jit(solution)/shard_map/ppermute | solution.py:442
  207.7 8.1 %collective-permute-start.30 = (bf16[2,128,256]{2,1,0:T(8,128)(2,1)S(1)}, bf16[2,128,256]{2,1,0:T(8,128)(2,1)S(1)}, u32[]{:S(2)}, u32[]{:S(2)}) collective-permute-start(bf16[2,128,256]{2,1,0:T(8,128)(2,1)S(1)} %get-tuple-element.401), channel_id=1, source_target_pairs={{0,3},{1,2},{2,1},{3,0},{4,7},{5,6},{6,5},{7,4},{8,11},{9,10},{10,... | collective-permute-start | bytes 393224 | tf_op jit(solution)/shard_map/ppermute | solution.py:422
  210.2 9.4 %collective-permute-start.29 = (bf16[2,128,256]{2,1,0:T(8,128)(2,1)S(1)}, bf16[2,128,256]{2,1,0:T(8,128)(2,1)S(1)}, u32[]{:S(2)}, u32[]{:S(2)}) collective-permute-start(bf16[2,128,256]{2,1,0:T(8,128)(2,1)S(1)} %get-tuple-element.401), channel_id=1, source_target_pairs={{0,2},{1,3},{2,0},{3,1},{4,6},{5,7},{6,4},{7,5},{8,10},{9,11},{10,... | collective-permute-start | bytes 393224 | tf_op jit(solution)/shard_map/ppermute | solution.py:422
  213.4 6.2 %collective-permute-start.28 = (bf16[2,128,256]{2,1,0:T(8,128)(2,1)S(1)}, bf16[2,128,256]{2,1,0:T(8,128)(2,1)S(1)}, u32[]{:S(2)}, u32[]{:S(2)}) collective-permute-start(bf16[2,128,256]{2,1,0:T(8,128)(2,1)S(1)} %get-tuple-element.401), channel_id=1, source_target_pairs={{0,1},{1,0},{2,3},{3,2},{4,5},{5,4},{6,7},{7,6},{8,9},{9,8},{10,11... | collective-permute-start | bytes 393224 | tf_op jit(solution)/shard_map/ppermute | solution.py:422
  219.7 14.9 %collective-permute-start.36 = (bf16[4,2,128,256]{3,2,1,0:T(8,128)(2,1)S(1)}, bf16[4,2,128,256]{3,2,1,0:T(8,128)(2,1)S(1)}, u32[]{:S(2)}, u32[]{:S(2)}) collective-permute-start(bf16[4,2,128,256]{3,2,1,0:T(8,128)(2,1)S(1)} %pad_maximum_fusion.1.refs_0_), channel_id=1, source_target_pairs={{0,16},{4,12},{8,24},{12,4},{16,0},{20,28},{24,8},{28,20},{1,17},{... | collective-permute-start | bytes 1572872 | tf_op jit(solution)/shard_map/ppermute | solution.py:442
  220.0 26.9 %collective-permute-start.39 = (bf16[3,704,128]{2,1,0:T(8,128)(2,1)S(1)}, bf16[3,704,128]{2,1,0:T(8,128)(2,1)S(1)}, u32[]{:S(2)}, u32[]{:S(2)}) collective-permute-start(bf16[3,704,128]{2,1,0:T(8,128)(2,1)S(1)} %collective-permute-done.31.refs_1_), channel_id=1, source_target_pairs={{0,8},{4,20},{8,0},{12,28},{16,24},{20,4},{24,16},{28,12},{1,9},{5... | collective-permute-start | bytes 1622024 | tf_op jit(solution)/shard_map/ppermute | solution.py:442
  221.8 15.8 %collective-permute-start.33 = (bf16[3,128,256]{2,1,0:T(8,128)(2,1)S(1)}, bf16[3,128,256]{2,1,0:T(8,128)(2,1)S(1)}, u32[]{:S(2)}, u32[]{:S(2)}) collective-permute-start(bf16[3,128,256]{2,1,0:T(8,128)(2,1)S(1)} %slice_bitcast_fusion), channel_id=1, source_target_pairs={{0,1},{1,0},{2,3},{3,2},{4,5},{5,4},{6,7},{7,6},{8,9},{9,8},{10,11... | collective-permute-start | bytes 589832 | tf_op jit(solution)/shard_map/ppermute | solution.py:422
  222.0 24.8 %collective-permute-start.37 = (bf16[4,2,128,256]{3,2,1,0:T(8,128)(2,1)S(1)}, bf16[4,2,128,256]{3,2,1,0:T(8,128)(2,1)S(1)}, u32[]{:S(2)}, u32[]{:S(2)}) collective-permute-start(bf16[4,2,128,256]{3,2,1,0:T(8,128)(2,1)S(1)} %pad_maximum_fusion.1.refs_0_), channel_id=1, source_target_pairs={{0,8},{4,20},{8,0},{12,28},{16,24},{20,4},{24,16},{28,12},{1,9},{5... | collective-permute-start | bytes 1572872 | tf_op jit(solution)/shard_map/ppermute | solution.py:442
  234.6 12.3 %collective-permute-start.38 = (bf16[4,2,128,256]{3,2,1,0:T(8,128)(2,1)S(1)}, bf16[4,2,128,256]{3,2,1,0:T(8,128)(2,1)S(1)}, u32[]{:S(2)}, u32[]{:S(2)}) collective-permute-start(bf16[4,2,128,256]{3,2,1,0:T(8,128)(2,1)S(1)} %collective-permute-done.36.refs_1_), channel_id=1, source_target_pairs={{0,8},{4,20},{8,0},{12,28},{16,24},{20,4},{24,16},{28,12},{1,9},{5... | collective-permute-start | bytes 1572872 | tf_op jit(solution)/shard_map/ppermute | solution.py:442
  234.8 11.7 %collective-permute-start.35 = (bf16[3,128,256]{2,1,0:T(8,128)(2,1)S(1)}, bf16[3,128,256]{2,1,0:T(8,128)(2,1)S(1)}, u32[]{:S(2)}, u32[]{:S(2)}) collective-permute-start(bf16[3,128,256]{2,1,0:T(8,128)(2,1)S(1)} %slice_bitcast_fusion), channel_id=1, source_target_pairs={{0,3},{1,2},{2,1},{3,0},{4,7},{5,6},{6,5},{7,4},{8,11},{9,10},{10,... | collective-permute-start | bytes 589832 | tf_op jit(solution)/shard_map/ppermute | solution.py:422
  237.6 9.1 %collective-permute-start.34 = (bf16[3,128,256]{2,1,0:T(8,128)(2,1)S(1)}, bf16[3,128,256]{2,1,0:T(8,128)(2,1)S(1)}, u32[]{:S(2)}, u32[]{:S(2)}) collective-permute-start(bf16[3,128,256]{2,1,0:T(8,128)(2,1)S(1)} %slice_bitcast_fusion), channel_id=1, source_target_pairs={{0,2},{1,3},{2,0},{3,1},{4,6},{5,7},{6,4},{7,5},{8,10},{9,11},{10,... | collective-permute-start | bytes 589832 | tf_op jit(solution)/shard_map/ppermute | solution.py:422
  249.8 19.9 %collective-permute-start.41 = (bf16[4,3,128,256]{3,2,1,0:T(8,128)(2,1)S(1)}, bf16[4,3,128,256]{3,2,1,0:T(8,128)(2,1)S(1)}, u32[]{:S(2)}, u32[]{:S(2)}) collective-permute-start(bf16[4,3,128,256]{3,2,1,0:T(8,128)(2,1)S(1)} %pad_maximum_fusion.refs_0_), channel_id=1, source_target_pairs={{0,8},{4,20},{8,0},{12,28},{16,24},{20,4},{24,16},{28,12},{1,9},{5... | collective-permute-start | bytes 2359304 | tf_op jit(solution)/shard_map/ppermute | solution.py:442
  251.4 18.4 %collective-permute-start.40 = (bf16[4,3,128,256]{3,2,1,0:T(8,128)(2,1)S(1)}, bf16[4,3,128,256]{3,2,1,0:T(8,128)(2,1)}, u32[]{:S(2)}, u32[]{:S(2)}) collective-permute-start(bf16[4,3,128,256]{3,2,1,0:T(8,128)(2,1)S(1)} %pad_maximum_fusion.refs_0_), channel_id=1, source_target_pairs={{0,16},{4,12},{8,24},{12,4},{16,0},{20,28},{24,8},{28,20},{1,17},{... | collective-permute-start | bytes 2359304 | tf_op jit(solution)/shard_map/ppermute | solution.py:442
  251.8 15.1 %collective-permute-start.47 = (bf16[4,2,128,256]{3,2,1,0:T(8,128)(2,1)S(1)}, bf16[4,2,128,256]{3,2,1,0:T(8,128)(2,1)S(1)}, u32[]{:S(2)}, u32[]{:S(2)}) collective-permute-start(bf16[4,2,128,256]{3,2,1,0:T(8,128)(2,1)S(1)} %collective-permute-done.36.refs_1_), channel_id=1, source_target_pairs={{0,4},{4,0},{8,12},{12,8},{16,20},{20,16},{24,28},{28,24},{1,5},{5... | collective-permute-start | bytes 1572872 | tf_op jit(solution)/shard_map/ppermute | solution.py:435
  251.9 15.0 %collective-permute-start.48 = (bf16[4,2,128,256]{3,2,1,0:T(8,128)(2,1)S(1)}, bf16[4,2,128,256]{3,2,1,0:T(8,128)(2,1)S(1)}, u32[]{:S(2)}, u32[]{:S(2)}) collective-permute-start(bf16[4,2,128,256]{3,2,1,0:T(8,128)(2,1)S(1)} %collective-permute-done.37.refs_2_), channel_id=1, source_target_pairs={{0,4},{4,0},{8,12},{12,8},{16,20},{20,16},{24,28},{28,24},{1,5},{5... | collective-permute-start | bytes 1572872 | tf_op jit(solution)/shard_map/ppermute | solution.py:435
  252.4 14.5 %collective-permute-start.49 = (bf16[4,2,128,256]{3,2,1,0:T(8,128)(2,1)S(1)}, bf16[4,2,128,256]{3,2,1,0:T(8,128)(2,1)S(1)}, u32[]{:S(2)}, u32[]{:S(2)}) collective-permute-start(bf16[4,2,128,256]{3,2,1,0:T(8,128)(2,1)S(1)} %collective-permute-done.38.refs_3_), channel_id=1, source_target_pairs={{0,4},{4,0},{8,12},{12,8},{16,20},{20,16},{24,28},{28,24},{1,5},{5... | collective-permute-start | bytes 1572872 | tf_op jit(solution)/shard_map/ppermute | solution.py:435
  269.8 16.4 %collective-permute-start.50 = (bf16[4,3,128,256]{3,2,1,0:T(8,128)(2,1)}, bf16[4,3,128,256]{3,2,1,0:T(8,128)(2,1)S(1)}, u32[]{:S(2)}, u32[]{:S(2)}) collective-permute-start(bf16[4,3,128,256]{3,2,1,0:T(8,128)(2,1)} %collective-permute-done.40.refs_1_), channel_id=1, source_target_pairs={{0,8},{4,20},{8,0},{12,28},{16,24},{20,4},{24,16},{28,12},{1,9},{5... | collective-permute-start | bytes 2359304 | tf_op jit(solution)/shard_map/ppermute | solution.py:442
  271.2 12.8 %collective-permute-start.51 = (bf16[128,1024]{1,0:T(8,128)(2,1)S(1)}, bf16[128,1024]{1,0:T(8,128)(2,1)S(1)}, u32[]{:S(2)}, u32[]{:S(2)}) collective-permute-start(bf16[128,1024]{1,0:T(8,128)(2,1)S(1)} %copy-done.50), channel_id=1, source_target_pairs={{0,3},{1,2},{2,1},{3,0},{4,7},{5,6},{6,5},{7,4},{8,11},{9,10},{10,... | collective-permute-start | bytes 786440 | tf_op jit(solution)/shard_map/ppermute | solution.py:422
  273.8 12.4 %collective-permute-start.52 = (bf16[128,1024]{1,0:T(8,128)(2,1)S(1)}, bf16[128,1024]{1,0:T(8,128)(2,1)S(1)}, u32[]{:S(2)}, u32[]{:S(2)}) collective-permute-start(bf16[128,1024]{1,0:T(8,128)(2,1)S(1)} %copy-done.49), channel_id=1, source_target_pairs={{0,1},{1,0},{2,3},{3,2},{4,5},{5,4},{6,7},{7,6},{8,9},{9,8},{10,11... | collective-permute-start | bytes 786440 | tf_op jit(solution)/shard_map/ppermute | solution.py:422
  286.2 6.3 %collective-permute-start.53 = (bf16[4,3,128,256]{3,2,1,0:T(8,128)(2,1)S(1)}, bf16[4,3,128,256]{3,2,1,0:T(8,128)(2,1)S(1)}, u32[]{:S(2)}, u32[]{:S(2)}) collective-permute-start(bf16[4,3,128,256]{3,2,1,0:T(8,128)(2,1)S(1)} %copy-done.3), channel_id=1, source_target_pairs={{0,4},{4,0},{8,12},{12,8},{16,20},{20,16},{24,28},{28,24},{1,5},{5... | collective-permute-start | bytes 2359304 | tf_op jit(solution)/shard_map/ppermute | solution.py:435
  286.2 6.2 %collective-permute-start.54 = (bf16[4,3,128,256]{3,2,1,0:T(8,128)(2,1)}, bf16[4,3,128,256]{3,2,1,0:T(8,128)(2,1)S(1)}, u32[]{:S(2)}, u32[]{:S(2)}) collective-permute-start(bf16[4,3,128,256]{3,2,1,0:T(8,128)(2,1)} %collective-permute-done.40.refs_1_), channel_id=1, source_target_pairs={{0,4},{4,0},{8,12},{12,8},{16,20},{20,16},{24,28},{28,24},{1,5},{5... | collective-permute-start | bytes 2359304 | tf_op jit(solution)/shard_map/ppermute | solution.py:435
  (63 other events, 525.2 us)

commit v5 on v4

--- a/solution.py
+++ b/solution.py
@@ -13,8 +13,11 @@
 f32 = jnp.float32
 SMEM = pl.BlockSpec(memory_space=pltpu.SMEM)
 ANY = pl.BlockSpec(memory_space=pl.ANY)
-PARAMS = pltpu.CompilerParams(dimension_semantics=("arbitrary",), vmem_limit_bytes=56 << 20)
 sds = jax.ShapeDtypeStruct
+
+
+def budget(mebibytes):
+    return pltpu.CompilerParams(vmem_limit_bytes=mebibytes << 20)
 
 
 def cost(micros):
@@ -38,7 +41,7 @@
 
 
 def sigmoid(values):
-    return 1.0 / (1.0 + jnp.exp(-values))
+    return 0.5 * jnp.tanh(0.5 * values) + 0.5
 
 
 def slope(values):
@@ -68,7 +71,7 @@
 
 
 def decay_weights(causal, g_col, g_row):
-    return jnp.where(causal, jnp.exp(jnp.where(causal, g_col - g_row, 0.0)), 0.0)
+    return jnp.exp(jnp.where(causal, g_col - g_row, -1e30))
 
 
 def flip_of(own, share):
@@ -153,11 +156,8 @@
     q_lin = mm(normed, wq[...])
     k_lin = mm(normed, wk[...])
 
-    @pl.when(i == own[1])
-    def _():
-        ql[...] = q_lin
-        kl[...] = k_lin
-
+    ql[...] = q_lin
+    kl[...] = k_lin
     q[...] = (q_lin * sigmoid(q_lin)).astype(bf16)
     k[...] = (k_lin * sigmoid(k_lin) * live[...]).astype(bf16)
     v[...] = mm(normed, wv[...]).astype(bf16)
@@ -186,11 +186,7 @@
             base = jnp.where(part == j, states[j][h % hn].astype(f32), base)
         entering = coefs[ENTER, b, h] * base + coefs[SECOND, b, h] * contrib[1 - b, h]
         kept = (coefs[KEEP, b, h] * entering).astype(bf16)
-
-        @pl.when(part == 0)
-        def _():
-            kent[0, h % hn] = kept
-
+        kent[0, h] = kept
         att[:, at] = (intra[:, at] + rise[h // hn, :, h % hn : h % hn + 1] * mm(q[:, at], kept)).astype(bf16)
     values = att[...].astype(f32)
     scale = inv_rms(values)
@@ -325,13 +321,7 @@
         now = coefs[KEEP, b, head] * tm((qh.astype(f32) * up).astype(bf16), g)
         direct[0, h] = now
 
-        @pl.when(b == 0)
-        def _():
-            first[h] = coefs[ENTER, b, head] * now
-
-        @pl.when(b > 0)
-        def _():
-            first[h] += coefs[ENTER, b, head] * now
+        first[h] = jnp.where(b == 0, 0.0, first[h]) + coefs[ENTER, b, head] * now
 
 
 def key_kernel(hn, hd, wide, share, own, coefs, arrived, direct, n1, dq, k, v, kl, gk, gv,
@@ -351,17 +341,10 @@
         dv[:, at] = (gv[:, at] + down * mm(k[:, at], low)).astype(bf16)
     normed = n1[...]
     tall = normed.shape[1] // wide
-    for item, (acc, part) in enumerate(((aq, dq), (ak, dk), (av, dv))):
-        now = tm(normed, part[...])
-
-        @pl.when(b == 0)
-        def _():
-            acc[...] = now
-
-        @pl.when(b > 0)
-        def _():
-            acc[...] += now
-
+    for acc, part in ((aq, dq), (ak, dk), (av, dv)):
+        acc[...] = jnp.where(b == 0, 0.0, acc[...]) + tm(normed, part[...])
+
+    for item, acc in enumerate((aq, ak, av)):
         @pl.when(b == last)
         def _():
             scatter(wide, own, kept, sent, item, lambda t: acc[t * tall : (t + 1) * tall, :])
@@ -393,20 +376,29 @@
 
 def tokens_kernel(narrow, own, *refs):
     parts = refs[:narrow]
-    ggl, wq, wk, wv, wg, tok, gh, out, *grads = refs[narrow:]
+    ggl, wq, wk, wv, wg, tok, gh, out, *grads, total = refs[narrow:]
+    step = pl.program_id(0)
     cols = parts[0].shape[1] // 3
-    for i in range(narrow):
-        for k in range(narrow):
-            @pl.when(own[1] ^ i == k)
-            def _():
-                for item, full in enumerate(grads):
-                    full[:, i * cols : (i + 1) * cols] = parts[k][:, item * cols : (item + 1) * cols]
+
+    @pl.when(step == 0)
+    def _():
+        for i in range(narrow):
+            for k in range(narrow):
+                @pl.when(own[1] ^ i == k)
+                def _():
+                    for item, full in enumerate(grads):
+                        full[:, i * cols : (i + 1) * cols] = parts[k][:, item * cols : (item + 1) * cols]
 
     grad = mt(ggl[...], wg[...])
     for full, weight in zip(grads, (wq, wk, wv)):
         grad = grad + mt(full[...], weight[...])
-    values = tok[...].astype(f32)
-    out[...] = gh[...] + rms_back(values, inv_rms(values), grad)
+    total[step] = grad
+
+    @pl.when(step == narrow - 1)
+    def _():
+        grad = jnp.concatenate([total[i] for i in range(narrow)], axis=1)
+        values = tok[...].astype(f32)
+        out[...] = gh[...] + rms_back(values, inv_rms(values), grad)
 
 
 def output_kernel(narrow, *refs):
@@ -499,7 +491,7 @@
         ),
         out_shape=[sds(shape, f32)] * count,
         input_output_aliases={1 + places + i: i for i in range(len(outs))},
-        compiler_params=PARAMS,
+        compiler_params=budget(16),
         cost_estimate=cost(4),
         name=f"{name}_{other}",
     )(own, *pieces, *outs)
@@ -560,6 +552,7 @@
         in_specs=[SMEM, SMEM, SMEM, pl.BlockSpec(memory_space=pltpu.VMEM)],
         out_shape=[columns, columns, columns, sds((blocks * narrow, hn, BLOCK), f32), sds((local, 1), f32),
                    sds((5, blocks, heads), f32), sds((1, heads), f32)],
+        compiler_params=budget(16),
         cost_estimate=cost(3),
         name="layout",
     )(own, lengths, pad_counts, log_decay)
@@ -567,7 +560,7 @@
     def own_heads(values):
         return lax.dynamic_slice_in_dim(values, own_narrow * hn, hn, 1)
 
-    shapes = [sds((local, width), bf16), sds((local, width), bf16), *[sds((local, cols), f32)] * 2,
+    shapes = [sds((local, width), bf16), sds((local, width), bf16), *[sds((local, width), f32)] * 2,
               *[sds((local, width), bf16)] * 3, *[sds((local, width), f32)] * 2,
               sds((blocks, heads, hd, hd), f32)]
     made = []
@@ -578,7 +571,6 @@
         weight = pl.BlockSpec((width, cols), lambda i, own: (0, i))
         column = pl.BlockSpec((1, BLOCK, hn), lambda i, own, s=s: (i, s, 0))
         full = pl.BlockSpec((BLOCK, width), lambda i, own, s=s: (s, 0))
-        mine = pl.BlockSpec((BLOCK, cols), lambda i, own, s=s: (s, 0))
         part = pl.BlockSpec((BLOCK, cols), lambda i, own, s=s: (s, i))
         made = pl.pallas_call(
             functools.partial(forward_kernel, hn, hd, share),
@@ -589,12 +581,12 @@
                           pl.BlockSpec((BLOCK, 1), lambda i, own, s=s: (s, 0)), column,
                           pl.BlockSpec((1, hn, BLOCK), lambda i, own, s=s: (s * narrow + i, 0, 0)),
                           column, *[ANY] * len(made)],
-                out_specs=[full, full, mine, mine, *[part] * 5,
+                out_specs=[full, full, *[part] * 7,
                            pl.BlockSpec((1, hn, hd, hd), lambda i, own, s=s: (s, i, 0, 0))],
             ),
             out_shape=shapes,
             input_output_aliases={11 + i: i for i in range(len(made))},
-            compiler_params=PARAMS,
+            compiler_params=budget(56),
             cost_estimate=cost(10),
             name=f"mixer_forward_{s}",
         )(own, tok[per * s], tok[per * s + 1], w_query, w_key, w_value, w_gate, live, gcol, grow, tail, *made)
@@ -613,7 +605,8 @@
     up = lambda b: b
     all_blk, part_blk = rows((BLOCK, width), up), rows((BLOCK, cols), up)
     own_blk = pl.BlockSpec((BLOCK, cols), lambda b, own: (b, own[1]))
-    own_kent = rows((1, hn, hd, hd), up)
+    own_kent = pl.BlockSpec((1, hn, hd, hd), lambda b, own: (b, own[1], 0, 0))
+    own_direct = rows((1, hn, hd, hd), up)
     att, inverse, gated, hidden, n2, kent = pl.pallas_call(
         functools.partial(out_kernel, heads, hn, hd, share),
         grid_spec=pltpu.PrefetchScalarGridSpec(
@@ -622,11 +615,11 @@
             in_specs=[SMEM, *[whole((hn, hd, hd))] * narrow, whole((blocks, heads, hd, hd)),
                       *[all_blk] * 4, pl.BlockSpec((narrow, BLOCK, hn), lambda b, own: (0, b, 0)),
                       whole((width, width))],
-            out_specs=[all_blk, rows((BLOCK, 1), up), all_blk, whole((share, width)), all_blk, own_kent],
+            out_specs=[all_blk, rows((BLOCK, 1), up), all_blk, whole((share, width)), all_blk, rows((1, heads, hd, hd), up)],
         ),
         out_shape=[sds((local, width), bf16), sds((local, 1), f32), sds((local, width), bf16), sds((share, width), f32),
-                   sds((local, width), bf16), sds((blocks, hn, hd, hd), bf16)],
-        compiler_params=PARAMS,
+                   sds((local, width), bf16), sds((blocks, heads, hd, hd), bf16)],
+        compiler_params=budget(56),
         cost_estimate=cost(9.5),
         name="mixer_out",
     )(own, coefs, *states, contrib, q, intra, act, tok_all, rise, w_out)
@@ -638,7 +631,7 @@
     product, gf, gs, *gn2 = pl.pallas_call(
         functools.partial(ffn_kernel, share),
         out_shape=[*[sds((local, ff), bf16)] * 3, *[piece_shape] * narrow],
-        compiler_params=pltpu.CompilerParams(vmem_limit_bytes=56 << 20),
+        compiler_params=budget(16),
         cost_estimate=cost(10),
         name="ffn",
     )(n2, cot_all, first_t, second_t, w_third)
@@ -658,7 +651,7 @@
             scratch_shapes=[pltpu.VMEM((ff, width), f32)],
         ),
         out_shape=[sds(slot, bf16), sds(slot, bf16), *[piece_shape] * narrow],
-        compiler_params=PARAMS,
+        compiler_params=budget(16),
         cost_estimate=cost(10),
         name="ffn_grads",
     )(own, n2, cot_all, product_now, gf, gs, w_third)
@@ -680,7 +673,7 @@
         ),
         out_shape=[sds((share, width), f32), sds((share, width), bf16),
                    *[sds((share, 3 * cols), bf16)] * narrow],
-        compiler_params=PARAMS,
+        compiler_params=budget(16),
         cost_estimate=cost(5),
         name="residual_back",
     )(own, *gn2, hidden, cotangent, w_out, att, inverse, act)
@@ -696,14 +689,14 @@
         grid_spec=pltpu.PrefetchScalarGridSpec(
             num_scalar_prefetch=1,
             grid=(blocks,),
-            in_specs=[SMEM, *[whole((share, 3 * cols))] * narrow, *[own_blk] * 3, part_blk, own_kent,
+            in_specs=[SMEM, *[whole((share, 3 * cols))] * narrow, *[own_blk] * 4, own_kent,
                       own_col, own_row, own_col],
-            out_specs=[*[part_blk] * 3, own_kent, whole((hn, hd, hd))],
+            out_specs=[*[part_blk] * 3, own_direct, whole((hn, hd, hd))],
             scratch_shapes=[pltpu.VMEM((BLOCK, cols), bf16)],
         ),
         out_shape=[sds((local, cols), bf16), *[sds((local, cols), f32)] * 2,
                    sds((blocks, hn, hd, hd), f32), sds((hn, hd, hd), f32)],
-        compiler_params=PARAMS,
+        compiler_params=budget(56),
         cost_estimate=cost(5.4),
         name="mixer_query_back",
     )(own, coefs, *trios, q, k, v, ql, kent, gcol, grow, rise)
@@ -724,7 +717,7 @@
             scratch_shapes=[pltpu.VMEM((local, cols), bf16), pltpu.VMEM((width, cols), f32)],
         ),
         out_shape=[sds(five, bf16)] * 2,
-        compiler_params=PARAMS,
+        compiler_params=budget(16),
         cost_estimate=cost(5),
         name="gate_back",
     )(own, *trios, n1, gated)
@@ -736,13 +729,13 @@
             num_scalar_prefetch=1,
             grid=(blocks,),
             in_specs=[SMEM, whole((hn, hd, hd)), whole((blocks, hn, hd, hd)), all_blk, part_blk,
-                      own_blk, own_blk, *[part_blk] * 3, own_col, rows((BLOCK, 1), up), ANY, ANY],
+                      *[own_blk] * 3, *[part_blk] * 2, own_col, rows((BLOCK, 1), up), ANY, ANY],
             out_specs=[three, three, *[trio_spec] * narrow],
             scratch_shapes=[*[pltpu.VMEM((BLOCK, cols), bf16)] * 2, *[pltpu.VMEM((width, cols), f32)] * 3],
         ),
         out_shape=[*[sds(five, bf16)] * 2, *[trio_shape] * narrow],
         input_output_aliases={13: 0, 14: 1},
-        compiler_params=PARAMS,
+        compiler_params=budget(56),
         cost_estimate=cost(9),
         name="mixer_key_back",
     )(own, coefs, arrived, direct, n1, dq, k, v, kl, gk, gv, tail, live, kept, sent)
@@ -784,14 +777,14 @@
         functools.partial(tokens_kernel, narrow),
         grid_spec=pltpu.PrefetchScalarGridSpec(
             num_scalar_prefetch=1,
-            grid=(1,),
-            in_specs=[*[single((share, 3 * cols))] * narrow, row_spec, *[single((width, width))] * 4,
+            grid=(narrow,),
+            in_specs=[*[single((share, 3 * cols))] * narrow, row_spec, *[pl.BlockSpec((cols, width), lambda i, own: (i, 0))] * 4,
                       row_spec, row_spec],
             out_specs=row_spec,
-            scratch_shapes=[pltpu.VMEM((share, width), bf16)] * 3,
+            scratch_shapes=[*[pltpu.VMEM((share, width), bf16)] * 3, pltpu.VMEM((narrow, share, cols), f32)],
         ),
         out_shape=sds((share, width), f32),
-        compiler_params=PARAMS,
+        compiler_params=budget(16),
         cost_estimate=cost(8),
         name="tokens_back",
     )(own, *dqkv, ggl, w_query, w_key, w_value, w_gate, tokens, grad_hidden)
@@ -824,7 +817,7 @@
     output = pl.pallas_call(
         functools.partial(output_kernel, narrow),
         out_shape=sds((share, width), bf16),
-        compiler_params=pltpu.CompilerParams(vmem_limit_bytes=56 << 20),
+        compiler_params=budget(16),
         cost_estimate=cost(2),
         name="output",
     )(ffn_part[0], part_one, part_two, part_three, hidden)

time: 301 us -> 286 us (0.950)
  Pallas kernels: 122 us -> 86 us
  waiting for transfers between devices: 81.9 us -> 95.2 us
  local copies, waits for them, and re-layouts: 5.59 us -> 11 us
  other arithmetic: 4.56 us -> 7.64 us
    pallas_call x7, Pallas kernels: 32.5 us -> 20.7 us  [widen(): pl.pallas_call(functools.partial(kernel, places), grid_spec=pltpu.Prefetc...]
    ppermute x27, waiting for transfers between devices: 54.1 us -> 62.2 us  [swap_narrow(): return lax.ppermute(values, 'narrow', [(i, i ^ k) for i in range(size)])]
    unnamed x111 -> x107, local copies, waits for them, and re-layouts: 4.48 us -> 10.5 us
    ppermute x13, waiting for transfers between devices: 22.2 us -> 26.5 us  [swap_step(): return lax.ppermute(values, 'wide', [(i, flip(i)) for i in range(size)])]
    pallas_call x1, Pallas kernels: 6.29 us -> 2.17 us  [body(): pl.pallas_call(functools.partial(residual_kernel, narrow), grid_spec=pltp...]
    pallas_call x1, Pallas kernels: 10.2 us -> 6.12 us  [body(): pl.pallas_call(functools.partial(ffn_grad_kernel, wide, share), grid_spec...]
    pallas_call x1, Pallas kernels: 9.42 us -> 5.66 us  [body(): pl.pallas_call(functools.partial(ffn_kernel, share), out_shape=[*[sds((lo...]
    pallas_call x1, Pallas kernels: 8.84 us -> 5.13 us  [body(): pl.pallas_call(functools.partial(tokens_kernel, narrow), grid_spec=pltpu....]
  transfers between devices with their start and end apart: 57 -> 57, of which waited for: 18 -> 22; matrix products, arithmetic and copies ran while one was open for 2% -> 2% of each run, Pallas kernels for 28% -> 21%
where the time goes in v5:
time: 286 us
  waiting for transfers between devices  95.2 us (33%)
  Pallas kernels  86 us (30%)
  starting transfers between devices  63.6 us (22%)
  blocking collectives  19.8 us (7%)
  local copies, waits for them, and re-layouts  11 us (4%)
  other arithmetic  7.64 us (3%)
    ppermute x27, waiting for transfers between devices, swap_narrow(): return lax.ppermute(values, 'narrow', [(i, i ^ k) for i in range(size)])  62.2 us
    ppermute x27, starting transfers between devices, swap_narrow(): return lax.ppermute(values, 'narrow', [(i, i ^ k) for i in range(size)])  45.4 us
    ppermute x13, waiting for transfers between devices, swap_step(): return lax.ppermute(values, 'wide', [(i, flip(i)) for i in range(size)])  26.5 us
    pallas_call x7, Pallas kernels, widen(): pl.pallas_call(functools.partial(kernel, places), grid_spec=pltpu.Prefetc...  20.7 us
    pallas_call x2, Pallas kernels, body(): pl.pallas_call(functools.partial(forward_kernel, hn, hd, share), grid_spe...  20.4 us
    all_gather x2, blocking collectives, pass_states(): gathered = lax.all_gather(message, 'wide', axis=0)  19.8 us
    ppermute x13, starting transfers between devices, swap_step(): return lax.ppermute(values, 'wide', [(i, flip(i)) for i in range(size)])  11.9 us
    unnamed x107, local copies, waits for them, and re-layouts  10.5 us
  transfers between devices with their start and end apart: 57, of which 22 were waited for; matrix products, arithmetic and copies ran while one was open for 2% of the time, Pallas kernels for 21%

profile of v5, /device:TPU:0, one launch (start us, length us, event | category | flops | bytes accessed | tf_op | source)
XLA Modules:
  0.0 285.9 jit_solution(11600407451957847018)
XLA Ops:
  0.6 4.1 %collective-permute-start.1 = (bf16[128,1024]{1,0:T(8,128)(2,1)}, bf16[128,1024]{1,0:T(8,128)(2,1)S(1)}, u32[]{:S(2)}, u32[]{:S(2)}) collective-permute-start(bf16[128,1024]{1,0:T(8,128)(2,1)} %refs_9_.1), channel_id=1, source_target_pairs={{0,2},{1,3},{2,0},{3,1},{4,6},{5,7},{6,4},{7,5},{8,10},{9,11},{10,... | collective-permute-start | bytes 786440 | tf_op jit(solution)/shard_map/ppermute | solution.py:414
  8.5 2.1 layout.1
  14.9 2.6 collective-permute-done.tok_b
  18.1 10.3 %mixer_forward_0.1 = (bf16[512,1024]{1,0:T(8,128)(2,1)}, bf16[512,1024]{1,0:T(8,128)(2,1)}, f32[512,1024]{1,0:T(8,128)}, f32[512,1024]{1,0:T(8,128)}, bf16[512,1...) custom-call(s32[2]{0:T(128)} %copy-done.34, ...), custom_call_target="tpu_custom_call" | custom-call | bytes 32000000 | tf_op jit(solution)/shard_map/mixer_forward_0/pallas_call | solution.py:575
  29.9 2.5 collective-permute-start.7
  33.0 10.1 %mixer_forward_1.1 = (bf16[512,1024]{1,0:T(8,128)(2,1)}, bf16[512,1024]{1,0:T(8,128)(2,1)}, f32[512,1024]{1,0:T(8,128)}, f32[512,1024]{1,0:T(8,128)}, bf16[512,1...) custom-call(s32[2]{0:T(128)} %copy-done.34, ...), custom_call_target="tpu_custom_call", output_to_operand_aliasing={{0}: (11, {}), {1}: (12, {}), {2}: (13, {}), {3}: (14, {}),... | custom-call | bytes 32000000 | tf_op jit(solution)/shard_map/mixer_forward_1/pallas_call | solution.py:575
  48.4 10.0 %all-gather = bf16[16,128,128]{2,1,0:T(8,128)(2,1)S(1)} all-gather(bf16[2,128,128]{2,1,0:T(8,128)(2,1)S(1)} %multiply_reduce_fusion), channel_id=2, replica_groups=mesh['wide'=8,'narrow'=4] {'wide'}, dimensions={0}, use_global_device_ids=true | all-gather | bytes 589824 | tf_op jit(solution)/shard_map/all_gather | solution.py:533
  63.7 2.4 collective-permute-done.11.refs_3_
  66.0 2.6 collective-permute-done.10.refs_2_
  69.3 9.1 %mixer_out.1 = (bf16[512,1024]{1,0:T(8,128)(2,1)}, f32[512,1]{1,0:T(8,128)}, bf16[512,1024]{1,0:T(8,128)(2,1)}, f32[128,1024]{1,0:T(8,128)}, bf16[512,1024]{1,0:...) custom-call(s32[2]{0:T(128)} %copy-done.34, f32[5,2,8]{2,1,0:T(2,128)} %copy-done.39, bf16[2,128,128]{2,1,0:T(8,128)(2,1)} %copy-done.44, ...), custom_call_target="tpu_custom_call" | custom-call | bytes 30400000 | tf_op jit(solution)/shard_map/mixer_out/pallas_call | solution.py:610
  79.6 5.7 %ffn.1 = (bf16[512,704]{1,0:T(8,128)(2,1)S(1)}, bf16[512,704]{1,0:T(8,128)(2,1)S(1)}, bf16[512,704]{1,0:T(8,128)(2,1)S(1)}, bf16[128,1024]{1,0:T(8,128)(2,1)S(1)...) custom-call(bf16[512,1024]{1,0:T(8,128)(2,1)S(1)} %copy-done.12, ...), custom_call_target="tpu_custom_call" | custom-call | bytes 32000000 | tf_op jit(solution)/shard_map/ffn/pallas_call | solution.py:631
  85.4 1.9 collective-permute-start.13
  87.2 2.5 collective-permute-start.14
  89.7 7.9 %collective-permute-done.12.refs_1_ = bf16[128,1024]{1,0:T(8,128)(2,1)S(1)} collective-permute-done((bf16[128,1024]{1,0:T(8,128)(2,1)S(1)}, bf16[128,1024]{1,0:T(8,128)(2,1)S(1)}, u32[]{:S(2)}, u32[]{:S(2)}) %collective-permute-start.12) | collective-permute-done | bytes 262176 | tf_op jit(solution)/shard_map/ppermute | solution.py:414
  97.7 6.1 %ffn_grads.1 = (bf16[4,3,704,128]{3,2,1,0:T(8,128)(2,1)S(1)}, bf16[4,3,704,128]{3,2,1,0:T(8,128)(2,1)S(1)}, bf16[128,1024]{1,0:T(8,128)(2,1)S(1)}, bf16[128,1024...) custom-call(s32[2]{0:T(128)S(1)} %copy-done.35, bf16[512,1024]{1,0:T(8,128)(2,1)S(1)} %copy-done.13, ...), custom_call_target="tpu_custom_call" | custom-call | bytes 32000000 | tf_op jit(solution)/shard_map/ffn_grads/pallas_call | solution.py:644
  103.9 2.9 %collective-permute-done.13.refs_2_ = bf16[128,1024]{1,0:T(8,128)(2,1)S(1)} collective-permute-done((bf16[128,1024]{1,0:T(8,128)(2,1)S(1)}, bf16[128,1024]{1,0:T(8,128)(2,1)S(1)}, u32[]{:S(2)}, u32[]{:S(2)}) %collective-permute-start.13) | collective-permute-done | bytes 262176 | tf_op jit(solution)/shard_map/ppermute | solution.py:414
  106.8 2.2 residual_back.1
  109.7 4.9 %collective-permute-start.15 = (bf16[128,768]{1,0:T(8,128)(2,1)S(1)}, bf16[128,768]{1,0:T(8,128)(2,1)S(1)}, u32[]{:S(2)}, u32[]{:S(2)}) collective-permute-start(bf16[128,768]{1,0:T(8,128)(2,1)S(1)} %get-tuple-element.268), channel_id=1, source_target_pairs={{0,1},{1,0},{2,3},{3,2},{4,5},{5,4},{6,7},{7,6},{8,9},{9,8},{10,11... | collective-permute-start | bytes 589832 | tf_op jit(solution)/shard_map/ppermute | solution.py:414
  114.6 2.4 collective-permute-start.17
  117.0 6.2 %collective-permute-done.15.refs_1_ = bf16[128,768]{1,0:T(8,128)(2,1)S(1)} collective-permute-done((bf16[128,768]{1,0:T(8,128)(2,1)S(1)}, bf16[128,768]{1,0:T(8,128)(2,1)S(1)}, u32[]{:S(2)}, u32[]{:S(2)}) %collective-permute-start.15) | collective-permute-done | bytes 196640 | tf_op jit(solution)/shard_map/ppermute | solution.py:414
  123.2 8.6 %collective-permute-done.16.refs_2_ = bf16[128,768]{1,0:T(8,128)(2,1)S(1)} collective-permute-done((bf16[128,768]{1,0:T(8,128)(2,1)S(1)}, bf16[128,768]{1,0:T(8,128)(2,1)S(1)}, u32[]{:S(2)}, u32[]{:S(2)}) %collective-permute-start.16) | collective-permute-done | bytes 196640 | tf_op jit(solution)/shard_map/ppermute | solution.py:414
  133.9 3.9 %collective-permute-start.20 = (bf16[128,1024]{1,0:T(8,128)(2,1)S(1)}, bf16[128,1024]{1,0:T(8,128)(2,1)S(1)}, u32[]{:S(2)}, u32[]{:S(2)}) collective-permute-start(bf16[128,1024]{1,0:T(8,128)(2,1)S(1)} %get-tuple-element.288), channel_id=1, source_target_pairs={{0,2},{1,3},{2,0},{3,1},{4,6},{5,7},{6,4},{7,5},{8,10},{9,11},{10,... | collective-permute-start | bytes 786440 | tf_op jit(solution)/shard_map/ppermute | solution.py:414
  138.0 5.2 %mixer_query_back.1 = (bf16[512,256]{1,0:T(8,128)(2,1)}, f32[512,256]{1,0:T(8,128)}, f32[512,256]{1,0:T(8,128)}, f32[2,2,128,128]{3,2,1,0:T(8,128)}, f32[2,128,128]{2,1,0:T(8,128)}) custom-call(s32[2]{0:T(128)} %copy-done.34, f32[5,2,8]{2,1,0:T(2,128)} %copy-done.39, bf16[128,768]{1,0:T(8,128)(2,1)} %copy-done.24, bf16[128,768]{1,0:T(8,128)(2,1)} %copy-done.26, ...), custom_call_target="tpu_custom_call" | custom-call | bytes 17280000 | tf_op jit(solution)/shard_map/mixer_query_back/pallas_call | solution.py:687
  144.2 2.0 gate_back.1
  148.3 9.8 %all-gather.1 = bf16[16,128,128]{2,1,0:T(8,128)(2,1)S(1)} all-gather(bf16[2,128,128]{2,1,0:T(8,128)(2,1)S(1)} %convert_element_type.29), channel_id=3, replica_groups=mesh['wide'=8,'narrow'=4] {'wide'}, dimensions={0}, use_global_device_ids=true | all-gather | bytes 589824 | tf_op jit(solution)/shard_map/all_gather | solution.py:533
  159.0 6.6 %mixer_key_back.1 = (bf16[4,5,128,256]{3,2,1,0:T(8,128)(2,1)}, bf16[4,5,128,256]{3,2,1,0:T(8,128)(2,1)}, bf16[128,768]{1,0:T(8,128)(2,1)}, bf16[128,768]{1,0:T(8...) custom-call(s32[2]{0:T(128)} %copy-done.34, ...), custom_call_target="tpu_custom_call", output_to_operand_aliasing={{0}: (13, {}), {1}: (14, {})} | custom-call | bytes 28800000 | tf_op jit(solution)/shard_map/mixer_key_back/pallas_call | solution.py:726
  167.1 1.7 collective-permute-done.21
  171.2 2.9 %collective-permute-start.24 = (bf16[128,768]{1,0:T(8,128)(2,1)S(1)}, bf16[128,768]{1,0:T(8,128)(2,1)S(1)}, u32[]{:S(2)}, u32[]{:S(2)}) collective-permute-start(bf16[128,768]{1,0:T(8,128)(2,1)S(1)} %copy-done.50), channel_id=1, source_target_pairs={{0,2},{1,3},{2,0},{3,1},{4,6},{5,7},{6,4},{7,5},{8,10},{9,11},{10,... | collective-permute-start | bytes 589832 | tf_op jit(solution)/shard_map/ppermute | solution.py:414
  175.5 5.7 %collective-permute-done.23.refs_1_ = bf16[128,768]{1,0:T(8,128)(2,1)S(1)} collective-permute-done((bf16[128,768]{1,0:T(8,128)(2,1)S(1)}, bf16[128,768]{1,0:T(8,128)(2,1)S(1)}, u32[]{:S(2)}, u32[]{:S(2)}) %collective-permute-start.23) | collective-permute-done | bytes 196640 | tf_op jit(solution)/shard_map/ppermute | solution.py:414
  181.3 7.1 %collective-permute-done.24.refs_2_ = bf16[128,768]{1,0:T(8,128)(2,1)S(1)} collective-permute-done((bf16[128,768]{1,0:T(8,128)(2,1)S(1)}, bf16[128,768]{1,0:T(8,128)(2,1)S(1)}, u32[]{:S(2)}, u32[]{:S(2)}) %collective-permute-start.24) | collective-permute-done | bytes 196640 | tf_op jit(solution)/shard_map/ppermute | solution.py:414
  192.4 6.6 %collective-permute-done.27 = bf16[1,5,128,256]{3,2,1,0:T(8,128)(2,1)S(1)} collective-permute-done((bf16[1,5,128,256]{3,2,1,0:T(8,128)(2,1)S(1)}, bf16[1,5,128,256]{3,2,1,0:T(8,128)(2,1)S(1)}, u32[]{:S(2)}, u32[]{:S(2)}) %collective-permute-start.27) | collective-permute-done | bytes 327712 | tf_op jit(solution)/shard_map/ppermute | solution.py:434
  199.1 2.5 collective-permute-start.30
  201.6 2.7 collective-permute-start.29
  206.0 4.2 %collective-permute-done.29 = bf16[2,128,256]{2,1,0:T(8,128)(2,1)S(1)} collective-permute-done((bf16[2,128,256]{2,1,0:T(8,128)(2,1)S(1)}, bf16[2,128,256]{2,1,0:T(8,128)(2,1)S(1)}, u32[]{:S(2)}, u32[]{:S(2)}) %collective-permute-start.29) | collective-permute-done | bytes 131104 | tf_op jit(solution)/shard_map/ppermute | solution.py:414
  213.3 11.8 %collective-permute-done.36.refs_1_ = bf16[4,2,128,256]{3,2,1,0:T(8,128)(2,1)S(1)} collective-permute-done((bf16[4,2,128,256]{3,2,1,0:T(8,128)(2,1)S(1)}, bf16[4,2,128,256]{3,2,1,0:T(8,128)(2,1)S(1)}, u32[]{:S(2)}, u32[]{:S(2)}) %collective-permute-start.36) | collective-permute-done | bytes 524320 | tf_op jit(solution)/shard_map/ppermute | solution.py:434
  225.7 2.4 collective-permute-start.35
  228.2 5.1 %tokens_back.1 = f32[128,1024]{1,0:T(8,128)} custom-call(s32[2]{0:T(128)S(1)} %copy-done.37, bf16[128,768]{1,0:T(8,128)(2,1)S(1)} %copy-done.33, bf16[128,768]{1,0:T(8,128)(2,1)S(1)} %collective-permute-done.23.refs_1_, bf16[128,768]{1,0:T(8,128)(2,1)S(1)} %collective-permute-done.24.refs_2_, bf16[128,768]{1,0:T(8,128)(2,1)S(1)} %collective-permute-done.25.refs_3_, ...), custom_call_target="tpu_custom_call" | custom-call | bytes 25600000 | tf_op jit(solution)/shard_map/tokens_back/pallas_call | solution.py:776
  233.3 4.2 %collective-permute-done.34 = bf16[3,128,256]{2,1,0:T(8,128)(2,1)S(1)} collective-permute-done((bf16[3,128,256]{2,1,0:T(8,128)(2,1)S(1)}, bf16[3,128,256]{2,1,0:T(8,128)(2,1)S(1)}, u32[]{:S(2)}, u32[]{:S(2)}) %collective-permute-start.34) | collective-permute-done | bytes 196640 | tf_op jit(solution)/shard_map/ppermute | solution.py:414
  243.0 3.0 %widen_gate_0.1 = (f32[1024,1024]{1,0:T(8,128)}, f32[1024,1024]{1,0:T(8,128)}) custom-call(s32[2]{0:T(128)S(1)} %copy-done.37, bf16[4,2,128,256]{3,2,1,0:T(8,128)(2,1)S(1)} %pad_maximum_fusion.1.refs_0_, bf16[4,2,128,256]{3,2,1,0:T(8,128)(2,1)S(1)} %collective-permute-done.36.refs_1_, bf16[4,2,128,256]{3,2,1,0:T(8,128)(2,1)S(1)} %collective-permute-done.37.refs_2_, ...), custom_call_target="tpu_custom_call" | custom-call | bytes 12800000 | tf_op jit(solution)/shard_map/widen_gate_0/pallas_call | solution.py:484
  246.0 3.1 %widen_ffn_0.1 = (f32[704,1024]{1,0:T(8,128)}, f32[704,1024]{1,0:T(8,128)}, f32[704,1024]{1,0:T(8,128)}) custom-call(s32[2]{0:T(128)S(1)} %copy-done.37, bf16[3,704,128]{2,1,0:T(8,128)(2,1)S(1)} %add_bitcast_fusion.refs_0_, bf16[3,704,128]{2,1,0:T(8,128)(2,1)S(1)} %collective-permute-done.31.refs_1_, ...), custom_call_target="tpu_custom_call" | custom-call | bytes 12800000 | tf_op jit(solution)/shard_map/widen_ffn_0/pallas_call | solution.py:484
  249.2 3.1 %widen_ffn_1.1 = (f32[704,1024]{1,0:T(8,128)}, f32[704,1024]{1,0:T(8,128)}, f32[704,1024]{1,0:T(8,128)}) custom-call(s32[2]{0:T(128)S(1)} %copy-done.37, bf16[3,704,128]{2,1,0:T(8,128)(2,1)S(1)} %collective-permute-done.42.refs_0_, ...), custom_call_target="tpu_custom_call", output_to_operand_aliasing={{0}: (5, {}), {1}: (6, {}), {2}: (7, {})} | custom-call | bytes 12800000 | tf_op jit(solution)/shard_map/widen_ffn_1/pallas_call | solution.py:484
  252.3 8.0 %collective-permute-done.41.refs_2_ = bf16[4,3,128,256]{3,2,1,0:T(8,128)(2,1)S(1)} collective-permute-done((bf16[4,3,128,256]{3,2,1,0:T(8,128)(2,1)S(1)}, bf16[4,3,128,256]{3,2,1,0:T(8,128)(2,1)S(1)}, u32[]{:S(2)}, u32[]{:S(2)}) %collective-permute-start.41) | collective-permute-done | bytes 786464 | tf_op jit(solution)/shard_map/ppermute | solution.py:434
  261.7 2.5 collective-permute-start.51
  264.2 3.1 %widen_square_0.1 = (f32[1024,1024]{1,0:T(8,128)}, f32[1024,1024]{1,0:T(8,128)}, f32[1024,1024]{1,0:T(8,128)}) custom-call(s32[2]{0:T(128)S(1)} %copy-done.37, bf16[4,3,128,256]{3,2,1,0:T(8,128)(2,1)S(1)} %pad_maximum_fusion.refs_0_, bf16[4,3,128,256]{3,2,1,0:T(8,128)(2,1)S(1)} %collective-permute-done.40.refs_1_, ...), custom_call_target="tpu_custom_call" | custom-call | bytes 12800000 | tf_op jit(solution)/shard_map/widen_square_0/pallas_call | solution.py:484
  267.3 3.0 %widen_gate_1.1 = (f32[1024,1024]{1,0:T(8,128)}, f32[1024,1024]{1,0:T(8,128)}) custom-call(s32[2]{0:T(128)S(1)} %copy-done.37, bf16[4,2,128,256]{3,2,1,0:T(8,128)(2,1)S(1)} %collective-permute-done.46.refs_0_, bf16[4,2,128,256]{3,2,1,0:T(8,128)(2,1)S(1)} %collective-permute-done.47.refs_1_, ...), custom_call_target="tpu_custom_call", output_to_operand_aliasing={{0}: (5, {}), {1}: (6, {})} | custom-call | bytes 12800000 | tf_op jit(solution)/shard_map/widen_gate_1/pallas_call | solution.py:484
  270.4 2.4 collective-permute-done.51.refs_3_
  272.7 3.8 %collective-permute-done.52.refs_1_ = bf16[128,1024]{1,0:T(8,128)(2,1)S(1)} collective-permute-done((bf16[128,1024]{1,0:T(8,128)(2,1)S(1)}, bf16[128,1024]{1,0:T(8,128)(2,1)S(1)}, u32[]{:S(2)}, u32[]{:S(2)}) %collective-permute-start.52) | collective-permute-done | bytes 262176 | tf_op jit(solution)/shard_map/ppermute | solution.py:414
  282.3 3.6 %widen_square_1.1 = (f32[1024,1024]{1,0:T(8,128)}, f32[1024,1024]{1,0:T(8,128)}, f32[1024,1024]{1,0:T(8,128)}) custom-call(s32[2]{0:T(128)S(1)} %copy-done.37, bf16[4,3,128,256]{3,2,1,0:T(8,128)(2,1)S(1)} %collective-permute-done.53.refs_0_, ...), custom_call_target="tpu_custom_call", output_to_operand_aliasing={{0}: (5, {}), {1}: (6, {}), {2}: (7, {})} | custom-call | bytes 12800000 | tf_op jit(solution)/shard_map/widen_square_1/pallas_call | solution.py:484
  (229 shorter events, 55.9 us)
Async XLA Ops:
  0.6 27.9 %collective-permute-start.1 = (bf16[128,1024]{1,0:T(8,128)(2,1)}, bf16[128,1024]{1,0:T(8,128)(2,1)S(1)}, u32[]{:S(2)}, u32[]{:S(2)}) collective-permute-start(bf16[128,1024]{1,0:T(8,128)(2,1)} %refs_9_.1), channel_id=1, source_target_pairs={{0,2},{1,3},{2,0},{3,1},{4,6},{5,7},{6,4},{7,5},{8,10},{9,11},{10,... | collective-permute-start | bytes 786440 | tf_op jit(solution)/shard_map/ppermute | solution.py:414
  4.8 12.7 %collective-permute-start = (bf16[128,1024]{1,0:T(8,128)(2,1)}, bf16[128,1024]{1,0:T(8,128)(2,1)S(1)}, u32[]{:S(2)}, u32[]{:S(2)}) collective-permute-start(bf16[128,1024]{1,0:T(8,128)(2,1)} %refs_9_.1), channel_id=1, source_target_pairs={{0,1},{1,0},{2,3},{3,2},{4,5},{5,4},{6,7},{7,6},{8,9},{9,8},{10,11... | collective-permute-start | bytes 786440 | tf_op jit(solution)/shard_map/ppermute | solution.py:414
  6.3 22.2 %collective-permute-start.2 = (bf16[128,1024]{1,0:T(8,128)(2,1)}, bf16[128,1024]{1,0:T(8,128)(2,1)S(1)}, u32[]{:S(2)}, u32[]{:S(2)}) collective-permute-start(bf16[128,1024]{1,0:T(8,128)(2,1)} %refs_9_.1), channel_id=1, source_target_pairs={{0,3},{1,2},{2,1},{3,0},{4,7},{5,6},{6,5},{7,4},{8,11},{9,10},{10,... | collective-permute-start | bytes 786440 | tf_op jit(solution)/shard_map/ppermute | solution.py:414
  28.5 30.5 %collective-permute-start.8 = (bf16[128,1024]{1,0:T(8,128)(2,1)S(1)}, bf16[128,1024]{1,0:T(8,128)(2,1)S(1)}, u32[]{:S(2)}, u32[]{:S(2)}) collective-permute-start(bf16[128,1024]{1,0:T(8,128)(2,1)S(1)} %copy-done.23), channel_id=1, source_target_pairs={{0,3},{1,2},{2,1},{3,0},{4,7},{5,6},{6,5},{7,4},{8,11},{9,10},{10,... | collective-permute-start | bytes 786440 | tf_op jit(solution)/shard_map/ppermute | solution.py:414
  29.9 29.2 %collective-permute-start.7 = (bf16[128,1024]{1,0:T(8,128)(2,1)S(1)}, bf16[128,1024]{1,0:T(8,128)(2,1)S(1)}, u32[]{:S(2)}, u32[]{:S(2)}) collective-permute-start(bf16[128,1024]{1,0:T(8,128)(2,1)S(1)} %copy-done.23), channel_id=1, source_target_pairs={{0,2},{1,3},{2,0},{3,1},{4,6},{5,7},{6,4},{7,5},{8,10},{9,11},{10,... | collective-permute-start | bytes 786440 | tf_op jit(solution)/shard_map/ppermute | solution.py:414
  32.5 26.6 %collective-permute-start.6 = (bf16[128,1024]{1,0:T(8,128)(2,1)S(1)}, bf16[128,1024]{1,0:T(8,128)(2,1)S(1)}, u32[]{:S(2)}, u32[]{:S(2)}) collective-permute-start(bf16[128,1024]{1,0:T(8,128)(2,1)S(1)} %copy-done.23), channel_id=1, source_target_pairs={{0,1},{1,0},{2,3},{3,2},{4,5},{5,4},{6,7},{7,6},{8,9},{9,8},{10,11... | collective-permute-start | bytes 786440 | tf_op jit(solution)/shard_map/ppermute | solution.py:414
  33.0 10.1 %collective-permute-start.3 = (f32[1,8]{1,0:T(1,128)S(1)}, f32[1,8]{1,0:T(1,128)S(1)}, u32[]{:S(2)}, u32[]{:S(2)}) collective-permute-start(f32[1,8]{1,0:T(1,128)S(1)} %get-tuple-element.218), channel_id=1, source_target_pairs={{0,4},{4,0},{8,12},{12,8},{16,20},{20,16},{24,28},{28,24},{1,5},{5... | collective-permute-start | bytes 104 | tf_op jit(solution)/shard_map/ppermute | solution.py:515
  46.8 11.6 %collective-permute-start.5 = (f32[4,8]{1,0:T(4,128)S(1)}, f32[4,8]{1,0:T(4,128)S(1)}, u32[]{:S(2)}, u32[]{:S(2)}) collective-permute-start(f32[4,8]{1,0:T(4,128)S(1)} %pad_maximum_fusion.3), channel_id=1, source_target_pairs={{0,16},{4,20},{8,24},{12,28},{16,0},{20,4},{24,8},{28,12},{1,17},{... | collective-permute-start | bytes 392 | tf_op jit(solution)/shard_map/ppermute | solution.py:515
  59.1 6.9 %collective-permute-start.11 = (bf16[2,128,128]{2,1,0:T(8,128)(2,1)S(1)}, bf16[2,128,128]{2,1,0:T(8,128)(2,1)S(1)}, u32[]{:S(2)}, u32[]{:S(2)}) collective-permute-start(bf16[2,128,128]{2,1,0:T(8,128)(2,1)S(1)} %fusion.1.refs_0_), channel_id=1, source_target_pairs={{0,3},{1,2},{2,1},{3,0},{4,7},{5,6},{6,5},{7,4},{8,11},{9,10},{10,... | collective-permute-start | bytes 196616 | tf_op jit(solution)/shard_map/ppermute | solution.py:414
  60.5 8.2 %collective-permute-start.10 = (bf16[2,128,128]{2,1,0:T(8,128)(2,1)S(1)}, bf16[2,128,128]{2,1,0:T(8,128)(2,1)S(1)}, u32[]{:S(2)}, u32[]{:S(2)}) collective-permute-start(bf16[2,128,128]{2,1,0:T(8,128)(2,1)S(1)} %fusion.1.refs_0_), channel_id=1, source_target_pairs={{0,2},{1,3},{2,0},{3,1},{4,6},{5,7},{6,4},{7,5},{8,10},{9,11},{10,... | collective-permute-start | bytes 196616 | tf_op jit(solution)/shard_map/ppermute | solution.py:414
  62.1 6.5 %collective-permute-start.9 = (bf16[2,128,128]{2,1,0:T(8,128)(2,1)S(1)}, bf16[2,128,128]{2,1,0:T(8,128)(2,1)S(1)}, u32[]{:S(2)}, u32[]{:S(2)}) collective-permute-start(bf16[2,128,128]{2,1,0:T(8,128)(2,1)S(1)} %fusion.1.refs_0_), channel_id=1, source_target_pairs={{0,1},{1,0},{2,3},{3,2},{4,5},{5,4},{6,7},{7,6},{8,9},{9,8},{10,11... | collective-permute-start | bytes 196616 | tf_op jit(solution)/shard_map/ppermute | solution.py:414
  85.3 12.4 %collective-permute-start.12 = (bf16[128,1024]{1,0:T(8,128)(2,1)S(1)}, bf16[128,1024]{1,0:T(8,128)(2,1)S(1)}, u32[]{:S(2)}, u32[]{:S(2)}) collective-permute-start(bf16[128,1024]{1,0:T(8,128)(2,1)S(1)} %get-tuple-element.245), channel_id=1, source_target_pairs={{0,1},{1,0},{2,3},{3,2},{4,5},{5,4},{6,7},{7,6},{8,9},{9,8},{10,11... | collective-permute-start | bytes 786440 | tf_op jit(solution)/shard_map/ppermute | solution.py:414
  85.4 21.4 %collective-permute-start.13 = (bf16[128,1024]{1,0:T(8,128)(2,1)S(1)}, bf16[128,1024]{1,0:T(8,128)(2,1)S(1)}, u32[]{:S(2)}, u32[]{:S(2)}) collective-permute-start(bf16[128,1024]{1,0:T(8,128)(2,1)S(1)} %get-tuple-element.246), channel_id=1, source_target_pairs={{0,2},{1,3},{2,0},{3,1},{4,6},{5,7},{6,4},{7,5},{8,10},{9,11},{10,... | collective-permute-start | bytes 786440 | tf_op jit(solution)/shard_map/ppermute | solution.py:414
  87.2 19.5 %collective-permute-start.14 = (bf16[128,1024]{1,0:T(8,128)(2,1)S(1)}, bf16[128,1024]{1,0:T(8,128)(2,1)S(1)}, u32[]{:S(2)}, u32[]{:S(2)}) collective-permute-start(bf16[128,1024]{1,0:T(8,128)(2,1)S(1)} %get-tuple-element.247), channel_id=1, source_target_pairs={{0,3},{1,2},{2,1},{3,0},{4,7},{5,6},{6,5},{7,4},{8,11},{9,10},{10,... | collective-permute-start | bytes 786440 | tf_op jit(solution)/shard_map/ppermute | solution.py:414
  109.7 22.1 %collective-permute-start.18 = (bf16[4,3,704,128]{3,2,1,0:T(8,128)(2,1)S(1)}, bf16[4,3,704,128]{3,2,1,0:T(8,128)(2,1)S(1)}, u32[]{:S(2)}, u32[]{:S(2)}) collective-permute-start(bf16[4,3,704,128]{3,2,1,0:T(8,128)(2,1)S(1)} %get-tuple-element.272), channel_id=1, source_target_pairs={{0,4},{4,0},{8,12},{12,8},{16,20},{20,16},{24,28},{28,24},{1,5},{5... | collective-permute-start | bytes 6488072 | tf_op jit(solution)/shard_map/ppermute | solution.py:427
  109.7 13.5 %collective-permute-start.15 = (bf16[128,768]{1,0:T(8,128)(2,1)S(1)}, bf16[128,768]{1,0:T(8,128)(2,1)S(1)}, u32[]{:S(2)}, u32[]{:S(2)}) collective-permute-start(bf16[128,768]{1,0:T(8,128)(2,1)S(1)} %get-tuple-element.268), channel_id=1, source_target_pairs={{0,1},{1,0},{2,3},{3,2},{4,5},{5,4},{6,7},{7,6},{8,9},{9,8},{10,11... | collective-permute-start | bytes 589832 | tf_op jit(solution)/shard_map/ppermute | solution.py:414
  114.6 17.1 %collective-permute-start.16 = (bf16[128,768]{1,0:T(8,128)(2,1)S(1)}, bf16[128,768]{1,0:T(8,128)(2,1)S(1)}, u32[]{:S(2)}, u32[]{:S(2)}) collective-permute-start(bf16[128,768]{1,0:T(8,128)(2,1)S(1)} %get-tuple-element.269), channel_id=1, source_target_pairs={{0,2},{1,3},{2,0},{3,1},{4,6},{5,7},{6,4},{7,5},{8,10},{9,11},{10,... | collective-permute-start | bytes 589832 | tf_op jit(solution)/shard_map/ppermute | solution.py:414
  114.6 17.1 %collective-permute-start.17 = (bf16[128,768]{1,0:T(8,128)(2,1)S(1)}, bf16[128,768]{1,0:T(8,128)(2,1)S(1)}, u32[]{:S(2)}, u32[]{:S(2)}) collective-permute-start(bf16[128,768]{1,0:T(8,128)(2,1)S(1)} %get-tuple-element.270), channel_id=1, source_target_pairs={{0,3},{1,2},{2,1},{3,0},{4,7},{5,6},{6,5},{7,4},{8,11},{9,10},{10,... | collective-permute-start | bytes 589832 | tf_op jit(solution)/shard_map/ppermute | solution.py:414
  133.3 25.6 %collective-permute-start.19 = (bf16[2,3,704,128]{3,2,1,0:T(8,128)(2,1)}, bf16[2,3,704,128]{3,2,1,0:T(8,128)(2,1)}, u32[]{:S(2)}, u32[]{:S(2)}) collective-permute-start(bf16[2,3,704,128]{3,2,1,0:T(8,128)(2,1)} %get-tuple-element.396), channel_id=1, source_target_pairs={{0,8},{4,20},{8,0},{12,28},{16,24},{20,4},{24,16},{28,12},{1,9},{5... | collective-permute-start | bytes 3244040 | tf_op jit(solution)/shard_map/ppermute | solution.py:434
  133.9 25.0 %collective-permute-start.20 = (bf16[128,1024]{1,0:T(8,128)(2,1)S(1)}, bf16[128,1024]{1,0:T(8,128)(2,1)S(1)}, u32[]{:S(2)}, u32[]{:S(2)}) collective-permute-start(bf16[128,1024]{1,0:T(8,128)(2,1)S(1)} %get-tuple-element.288), channel_id=1, source_target_pairs={{0,2},{1,3},{2,0},{3,1},{4,6},{5,7},{6,4},{7,5},{8,10},{9,11},{10,... | collective-permute-start | bytes 786440 | tf_op jit(solution)/shard_map/ppermute | solution.py:414
  169.0 19.3 %collective-permute-start.22 = (bf16[2,5,128,256]{3,2,1,0:T(8,128)(2,1)S(1)}, bf16[2,5,128,256]{3,2,1,0:T(8,128)(2,1)S(1)}, u32[]{:S(2)}, u32[]{:S(2)}) collective-permute-start(bf16[2,5,128,256]{3,2,1,0:T(8,128)(2,1)S(1)} %get-tuple-element.308), channel_id=1, source_target_pairs={{0,8},{4,20},{8,0},{12,28},{16,24},{20,4},{24,16},{28,12},{1,9},{5... | collective-permute-start | bytes 1966088 | tf_op jit(solution)/shard_map/ppermute | solution.py:434
  169.6 18.7 %collective-permute-start.26 = (bf16[1,3,704,128]{3,2,1,0:T(8,128)(2,1)S(1)}, bf16[1,3,704,128]{3,2,1,0:T(8,128)(2,1)S(1)}, u32[]{:S(2)}, u32[]{:S(2)}) collective-permute-start(bf16[1,3,704,128]{3,2,1,0:T(8,128)(2,1)S(1)} %slice_add_fusion.4), channel_id=1, source_target_pairs={{0,16},{4,12},{8,24},{12,4},{16,0},{20,28},{24,8},{28,20},{1,17},{... | collective-permute-start | bytes 1622024 | tf_op jit(solution)/shard_map/ppermute | solution.py:434
  171.1 10.1 %collective-permute-start.23 = (bf16[128,768]{1,0:T(8,128)(2,1)S(1)}, bf16[128,768]{1,0:T(8,128)(2,1)S(1)}, u32[]{:S(2)}, u32[]{:S(2)}) collective-permute-start(bf16[128,768]{1,0:T(8,128)(2,1)S(1)} %copy-done.51), channel_id=1, source_target_pairs={{0,1},{1,0},{2,3},{3,2},{4,5},{5,4},{6,7},{7,6},{8,9},{9,8},{10,11... | collective-permute-start | bytes 589832 | tf_op jit(solution)/shard_map/ppermute | solution.py:414
  171.2 17.1 %collective-permute-start.24 = (bf16[128,768]{1,0:T(8,128)(2,1)S(1)}, bf16[128,768]{1,0:T(8,128)(2,1)S(1)}, u32[]{:S(2)}, u32[]{:S(2)}) collective-permute-start(bf16[128,768]{1,0:T(8,128)(2,1)S(1)} %copy-done.50), channel_id=1, source_target_pairs={{0,2},{1,3},{2,0},{3,1},{4,6},{5,7},{6,4},{7,5},{8,10},{9,11},{10,... | collective-permute-start | bytes 589832 | tf_op jit(solution)/shard_map/ppermute | solution.py:414
  174.1 14.2 %collective-permute-start.25 = (bf16[128,768]{1,0:T(8,128)(2,1)S(1)}, bf16[128,768]{1,0:T(8,128)(2,1)S(1)}, u32[]{:S(2)}, u32[]{:S(2)}) collective-permute-start(bf16[128,768]{1,0:T(8,128)(2,1)S(1)} %copy-done.49), channel_id=1, source_target_pairs={{0,3},{1,2},{2,1},{3,0},{4,7},{5,6},{6,5},{7,4},{8,11},{9,10},{10,... | collective-permute-start | bytes 589832 | tf_op jit(solution)/shard_map/ppermute | solution.py:414
  188.4 10.6 %collective-permute-start.27 = (bf16[1,5,128,256]{3,2,1,0:T(8,128)(2,1)S(1)}, bf16[1,5,128,256]{3,2,1,0:T(8,128)(2,1)S(1)}, u32[]{:S(2)}, u32[]{:S(2)}) collective-permute-start(bf16[1,5,128,256]{3,2,1,0:T(8,128)(2,1)S(1)} %slice_add_fusion.5), channel_id=1, source_target_pairs={{0,16},{4,12},{8,24},{12,4},{16,0},{20,28},{24,8},{28,20},{1,17},{... | collective-permute-start | bytes 983048 | tf_op jit(solution)/shard_map/ppermute | solution.py:434
  190.3 19.9 %collective-permute-start.32 = (bf16[3,704,128]{2,1,0:T(8,128)(2,1)S(1)}, bf16[3,704,128]{2,1,0:T(8,128)(2,1)S(1)}, u32[]{:S(2)}, u32[]{:S(2)}) collective-permute-start(bf16[3,704,128]{2,1,0:T(8,128)(2,1)S(1)} %add_bitcast_fusion.refs_0_), channel_id=1, source_target_pairs={{0,8},{4,20},{8,0},{12,28},{16,24},{20,4},{24,16},{28,12},{1,9},{5... | collective-permute-start | bytes 1622024 | tf_op jit(solution)/shard_map/ppermute | solution.py:434
  191.9 18.4 %collective-permute-start.31 = (bf16[3,704,128]{2,1,0:T(8,128)(2,1)S(1)}, bf16[3,704,128]{2,1,0:T(8,128)(2,1)S(1)}, u32[]{:S(2)}, u32[]{:S(2)}) collective-permute-start(bf16[3,704,128]{2,1,0:T(8,128)(2,1)S(1)} %add_bitcast_fusion.refs_0_), channel_id=1, source_target_pairs={{0,16},{4,12},{8,24},{12,4},{16,0},{20,28},{24,8},{28,20},{1,17},{... | collective-permute-start | bytes 1622024 | tf_op jit(solution)/shard_map/ppermute | solution.py:434
  199.1 6.8 %collective-permute-start.30 = (bf16[2,128,256]{2,1,0:T(8,128)(2,1)S(1)}, bf16[2,128,256]{2,1,0:T(8,128)(2,1)S(1)}, u32[]{:S(2)}, u32[]{:S(2)}) collective-permute-start(bf16[2,128,256]{2,1,0:T(8,128)(2,1)S(1)} %get-tuple-element.401), channel_id=1, source_target_pairs={{0,3},{1,2},{2,1},{3,0},{4,7},{5,6},{6,5},{7,4},{8,11},{9,10},{10,... | collective-permute-start | bytes 393224 | tf_op jit(solution)/shard_map/ppermute | solution.py:414
  201.6 8.6 %collective-permute-start.29 = (bf16[2,128,256]{2,1,0:T(8,128)(2,1)S(1)}, bf16[2,128,256]{2,1,0:T(8,128)(2,1)S(1)}, u32[]{:S(2)}, u32[]{:S(2)}) collective-permute-start(bf16[2,128,256]{2,1,0:T(8,128)(2,1)S(1)} %get-tuple-element.401), channel_id=1, source_target_pairs={{0,2},{1,3},{2,0},{3,1},{4,6},{5,7},{6,4},{7,5},{8,10},{9,11},{10,... | collective-permute-start | bytes 393224 | tf_op jit(solution)/shard_map/ppermute | solution.py:414
  204.3 5.9 %collective-permute-start.28 = (bf16[2,128,256]{2,1,0:T(8,128)(2,1)S(1)}, bf16[2,128,256]{2,1,0:T(8,128)(2,1)S(1)}, u32[]{:S(2)}, u32[]{:S(2)}) collective-permute-start(bf16[2,128,256]{2,1,0:T(8,128)(2,1)S(1)} %get-tuple-element.401), channel_id=1, source_target_pairs={{0,1},{1,0},{2,3},{3,2},{4,5},{5,4},{6,7},{7,6},{8,9},{9,8},{10,11... | collective-permute-start | bytes 393224 | tf_op jit(solution)/shard_map/ppermute | solution.py:414
  210.3 14.9 %collective-permute-start.36 = (bf16[4,2,128,256]{3,2,1,0:T(8,128)(2,1)S(1)}, bf16[4,2,128,256]{3,2,1,0:T(8,128)(2,1)S(1)}, u32[]{:S(2)}, u32[]{:S(2)}) collective-permute-start(bf16[4,2,128,256]{3,2,1,0:T(8,128)(2,1)S(1)} %pad_maximum_fusion.1.refs_0_), channel_id=1, source_target_pairs={{0,16},{4,12},{8,24},{12,4},{16,0},{20,28},{24,8},{28,20},{1,17},{... | collective-permute-start | bytes 1572872 | tf_op jit(solution)/shard_map/ppermute | solution.py:434
  210.9 26.7 %collective-permute-start.39 = (bf16[3,704,128]{2,1,0:T(8,128)(2,1)S(1)}, bf16[3,704,128]{2,1,0:T(8,128)(2,1)S(1)}, u32[]{:S(2)}, u32[]{:S(2)}) collective-permute-start(bf16[3,704,128]{2,1,0:T(8,128)(2,1)S(1)} %collective-permute-done.31.refs_1_), channel_id=1, source_target_pairs={{0,8},{4,20},{8,0},{12,28},{16,24},{20,4},{24,16},{28,12},{1,9},{5... | collective-permute-start | bytes 1622024 | tf_op jit(solution)/shard_map/ppermute | solution.py:434
  212.4 15.7 %collective-permute-start.33 = (bf16[3,128,256]{2,1,0:T(8,128)(2,1)S(1)}, bf16[3,128,256]{2,1,0:T(8,128)(2,1)S(1)}, u32[]{:S(2)}, u32[]{:S(2)}) collective-permute-start(bf16[3,128,256]{2,1,0:T(8,128)(2,1)S(1)} %slice_bitcast_fusion), channel_id=1, source_target_pairs={{0,1},{1,0},{2,3},{3,2},{4,5},{5,4},{6,7},{7,6},{8,9},{9,8},{10,11... | collective-permute-start | bytes 589832 | tf_op jit(solution)/shard_map/ppermute | solution.py:414
  212.9 24.7 %collective-permute-start.37 = (bf16[4,2,128,256]{3,2,1,0:T(8,128)(2,1)S(1)}, bf16[4,2,128,256]{3,2,1,0:T(8,128)(2,1)S(1)}, u32[]{:S(2)}, u32[]{:S(2)}) collective-permute-start(bf16[4,2,128,256]{3,2,1,0:T(8,128)(2,1)S(1)} %pad_maximum_fusion.1.refs_0_), channel_id=1, source_target_pairs={{0,8},{4,20},{8,0},{12,28},{16,24},{20,4},{24,16},{28,12},{1,9},{5... | collective-permute-start | bytes 1572872 | tf_op jit(solution)/shard_map/ppermute | solution.py:434
  225.1 12.5 %collective-permute-start.38 = (bf16[4,2,128,256]{3,2,1,0:T(8,128)(2,1)S(1)}, bf16[4,2,128,256]{3,2,1,0:T(8,128)(2,1)S(1)}, u32[]{:S(2)}, u32[]{:S(2)}) collective-permute-start(bf16[4,2,128,256]{3,2,1,0:T(8,128)(2,1)S(1)} %collective-permute-done.36.refs_1_), channel_id=1, source_target_pairs={{0,8},{4,20},{8,0},{12,28},{16,24},{20,4},{24,16},{28,12},{1,9},{5... | collective-permute-start | bytes 1572872 | tf_op jit(solution)/shard_map/ppermute | solution.py:434
  225.7 7.6 %collective-permute-start.35 = (bf16[3,128,256]{2,1,0:T(8,128)(2,1)S(1)}, bf16[3,128,256]{2,1,0:T(8,128)(2,1)S(1)}, u32[]{:S(2)}, u32[]{:S(2)}) collective-permute-start(bf16[3,128,256]{2,1,0:T(8,128)(2,1)S(1)} %slice_bitcast_fusion), channel_id=1, source_target_pairs={{0,3},{1,2},{2,1},{3,0},{4,7},{5,6},{6,5},{7,4},{8,11},{9,10},{10,... | collective-permute-start | bytes 589832 | tf_op jit(solution)/shard_map/ppermute | solution.py:414
  228.1 9.4 %collective-permute-start.34 = (bf16[3,128,256]{2,1,0:T(8,128)(2,1)S(1)}, bf16[3,128,256]{2,1,0:T(8,128)(2,1)S(1)}, u32[]{:S(2)}, u32[]{:S(2)}) collective-permute-start(bf16[3,128,256]{2,1,0:T(8,128)(2,1)S(1)} %slice_bitcast_fusion), channel_id=1, source_target_pairs={{0,2},{1,3},{2,0},{3,1},{4,6},{5,7},{6,4},{7,5},{8,10},{9,11},{10,... | collective-permute-start | bytes 589832 | tf_op jit(solution)/shard_map/ppermute | solution.py:414
  237.6 4.4 %collective-permute-start.42 = (bf16[3,704,128]{2,1,0:T(8,128)(2,1)S(1)}, bf16[3,704,128]{2,1,0:T(8,128)(2,1)S(1)}, u32[]{:S(2)}, u32[]{:S(2)}) collective-permute-start(bf16[3,704,128]{2,1,0:T(8,128)(2,1)S(1)} %add_bitcast_fusion.refs_0_), channel_id=1, source_target_pairs={{0,4},{4,0},{8,12},{12,8},{16,20},{20,16},{24,28},{28,24},{1,5},{5... | collective-permute-start | bytes 1622024 | tf_op jit(solution)/shard_map/ppermute | solution.py:427
  240.4 19.9 %collective-permute-start.41 = (bf16[4,3,128,256]{3,2,1,0:T(8,128)(2,1)S(1)}, bf16[4,3,128,256]{3,2,1,0:T(8,128)(2,1)S(1)}, u32[]{:S(2)}, u32[]{:S(2)}) collective-permute-start(bf16[4,3,128,256]{3,2,1,0:T(8,128)(2,1)S(1)} %pad_maximum_fusion.refs_0_), channel_id=1, source_target_pairs={{0,8},{4,20},{8,0},{12,28},{16,24},{20,4},{24,16},{28,12},{1,9},{5... | collective-permute-start | bytes 2359304 | tf_op jit(solution)/shard_map/ppermute | solution.py:434
  242.0 18.3 %collective-permute-start.40 = (bf16[4,3,128,256]{3,2,1,0:T(8,128)(2,1)S(1)}, bf16[4,3,128,256]{3,2,1,0:T(8,128)(2,1)S(1)}, u32[]{:S(2)}, u32[]{:S(2)}) collective-permute-start(bf16[4,3,128,256]{3,2,1,0:T(8,128)(2,1)S(1)} %pad_maximum_fusion.refs_0_), channel_id=1, source_target_pairs={{0,16},{4,12},{8,24},{12,4},{16,0},{20,28},{24,8},{28,20},{1,17},{... | collective-permute-start | bytes 2359304 | tf_op jit(solution)/shard_map/ppermute | solution.py:434
  242.4 9.8 %collective-permute-start.47 = (bf16[4,2,128,256]{3,2,1,0:T(8,128)(2,1)S(1)}, bf16[4,2,128,256]{3,2,1,0:T(8,128)(2,1)S(1)}, u32[]{:S(2)}, u32[]{:S(2)}) collective-permute-start(bf16[4,2,128,256]{3,2,1,0:T(8,128)(2,1)S(1)} %collective-permute-done.36.refs_1_), channel_id=1, source_target_pairs={{0,4},{4,0},{8,12},{12,8},{16,20},{20,16},{24,28},{28,24},{1,5},{5... | collective-permute-start | bytes 1572872 | tf_op jit(solution)/shard_map/ppermute | solution.py:427
  242.4 9.8 %collective-permute-start.48 = (bf16[4,2,128,256]{3,2,1,0:T(8,128)(2,1)S(1)}, bf16[4,2,128,256]{3,2,1,0:T(8,128)(2,1)S(1)}, u32[]{:S(2)}, u32[]{:S(2)}) collective-permute-start(bf16[4,2,128,256]{3,2,1,0:T(8,128)(2,1)S(1)} %collective-permute-done.37.refs_2_), channel_id=1, source_target_pairs={{0,4},{4,0},{8,12},{12,8},{16,20},{20,16},{24,28},{28,24},{1,5},{5... | collective-permute-start | bytes 1572872 | tf_op jit(solution)/shard_map/ppermute | solution.py:427
  242.9 9.3 %collective-permute-start.49 = (bf16[4,2,128,256]{3,2,1,0:T(8,128)(2,1)S(1)}, bf16[4,2,128,256]{3,2,1,0:T(8,128)(2,1)S(1)}, u32[]{:S(2)}, u32[]{:S(2)}) collective-permute-start(bf16[4,2,128,256]{3,2,1,0:T(8,128)(2,1)S(1)} %collective-permute-done.38.refs_3_), channel_id=1, source_target_pairs={{0,4},{4,0},{8,12},{12,8},{16,20},{20,16},{24,28},{28,24},{1,5},{5... | collective-permute-start | bytes 1572872 | tf_op jit(solution)/shard_map/ppermute | solution.py:427
  260.3 16.3 %collective-permute-start.50 = (bf16[4,3,128,256]{3,2,1,0:T(8,128)(2,1)S(1)}, bf16[4,3,128,256]{3,2,1,0:T(8,128)(2,1)S(1)}, u32[]{:S(2)}, u32[]{:S(2)}) collective-permute-start(bf16[4,3,128,256]{3,2,1,0:T(8,128)(2,1)S(1)} %collective-permute-done.40.refs_1_), channel_id=1, source_target_pairs={{0,8},{4,20},{8,0},{12,28},{16,24},{20,4},{24,16},{28,12},{1,9},{5... | collective-permute-start | bytes 2359304 | tf_op jit(solution)/shard_map/ppermute | solution.py:434
  261.7 11.0 %collective-permute-start.51 = (bf16[128,1024]{1,0:T(8,128)(2,1)S(1)}, bf16[128,1024]{1,0:T(8,128)(2,1)S(1)}, u32[]{:S(2)}, u32[]{:S(2)}) collective-permute-start(bf16[128,1024]{1,0:T(8,128)(2,1)S(1)} %get-tuple-element.370), channel_id=1, source_target_pairs={{0,3},{1,2},{2,1},{3,0},{4,7},{5,6},{6,5},{7,4},{8,11},{9,10},{10,... | collective-permute-start | bytes 786440 | tf_op jit(solution)/shard_map/ppermute | solution.py:414
  264.2 12.3 %collective-permute-start.52 = (bf16[128,1024]{1,0:T(8,128)(2,1)S(1)}, bf16[128,1024]{1,0:T(8,128)(2,1)S(1)}, u32[]{:S(2)}, u32[]{:S(2)}) collective-permute-start(bf16[128,1024]{1,0:T(8,128)(2,1)S(1)} %get-tuple-element.371), channel_id=1, source_target_pairs={{0,1},{1,0},{2,3},{3,2},{4,5},{5,4},{6,7},{7,6},{8,9},{9,8},{10,11... | collective-permute-start | bytes 786440 | tf_op jit(solution)/shard_map/ppermute | solution.py:414
  277.1 5.1 %collective-permute-start.56 = (bf16[4,3,128,256]{3,2,1,0:T(8,128)(2,1)S(1)}, bf16[4,3,128,256]{3,2,1,0:T(8,128)(2,1)S(1)}, u32[]{:S(2)}, u32[]{:S(2)}) collective-permute-start(bf16[4,3,128,256]{3,2,1,0:T(8,128)(2,1)S(1)} %collective-permute-done.50.refs_0_), channel_id=1, source_target_pairs={{0,4},{4,0},{8,12},{12,8},{16,20},{20,16},{24,28},{28,24},{1,5},{5... | collective-permute-start | bytes 2359304 | tf_op jit(solution)/shard_map/ppermute | solution.py:427
  (61 other events, 639.6 us)

commit v6 on v5

--- a/solution.py
+++ b/solution.py
@@ -735,7 +735,7 @@
         ),
         out_shape=[*[sds(five, bf16)] * 2, *[trio_shape] * narrow],
         input_output_aliases={13: 0, 14: 1},
-        compiler_params=budget(56),
+        compiler_params=budget(16),
         cost_estimate=cost(9),
         name="mixer_key_back",
     )(own, coefs, arrived, direct, n1, dq, k, v, kl, gk, gv, tail, live, kept, sent)

time: 286 us -> 284 us (level)
    ppermute x13, starting transfers between devices: 11.9 us -> 14.8 us  [swap_step(): return lax.ppermute(values, 'wide', [(i, flip(i)) for i in range(size)])]
    unnamed x107 -> x111, local copies, waits for them, and re-layouts: 10.5 us -> 10.4 us
  transfers between devices with their start and end apart: 57 -> 57, of which waited for: 22 -> 23; matrix products, arithmetic and copies ran while one was open for 2% -> 2% of each run, Pallas kernels for 21% -> 21%
where the time goes in v6:
time: 284 us
  waiting for transfers between devices  94.8 us (33%)
  Pallas kernels  83.7 us (29%)
  starting transfers between devices  64.7 us (23%)
  blocking collectives  19.8 us (7%)
  local copies, waits for them, and re-layouts  10.8 us (4%)
  other arithmetic  7 us (2%)
    ppermute x27, waiting for transfers between devices, swap_narrow(): return lax.ppermute(values, 'narrow', [(i, i ^ k) for i in range(size)])  64.5 us
    ppermute x27, starting transfers between devices, swap_narrow(): return lax.ppermute(values, 'narrow', [(i, i ^ k) for i in range(size)])  43.5 us
    ppermute x13, waiting for transfers between devices, swap_step(): return lax.ppermute(values, 'wide', [(i, flip(i)) for i in range(size)])  24 us
    pallas_call x7, Pallas kernels, widen(): pl.pallas_call(functools.partial(kernel, places), grid_spec=pltpu.Prefetc...  20.7 us
    pallas_call x2, Pallas kernels, body(): pl.pallas_call(functools.partial(forward_kernel, hn, hd, share), grid_spe...  20.4 us
    all_gather x2, blocking collectives, pass_states(): gathered = lax.all_gather(message, 'wide', axis=0)  19.8 us
    ppermute x13, starting transfers between devices, swap_step(): return lax.ppermute(values, 'wide', [(i, flip(i)) for i in range(size)])  14.8 us
    unnamed x111, local copies, waits for them, and re-layouts  10.4 us
  transfers between devices with their start and end apart: 57, of which 23 were waited for; matrix products, arithmetic and copies ran while one was open for 2% of the time, Pallas kernels for 21%

profile of v6, /device:TPU:0, one launch (start us, length us, event | category | flops | bytes accessed | tf_op | source)
XLA Modules:
  0.0 283.5 jit_solution(3775068118013826440)
XLA Ops:
  0.6 4.1 %collective-permute-start.1 = (bf16[128,1024]{1,0:T(8,128)(2,1)}, bf16[128,1024]{1,0:T(8,128)(2,1)S(1)}, u32[]{:S(2)}, u32[]{:S(2)}) collective-permute-start(bf16[128,1024]{1,0:T(8,128)(2,1)} %refs_9_.1), channel_id=1, source_target_pairs={{0,2},{1,3},{2,0},{3,1},{4,6},{5,7},{6,4},{7,5},{8,10},{9,11},{10,... | collective-permute-start | bytes 786440 | tf_op jit(solution)/shard_map/ppermute | solution.py:414
  8.5 2.1 layout.1
  14.9 2.5 collective-permute-done.tok_b
  18.1 10.3 %mixer_forward_0.1 = (bf16[512,1024]{1,0:T(8,128)(2,1)}, bf16[512,1024]{1,0:T(8,128)(2,1)}, f32[512,1024]{1,0:T(8,128)}, f32[512,1024]{1,0:T(8,128)}, bf16[512,1...) custom-call(s32[2]{0:T(128)} %copy-done.39, ...), custom_call_target="tpu_custom_call" | custom-call | bytes 32000000 | tf_op jit(solution)/shard_map/mixer_forward_0/pallas_call | solution.py:575
  29.9 2.5 collective-permute-start.7
  33.0 10.1 %mixer_forward_1.1 = (bf16[512,1024]{1,0:T(8,128)(2,1)}, bf16[512,1024]{1,0:T(8,128)(2,1)}, f32[512,1024]{1,0:T(8,128)}, f32[512,1024]{1,0:T(8,128)}, bf16[512,1...) custom-call(s32[2]{0:T(128)} %copy-done.39, ...), custom_call_target="tpu_custom_call", output_to_operand_aliasing={{0}: (11, {}), {1}: (12, {}), {2}: (13, {}), {3}: (14, {}),... | custom-call | bytes 32000000 | tf_op jit(solution)/shard_map/mixer_forward_1/pallas_call | solution.py:575
  48.4 10.0 %all-gather = bf16[16,128,128]{2,1,0:T(8,128)(2,1)S(1)} all-gather(bf16[2,128,128]{2,1,0:T(8,128)(2,1)S(1)} %multiply_reduce_fusion), channel_id=2, replica_groups=mesh['wide'=8,'narrow'=4] {'wide'}, dimensions={0}, use_global_device_ids=true | all-gather | bytes 589824 | tf_op jit(solution)/shard_map/all_gather | solution.py:533
  63.7 2.4 collective-permute-done.11.refs_3_
  66.0 2.6 collective-permute-done.10.refs_2_
  69.3 9.1 %mixer_out.1 = (bf16[512,1024]{1,0:T(8,128)(2,1)}, f32[512,1]{1,0:T(8,128)}, bf16[512,1024]{1,0:T(8,128)(2,1)}, f32[128,1024]{1,0:T(8,128)}, bf16[512,1024]{1,0:...) custom-call(s32[2]{0:T(128)} %copy-done.39, f32[5,2,8]{2,1,0:T(2,128)} %copy-done.43, bf16[2,128,128]{2,1,0:T(8,128)(2,1)} %copy-done.49, ...), custom_call_target="tpu_custom_call" | custom-call | bytes 30400000 | tf_op jit(solution)/shard_map/mixer_out/pallas_call | solution.py:610
  79.6 5.7 %ffn.1 = (bf16[512,704]{1,0:T(8,128)(2,1)S(1)}, bf16[512,704]{1,0:T(8,128)(2,1)S(1)}, bf16[512,704]{1,0:T(8,128)(2,1)S(1)}, bf16[128,1024]{1,0:T(8,128)(2,1)S(1)...) custom-call(bf16[512,1024]{1,0:T(8,128)(2,1)S(1)} %copy-done.14, ...), custom_call_target="tpu_custom_call" | custom-call | bytes 32000000 | tf_op jit(solution)/shard_map/ffn/pallas_call | solution.py:631
  87.2 2.5 collective-permute-start.14
  89.7 8.0 %collective-permute-done.12.refs_1_ = bf16[128,1024]{1,0:T(8,128)(2,1)S(1)} collective-permute-done((bf16[128,1024]{1,0:T(8,128)(2,1)S(1)}, bf16[128,1024]{1,0:T(8,128)(2,1)S(1)}, u32[]{:S(2)}, u32[]{:S(2)}) %collective-permute-start.12) | collective-permute-done | bytes 262176 | tf_op jit(solution)/shard_map/ppermute | solution.py:414
  97.7 6.1 %ffn_grads.1 = (bf16[4,3,704,128]{3,2,1,0:T(8,128)(2,1)S(1)}, bf16[4,3,704,128]{3,2,1,0:T(8,128)(2,1)S(1)}, bf16[128,1024]{1,0:T(8,128)(2,1)S(1)}, bf16[128,1024...) custom-call(s32[2]{0:T(128)S(1)} %copy-done.40, bf16[512,1024]{1,0:T(8,128)(2,1)S(1)} %copy-done.15, ...), custom_call_target="tpu_custom_call" | custom-call | bytes 32000000 | tf_op jit(solution)/shard_map/ffn_grads/pallas_call | solution.py:644
  103.9 2.9 %collective-permute-done.13.refs_2_ = bf16[128,1024]{1,0:T(8,128)(2,1)S(1)} collective-permute-done((bf16[128,1024]{1,0:T(8,128)(2,1)S(1)}, bf16[128,1024]{1,0:T(8,128)(2,1)S(1)}, u32[]{:S(2)}, u32[]{:S(2)}) %collective-permute-start.13) | collective-permute-done | bytes 262176 | tf_op jit(solution)/shard_map/ppermute | solution.py:414
  106.8 2.2 residual_back.1
  109.6 4.9 %collective-permute-start.15 = (bf16[128,768]{1,0:T(8,128)(2,1)S(1)}, bf16[128,768]{1,0:T(8,128)(2,1)S(1)}, u32[]{:S(2)}, u32[]{:S(2)}) collective-permute-start(bf16[128,768]{1,0:T(8,128)(2,1)S(1)} %get-tuple-element.268), channel_id=1, source_target_pairs={{0,1},{1,0},{2,3},{3,2},{4,5},{5,4},{6,7},{7,6},{8,9},{9,8},{10,11... | collective-permute-start | bytes 589832 | tf_op jit(solution)/shard_map/ppermute | solution.py:414
  114.6 2.4 collective-permute-start.17
  117.0 6.2 %collective-permute-done.15.refs_1_ = bf16[128,768]{1,0:T(8,128)(2,1)S(1)} collective-permute-done((bf16[128,768]{1,0:T(8,128)(2,1)S(1)}, bf16[128,768]{1,0:T(8,128)(2,1)S(1)}, u32[]{:S(2)}, u32[]{:S(2)}) %collective-permute-start.15) | collective-permute-done | bytes 196640 | tf_op jit(solution)/shard_map/ppermute | solution.py:414
  123.2 8.6 %collective-permute-done.16.refs_2_ = bf16[128,768]{1,0:T(8,128)(2,1)S(1)} collective-permute-done((bf16[128,768]{1,0:T(8,128)(2,1)S(1)}, bf16[128,768]{1,0:T(8,128)(2,1)S(1)}, u32[]{:S(2)}, u32[]{:S(2)}) %collective-permute-start.16) | collective-permute-done | bytes 196640 | tf_op jit(solution)/shard_map/ppermute | solution.py:414
  133.9 3.9 %collective-permute-start.20 = (bf16[128,1024]{1,0:T(8,128)(2,1)S(1)}, bf16[128,1024]{1,0:T(8,128)(2,1)S(1)}, u32[]{:S(2)}, u32[]{:S(2)}) collective-permute-start(bf16[128,1024]{1,0:T(8,128)(2,1)S(1)} %get-tuple-element.288), channel_id=1, source_target_pairs={{0,2},{1,3},{2,0},{3,1},{4,6},{5,7},{6,4},{7,5},{8,10},{9,11},{10,... | collective-permute-start | bytes 786440 | tf_op jit(solution)/shard_map/ppermute | solution.py:414
  138.0 5.6 %mixer_query_back.1 = (bf16[512,256]{1,0:T(8,128)(2,1)}, f32[512,256]{1,0:T(8,128)}, f32[512,256]{1,0:T(8,128)}, f32[2,2,128,128]{3,2,1,0:T(8,128)}, f32[2,128,128]{2,1,0:T(8,128)}) custom-call(s32[2]{0:T(128)} %copy-done.39, f32[5,2,8]{2,1,0:T(2,128)} %copy-done.43, bf16[128,768]{1,0:T(8,128)(2,1)} %copy-done.26, bf16[128,768]{1,0:T(8,128)(2,1)} %copy-done.28, ...), custom_call_target="tpu_custom_call" | custom-call | bytes 17280000 | tf_op jit(solution)/shard_map/mixer_query_back/pallas_call | solution.py:687
  144.7 2.0 gate_back.1
  146.8 9.8 %all-gather.1 = bf16[16,128,128]{2,1,0:T(8,128)(2,1)S(1)} all-gather(bf16[2,128,128]{2,1,0:T(8,128)(2,1)S(1)} %convert_element_type.29), channel_id=3, replica_groups=mesh['wide'=8,'narrow'=4] {'wide'}, dimensions={0}, use_global_device_ids=true | all-gather | bytes 589824 | tf_op jit(solution)/shard_map/all_gather | solution.py:533
  158.9 3.8 %mixer_key_back.1 = (bf16[4,5,128,256]{3,2,1,0:T(8,128)(2,1)S(1)}, bf16[4,5,128,256]{3,2,1,0:T(8,128)(2,1)S(1)}, bf16[128,768]{1,0:T(8,128)(2,1)S(1)}, bf16[128,...) custom-call(s32[2]{0:T(128)S(1)} %copy-done.41, ...), custom_call_target="tpu_custom_call", output_to_operand_aliasing={{0}: (13, {}), {1}: (14, {})} | custom-call | bytes 28800000 | tf_op jit(solution)/shard_map/mixer_key_back/pallas_call | solution.py:726
  168.5 2.5 collective-permute-start.24
  172.4 5.5 %collective-permute-done.23.refs_1_ = bf16[128,768]{1,0:T(8,128)(2,1)S(1)} collective-permute-done((bf16[128,768]{1,0:T(8,128)(2,1)S(1)}, bf16[128,768]{1,0:T(8,128)(2,1)S(1)}, u32[]{:S(2)}, u32[]{:S(2)}) %collective-permute-start.23) | collective-permute-done | bytes 196640 | tf_op jit(solution)/shard_map/ppermute | solution.py:414
  177.9 7.7 %collective-permute-done.24.refs_2_ = bf16[128,768]{1,0:T(8,128)(2,1)S(1)} collective-permute-done((bf16[128,768]{1,0:T(8,128)(2,1)S(1)}, bf16[128,768]{1,0:T(8,128)(2,1)S(1)}, u32[]{:S(2)}, u32[]{:S(2)}) %collective-permute-start.24) | collective-permute-done | bytes 196640 | tf_op jit(solution)/shard_map/ppermute | solution.py:414
  190.9 5.5 %collective-permute-done.27 = bf16[1,5,128,256]{3,2,1,0:T(8,128)(2,1)S(1)} collective-permute-done((bf16[1,5,128,256]{3,2,1,0:T(8,128)(2,1)S(1)}, bf16[1,5,128,256]{3,2,1,0:T(8,128)(2,1)S(1)}, u32[]{:S(2)}, u32[]{:S(2)}) %collective-permute-start.27) | collective-permute-done | bytes 327712 | tf_op jit(solution)/shard_map/ppermute | solution.py:434
  198.4 2.4 collective-permute-start.29
  201.2 2.2 collective-permute-done.30
  203.4 4.1 %collective-permute-done.29 = bf16[2,128,256]{2,1,0:T(8,128)(2,1)S(1)} collective-permute-done((bf16[2,128,256]{2,1,0:T(8,128)(2,1)S(1)}, bf16[2,128,256]{2,1,0:T(8,128)(2,1)S(1)}, u32[]{:S(2)}, u32[]{:S(2)}) %collective-permute-start.29) | collective-permute-done | bytes 131104 | tf_op jit(solution)/shard_map/ppermute | solution.py:414
  207.6 2.1 collective-permute-start.36
  211.7 10.8 %collective-permute-done.36.refs_1_ = bf16[4,2,128,256]{3,2,1,0:T(8,128)(2,1)S(1)} collective-permute-done((bf16[4,2,128,256]{3,2,1,0:T(8,128)(2,1)S(1)}, bf16[4,2,128,256]{3,2,1,0:T(8,128)(2,1)S(1)}, u32[]{:S(2)}, u32[]{:S(2)}) %collective-permute-start.36) | collective-permute-done | bytes 524320 | tf_op jit(solution)/shard_map/ppermute | solution.py:434
  222.5 2.0 collective-permute-start.38
  225.9 5.1 %tokens_back.1 = f32[128,1024]{1,0:T(8,128)} custom-call(s32[2]{0:T(128)S(1)} %copy-done.41, bf16[128,768]{1,0:T(8,128)(2,1)S(1)} %get-tuple-element.329.refs_0_, bf16[128,768]{1,0:T(8,128)(2,1)S(1)} %collective-permute-done.23.refs_1_, bf16[128,768]{1,0:T(8,128)(2,1)S(1)} %collective-permute-done.24.refs_2_, ...), custom_call_target="tpu_custom_call" | custom-call | bytes 25600000 | tf_op jit(solution)/shard_map/tokens_back/pallas_call | solution.py:776
  232.0 4.1 %collective-permute-done.34 = bf16[3,128,256]{2,1,0:T(8,128)(2,1)S(1)} collective-permute-done((bf16[3,128,256]{2,1,0:T(8,128)(2,1)S(1)}, bf16[3,128,256]{2,1,0:T(8,128)(2,1)S(1)}, u32[]{:S(2)}, u32[]{:S(2)}) %collective-permute-start.34) | collective-permute-done | bytes 196640 | tf_op jit(solution)/shard_map/ppermute | solution.py:414
  239.0 2.0 collective-permute-start.40
  241.6 3.0 %widen_gate_0.1 = (f32[1024,1024]{1,0:T(8,128)}, f32[1024,1024]{1,0:T(8,128)}) custom-call(s32[2]{0:T(128)S(1)} %copy-done.41, bf16[4,2,128,256]{3,2,1,0:T(8,128)(2,1)S(1)} %pad_maximum_fusion.1.refs_0_, bf16[4,2,128,256]{3,2,1,0:T(8,128)(2,1)S(1)} %collective-permute-done.36.refs_1_, bf16[4,2,128,256]{3,2,1,0:T(8,128)(2,1)S(1)} %collective-permute-done.37.refs_2_, ...), custom_call_target="tpu_custom_call" | custom-call | bytes 12800000 | tf_op jit(solution)/shard_map/widen_gate_0/pallas_call | solution.py:484
  244.7 3.1 %widen_ffn_0.1 = (f32[704,1024]{1,0:T(8,128)}, f32[704,1024]{1,0:T(8,128)}, f32[704,1024]{1,0:T(8,128)}) custom-call(s32[2]{0:T(128)S(1)} %copy-done.41, bf16[3,704,128]{2,1,0:T(8,128)(2,1)S(1)} %add_bitcast_fusion.refs_0_, bf16[3,704,128]{2,1,0:T(8,128)(2,1)S(1)} %collective-permute-done.31.refs_1_, ...), custom_call_target="tpu_custom_call" | custom-call | bytes 12800000 | tf_op jit(solution)/shard_map/widen_ffn_0/pallas_call | solution.py:484
  247.8 3.1 %widen_ffn_1.1 = (f32[704,1024]{1,0:T(8,128)}, f32[704,1024]{1,0:T(8,128)}, f32[704,1024]{1,0:T(8,128)}) custom-call(s32[2]{0:T(128)S(1)} %copy-done.41, bf16[3,704,128]{2,1,0:T(8,128)(2,1)S(1)} %collective-permute-done.42.refs_0_, ...), custom_call_target="tpu_custom_call", output_to_operand_aliasing={{0}: (5, {}), {1}: (6, {}), {2}: (7, {})} | custom-call | bytes 12800000 | tf_op jit(solution)/shard_map/widen_ffn_1/pallas_call | solution.py:484
  250.9 7.7 %collective-permute-done.41.refs_2_ = bf16[4,3,128,256]{3,2,1,0:T(8,128)(2,1)S(1)} collective-permute-done((bf16[4,3,128,256]{3,2,1,0:T(8,128)(2,1)S(1)}, bf16[4,3,128,256]{3,2,1,0:T(8,128)(2,1)S(1)}, u32[]{:S(2)}, u32[]{:S(2)}) %collective-permute-start.41) | collective-permute-done | bytes 786464 | tf_op jit(solution)/shard_map/ppermute | solution.py:434
  258.9 2.6 collective-permute-start.51
  261.5 3.1 %widen_square_0.1 = (f32[1024,1024]{1,0:T(8,128)}, f32[1024,1024]{1,0:T(8,128)}, f32[1024,1024]{1,0:T(8,128)}) custom-call(s32[2]{0:T(128)S(1)} %copy-done.41, bf16[4,3,128,256]{3,2,1,0:T(8,128)(2,1)S(1)} %pad_maximum_fusion.refs_0_, bf16[4,3,128,256]{3,2,1,0:T(8,128)(2,1)S(1)} %collective-permute-done.40.refs_1_, ...), custom_call_target="tpu_custom_call" | custom-call | bytes 12800000 | tf_op jit(solution)/shard_map/widen_square_0/pallas_call | solution.py:484
  264.6 3.0 %widen_gate_1.1 = (f32[1024,1024]{1,0:T(8,128)}, f32[1024,1024]{1,0:T(8,128)}) custom-call(s32[2]{0:T(128)S(1)} %copy-done.41, bf16[4,2,128,256]{3,2,1,0:T(8,128)(2,1)S(1)} %collective-permute-done.46.refs_0_, bf16[4,2,128,256]{3,2,1,0:T(8,128)(2,1)S(1)} %collective-permute-done.47.refs_1_, ...), custom_call_target="tpu_custom_call", output_to_operand_aliasing={{0}: (5, {}), {1}: (6, {})} | custom-call | bytes 12800000 | tf_op jit(solution)/shard_map/widen_gate_1/pallas_call | solution.py:484
  267.6 2.3 collective-permute-done.51.refs_3_
  269.9 4.3 %collective-permute-done.52.refs_1_ = bf16[128,1024]{1,0:T(8,128)(2,1)S(1)} collective-permute-done((bf16[128,1024]{1,0:T(8,128)(2,1)S(1)}, bf16[128,1024]{1,0:T(8,128)(2,1)S(1)}, u32[]{:S(2)}, u32[]{:S(2)}) %collective-permute-start.52) | collective-permute-done | bytes 262176 | tf_op jit(solution)/shard_map/ppermute | solution.py:414
  279.9 3.6 %widen_square_1.1 = (f32[1024,1024]{1,0:T(8,128)}, f32[1024,1024]{1,0:T(8,128)}, f32[1024,1024]{1,0:T(8,128)}) custom-call(s32[2]{0:T(128)S(1)} %copy-done.41, bf16[4,3,128,256]{3,2,1,0:T(8,128)(2,1)S(1)} %collective-permute-done.53.refs_0_, ...), custom_call_target="tpu_custom_call", output_to_operand_aliasing={{0}: (5, {}), {1}: (6, {}), {2}: (7, {})} | custom-call | bytes 12800000 | tf_op jit(solution)/shard_map/widen_square_1/pallas_call | solution.py:484
  (233 shorter events, 58.4 us)
Async XLA Ops:
  0.6 27.9 %collective-permute-start.1 = (bf16[128,1024]{1,0:T(8,128)(2,1)}, bf16[128,1024]{1,0:T(8,128)(2,1)S(1)}, u32[]{:S(2)}, u32[]{:S(2)}) collective-permute-start(bf16[128,1024]{1,0:T(8,128)(2,1)} %refs_9_.1), channel_id=1, source_target_pairs={{0,2},{1,3},{2,0},{3,1},{4,6},{5,7},{6,4},{7,5},{8,10},{9,11},{10,... | collective-permute-start | bytes 786440 | tf_op jit(solution)/shard_map/ppermute | solution.py:414
  4.8 12.7 %collective-permute-start = (bf16[128,1024]{1,0:T(8,128)(2,1)}, bf16[128,1024]{1,0:T(8,128)(2,1)S(1)}, u32[]{:S(2)}, u32[]{:S(2)}) collective-permute-start(bf16[128,1024]{1,0:T(8,128)(2,1)} %refs_9_.1), channel_id=1, source_target_pairs={{0,1},{1,0},{2,3},{3,2},{4,5},{5,4},{6,7},{7,6},{8,9},{9,8},{10,11... | collective-permute-start | bytes 786440 | tf_op jit(solution)/shard_map/ppermute | solution.py:414
  6.3 22.2 %collective-permute-start.2 = (bf16[128,1024]{1,0:T(8,128)(2,1)}, bf16[128,1024]{1,0:T(8,128)(2,1)S(1)}, u32[]{:S(2)}, u32[]{:S(2)}) collective-permute-start(bf16[128,1024]{1,0:T(8,128)(2,1)} %refs_9_.1), channel_id=1, source_target_pairs={{0,3},{1,2},{2,1},{3,0},{4,7},{5,6},{6,5},{7,4},{8,11},{9,10},{10,... | collective-permute-start | bytes 786440 | tf_op jit(solution)/shard_map/ppermute | solution.py:414
  28.5 30.5 %collective-permute-start.8 = (bf16[128,1024]{1,0:T(8,128)(2,1)S(1)}, bf16[128,1024]{1,0:T(8,128)(2,1)S(1)}, u32[]{:S(2)}, u32[]{:S(2)}) collective-permute-start(bf16[128,1024]{1,0:T(8,128)(2,1)S(1)} %copy-done.25), channel_id=1, source_target_pairs={{0,3},{1,2},{2,1},{3,0},{4,7},{5,6},{6,5},{7,4},{8,11},{9,10},{10,... | collective-permute-start | bytes 786440 | tf_op jit(solution)/shard_map/ppermute | solution.py:414
  29.9 29.2 %collective-permute-start.7 = (bf16[128,1024]{1,0:T(8,128)(2,1)S(1)}, bf16[128,1024]{1,0:T(8,128)(2,1)S(1)}, u32[]{:S(2)}, u32[]{:S(2)}) collective-permute-start(bf16[128,1024]{1,0:T(8,128)(2,1)S(1)} %copy-done.25), channel_id=1, source_target_pairs={{0,2},{1,3},{2,0},{3,1},{4,6},{5,7},{6,4},{7,5},{8,10},{9,11},{10,... | collective-permute-start | bytes 786440 | tf_op jit(solution)/shard_map/ppermute | solution.py:414
  32.5 26.6 %collective-permute-start.6 = (bf16[128,1024]{1,0:T(8,128)(2,1)S(1)}, bf16[128,1024]{1,0:T(8,128)(2,1)S(1)}, u32[]{:S(2)}, u32[]{:S(2)}) collective-permute-start(bf16[128,1024]{1,0:T(8,128)(2,1)S(1)} %copy-done.25), channel_id=1, source_target_pairs={{0,1},{1,0},{2,3},{3,2},{4,5},{5,4},{6,7},{7,6},{8,9},{9,8},{10,11... | collective-permute-start | bytes 786440 | tf_op jit(solution)/shard_map/ppermute | solution.py:414
  33.0 10.1 %collective-permute-start.3 = (f32[1,8]{1,0:T(1,128)S(1)}, f32[1,8]{1,0:T(1,128)S(1)}, u32[]{:S(2)}, u32[]{:S(2)}) collective-permute-start(f32[1,8]{1,0:T(1,128)S(1)} %get-tuple-element.218), channel_id=1, source_target_pairs={{0,4},{4,0},{8,12},{12,8},{16,20},{20,16},{24,28},{28,24},{1,5},{5... | collective-permute-start | bytes 104 | tf_op jit(solution)/shard_map/ppermute | solution.py:515
  46.8 11.6 %collective-permute-start.5 = (f32[4,8]{1,0:T(4,128)S(1)}, f32[4,8]{1,0:T(4,128)S(1)}, u32[]{:S(2)}, u32[]{:S(2)}) collective-permute-start(f32[4,8]{1,0:T(4,128)S(1)} %pad_maximum_fusion.3), channel_id=1, source_target_pairs={{0,16},{4,20},{8,24},{12,28},{16,0},{20,4},{24,8},{28,12},{1,17},{... | collective-permute-start | bytes 392 | tf_op jit(solution)/shard_map/ppermute | solution.py:515
  59.1 6.9 %collective-permute-start.11 = (bf16[2,128,128]{2,1,0:T(8,128)(2,1)S(1)}, bf16[2,128,128]{2,1,0:T(8,128)(2,1)S(1)}, u32[]{:S(2)}, u32[]{:S(2)}) collective-permute-start(bf16[2,128,128]{2,1,0:T(8,128)(2,1)S(1)} %fusion.1.refs_0_), channel_id=1, source_target_pairs={{0,3},{1,2},{2,1},{3,0},{4,7},{5,6},{6,5},{7,4},{8,11},{9,10},{10,... | collective-permute-start | bytes 196616 | tf_op jit(solution)/shard_map/ppermute | solution.py:414
  60.5 8.2 %collective-permute-start.10 = (bf16[2,128,128]{2,1,0:T(8,128)(2,1)S(1)}, bf16[2,128,128]{2,1,0:T(8,128)(2,1)S(1)}, u32[]{:S(2)}, u32[]{:S(2)}) collective-permute-start(bf16[2,128,128]{2,1,0:T(8,128)(2,1)S(1)} %fusion.1.refs_0_), channel_id=1, source_target_pairs={{0,2},{1,3},{2,0},{3,1},{4,6},{5,7},{6,4},{7,5},{8,10},{9,11},{10,... | collective-permute-start | bytes 196616 | tf_op jit(solution)/shard_map/ppermute | solution.py:414
  62.1 6.5 %collective-permute-start.9 = (bf16[2,128,128]{2,1,0:T(8,128)(2,1)S(1)}, bf16[2,128,128]{2,1,0:T(8,128)(2,1)S(1)}, u32[]{:S(2)}, u32[]{:S(2)}) collective-permute-start(bf16[2,128,128]{2,1,0:T(8,128)(2,1)S(1)} %fusion.1.refs_0_), channel_id=1, source_target_pairs={{0,1},{1,0},{2,3},{3,2},{4,5},{5,4},{6,7},{7,6},{8,9},{9,8},{10,11... | collective-permute-start | bytes 196616 | tf_op jit(solution)/shard_map/ppermute | solution.py:414
  85.3 12.4 %collective-permute-start.12 = (bf16[128,1024]{1,0:T(8,128)(2,1)S(1)}, bf16[128,1024]{1,0:T(8,128)(2,1)S(1)}, u32[]{:S(2)}, u32[]{:S(2)}) collective-permute-start(bf16[128,1024]{1,0:T(8,128)(2,1)S(1)} %get-tuple-element.245), channel_id=1, source_target_pairs={{0,1},{1,0},{2,3},{3,2},{4,5},{5,4},{6,7},{7,6},{8,9},{9,8},{10,11... | collective-permute-start | bytes 786440 | tf_op jit(solution)/shard_map/ppermute | solution.py:414
  85.4 21.4 %collective-permute-start.13 = (bf16[128,1024]{1,0:T(8,128)(2,1)S(1)}, bf16[128,1024]{1,0:T(8,128)(2,1)S(1)}, u32[]{:S(2)}, u32[]{:S(2)}) collective-permute-start(bf16[128,1024]{1,0:T(8,128)(2,1)S(1)} %get-tuple-element.246), channel_id=1, source_target_pairs={{0,2},{1,3},{2,0},{3,1},{4,6},{5,7},{6,4},{7,5},{8,10},{9,11},{10,... | collective-permute-start | bytes 786440 | tf_op jit(solution)/shard_map/ppermute | solution.py:414
  87.2 19.5 %collective-permute-start.14 = (bf16[128,1024]{1,0:T(8,128)(2,1)S(1)}, bf16[128,1024]{1,0:T(8,128)(2,1)S(1)}, u32[]{:S(2)}, u32[]{:S(2)}) collective-permute-start(bf16[128,1024]{1,0:T(8,128)(2,1)S(1)} %get-tuple-element.247), channel_id=1, source_target_pairs={{0,3},{1,2},{2,1},{3,0},{4,7},{5,6},{6,5},{7,4},{8,11},{9,10},{10,... | collective-permute-start | bytes 786440 | tf_op jit(solution)/shard_map/ppermute | solution.py:414
  109.6 22.1 %collective-permute-start.18 = (bf16[4,3,704,128]{3,2,1,0:T(8,128)(2,1)S(1)}, bf16[4,3,704,128]{3,2,1,0:T(8,128)(2,1)S(1)}, u32[]{:S(2)}, u32[]{:S(2)}) collective-permute-start(bf16[4,3,704,128]{3,2,1,0:T(8,128)(2,1)S(1)} %get-tuple-element.272), channel_id=1, source_target_pairs={{0,4},{4,0},{8,12},{12,8},{16,20},{20,16},{24,28},{28,24},{1,5},{5... | collective-permute-start | bytes 6488072 | tf_op jit(solution)/shard_map/ppermute | solution.py:427
  109.6 13.5 %collective-permute-start.15 = (bf16[128,768]{1,0:T(8,128)(2,1)S(1)}, bf16[128,768]{1,0:T(8,128)(2,1)S(1)}, u32[]{:S(2)}, u32[]{:S(2)}) collective-permute-start(bf16[128,768]{1,0:T(8,128)(2,1)S(1)} %get-tuple-element.268), channel_id=1, source_target_pairs={{0,1},{1,0},{2,3},{3,2},{4,5},{5,4},{6,7},{7,6},{8,9},{9,8},{10,11... | collective-permute-start | bytes 589832 | tf_op jit(solution)/shard_map/ppermute | solution.py:414
  114.6 17.1 %collective-permute-start.16 = (bf16[128,768]{1,0:T(8,128)(2,1)S(1)}, bf16[128,768]{1,0:T(8,128)(2,1)S(1)}, u32[]{:S(2)}, u32[]{:S(2)}) collective-permute-start(bf16[128,768]{1,0:T(8,128)(2,1)S(1)} %get-tuple-element.269), channel_id=1, source_target_pairs={{0,2},{1,3},{2,0},{3,1},{4,6},{5,7},{6,4},{7,5},{8,10},{9,11},{10,... | collective-permute-start | bytes 589832 | tf_op jit(solution)/shard_map/ppermute | solution.py:414
  114.6 17.1 %collective-permute-start.17 = (bf16[128,768]{1,0:T(8,128)(2,1)S(1)}, bf16[128,768]{1,0:T(8,128)(2,1)S(1)}, u32[]{:S(2)}, u32[]{:S(2)}) collective-permute-start(bf16[128,768]{1,0:T(8,128)(2,1)S(1)} %get-tuple-element.270), channel_id=1, source_target_pairs={{0,3},{1,2},{2,1},{3,0},{4,7},{5,6},{6,5},{7,4},{8,11},{9,10},{10,... | collective-permute-start | bytes 589832 | tf_op jit(solution)/shard_map/ppermute | solution.py:414
  133.3 23.4 %collective-permute-start.19 = (bf16[2,3,704,128]{3,2,1,0:T(8,128)(2,1)}, bf16[2,3,704,128]{3,2,1,0:T(8,128)(2,1)}, u32[]{:S(2)}, u32[]{:S(2)}) collective-permute-start(bf16[2,3,704,128]{3,2,1,0:T(8,128)(2,1)} %get-tuple-element.396), channel_id=1, source_target_pairs={{0,8},{4,20},{8,0},{12,28},{16,24},{20,4},{24,16},{28,12},{1,9},{5... | collective-permute-start | bytes 3244040 | tf_op jit(solution)/shard_map/ppermute | solution.py:434
  133.9 22.8 %collective-permute-start.20 = (bf16[128,1024]{1,0:T(8,128)(2,1)S(1)}, bf16[128,1024]{1,0:T(8,128)(2,1)S(1)}, u32[]{:S(2)}, u32[]{:S(2)}) collective-permute-start(bf16[128,1024]{1,0:T(8,128)(2,1)S(1)} %get-tuple-element.288), channel_id=1, source_target_pairs={{0,2},{1,3},{2,0},{3,1},{4,6},{5,7},{6,4},{7,5},{8,10},{9,11},{10,... | collective-permute-start | bytes 786440 | tf_op jit(solution)/shard_map/ppermute | solution.py:414
  165.9 19.7 %collective-permute-start.22 = (bf16[2,5,128,256]{3,2,1,0:T(8,128)(2,1)S(1)}, bf16[2,5,128,256]{3,2,1,0:T(8,128)(2,1)S(1)}, u32[]{:S(2)}, u32[]{:S(2)}) collective-permute-start(bf16[2,5,128,256]{3,2,1,0:T(8,128)(2,1)S(1)} %get-tuple-element.308), channel_id=1, source_target_pairs={{0,8},{4,20},{8,0},{12,28},{16,24},{20,4},{24,16},{28,12},{1,9},{5... | collective-permute-start | bytes 1966088 | tf_op jit(solution)/shard_map/ppermute | solution.py:434
  166.5 19.1 %collective-permute-start.26 = (bf16[1,3,704,128]{3,2,1,0:T(8,128)(2,1)S(1)}, bf16[1,3,704,128]{3,2,1,0:T(8,128)(2,1)S(1)}, u32[]{:S(2)}, u32[]{:S(2)}) collective-permute-start(bf16[1,3,704,128]{3,2,1,0:T(8,128)(2,1)S(1)} %slice_add_fusion.4), channel_id=1, source_target_pairs={{0,16},{4,12},{8,24},{12,4},{16,0},{20,28},{24,8},{28,20},{1,17},{... | collective-permute-start | bytes 1622024 | tf_op jit(solution)/shard_map/ppermute | solution.py:434
  168.0 9.9 %collective-permute-start.23 = (bf16[128,768]{1,0:T(8,128)(2,1)S(1)}, bf16[128,768]{1,0:T(8,128)(2,1)S(1)}, u32[]{:S(2)}, u32[]{:S(2)}) collective-permute-start(bf16[128,768]{1,0:T(8,128)(2,1)S(1)} %get-tuple-element.310), channel_id=1, source_target_pairs={{0,1},{1,0},{2,3},{3,2},{4,5},{5,4},{6,7},{7,6},{8,9},{9,8},{10,11... | collective-permute-start | bytes 589832 | tf_op jit(solution)/shard_map/ppermute | solution.py:414
  168.5 17.1 %collective-permute-start.24 = (bf16[128,768]{1,0:T(8,128)(2,1)S(1)}, bf16[128,768]{1,0:T(8,128)(2,1)S(1)}, u32[]{:S(2)}, u32[]{:S(2)}) collective-permute-start(bf16[128,768]{1,0:T(8,128)(2,1)S(1)} %get-tuple-element.311), channel_id=1, source_target_pairs={{0,2},{1,3},{2,0},{3,1},{4,6},{5,7},{6,4},{7,5},{8,10},{9,11},{10,... | collective-permute-start | bytes 589832 | tf_op jit(solution)/shard_map/ppermute | solution.py:414
  171.0 14.6 %collective-permute-start.25 = (bf16[128,768]{1,0:T(8,128)(2,1)S(1)}, bf16[128,768]{1,0:T(8,128)(2,1)S(1)}, u32[]{:S(2)}, u32[]{:S(2)}) collective-permute-start(bf16[128,768]{1,0:T(8,128)(2,1)S(1)} %get-tuple-element.312), channel_id=1, source_target_pairs={{0,3},{1,2},{2,1},{3,0},{4,7},{5,6},{6,5},{7,4},{8,11},{9,10},{10,... | collective-permute-start | bytes 589832 | tf_op jit(solution)/shard_map/ppermute | solution.py:414
  185.7 10.6 %collective-permute-start.27 = (bf16[1,5,128,256]{3,2,1,0:T(8,128)(2,1)S(1)}, bf16[1,5,128,256]{3,2,1,0:T(8,128)(2,1)S(1)}, u32[]{:S(2)}, u32[]{:S(2)}) collective-permute-start(bf16[1,5,128,256]{3,2,1,0:T(8,128)(2,1)S(1)} %slice_add_fusion.5), channel_id=1, source_target_pairs={{0,16},{4,12},{8,24},{12,4},{16,0},{20,28},{24,8},{28,20},{1,17},{... | collective-permute-start | bytes 983048 | tf_op jit(solution)/shard_map/ppermute | solution.py:434
  188.8 18.8 %collective-permute-start.32 = (bf16[3,704,128]{2,1,0:T(8,128)(2,1)S(1)}, bf16[3,704,128]{2,1,0:T(8,128)(2,1)S(1)}, u32[]{:S(2)}, u32[]{:S(2)}) collective-permute-start(bf16[3,704,128]{2,1,0:T(8,128)(2,1)S(1)} %add_bitcast_fusion.refs_0_), channel_id=1, source_target_pairs={{0,8},{4,20},{8,0},{12,28},{16,24},{20,4},{24,16},{28,12},{1,9},{5... | collective-permute-start | bytes 1622024 | tf_op jit(solution)/shard_map/ppermute | solution.py:434
  189.2 18.4 %collective-permute-start.31 = (bf16[3,704,128]{2,1,0:T(8,128)(2,1)S(1)}, bf16[3,704,128]{2,1,0:T(8,128)(2,1)S(1)}, u32[]{:S(2)}, u32[]{:S(2)}) collective-permute-start(bf16[3,704,128]{2,1,0:T(8,128)(2,1)S(1)} %add_bitcast_fusion.refs_0_), channel_id=1, source_target_pairs={{0,16},{4,12},{8,24},{12,4},{16,0},{20,28},{24,8},{28,20},{1,17},{... | collective-permute-start | bytes 1622024 | tf_op jit(solution)/shard_map/ppermute | solution.py:434
  196.4 6.9 %collective-permute-start.30 = (bf16[2,128,256]{2,1,0:T(8,128)(2,1)S(1)}, bf16[2,128,256]{2,1,0:T(8,128)(2,1)S(1)}, u32[]{:S(2)}, u32[]{:S(2)}) collective-permute-start(bf16[2,128,256]{2,1,0:T(8,128)(2,1)S(1)} %get-tuple-element.401), channel_id=1, source_target_pairs={{0,3},{1,2},{2,1},{3,0},{4,7},{5,6},{6,5},{7,4},{8,11},{9,10},{10,... | collective-permute-start | bytes 393224 | tf_op jit(solution)/shard_map/ppermute | solution.py:414
  198.4 9.1 %collective-permute-start.29 = (bf16[2,128,256]{2,1,0:T(8,128)(2,1)S(1)}, bf16[2,128,256]{2,1,0:T(8,128)(2,1)S(1)}, u32[]{:S(2)}, u32[]{:S(2)}) collective-permute-start(bf16[2,128,256]{2,1,0:T(8,128)(2,1)S(1)} %get-tuple-element.401), channel_id=1, source_target_pairs={{0,2},{1,3},{2,0},{3,1},{4,6},{5,7},{6,4},{7,5},{8,10},{9,11},{10,... | collective-permute-start | bytes 393224 | tf_op jit(solution)/shard_map/ppermute | solution.py:414
  200.9 6.6 %collective-permute-start.28 = (bf16[2,128,256]{2,1,0:T(8,128)(2,1)S(1)}, bf16[2,128,256]{2,1,0:T(8,128)(2,1)S(1)}, u32[]{:S(2)}, u32[]{:S(2)}) collective-permute-start(bf16[2,128,256]{2,1,0:T(8,128)(2,1)S(1)} %get-tuple-element.401), channel_id=1, source_target_pairs={{0,1},{1,0},{2,3},{3,2},{4,5},{5,4},{6,7},{7,6},{8,9},{9,8},{10,11... | collective-permute-start | bytes 393224 | tf_op jit(solution)/shard_map/ppermute | solution.py:414
  207.6 14.9 %collective-permute-start.36 = (bf16[4,2,128,256]{3,2,1,0:T(8,128)(2,1)S(1)}, bf16[4,2,128,256]{3,2,1,0:T(8,128)(2,1)S(1)}, u32[]{:S(2)}, u32[]{:S(2)}) collective-permute-start(bf16[4,2,128,256]{3,2,1,0:T(8,128)(2,1)S(1)} %pad_maximum_fusion.1.refs_0_), channel_id=1, source_target_pairs={{0,16},{4,12},{8,24},{12,4},{16,0},{20,28},{24,8},{28,20},{1,17},{... | collective-permute-start | bytes 1572872 | tf_op jit(solution)/shard_map/ppermute | solution.py:434
  209.7 26.6 %collective-permute-start.39 = (bf16[3,704,128]{2,1,0:T(8,128)(2,1)S(1)}, bf16[3,704,128]{2,1,0:T(8,128)(2,1)S(1)}, u32[]{:S(2)}, u32[]{:S(2)}) collective-permute-start(bf16[3,704,128]{2,1,0:T(8,128)(2,1)S(1)} %collective-permute-done.31.refs_1_), channel_id=1, source_target_pairs={{0,8},{4,20},{8,0},{12,28},{16,24},{20,4},{24,16},{28,12},{1,9},{5... | collective-permute-start | bytes 1622024 | tf_op jit(solution)/shard_map/ppermute | solution.py:434
  209.7 15.8 %collective-permute-start.33 = (bf16[3,128,256]{2,1,0:T(8,128)(2,1)S(1)}, bf16[3,128,256]{2,1,0:T(8,128)(2,1)S(1)}, u32[]{:S(2)}, u32[]{:S(2)}) collective-permute-start(bf16[3,128,256]{2,1,0:T(8,128)(2,1)S(1)} %slice_bitcast_fusion), channel_id=1, source_target_pairs={{0,1},{1,0},{2,3},{3,2},{4,5},{5,4},{6,7},{7,6},{8,9},{9,8},{10,11... | collective-permute-start | bytes 589832 | tf_op jit(solution)/shard_map/ppermute | solution.py:414
  209.8 26.4 %collective-permute-start.37 = (bf16[4,2,128,256]{3,2,1,0:T(8,128)(2,1)S(1)}, bf16[4,2,128,256]{3,2,1,0:T(8,128)(2,1)S(1)}, u32[]{:S(2)}, u32[]{:S(2)}) collective-permute-start(bf16[4,2,128,256]{3,2,1,0:T(8,128)(2,1)S(1)} %pad_maximum_fusion.1.refs_0_), channel_id=1, source_target_pairs={{0,8},{4,20},{8,0},{12,28},{16,24},{20,4},{24,16},{28,12},{1,9},{5... | collective-permute-start | bytes 1572872 | tf_op jit(solution)/shard_map/ppermute | solution.py:434
  222.5 13.8 %collective-permute-start.38 = (bf16[4,2,128,256]{3,2,1,0:T(8,128)(2,1)S(1)}, bf16[4,2,128,256]{3,2,1,0:T(8,128)(2,1)S(1)}, u32[]{:S(2)}, u32[]{:S(2)}) collective-permute-start(bf16[4,2,128,256]{3,2,1,0:T(8,128)(2,1)S(1)} %collective-permute-done.36.refs_1_), channel_id=1, source_target_pairs={{0,8},{4,20},{8,0},{12,28},{16,24},{20,4},{24,16},{28,12},{1,9},{5... | collective-permute-start | bytes 1572872 | tf_op jit(solution)/shard_map/ppermute | solution.py:434
  224.5 7.6 %collective-permute-start.35 = (bf16[3,128,256]{2,1,0:T(8,128)(2,1)S(1)}, bf16[3,128,256]{2,1,0:T(8,128)(2,1)S(1)}, u32[]{:S(2)}, u32[]{:S(2)}) collective-permute-start(bf16[3,128,256]{2,1,0:T(8,128)(2,1)S(1)} %slice_bitcast_fusion), channel_id=1, source_target_pairs={{0,3},{1,2},{2,1},{3,0},{4,7},{5,6},{6,5},{7,4},{8,11},{9,10},{10,... | collective-permute-start | bytes 589832 | tf_op jit(solution)/shard_map/ppermute | solution.py:414
  225.6 10.6 %collective-permute-start.34 = (bf16[3,128,256]{2,1,0:T(8,128)(2,1)S(1)}, bf16[3,128,256]{2,1,0:T(8,128)(2,1)S(1)}, u32[]{:S(2)}, u32[]{:S(2)}) collective-permute-start(bf16[3,128,256]{2,1,0:T(8,128)(2,1)S(1)} %slice_bitcast_fusion), channel_id=1, source_target_pairs={{0,2},{1,3},{2,0},{3,1},{4,6},{5,7},{6,4},{7,5},{8,10},{9,11},{10,... | collective-permute-start | bytes 589832 | tf_op jit(solution)/shard_map/ppermute | solution.py:414
  237.4 4.2 %collective-permute-start.45 = (bf16[3,704,128]{2,1,0:T(8,128)(2,1)S(1)}, bf16[3,704,128]{2,1,0:T(8,128)(2,1)S(1)}, u32[]{:S(2)}, u32[]{:S(2)}) collective-permute-start(bf16[3,704,128]{2,1,0:T(8,128)(2,1)S(1)} %collective-permute-done.39.refs_3_), channel_id=1, source_target_pairs={{0,4},{4,0},{8,12},{12,8},{16,20},{20,16},{24,28},{28,24},{1,5},{5... | collective-permute-start | bytes 1622024 | tf_op jit(solution)/shard_map/ppermute | solution.py:427
  239.0 19.6 %collective-permute-start.41 = (bf16[4,3,128,256]{3,2,1,0:T(8,128)(2,1)S(1)}, bf16[4,3,128,256]{3,2,1,0:T(8,128)(2,1)S(1)}, u32[]{:S(2)}, u32[]{:S(2)}) collective-permute-start(bf16[4,3,128,256]{3,2,1,0:T(8,128)(2,1)S(1)} %pad_maximum_fusion.refs_0_), channel_id=1, source_target_pairs={{0,8},{4,20},{8,0},{12,28},{16,24},{20,4},{24,16},{28,12},{1,9},{5... | collective-permute-start | bytes 2359304 | tf_op jit(solution)/shard_map/ppermute | solution.py:434
  239.0 19.6 %collective-permute-start.40 = (bf16[4,3,128,256]{3,2,1,0:T(8,128)(2,1)S(1)}, bf16[4,3,128,256]{3,2,1,0:T(8,128)(2,1)S(1)}, u32[]{:S(2)}, u32[]{:S(2)}) collective-permute-start(bf16[4,3,128,256]{3,2,1,0:T(8,128)(2,1)S(1)} %pad_maximum_fusion.refs_0_), channel_id=1, source_target_pairs={{0,16},{4,12},{8,24},{12,4},{16,0},{20,28},{24,8},{28,20},{1,17},{... | collective-permute-start | bytes 2359304 | tf_op jit(solution)/shard_map/ppermute | solution.py:434
  241.1 9.8 %collective-permute-start.47 = (bf16[4,2,128,256]{3,2,1,0:T(8,128)(2,1)S(1)}, bf16[4,2,128,256]{3,2,1,0:T(8,128)(2,1)S(1)}, u32[]{:S(2)}, u32[]{:S(2)}) collective-permute-start(bf16[4,2,128,256]{3,2,1,0:T(8,128)(2,1)S(1)} %collective-permute-done.36.refs_1_), channel_id=1, source_target_pairs={{0,4},{4,0},{8,12},{12,8},{16,20},{20,16},{24,28},{28,24},{1,5},{5... | collective-permute-start | bytes 1572872 | tf_op jit(solution)/shard_map/ppermute | solution.py:427
  241.1 9.8 %collective-permute-start.48 = (bf16[4,2,128,256]{3,2,1,0:T(8,128)(2,1)S(1)}, bf16[4,2,128,256]{3,2,1,0:T(8,128)(2,1)S(1)}, u32[]{:S(2)}, u32[]{:S(2)}) collective-permute-start(bf16[4,2,128,256]{3,2,1,0:T(8,128)(2,1)S(1)} %collective-permute-done.37.refs_2_), channel_id=1, source_target_pairs={{0,4},{4,0},{8,12},{12,8},{16,20},{20,16},{24,28},{28,24},{1,5},{5... | collective-permute-start | bytes 1572872 | tf_op jit(solution)/shard_map/ppermute | solution.py:427
  241.6 9.3 %collective-permute-start.49 = (bf16[4,2,128,256]{3,2,1,0:T(8,128)(2,1)S(1)}, bf16[4,2,128,256]{3,2,1,0:T(8,128)(2,1)S(1)}, u32[]{:S(2)}, u32[]{:S(2)}) collective-permute-start(bf16[4,2,128,256]{3,2,1,0:T(8,128)(2,1)S(1)} %collective-permute-done.38.refs_3_), channel_id=1, source_target_pairs={{0,4},{4,0},{8,12},{12,8},{16,20},{20,16},{24,28},{28,24},{1,5},{5... | collective-permute-start | bytes 1572872 | tf_op jit(solution)/shard_map/ppermute | solution.py:427
  258.6 15.7 %collective-permute-start.50 = (bf16[4,3,128,256]{3,2,1,0:T(8,128)(2,1)S(1)}, bf16[4,3,128,256]{3,2,1,0:T(8,128)(2,1)S(1)}, u32[]{:S(2)}, u32[]{:S(2)}) collective-permute-start(bf16[4,3,128,256]{3,2,1,0:T(8,128)(2,1)S(1)} %collective-permute-done.40.refs_1_), channel_id=1, source_target_pairs={{0,8},{4,20},{8,0},{12,28},{16,24},{20,4},{24,16},{28,12},{1,9},{5... | collective-permute-start | bytes 2359304 | tf_op jit(solution)/shard_map/ppermute | solution.py:434
  258.9 11.0 %collective-permute-start.51 = (bf16[128,1024]{1,0:T(8,128)(2,1)S(1)}, bf16[128,1024]{1,0:T(8,128)(2,1)S(1)}, u32[]{:S(2)}, u32[]{:S(2)}) collective-permute-start(bf16[128,1024]{1,0:T(8,128)(2,1)S(1)} %get-tuple-element.370), channel_id=1, source_target_pairs={{0,3},{1,2},{2,1},{3,0},{4,7},{5,6},{6,5},{7,4},{8,11},{9,10},{10,... | collective-permute-start | bytes 786440 | tf_op jit(solution)/shard_map/ppermute | solution.py:414
  261.5 12.8 %collective-permute-start.52 = (bf16[128,1024]{1,0:T(8,128)(2,1)S(1)}, bf16[128,1024]{1,0:T(8,128)(2,1)S(1)}, u32[]{:S(2)}, u32[]{:S(2)}) collective-permute-start(bf16[128,1024]{1,0:T(8,128)(2,1)S(1)} %get-tuple-element.371), channel_id=1, source_target_pairs={{0,1},{1,0},{2,3},{3,2},{4,5},{5,4},{6,7},{7,6},{8,9},{9,8},{10,11... | collective-permute-start | bytes 786440 | tf_op jit(solution)/shard_map/ppermute | solution.py:414
  274.8 5.1 %collective-permute-start.56 = (bf16[4,3,128,256]{3,2,1,0:T(8,128)(2,1)S(1)}, bf16[4,3,128,256]{3,2,1,0:T(8,128)(2,1)S(1)}, u32[]{:S(2)}, u32[]{:S(2)}) collective-permute-start(bf16[4,3,128,256]{3,2,1,0:T(8,128)(2,1)S(1)} %collective-permute-done.50.refs_0_), channel_id=1, source_target_pairs={{0,4},{4,0},{8,12},{12,8},{16,20},{20,16},{24,28},{28,24},{1,5},{5... | collective-permute-start | bytes 2359304 | tf_op jit(solution)/shard_map/ppermute | solution.py:427
  (63 other events, 629.2 us)

commit v7 on v6

--- a/solution.py
+++ b/solution.py
@@ -297,8 +297,8 @@
 
 def query_kernel(hn, hd, share, own, coefs, *refs):
     per = BLOCK // share
-    ga = refs[: -14]
-    q, k, v, ql, kent, gcol, grow, rise, dq, gk, gv, direct, first, grad = refs[-14:]
+    ga = refs[:-15]
+    q, k, v, ql, kent, gcol, grow, rise, dq, gk, gv, direct, message, grad, first = refs[-15:]
     b = pl.program_id(0)
     for i, piece in enumerate(ga):
         @pl.when(b == i // per)
@@ -322,6 +322,7 @@
         direct[0, h] = now
 
         first[h] = jnp.where(b == 0, 0.0, first[h]) + coefs[ENTER, b, head] * now
+        message[h] = first[h].astype(bf16)
 
 
 def key_kernel(hn, hd, wide, share, own, coefs, arrived, direct, n1, dq, k, v, kl, gk, gv,
@@ -692,17 +693,17 @@
             in_specs=[SMEM, *[whole((share, 3 * cols))] * narrow, *[own_blk] * 4, own_kent,
                       own_col, own_row, own_col],
             out_specs=[*[part_blk] * 3, own_direct, whole((hn, hd, hd))],
-            scratch_shapes=[pltpu.VMEM((BLOCK, cols), bf16)],
+            scratch_shapes=[pltpu.VMEM((BLOCK, cols), bf16), pltpu.VMEM((hn, hd, hd), f32)],
         ),
         out_shape=[sds((local, cols), bf16), *[sds((local, cols), f32)] * 2,
-                   sds((blocks, hn, hd, hd), f32), sds((hn, hd, hd), f32)],
+                   sds((blocks, hn, hd, hd), f32), sds((hn, hd, hd), bf16)],
         compiler_params=budget(56),
         cost_estimate=cost(5.4),
         name="mixer_query_back",
     )(own, coefs, *trios, q, k, v, ql, kent, gcol, grow, rise)
 
     part_two = swap_narrow(ffn_part[2], 2)
-    arrived, low, got, part_two = fence(pass_states(message.astype(bf16), coef_out), low, got, part_two)
+    arrived, low, got, part_two = fence(pass_states(message, coef_out), low, got, part_two)
     low_ff, away_ff = halved(low, got)
 
     five = (wide // 2, 5, width // wide, cols)

time: 284 us -> 289 us (1.018)
  local copies, waits for them, and re-layouts: 10.8 us -> 16.1 us
    unnamed x111 -> x129, local copies, waits for them, and re-layouts: 10.4 us -> 15.7 us
  transfers between devices with their start and end apart: 57 -> 57, of which waited for: 23 -> 22; matrix products, arithmetic and copies ran while one was open for 2% -> 2% of each run, Pallas kernels for 21% -> 21%
where the time goes in v7:
time: 289 us; the launch traced here: 288 us
  waiting for transfers between devices  93.1 us (32%)
  Pallas kernels  85.3 us (30%)
  starting transfers between devices  64.6 us (22%)
  blocking collectives  19.8 us (7%)
  local copies, waits for them, and re-layouts  16.1 us (6%)
  other arithmetic  6.18 us (2%)
    ppermute x27, waiting for transfers between devices, swap_narrow(): return lax.ppermute(values, 'narrow', [(i, i ^ k) for i in range(size)])  63.8 us
    ppermute x27, starting transfers between devices, swap_narrow(): return lax.ppermute(values, 'narrow', [(i, i ^ k) for i in range(size)])  43.5 us
    ppermute x13, waiting for transfers between devices, swap_step(): return lax.ppermute(values, 'wide', [(i, flip(i)) for i in range(size)])  24 us
    pallas_call x7, Pallas kernels, widen(): pl.pallas_call(functools.partial(kernel, places), grid_spec=pltpu.Prefetc...  20.7 us
    pallas_call x2, Pallas kernels, body(): pl.pallas_call(functools.partial(forward_kernel, hn, hd, share), grid_spe...  20.4 us
    all_gather x2, blocking collectives, pass_states(): gathered = lax.all_gather(message, 'wide', axis=0)  19.8 us
    unnamed x129, local copies, waits for them, and re-layouts  15.7 us
    ppermute x13, starting transfers between devices, swap_step(): return lax.ppermute(values, 'wide', [(i, flip(i)) for i in range(size)])  14.7 us
  transfers between devices with their start and end apart: 57, of which 22 were waited for; matrix products, arithmetic and copies ran while one was open for 2% of the time, Pallas kernels for 21%

profile of v7, /device:TPU:0, one launch (start us, length us, event | category | flops | bytes accessed | tf_op | source)
XLA Modules:
  0.0 287.9 jit_solution(9701232252678529199)
XLA Ops:
  0.6 4.1 %collective-permute-start.1 = (bf16[128,1024]{1,0:T(8,128)(2,1)}, bf16[128,1024]{1,0:T(8,128)(2,1)S(1)}, u32[]{:S(2)}, u32[]{:S(2)}) collective-permute-start(bf16[128,1024]{1,0:T(8,128)(2,1)} %refs_9_.1), channel_id=1, source_target_pairs={{0,2},{1,3},{2,0},{3,1},{4,6},{5,7},{6,4},{7,5},{8,10},{9,11},{10,... | collective-permute-start | bytes 786440 | tf_op jit(solution)/shard_map/ppermute | solution.py:415
  8.5 2.1 layout.1
  14.9 2.5 collective-permute-done.tok_b
  18.1 10.3 %mixer_forward_0.1 = (bf16[512,1024]{1,0:T(8,128)(2,1)}, bf16[512,1024]{1,0:T(8,128)(2,1)}, f32[512,1024]{1,0:T(8,128)}, f32[512,1024]{1,0:T(8,128)}, bf16[512,1...) custom-call(s32[2]{0:T(128)} %copy-done.44, ...), custom_call_target="tpu_custom_call" | custom-call | bytes 32000000 | tf_op jit(solution)/shard_map/mixer_forward_0/pallas_call | solution.py:576
  29.9 2.5 collective-permute-start.7
  33.0 10.1 %mixer_forward_1.1 = (bf16[512,1024]{1,0:T(8,128)(2,1)}, bf16[512,1024]{1,0:T(8,128)(2,1)}, f32[512,1024]{1,0:T(8,128)}, f32[512,1024]{1,0:T(8,128)}, bf16[512,1...) custom-call(s32[2]{0:T(128)} %copy-done.44, ...), custom_call_target="tpu_custom_call", output_to_operand_aliasing={{0}: (11, {}), {1}: (12, {}), {2}: (13, {}), {3}: (14, {}),... | custom-call | bytes 32000000 | tf_op jit(solution)/shard_map/mixer_forward_1/pallas_call | solution.py:576
  48.4 10.0 %all-gather = bf16[16,128,128]{2,1,0:T(8,128)(2,1)S(1)} all-gather(bf16[2,128,128]{2,1,0:T(8,128)(2,1)S(1)} %multiply_reduce_fusion), channel_id=2, replica_groups=mesh['wide'=8,'narrow'=4] {'wide'}, dimensions={0}, use_global_device_ids=true | all-gather | bytes 589824 | tf_op jit(solution)/shard_map/all_gather | solution.py:534
  63.7 2.4 collective-permute-done.11.refs_3_
  66.0 2.6 collective-permute-done.10.refs_2_
  69.3 9.1 %mixer_out.1 = (bf16[512,1024]{1,0:T(8,128)(2,1)}, f32[512,1]{1,0:T(8,128)}, bf16[512,1024]{1,0:T(8,128)(2,1)}, f32[128,1024]{1,0:T(8,128)}, bf16[512,1024]{1,0:...) custom-call(s32[2]{0:T(128)} %copy-done.44, f32[5,2,8]{2,1,0:T(2,128)} %copy-done.48, bf16[2,128,128]{2,1,0:T(8,128)(2,1)} %copy-done.58, ...), custom_call_target="tpu_custom_call" | custom-call | bytes 30400000 | tf_op jit(solution)/shard_map/mixer_out/pallas_call | solution.py:611
  79.6 5.7 %ffn.1 = (bf16[512,704]{1,0:T(8,128)(2,1)S(1)}, bf16[512,704]{1,0:T(8,128)(2,1)S(1)}, bf16[512,704]{1,0:T(8,128)(2,1)S(1)}, bf16[128,1024]{1,0:T(8,128)(2,1)S(1)...) custom-call(bf16[512,1024]{1,0:T(8,128)(2,1)S(1)} %copy-done.14, ...), custom_call_target="tpu_custom_call" | custom-call | bytes 32000000 | tf_op jit(solution)/shard_map/ffn/pallas_call | solution.py:632
  87.2 2.5 collective-permute-start.14
  89.7 8.0 %collective-permute-done.12.refs_1_ = bf16[128,1024]{1,0:T(8,128)(2,1)S(1)} collective-permute-done((bf16[128,1024]{1,0:T(8,128)(2,1)S(1)}, bf16[128,1024]{1,0:T(8,128)(2,1)S(1)}, u32[]{:S(2)}, u32[]{:S(2)}) %collective-permute-start.12) | collective-permute-done | bytes 262176 | tf_op jit(solution)/shard_map/ppermute | solution.py:415
  97.7 6.8 %ffn_grads.1 = (bf16[4,3,704,128]{3,2,1,0:T(8,128)(2,1)S(1)}, bf16[4,3,704,128]{3,2,1,0:T(8,128)(2,1)S(1)}, bf16[128,1024]{1,0:T(8,128)(2,1)S(1)}, bf16[128,1024...) custom-call(s32[2]{0:T(128)S(1)} %copy-done.45, bf16[512,1024]{1,0:T(8,128)(2,1)S(1)} %copy-done.15, ...), custom_call_target="tpu_custom_call" | custom-call | bytes 32000000 | tf_op jit(solution)/shard_map/ffn_grads/pallas_call | solution.py:645
  104.6 2.2 collective-permute-done.13.refs_2_
  106.8 2.2 residual_back.1
  110.6 4.9 %collective-permute-start.15 = (bf16[128,768]{1,0:T(8,128)(2,1)S(1)}, bf16[128,768]{1,0:T(8,128)(2,1)S(1)}, u32[]{:S(2)}, u32[]{:S(2)}) collective-permute-start(bf16[128,768]{1,0:T(8,128)(2,1)S(1)} %get-tuple-element.268), channel_id=1, source_target_pairs={{0,1},{1,0},{2,3},{3,2},{4,5},{5,4},{6,7},{7,6},{8,9},{9,8},{10,11... | collective-permute-start | bytes 589832 | tf_op jit(solution)/shard_map/ppermute | solution.py:415
  115.5 2.4 collective-permute-start.17
  117.9 6.1 %collective-permute-done.15.refs_1_ = bf16[128,768]{1,0:T(8,128)(2,1)S(1)} collective-permute-done((bf16[128,768]{1,0:T(8,128)(2,1)S(1)}, bf16[128,768]{1,0:T(8,128)(2,1)S(1)}, u32[]{:S(2)}, u32[]{:S(2)}) %collective-permute-start.15) | collective-permute-done | bytes 196640 | tf_op jit(solution)/shard_map/ppermute | solution.py:415
  124.1 8.6 %collective-permute-done.16.refs_2_ = bf16[128,768]{1,0:T(8,128)(2,1)S(1)} collective-permute-done((bf16[128,768]{1,0:T(8,128)(2,1)S(1)}, bf16[128,768]{1,0:T(8,128)(2,1)S(1)}, u32[]{:S(2)}, u32[]{:S(2)}) %collective-permute-start.16) | collective-permute-done | bytes 196640 | tf_op jit(solution)/shard_map/ppermute | solution.py:415
  134.9 3.9 %collective-permute-start.20 = (bf16[128,1024]{1,0:T(8,128)(2,1)}, bf16[128,1024]{1,0:T(8,128)(2,1)}, u32[]{:S(2)}, u32[]{:S(2)}) collective-permute-start(bf16[128,1024]{1,0:T(8,128)(2,1)} %get-tuple-element.288), channel_id=1, source_target_pairs={{0,2},{1,3},{2,0},{3,1},{4,6},{5,7},{6,4},{7,5},{8,10},{9,11},{10,... | collective-permute-start | bytes 786440 | tf_op jit(solution)/shard_map/ppermute | solution.py:415
  139.0 2.0 gate_back.1
  142.1 5.6 %mixer_query_back.1 = (bf16[512,256]{1,0:T(8,128)(2,1)}, f32[512,256]{1,0:T(8,128)}, f32[512,256]{1,0:T(8,128)}, f32[2,2,128,128]{3,2,1,0:T(8,128)}, bf16[2,128,128]{2,1,0:T(8,128)(2,1)}) custom-call(s32[2]{0:T(128)} %copy-done.44, f32[5,2,8]{2,1,0:T(2,128)} %copy-done.48, bf16[128,768]{1,0:T(8,128)(2,1)} %copy-done.29, bf16[128,768]{1,0:T(8,128)(2,1)} %copy-done.30, ...), custom_call_target="tpu_custom_call" | custom-call | bytes 17280000 | tf_op jit(solution)/shard_map/mixer_query_back/pallas_call | solution.py:688
  147.7 9.8 %all-gather.1 = bf16[16,128,128]{2,1,0:T(8,128)(2,1)S(1)} all-gather(bf16[2,128,128]{2,1,0:T(8,128)(2,1)} %get-tuple-element.285), channel_id=3, replica_groups=mesh['wide'=8,'narrow'=4] {'wide'}, dimensions={0}, use_global_device_ids=true | all-gather | bytes 589824 | tf_op jit(solution)/shard_map/all_gather | solution.py:534
  163.1 3.8 %mixer_key_back.1 = (bf16[4,5,128,256]{3,2,1,0:T(8,128)(2,1)S(1)}, bf16[4,5,128,256]{3,2,1,0:T(8,128)(2,1)S(1)}, bf16[128,768]{1,0:T(8,128)(2,1)S(1)}, bf16[128,...) custom-call(s32[2]{0:T(128)S(1)} %copy-done.46, ...), custom_call_target="tpu_custom_call", output_to_operand_aliasing={{0}: (13, {}), {1}: (14, {})} | custom-call | bytes 28800000 | tf_op jit(solution)/shard_map/mixer_key_back/pallas_call | solution.py:727
  172.8 2.4 collective-permute-start.24
  176.6 5.5 %collective-permute-done.23.refs_1_ = bf16[128,768]{1,0:T(8,128)(2,1)S(1)} collective-permute-done((bf16[128,768]{1,0:T(8,128)(2,1)S(1)}, bf16[128,768]{1,0:T(8,128)(2,1)S(1)}, u32[]{:S(2)}, u32[]{:S(2)}) %collective-permute-start.23) | collective-permute-done | bytes 196640 | tf_op jit(solution)/shard_map/ppermute | solution.py:415
  182.1 7.8 %collective-permute-done.24.refs_2_ = bf16[128,768]{1,0:T(8,128)(2,1)S(1)} collective-permute-done((bf16[128,768]{1,0:T(8,128)(2,1)S(1)}, bf16[128,768]{1,0:T(8,128)(2,1)S(1)}, u32[]{:S(2)}, u32[]{:S(2)}) %collective-permute-start.24) | collective-permute-done | bytes 196640 | tf_op jit(solution)/shard_map/ppermute | solution.py:415
  195.1 5.5 %collective-permute-done.27 = bf16[1,5,128,256]{3,2,1,0:T(8,128)(2,1)S(1)} collective-permute-done((bf16[1,5,128,256]{3,2,1,0:T(8,128)(2,1)S(1)}, bf16[1,5,128,256]{3,2,1,0:T(8,128)(2,1)S(1)}, u32[]{:S(2)}, u32[]{:S(2)}) %collective-permute-start.27) | collective-permute-done | bytes 327712 | tf_op jit(solution)/shard_map/ppermute | solution.py:435
  202.6 2.5 collective-permute-start.29
  205.4 2.3 collective-permute-done.30
  207.7 4.1 %collective-permute-done.29 = bf16[2,128,256]{2,1,0:T(8,128)(2,1)S(1)} collective-permute-done((bf16[2,128,256]{2,1,0:T(8,128)(2,1)S(1)}, bf16[2,128,256]{2,1,0:T(8,128)(2,1)S(1)}, u32[]{:S(2)}, u32[]{:S(2)}) %collective-permute-start.29) | collective-permute-done | bytes 131104 | tf_op jit(solution)/shard_map/ppermute | solution.py:415
  211.9 2.1 collective-permute-start.36
  216.0 10.8 %collective-permute-done.36.refs_1_ = bf16[4,2,128,256]{3,2,1,0:T(8,128)(2,1)S(1)} collective-permute-done((bf16[4,2,128,256]{3,2,1,0:T(8,128)(2,1)S(1)}, bf16[4,2,128,256]{3,2,1,0:T(8,128)(2,1)S(1)}, u32[]{:S(2)}, u32[]{:S(2)}) %collective-permute-start.36) | collective-permute-done | bytes 524320 | tf_op jit(solution)/shard_map/ppermute | solution.py:435
  226.7 2.0 collective-permute-start.38
  230.2 5.2 %tokens_back.1 = f32[128,1024]{1,0:T(8,128)} custom-call(s32[2]{0:T(128)S(1)} %copy-done.46, bf16[128,768]{1,0:T(8,128)(2,1)S(1)} %get-tuple-element.329.refs_0_, bf16[128,768]{1,0:T(8,128)(2,1)S(1)} %collective-permute-done.23.refs_1_, bf16[128,768]{1,0:T(8,128)(2,1)S(1)} %collective-permute-done.24.refs_2_, ...), custom_call_target="tpu_custom_call" | custom-call | bytes 25600000 | tf_op jit(solution)/shard_map/tokens_back/pallas_call | solution.py:777
  236.3 4.1 %collective-permute-done.34 = bf16[3,128,256]{2,1,0:T(8,128)(2,1)S(1)} collective-permute-done((bf16[3,128,256]{2,1,0:T(8,128)(2,1)S(1)}, bf16[3,128,256]{2,1,0:T(8,128)(2,1)S(1)}, u32[]{:S(2)}, u32[]{:S(2)}) %collective-permute-start.34) | collective-permute-done | bytes 196640 | tf_op jit(solution)/shard_map/ppermute | solution.py:415
  243.3 2.0 collective-permute-start.40
  245.9 3.0 %widen_gate_0.1 = (f32[1024,1024]{1,0:T(8,128)}, f32[1024,1024]{1,0:T(8,128)}) custom-call(s32[2]{0:T(128)S(1)} %copy-done.46, bf16[4,2,128,256]{3,2,1,0:T(8,128)(2,1)S(1)} %pad_maximum_fusion.1.refs_0_, bf16[4,2,128,256]{3,2,1,0:T(8,128)(2,1)S(1)} %collective-permute-done.36.refs_1_, bf16[4,2,128,256]{3,2,1,0:T(8,128)(2,1)S(1)} %collective-permute-done.37.refs_2_, ...), custom_call_target="tpu_custom_call" | custom-call | bytes 12800000 | tf_op jit(solution)/shard_map/widen_gate_0/pallas_call | solution.py:485
  249.0 3.1 %widen_ffn_0.1 = (f32[704,1024]{1,0:T(8,128)}, f32[704,1024]{1,0:T(8,128)}, f32[704,1024]{1,0:T(8,128)}) custom-call(s32[2]{0:T(128)S(1)} %copy-done.46, bf16[3,704,128]{2,1,0:T(8,128)(2,1)S(1)} %add_bitcast_fusion.refs_0_, bf16[3,704,128]{2,1,0:T(8,128)(2,1)S(1)} %collective-permute-done.31.refs_1_, ...), custom_call_target="tpu_custom_call" | custom-call | bytes 12800000 | tf_op jit(solution)/shard_map/widen_ffn_0/pallas_call | solution.py:485
  252.1 3.1 %widen_ffn_1.1 = (f32[704,1024]{1,0:T(8,128)}, f32[704,1024]{1,0:T(8,128)}, f32[704,1024]{1,0:T(8,128)}) custom-call(s32[2]{0:T(128)S(1)} %copy-done.46, bf16[3,704,128]{2,1,0:T(8,128)(2,1)S(1)} %collective-permute-done.42.refs_0_, ...), custom_call_target="tpu_custom_call", output_to_operand_aliasing={{0}: (5, {}), {1}: (6, {}), {2}: (7, {})} | custom-call | bytes 12800000 | tf_op jit(solution)/shard_map/widen_ffn_1/pallas_call | solution.py:485
  255.2 7.7 %collective-permute-done.41.refs_2_ = bf16[4,3,128,256]{3,2,1,0:T(8,128)(2,1)S(1)} collective-permute-done((bf16[4,3,128,256]{3,2,1,0:T(8,128)(2,1)S(1)}, bf16[4,3,128,256]{3,2,1,0:T(8,128)(2,1)S(1)}, u32[]{:S(2)}, u32[]{:S(2)}) %collective-permute-start.41) | collective-permute-done | bytes 786464 | tf_op jit(solution)/shard_map/ppermute | solution.py:435
  263.2 2.6 collective-permute-start.51
  265.8 3.1 %widen_square_0.1 = (f32[1024,1024]{1,0:T(8,128)}, f32[1024,1024]{1,0:T(8,128)}, f32[1024,1024]{1,0:T(8,128)}) custom-call(s32[2]{0:T(128)S(1)} %copy-done.46, bf16[4,3,128,256]{3,2,1,0:T(8,128)(2,1)S(1)} %pad_maximum_fusion.refs_0_, bf16[4,3,128,256]{3,2,1,0:T(8,128)(2,1)S(1)} %collective-permute-done.40.refs_1_, ...), custom_call_target="tpu_custom_call" | custom-call | bytes 12800000 | tf_op jit(solution)/shard_map/widen_square_0/pallas_call | solution.py:485
  268.9 3.0 %widen_gate_1.1 = (f32[1024,1024]{1,0:T(8,128)}, f32[1024,1024]{1,0:T(8,128)}) custom-call(s32[2]{0:T(128)S(1)} %copy-done.46, bf16[4,2,128,256]{3,2,1,0:T(8,128)(2,1)S(1)} %collective-permute-done.46.refs_0_, bf16[4,2,128,256]{3,2,1,0:T(8,128)(2,1)S(1)} %collective-permute-done.47.refs_1_, ...), custom_call_target="tpu_custom_call", output_to_operand_aliasing={{0}: (5, {}), {1}: (6, {})} | custom-call | bytes 12800000 | tf_op jit(solution)/shard_map/widen_gate_1/pallas_call | solution.py:485
  271.9 2.3 collective-permute-done.51.refs_3_
  274.2 4.4 %collective-permute-done.52.refs_1_ = bf16[128,1024]{1,0:T(8,128)(2,1)S(1)} collective-permute-done((bf16[128,1024]{1,0:T(8,128)(2,1)S(1)}, bf16[128,1024]{1,0:T(8,128)(2,1)S(1)}, u32[]{:S(2)}, u32[]{:S(2)}) %collective-permute-start.52) | collective-permute-done | bytes 262176 | tf_op jit(solution)/shard_map/ppermute | solution.py:415
  284.3 3.6 %widen_square_1.1 = (f32[1024,1024]{1,0:T(8,128)}, f32[1024,1024]{1,0:T(8,128)}, f32[1024,1024]{1,0:T(8,128)}) custom-call(s32[2]{0:T(128)S(1)} %copy-done.46, bf16[4,3,128,256]{3,2,1,0:T(8,128)(2,1)S(1)} %collective-permute-done.53.refs_0_, ...), custom_call_target="tpu_custom_call", output_to_operand_aliasing={{0}: (5, {}), {1}: (6, {}), {2}: (7, {})} | custom-call | bytes 12800000 | tf_op jit(solution)/shard_map/widen_square_1/pallas_call | solution.py:485
  (250 shorter events, 62.8 us)
Async XLA Ops:
  0.6 27.9 %collective-permute-start.1 = (bf16[128,1024]{1,0:T(8,128)(2,1)}, bf16[128,1024]{1,0:T(8,128)(2,1)S(1)}, u32[]{:S(2)}, u32[]{:S(2)}) collective-permute-start(bf16[128,1024]{1,0:T(8,128)(2,1)} %refs_9_.1), channel_id=1, source_target_pairs={{0,2},{1,3},{2,0},{3,1},{4,6},{5,7},{6,4},{7,5},{8,10},{9,11},{10,... | collective-permute-start | bytes 786440 | tf_op jit(solution)/shard_map/ppermute | solution.py:415
  4.8 12.7 %collective-permute-start = (bf16[128,1024]{1,0:T(8,128)(2,1)}, bf16[128,1024]{1,0:T(8,128)(2,1)S(1)}, u32[]{:S(2)}, u32[]{:S(2)}) collective-permute-start(bf16[128,1024]{1,0:T(8,128)(2,1)} %refs_9_.1), channel_id=1, source_target_pairs={{0,1},{1,0},{2,3},{3,2},{4,5},{5,4},{6,7},{7,6},{8,9},{9,8},{10,11... | collective-permute-start | bytes 786440 | tf_op jit(solution)/shard_map/ppermute | solution.py:415
  6.3 22.2 %collective-permute-start.2 = (bf16[128,1024]{1,0:T(8,128)(2,1)}, bf16[128,1024]{1,0:T(8,128)(2,1)S(1)}, u32[]{:S(2)}, u32[]{:S(2)}) collective-permute-start(bf16[128,1024]{1,0:T(8,128)(2,1)} %refs_9_.1), channel_id=1, source_target_pairs={{0,3},{1,2},{2,1},{3,0},{4,7},{5,6},{6,5},{7,4},{8,11},{9,10},{10,... | collective-permute-start | bytes 786440 | tf_op jit(solution)/shard_map/ppermute | solution.py:415
  28.5 30.5 %collective-permute-start.8 = (bf16[128,1024]{1,0:T(8,128)(2,1)S(1)}, bf16[128,1024]{1,0:T(8,128)(2,1)S(1)}, u32[]{:S(2)}, u32[]{:S(2)}) collective-permute-start(bf16[128,1024]{1,0:T(8,128)(2,1)S(1)} %copy-done.28), channel_id=1, source_target_pairs={{0,3},{1,2},{2,1},{3,0},{4,7},{5,6},{6,5},{7,4},{8,11},{9,10},{10,... | collective-permute-start | bytes 786440 | tf_op jit(solution)/shard_map/ppermute | solution.py:415
  29.9 29.1 %collective-permute-start.7 = (bf16[128,1024]{1,0:T(8,128)(2,1)S(1)}, bf16[128,1024]{1,0:T(8,128)(2,1)S(1)}, u32[]{:S(2)}, u32[]{:S(2)}) collective-permute-start(bf16[128,1024]{1,0:T(8,128)(2,1)S(1)} %copy-done.28), channel_id=1, source_target_pairs={{0,2},{1,3},{2,0},{3,1},{4,6},{5,7},{6,4},{7,5},{8,10},{9,11},{10,... | collective-permute-start | bytes 786440 | tf_op jit(solution)/shard_map/ppermute | solution.py:415
  32.5 26.6 %collective-permute-start.6 = (bf16[128,1024]{1,0:T(8,128)(2,1)S(1)}, bf16[128,1024]{1,0:T(8,128)(2,1)S(1)}, u32[]{:S(2)}, u32[]{:S(2)}) collective-permute-start(bf16[128,1024]{1,0:T(8,128)(2,1)S(1)} %copy-done.28), channel_id=1, source_target_pairs={{0,1},{1,0},{2,3},{3,2},{4,5},{5,4},{6,7},{7,6},{8,9},{9,8},{10,11... | collective-permute-start | bytes 786440 | tf_op jit(solution)/shard_map/ppermute | solution.py:415
  33.0 10.1 %collective-permute-start.3 = (f32[1,8]{1,0:T(1,128)S(1)}, f32[1,8]{1,0:T(1,128)S(1)}, u32[]{:S(2)}, u32[]{:S(2)}) collective-permute-start(f32[1,8]{1,0:T(1,128)S(1)} %get-tuple-element.218), channel_id=1, source_target_pairs={{0,4},{4,0},{8,12},{12,8},{16,20},{20,16},{24,28},{28,24},{1,5},{5... | collective-permute-start | bytes 104 | tf_op jit(solution)/shard_map/ppermute | solution.py:516
  46.8 11.6 %collective-permute-start.5 = (f32[4,8]{1,0:T(4,128)S(1)}, f32[4,8]{1,0:T(4,128)S(1)}, u32[]{:S(2)}, u32[]{:S(2)}) collective-permute-start(f32[4,8]{1,0:T(4,128)S(1)} %pad_maximum_fusion.3), channel_id=1, source_target_pairs={{0,16},{4,20},{8,24},{12,28},{16,0},{20,4},{24,8},{28,12},{1,17},{... | collective-permute-start | bytes 392 | tf_op jit(solution)/shard_map/ppermute | solution.py:516
  59.1 6.9 %collective-permute-start.11 = (bf16[2,128,128]{2,1,0:T(8,128)(2,1)S(1)}, bf16[2,128,128]{2,1,0:T(8,128)(2,1)S(1)}, u32[]{:S(2)}, u32[]{:S(2)}) collective-permute-start(bf16[2,128,128]{2,1,0:T(8,128)(2,1)S(1)} %fusion.1.refs_0_), channel_id=1, source_target_pairs={{0,3},{1,2},{2,1},{3,0},{4,7},{5,6},{6,5},{7,4},{8,11},{9,10},{10,... | collective-permute-start | bytes 196616 | tf_op jit(solution)/shard_map/ppermute | solution.py:415
  60.5 8.2 %collective-permute-start.10 = (bf16[2,128,128]{2,1,0:T(8,128)(2,1)S(1)}, bf16[2,128,128]{2,1,0:T(8,128)(2,1)S(1)}, u32[]{:S(2)}, u32[]{:S(2)}) collective-permute-start(bf16[2,128,128]{2,1,0:T(8,128)(2,1)S(1)} %fusion.1.refs_0_), channel_id=1, source_target_pairs={{0,2},{1,3},{2,0},{3,1},{4,6},{5,7},{6,4},{7,5},{8,10},{9,11},{10,... | collective-permute-start | bytes 196616 | tf_op jit(solution)/shard_map/ppermute | solution.py:415
  62.1 6.5 %collective-permute-start.9 = (bf16[2,128,128]{2,1,0:T(8,128)(2,1)S(1)}, bf16[2,128,128]{2,1,0:T(8,128)(2,1)S(1)}, u32[]{:S(2)}, u32[]{:S(2)}) collective-permute-start(bf16[2,128,128]{2,1,0:T(8,128)(2,1)S(1)} %fusion.1.refs_0_), channel_id=1, source_target_pairs={{0,1},{1,0},{2,3},{3,2},{4,5},{5,4},{6,7},{7,6},{8,9},{9,8},{10,11... | collective-permute-start | bytes 196616 | tf_op jit(solution)/shard_map/ppermute | solution.py:415
  85.3 12.4 %collective-permute-start.12 = (bf16[128,1024]{1,0:T(8,128)(2,1)S(1)}, bf16[128,1024]{1,0:T(8,128)(2,1)S(1)}, u32[]{:S(2)}, u32[]{:S(2)}) collective-permute-start(bf16[128,1024]{1,0:T(8,128)(2,1)S(1)} %get-tuple-element.245), channel_id=1, source_target_pairs={{0,1},{1,0},{2,3},{3,2},{4,5},{5,4},{6,7},{7,6},{8,9},{9,8},{10,11... | collective-permute-start | bytes 786440 | tf_op jit(solution)/shard_map/ppermute | solution.py:415
  85.4 21.4 %collective-permute-start.13 = (bf16[128,1024]{1,0:T(8,128)(2,1)S(1)}, bf16[128,1024]{1,0:T(8,128)(2,1)S(1)}, u32[]{:S(2)}, u32[]{:S(2)}) collective-permute-start(bf16[128,1024]{1,0:T(8,128)(2,1)S(1)} %get-tuple-element.246), channel_id=1, source_target_pairs={{0,2},{1,3},{2,0},{3,1},{4,6},{5,7},{6,4},{7,5},{8,10},{9,11},{10,... | collective-permute-start | bytes 786440 | tf_op jit(solution)/shard_map/ppermute | solution.py:415
  87.2 19.5 %collective-permute-start.14 = (bf16[128,1024]{1,0:T(8,128)(2,1)S(1)}, bf16[128,1024]{1,0:T(8,128)(2,1)S(1)}, u32[]{:S(2)}, u32[]{:S(2)}) collective-permute-start(bf16[128,1024]{1,0:T(8,128)(2,1)S(1)} %get-tuple-element.247), channel_id=1, source_target_pairs={{0,3},{1,2},{2,1},{3,0},{4,7},{5,6},{6,5},{7,4},{8,11},{9,10},{10,... | collective-permute-start | bytes 786440 | tf_op jit(solution)/shard_map/ppermute | solution.py:415
  110.6 22.1 %collective-permute-start.18 = (bf16[4,3,704,128]{3,2,1,0:T(8,128)(2,1)S(1)}, bf16[4,3,704,128]{3,2,1,0:T(8,128)(2,1)S(1)}, u32[]{:S(2)}, u32[]{:S(2)}) collective-permute-start(bf16[4,3,704,128]{3,2,1,0:T(8,128)(2,1)S(1)} %get-tuple-element.272), channel_id=1, source_target_pairs={{0,4},{4,0},{8,12},{12,8},{16,20},{20,16},{24,28},{28,24},{1,5},{5... | collective-permute-start | bytes 6488072 | tf_op jit(solution)/shard_map/ppermute | solution.py:428
  110.6 13.5 %collective-permute-start.15 = (bf16[128,768]{1,0:T(8,128)(2,1)S(1)}, bf16[128,768]{1,0:T(8,128)(2,1)S(1)}, u32[]{:S(2)}, u32[]{:S(2)}) collective-permute-start(bf16[128,768]{1,0:T(8,128)(2,1)S(1)} %get-tuple-element.268), channel_id=1, source_target_pairs={{0,1},{1,0},{2,3},{3,2},{4,5},{5,4},{6,7},{7,6},{8,9},{9,8},{10,11... | collective-permute-start | bytes 589832 | tf_op jit(solution)/shard_map/ppermute | solution.py:415
  115.5 17.1 %collective-permute-start.16 = (bf16[128,768]{1,0:T(8,128)(2,1)S(1)}, bf16[128,768]{1,0:T(8,128)(2,1)S(1)}, u32[]{:S(2)}, u32[]{:S(2)}) collective-permute-start(bf16[128,768]{1,0:T(8,128)(2,1)S(1)} %get-tuple-element.269), channel_id=1, source_target_pairs={{0,2},{1,3},{2,0},{3,1},{4,6},{5,7},{6,4},{7,5},{8,10},{9,11},{10,... | collective-permute-start | bytes 589832 | tf_op jit(solution)/shard_map/ppermute | solution.py:415
  115.5 17.1 %collective-permute-start.17 = (bf16[128,768]{1,0:T(8,128)(2,1)S(1)}, bf16[128,768]{1,0:T(8,128)(2,1)S(1)}, u32[]{:S(2)}, u32[]{:S(2)}) collective-permute-start(bf16[128,768]{1,0:T(8,128)(2,1)S(1)} %get-tuple-element.270), channel_id=1, source_target_pairs={{0,3},{1,2},{2,1},{3,0},{4,7},{5,6},{6,5},{7,4},{8,11},{9,10},{10,... | collective-permute-start | bytes 589832 | tf_op jit(solution)/shard_map/ppermute | solution.py:415
  134.4 23.3 %collective-permute-start.19 = (bf16[2,3,704,128]{3,2,1,0:T(8,128)(2,1)}, bf16[2,3,704,128]{3,2,1,0:T(8,128)(2,1)}, u32[]{:S(2)}, u32[]{:S(2)}) collective-permute-start(bf16[2,3,704,128]{3,2,1,0:T(8,128)(2,1)} %get-tuple-element.396), channel_id=1, source_target_pairs={{0,8},{4,20},{8,0},{12,28},{16,24},{20,4},{24,16},{28,12},{1,9},{5... | collective-permute-start | bytes 3244040 | tf_op jit(solution)/shard_map/ppermute | solution.py:435
  134.9 22.8 %collective-permute-start.20 = (bf16[128,1024]{1,0:T(8,128)(2,1)}, bf16[128,1024]{1,0:T(8,128)(2,1)}, u32[]{:S(2)}, u32[]{:S(2)}) collective-permute-start(bf16[128,1024]{1,0:T(8,128)(2,1)} %get-tuple-element.288), channel_id=1, source_target_pairs={{0,2},{1,3},{2,0},{3,1},{4,6},{5,7},{6,4},{7,5},{8,10},{9,11},{10,... | collective-permute-start | bytes 786440 | tf_op jit(solution)/shard_map/ppermute | solution.py:415
  170.1 19.8 %collective-permute-start.22 = (bf16[2,5,128,256]{3,2,1,0:T(8,128)(2,1)S(1)}, bf16[2,5,128,256]{3,2,1,0:T(8,128)(2,1)S(1)}, u32[]{:S(2)}, u32[]{:S(2)}) collective-permute-start(bf16[2,5,128,256]{3,2,1,0:T(8,128)(2,1)S(1)} %get-tuple-element.308), channel_id=1, source_target_pairs={{0,8},{4,20},{8,0},{12,28},{16,24},{20,4},{24,16},{28,12},{1,9},{5... | collective-permute-start | bytes 1966088 | tf_op jit(solution)/shard_map/ppermute | solution.py:435
  171.0 18.9 %collective-permute-start.26 = (bf16[1,3,704,128]{3,2,1,0:T(8,128)(2,1)S(1)}, bf16[1,3,704,128]{3,2,1,0:T(8,128)(2,1)S(1)}, u32[]{:S(2)}, u32[]{:S(2)}) collective-permute-start(bf16[1,3,704,128]{3,2,1,0:T(8,128)(2,1)S(1)} %slice_add_fusion.4), channel_id=1, source_target_pairs={{0,16},{4,12},{8,24},{12,4},{16,0},{20,28},{24,8},{28,20},{1,17},{... | collective-permute-start | bytes 1622024 | tf_op jit(solution)/shard_map/ppermute | solution.py:435
  172.2 9.9 %collective-permute-start.23 = (bf16[128,768]{1,0:T(8,128)(2,1)S(1)}, bf16[128,768]{1,0:T(8,128)(2,1)S(1)}, u32[]{:S(2)}, u32[]{:S(2)}) collective-permute-start(bf16[128,768]{1,0:T(8,128)(2,1)S(1)} %get-tuple-element.310), channel_id=1, source_target_pairs={{0,1},{1,0},{2,3},{3,2},{4,5},{5,4},{6,7},{7,6},{8,9},{9,8},{10,11... | collective-permute-start | bytes 589832 | tf_op jit(solution)/shard_map/ppermute | solution.py:415
  172.8 17.1 %collective-permute-start.24 = (bf16[128,768]{1,0:T(8,128)(2,1)S(1)}, bf16[128,768]{1,0:T(8,128)(2,1)S(1)}, u32[]{:S(2)}, u32[]{:S(2)}) collective-permute-start(bf16[128,768]{1,0:T(8,128)(2,1)S(1)} %get-tuple-element.311), channel_id=1, source_target_pairs={{0,2},{1,3},{2,0},{3,1},{4,6},{5,7},{6,4},{7,5},{8,10},{9,11},{10,... | collective-permute-start | bytes 589832 | tf_op jit(solution)/shard_map/ppermute | solution.py:415
  175.2 14.7 %collective-permute-start.25 = (bf16[128,768]{1,0:T(8,128)(2,1)S(1)}, bf16[128,768]{1,0:T(8,128)(2,1)S(1)}, u32[]{:S(2)}, u32[]{:S(2)}) collective-permute-start(bf16[128,768]{1,0:T(8,128)(2,1)S(1)} %get-tuple-element.312), channel_id=1, source_target_pairs={{0,3},{1,2},{2,1},{3,0},{4,7},{5,6},{6,5},{7,4},{8,11},{9,10},{10,... | collective-permute-start | bytes 589832 | tf_op jit(solution)/shard_map/ppermute | solution.py:415
  190.0 10.6 %collective-permute-start.27 = (bf16[1,5,128,256]{3,2,1,0:T(8,128)(2,1)S(1)}, bf16[1,5,128,256]{3,2,1,0:T(8,128)(2,1)S(1)}, u32[]{:S(2)}, u32[]{:S(2)}) collective-permute-start(bf16[1,5,128,256]{3,2,1,0:T(8,128)(2,1)S(1)} %slice_add_fusion.5), channel_id=1, source_target_pairs={{0,16},{4,12},{8,24},{12,4},{16,0},{20,28},{24,8},{28,20},{1,17},{... | collective-permute-start | bytes 983048 | tf_op jit(solution)/shard_map/ppermute | solution.py:435
  193.0 18.8 %collective-permute-start.32 = (bf16[3,704,128]{2,1,0:T(8,128)(2,1)S(1)}, bf16[3,704,128]{2,1,0:T(8,128)(2,1)S(1)}, u32[]{:S(2)}, u32[]{:S(2)}) collective-permute-start(bf16[3,704,128]{2,1,0:T(8,128)(2,1)S(1)} %add_bitcast_fusion.refs_0_), channel_id=1, source_target_pairs={{0,8},{4,20},{8,0},{12,28},{16,24},{20,4},{24,16},{28,12},{1,9},{5... | collective-permute-start | bytes 1622024 | tf_op jit(solution)/shard_map/ppermute | solution.py:435
  193.5 18.4 %collective-permute-start.31 = (bf16[3,704,128]{2,1,0:T(8,128)(2,1)S(1)}, bf16[3,704,128]{2,1,0:T(8,128)(2,1)S(1)}, u32[]{:S(2)}, u32[]{:S(2)}) collective-permute-start(bf16[3,704,128]{2,1,0:T(8,128)(2,1)S(1)} %add_bitcast_fusion.refs_0_), channel_id=1, source_target_pairs={{0,16},{4,12},{8,24},{12,4},{16,0},{20,28},{24,8},{28,20},{1,17},{... | collective-permute-start | bytes 1622024 | tf_op jit(solution)/shard_map/ppermute | solution.py:435
  200.7 6.9 %collective-permute-start.30 = (bf16[2,128,256]{2,1,0:T(8,128)(2,1)S(1)}, bf16[2,128,256]{2,1,0:T(8,128)(2,1)S(1)}, u32[]{:S(2)}, u32[]{:S(2)}) collective-permute-start(bf16[2,128,256]{2,1,0:T(8,128)(2,1)S(1)} %get-tuple-element.401), channel_id=1, source_target_pairs={{0,3},{1,2},{2,1},{3,0},{4,7},{5,6},{6,5},{7,4},{8,11},{9,10},{10,... | collective-permute-start | bytes 393224 | tf_op jit(solution)/shard_map/ppermute | solution.py:415
  202.6 9.1 %collective-permute-start.29 = (bf16[2,128,256]{2,1,0:T(8,128)(2,1)S(1)}, bf16[2,128,256]{2,1,0:T(8,128)(2,1)S(1)}, u32[]{:S(2)}, u32[]{:S(2)}) collective-permute-start(bf16[2,128,256]{2,1,0:T(8,128)(2,1)S(1)} %get-tuple-element.401), channel_id=1, source_target_pairs={{0,2},{1,3},{2,0},{3,1},{4,6},{5,7},{6,4},{7,5},{8,10},{9,11},{10,... | collective-permute-start | bytes 393224 | tf_op jit(solution)/shard_map/ppermute | solution.py:415
  205.1 6.7 %collective-permute-start.28 = (bf16[2,128,256]{2,1,0:T(8,128)(2,1)S(1)}, bf16[2,128,256]{2,1,0:T(8,128)(2,1)S(1)}, u32[]{:S(2)}, u32[]{:S(2)}) collective-permute-start(bf16[2,128,256]{2,1,0:T(8,128)(2,1)S(1)} %get-tuple-element.401), channel_id=1, source_target_pairs={{0,1},{1,0},{2,3},{3,2},{4,5},{5,4},{6,7},{7,6},{8,9},{9,8},{10,11... | collective-permute-start | bytes 393224 | tf_op jit(solution)/shard_map/ppermute | solution.py:415
  211.9 14.9 %collective-permute-start.36 = (bf16[4,2,128,256]{3,2,1,0:T(8,128)(2,1)S(1)}, bf16[4,2,128,256]{3,2,1,0:T(8,128)(2,1)S(1)}, u32[]{:S(2)}, u32[]{:S(2)}) collective-permute-start(bf16[4,2,128,256]{3,2,1,0:T(8,128)(2,1)S(1)} %pad_maximum_fusion.1.refs_0_), channel_id=1, source_target_pairs={{0,16},{4,12},{8,24},{12,4},{16,0},{20,28},{24,8},{28,20},{1,17},{... | collective-permute-start | bytes 1572872 | tf_op jit(solution)/shard_map/ppermute | solution.py:435
  213.9 26.6 %collective-permute-start.39 = (bf16[3,704,128]{2,1,0:T(8,128)(2,1)S(1)}, bf16[3,704,128]{2,1,0:T(8,128)(2,1)S(1)}, u32[]{:S(2)}, u32[]{:S(2)}) collective-permute-start(bf16[3,704,128]{2,1,0:T(8,128)(2,1)S(1)} %collective-permute-done.31.refs_1_), channel_id=1, source_target_pairs={{0,8},{4,20},{8,0},{12,28},{16,24},{20,4},{24,16},{28,12},{1,9},{5... | collective-permute-start | bytes 1622024 | tf_op jit(solution)/shard_map/ppermute | solution.py:435
  214.0 15.8 %collective-permute-start.33 = (bf16[3,128,256]{2,1,0:T(8,128)(2,1)S(1)}, bf16[3,128,256]{2,1,0:T(8,128)(2,1)S(1)}, u32[]{:S(2)}, u32[]{:S(2)}) collective-permute-start(bf16[3,128,256]{2,1,0:T(8,128)(2,1)S(1)} %slice_bitcast_fusion), channel_id=1, source_target_pairs={{0,1},{1,0},{2,3},{3,2},{4,5},{5,4},{6,7},{7,6},{8,9},{9,8},{10,11... | collective-permute-start | bytes 589832 | tf_op jit(solution)/shard_map/ppermute | solution.py:415
  214.1 26.4 %collective-permute-start.37 = (bf16[4,2,128,256]{3,2,1,0:T(8,128)(2,1)S(1)}, bf16[4,2,128,256]{3,2,1,0:T(8,128)(2,1)S(1)}, u32[]{:S(2)}, u32[]{:S(2)}) collective-permute-start(bf16[4,2,128,256]{3,2,1,0:T(8,128)(2,1)S(1)} %pad_maximum_fusion.1.refs_0_), channel_id=1, source_target_pairs={{0,8},{4,20},{8,0},{12,28},{16,24},{20,4},{24,16},{28,12},{1,9},{5... | collective-permute-start | bytes 1572872 | tf_op jit(solution)/shard_map/ppermute | solution.py:435
  226.7 13.8 %collective-permute-start.38 = (bf16[4,2,128,256]{3,2,1,0:T(8,128)(2,1)S(1)}, bf16[4,2,128,256]{3,2,1,0:T(8,128)(2,1)S(1)}, u32[]{:S(2)}, u32[]{:S(2)}) collective-permute-start(bf16[4,2,128,256]{3,2,1,0:T(8,128)(2,1)S(1)} %collective-permute-done.36.refs_1_), channel_id=1, source_target_pairs={{0,8},{4,20},{8,0},{12,28},{16,24},{20,4},{24,16},{28,12},{1,9},{5... | collective-permute-start | bytes 1572872 | tf_op jit(solution)/shard_map/ppermute | solution.py:435
  228.7 7.6 %collective-permute-start.35 = (bf16[3,128,256]{2,1,0:T(8,128)(2,1)S(1)}, bf16[3,128,256]{2,1,0:T(8,128)(2,1)S(1)}, u32[]{:S(2)}, u32[]{:S(2)}) collective-permute-start(bf16[3,128,256]{2,1,0:T(8,128)(2,1)S(1)} %slice_bitcast_fusion), channel_id=1, source_target_pairs={{0,3},{1,2},{2,1},{3,0},{4,7},{5,6},{6,5},{7,4},{8,11},{9,10},{10,... | collective-permute-start | bytes 589832 | tf_op jit(solution)/shard_map/ppermute | solution.py:415
  229.9 10.6 %collective-permute-start.34 = (bf16[3,128,256]{2,1,0:T(8,128)(2,1)S(1)}, bf16[3,128,256]{2,1,0:T(8,128)(2,1)S(1)}, u32[]{:S(2)}, u32[]{:S(2)}) collective-permute-start(bf16[3,128,256]{2,1,0:T(8,128)(2,1)S(1)} %slice_bitcast_fusion), channel_id=1, source_target_pairs={{0,2},{1,3},{2,0},{3,1},{4,6},{5,7},{6,4},{7,5},{8,10},{9,11},{10,... | collective-permute-start | bytes 589832 | tf_op jit(solution)/shard_map/ppermute | solution.py:415
  243.3 19.6 %collective-permute-start.41 = (bf16[4,3,128,256]{3,2,1,0:T(8,128)(2,1)S(1)}, bf16[4,3,128,256]{3,2,1,0:T(8,128)(2,1)S(1)}, u32[]{:S(2)}, u32[]{:S(2)}) collective-permute-start(bf16[4,3,128,256]{3,2,1,0:T(8,128)(2,1)S(1)} %pad_maximum_fusion.refs_0_), channel_id=1, source_target_pairs={{0,8},{4,20},{8,0},{12,28},{16,24},{20,4},{24,16},{28,12},{1,9},{5... | collective-permute-start | bytes 2359304 | tf_op jit(solution)/shard_map/ppermute | solution.py:435
  243.3 19.6 %collective-permute-start.40 = (bf16[4,3,128,256]{3,2,1,0:T(8,128)(2,1)S(1)}, bf16[4,3,128,256]{3,2,1,0:T(8,128)(2,1)S(1)}, u32[]{:S(2)}, u32[]{:S(2)}) collective-permute-start(bf16[4,3,128,256]{3,2,1,0:T(8,128)(2,1)S(1)} %pad_maximum_fusion.refs_0_), channel_id=1, source_target_pairs={{0,16},{4,12},{8,24},{12,4},{16,0},{20,28},{24,8},{28,20},{1,17},{... | collective-permute-start | bytes 2359304 | tf_op jit(solution)/shard_map/ppermute | solution.py:435
  245.3 9.8 %collective-permute-start.47 = (bf16[4,2,128,256]{3,2,1,0:T(8,128)(2,1)S(1)}, bf16[4,2,128,256]{3,2,1,0:T(8,128)(2,1)S(1)}, u32[]{:S(2)}, u32[]{:S(2)}) collective-permute-start(bf16[4,2,128,256]{3,2,1,0:T(8,128)(2,1)S(1)} %collective-permute-done.36.refs_1_), channel_id=1, source_target_pairs={{0,4},{4,0},{8,12},{12,8},{16,20},{20,16},{24,28},{28,24},{1,5},{5... | collective-permute-start | bytes 1572872 | tf_op jit(solution)/shard_map/ppermute | solution.py:428
  245.3 9.8 %collective-permute-start.48 = (bf16[4,2,128,256]{3,2,1,0:T(8,128)(2,1)S(1)}, bf16[4,2,128,256]{3,2,1,0:T(8,128)(2,1)S(1)}, u32[]{:S(2)}, u32[]{:S(2)}) collective-permute-start(bf16[4,2,128,256]{3,2,1,0:T(8,128)(2,1)S(1)} %collective-permute-done.37.refs_2_), channel_id=1, source_target_pairs={{0,4},{4,0},{8,12},{12,8},{16,20},{20,16},{24,28},{28,24},{1,5},{5... | collective-permute-start | bytes 1572872 | tf_op jit(solution)/shard_map/ppermute | solution.py:428
  245.9 9.3 %collective-permute-start.49 = (bf16[4,2,128,256]{3,2,1,0:T(8,128)(2,1)S(1)}, bf16[4,2,128,256]{3,2,1,0:T(8,128)(2,1)S(1)}, u32[]{:S(2)}, u32[]{:S(2)}) collective-permute-start(bf16[4,2,128,256]{3,2,1,0:T(8,128)(2,1)S(1)} %collective-permute-done.38.refs_3_), channel_id=1, source_target_pairs={{0,4},{4,0},{8,12},{12,8},{16,20},{20,16},{24,28},{28,24},{1,5},{5... | collective-permute-start | bytes 1572872 | tf_op jit(solution)/shard_map/ppermute | solution.py:428
  262.9 15.7 %collective-permute-start.50 = (bf16[4,3,128,256]{3,2,1,0:T(8,128)(2,1)S(1)}, bf16[4,3,128,256]{3,2,1,0:T(8,128)(2,1)S(1)}, u32[]{:S(2)}, u32[]{:S(2)}) collective-permute-start(bf16[4,3,128,256]{3,2,1,0:T(8,128)(2,1)S(1)} %collective-permute-done.40.refs_1_), channel_id=1, source_target_pairs={{0,8},{4,20},{8,0},{12,28},{16,24},{20,4},{24,16},{28,12},{1,9},{5... | collective-permute-start | bytes 2359304 | tf_op jit(solution)/shard_map/ppermute | solution.py:435
  263.2 11.0 %collective-permute-start.51 = (bf16[128,1024]{1,0:T(8,128)(2,1)S(1)}, bf16[128,1024]{1,0:T(8,128)(2,1)S(1)}, u32[]{:S(2)}, u32[]{:S(2)}) collective-permute-start(bf16[128,1024]{1,0:T(8,128)(2,1)S(1)} %copy-done.54), channel_id=1, source_target_pairs={{0,3},{1,2},{2,1},{3,0},{4,7},{5,6},{6,5},{7,4},{8,11},{9,10},{10,... | collective-permute-start | bytes 786440 | tf_op jit(solution)/shard_map/ppermute | solution.py:415
  265.8 12.8 %collective-permute-start.52 = (bf16[128,1024]{1,0:T(8,128)(2,1)S(1)}, bf16[128,1024]{1,0:T(8,128)(2,1)S(1)}, u32[]{:S(2)}, u32[]{:S(2)}) collective-permute-start(bf16[128,1024]{1,0:T(8,128)(2,1)S(1)} %copy-done.52), channel_id=1, source_target_pairs={{0,1},{1,0},{2,3},{3,2},{4,5},{5,4},{6,7},{7,6},{8,9},{9,8},{10,11... | collective-permute-start | bytes 786440 | tf_op jit(solution)/shard_map/ppermute | solution.py:415
  278.6 4.6 %collective-permute-start.53 = (bf16[4,3,128,256]{3,2,1,0:T(8,128)(2,1)S(1)}, bf16[4,3,128,256]{3,2,1,0:T(8,128)(2,1)S(1)}, u32[]{:S(2)}, u32[]{:S(2)}) collective-permute-start(bf16[4,3,128,256]{3,2,1,0:T(8,128)(2,1)S(1)} %pad_maximum_fusion.refs_0_), channel_id=1, source_target_pairs={{0,4},{4,0},{8,12},{12,8},{16,20},{20,16},{24,28},{28,24},{1,5},{5... | collective-permute-start | bytes 2359304 | tf_op jit(solution)/shard_map/ppermute | solution.py:428
  279.3 5.1 %collective-permute-start.56 = (bf16[4,3,128,256]{3,2,1,0:T(8,128)(2,1)S(1)}, bf16[4,3,128,256]{3,2,1,0:T(8,128)(2,1)S(1)}, u32[]{:S(2)}, u32[]{:S(2)}) collective-permute-start(bf16[4,3,128,256]{3,2,1,0:T(8,128)(2,1)S(1)} %collective-permute-done.50.refs_0_), channel_id=1, source_target_pairs={{0,4},{4,0},{8,12},{12,8},{16,20},{20,16},{24,28},{28,24},{1,5},{5... | collective-permute-start | bytes 2359304 | tf_op jit(solution)/shard_map/ppermute | solution.py:428
  (72 other events, 812.6 us)
